TPU v7x, 256 devices: a whole 4x4x8 slice. The times are simulated.
256 devices in a mesh: lat: 8 (over z), lon: 32 (over y, x, core).
Axes of the slice: x: 4, y: 4, z: 8, core: 2. Of those that a mesh axis runs over, the one named last changes fastest.
Arguments:
- corona: float32 [8, 128, 512, 128], P(None, 'lat', 'lon'), may hold values from -6 to 6
- kappa: float32 [128, 512, 128], P('lat', 'lon'), may hold values from 0.05 to 1
- mixing: float32 [8, 8], replicated, may hold values from -2 to 2
- helio_prev: float32 [8, 1024, 1024], P(None, 'lon', 'lat'), may hold values from -6 to 6
- owner: int32 [524288, 1], P(('lat', 'lon')), may hold values from 0 to 255; in each aligned block of 2048 rows (0 to 2047, 2048 to 4095, ...) at most 16 rows name the same one
- dest_cell: int32 [524288], P(('lat', 'lon')), may hold values from 0 to 4095
- corner_base: int32 [524288], P(('lat', 'lon')), may hold values from 0 to 1910, as said below
- fractions: float32 [3, 524288], P(None, ('lat', 'lon')), may hold values from 0 to 1
Outputs:
- stepped: float32 [8, 128, 512, 128], P(None, 'lat', 'lon')
- helio_face: float32 [8, 1024, 1024], P(None, 'lon', 'lat')
Inputs may be any that keep to these rules, and one draw needn't show every extreme that they name: Among the targets of one device no owner appears more than 16 times, a bound that some block reaches. corner_base = (t * 16 + p) * 8 + r with t < 15, p < 15, r < 7.
All inputs are finite; a program needn't handle non-finite values.
Results may differ from a plain program's by a relative error of at most 0.000075.
Values sent between devices are 32-bit elements; how exact they have to be, the bound alone decides.
No kernel may reach another device: no remote copies, remote signals or barrier semaphores. Data moves between devices by JAX's collectives and lax.ppermute only.
A program may use at most 64 MiB of HBM per device.

v0:
```python
import jax
import jax.numpy as jnp
from jax import lax
from jax.sharding import PartitionSpec as P

SH = 8


def extended(block, sides, width):
    for axis, dim in sides:
        count = lax.axis_size(axis)
        forward = [(i, i + 1) for i in range(count - 1)]
        backward = [(target, source) for source, target in forward]
        low = lax.ppermute(
            lax.slice_in_dim(block, block.shape[dim] - width, None, axis=dim), axis, forward
        )
        high = lax.ppermute(lax.slice_in_dim(block, 0, width, axis=dim), axis, backward)
        block = jnp.concatenate([low, block, high], axis=dim)
    return block


def shift_last(array, step):
    zero_col = jnp.zeros(array.shape[:-1] + (1,), array.dtype)
    if step > 0:
        return jnp.concatenate([array[..., 1:], zero_col], axis=-1)
    return jnp.concatenate([zero_col, array[..., :-1]], axis=-1)


def flux_step(field, cond, mixing):
    center = field[:, 1:-1, 1:-1, :]
    cond_c = cond[1:-1, 1:-1, :]
    pairs = [
        (field[:, 2:, 1:-1, :], cond[2:, 1:-1, :]),
        (field[:, :-2, 1:-1, :], cond[:-2, 1:-1, :]),
        (field[:, 1:-1, 2:, :], cond[1:-1, 2:, :]),
        (field[:, 1:-1, :-2, :], cond[1:-1, :-2, :]),
        (shift_last(center, 1), shift_last(cond_c, 1)),
        (shift_last(center, -1), shift_last(cond_c, -1)),
    ]
    lapl = jnp.zeros_like(center)
    for near, cond_n in pairs:
        lapl = lapl + (0.5 * (cond_c + cond_n))[None] * (near - center)
    mixed = jnp.einsum("gf,fabr->gabr", mixing, center, precision=lax.Precision.HIGHEST)
    return center + 0.15 * lapl + 0.3 * mixed


def body(corona, kappa, mixing, helio_prev, owner, dest_cell, corner_base, fractions):
    fields, tile_t, tile_p, radial_n = corona.shape
    stacked = jnp.concatenate([corona, kappa[None]], axis=0)
    wide = extended(stacked, (("lat", 1), ("lon", 2)), 1)
    cond_wide = wide[fields]
    first = flux_step(wide[:fields], cond_wide, mixing)
    again = extended(first, (("lat", 1), ("lon", 2)), 1)
    stepped = flux_step(again, cond_wide, mixing)
    shell_cells = tile_t * tile_p * SH
    shell = stepped[:, :, :, radial_n - SH :].reshape(fields, shell_cells)
    count = corner_base.shape[0]
    blocksz = min(512, count)
    nblocks = count // blocksz
    cell_iota = jnp.arange(shell_cells, dtype=jnp.int32)
    base_blocks = corner_base.reshape(nblocks, blocksz)
    frac_blocks = jnp.transpose(fractions.reshape(3, nblocks, blocksz), (1, 0, 2))

    def interpolate(pair):
        base, frac = pair
        table = jnp.zeros((blocksz, shell_cells), jnp.float32)
        for a in range(2):
            for b in range(2):
                for c in range(2):
                    weight = (
                        (frac[0] if a else 1.0 - frac[0])
                        * (frac[1] if b else 1.0 - frac[1])
                        * (frac[2] if c else 1.0 - frac[2])
                    )
                    offset = (a * tile_p + b) * SH + c
                    table = table + jnp.where(
                        cell_iota[None, :] == (base + offset)[:, None], weight[:, None], 0.0
                    )
        return lax.dot_general(
            shell,
            table,
            (((1,), (1,)), ((), ())),
            precision=lax.Precision.HIGHEST,
            preferred_element_type=jnp.float32,
        )

    value_blocks = lax.map(interpolate, (base_blocks, frac_blocks))
    n_lat = lax.axis_size("lat")
    n_lon = lax.axis_size("lon")
    n_dev = n_lat * n_lon
    slots_each = 2 * count // n_dev
    n_slots = n_dev * slots_each
    dest_owner = owner[:, 0]
    hits = (dest_owner[:, None] == jnp.arange(n_dev, dtype=jnp.int32)[None, :]).astype(jnp.int32)
    rank = jnp.sum(jnp.cumsum(hits, axis=0) * hits, axis=1) - 1
    slot_blocks = (dest_owner * slots_each + rank).reshape(nblocks, blocksz)
    dest_blocks = (dest_cell + 1).astype(jnp.float32).reshape(nblocks, 1, blocksz)
    slot_iota = jnp.arange(n_slots, dtype=jnp.int32)

    def pack(total, items):
        vals, dests, slots = items
        placing = (slots[:, None] == slot_iota[None, :]).astype(jnp.float32)
        rows = jnp.concatenate([vals, dests], axis=0)
        return (
            total
            + jnp.dot(
                rows, placing, precision=lax.Precision.HIGHEST, preferred_element_type=jnp.float32
            ),
            None,
        )

    packed, _ = lax.scan(
        pack,
        jnp.zeros((fields + 1, n_slots), jnp.float32),
        (value_blocks, dest_blocks, slot_blocks),
    )
    face_p, face_t = (helio_prev.shape[1], helio_prev.shape[2])
    cells = face_p * face_t
    send_vals = packed[:fields]
    dest_plus = packed[fields].astype(jnp.int32)
    send_dest = jnp.where(dest_plus > 0, dest_plus - 1, cells)
    got_vals, got_dest = (
        lax.all_to_all(
            lax.all_to_all(
                send_vals.reshape(fields, n_lat, n_lon * slots_each),
                "lat",
                split_axis=1,
                concat_axis=1,
                tiled=True,
            ),
            "lon",
            split_axis=2,
            concat_axis=2,
            tiled=True,
        ),
        lax.all_to_all(
            lax.all_to_all(
                send_dest.reshape(1, n_lat, n_lon * slots_each),
                "lat",
                split_axis=1,
                concat_axis=1,
                tiled=True,
            ),
            "lon",
            split_axis=2,
            concat_axis=2,
            tiled=True,
        ),
    )
    recv_block = min(512, n_slots)
    recv_n = n_slots // recv_block
    recv_vals = jnp.transpose(got_vals, (1, 0, 2))
    recv_dest = got_dest.reshape(recv_n, recv_block)
    face_iota = jnp.arange(cells, dtype=jnp.int32)

    def land(total, items):
        vals, dests = items
        placing = (dests[:, None] == face_iota[None, :]).astype(jnp.float32)
        return (
            total
            + jnp.dot(
                vals, placing, precision=lax.Precision.HIGHEST, preferred_element_type=jnp.float32
            ),
            None,
        )

    added, _ = lax.scan(land, jnp.zeros((fields, cells), jnp.float32), (recv_vals, recv_dest))
    coupled = helio_prev + added.reshape(fields, face_p, face_t)
    ext = extended(coupled, (("lat", 2), ("lon", 1)), 1)
    helio_face = coupled + 0.2 * (
        ext[:, 2:, 1:-1] + ext[:, :-2, 1:-1] + ext[:, 1:-1, 2:] + ext[:, 1:-1, :-2] - 4.0 * coupled
    )
    return (stepped, helio_face)


def solution(mesh):
    return jax.shard_map(
        body,
        mesh=mesh,
        in_specs=(
            P(None, "lat", "lon", None),
            P("lat", "lon", None),
            P(),
            P(None, "lon", "lat"),
            P(("lat", "lon"), None),
            P(("lat", "lon")),
            P(("lat", "lon")),
            P(None, ("lat", "lon")),
        ),
        out_specs=(P(None, "lat", "lon", None), P(None, "lon", "lat")),
        check_vma=False,
    )
```

profile of v0, /device:TPU:8, one launch (start us, length us, event | category | flops | bytes accessed | tf_op | source)
XLA Modules:
  0.0 209.4 jit_solution(18127881031472281032)
XLA Ops:
  0.7 1.8 copy.84
  3.9 3.8 %collective-permute-start = (f32[9,1,16,128]{3,0,2,1:T(8,128)}, f32[9,1,16,128]{3,0,2,1:T(8,128)S(1)}, u32[]{:S(2)}, u32[]{:S(2)}) collective-permute-start(f32[9,1,16,128]{3,0,2,1:T(8,128)} %get-tuple-element.260), channel_id=1, source_target_pairs={{0,32},{32,64},{64,96},{96,128},{128,160},{160,192},{192,224},{1,3... | collective-permute-start | bytes 221192 | tf_op jit(solution)/shard_map/ppermute | solution.py:14
  15.0 1.9 collective-permute-start.2
  17.0 5.8 %collective-permute-start.3 = (f32[9,18,1,128]{3,0,2,1:T(8,128)S(1)}, f32[9,18,1,128]{3,0,2,1:T(8,128)S(1)}, u32[]{:S(2)}, u32[]{:S(2)}) collective-permute-start(f32[9,18,1,128]{3,0,2,1:T(8,128)S(1)} %get-tuple-element.256), channel_id=1, source_target_pairs={{1,0},{2,1},{3,2},{4,3},{5,4},{6,5},{7,6},{8,7},{9,8},{10,9},{11,1... | collective-permute-start | bytes 248840 | tf_op jit(solution)/shard_map/ppermute | solution.py:17
  26.1 3.4 %fusion.67 = f32[8,16,16,128]{3,0,2,1:T(8,128)S(1)} fusion(f32[8,16,16,128]{3,0,2,1:T(8,128)S(1)} %copy.84, f32[9,18,1,128]{3,0,2,1:T(8,128)} %copy-done.3, f32[9,1,16,128]{3,0,2,1:T(8,128)S(1)} %collective-permute-done.1, f32[9,1,16,128]{3,0,2,1:T(8,128)S(1)} %collective-permute-done, f32[1,16,16,128]{3,0,2,1:T(1,128)S(1)} %bitcast.99, ...), kind=kOutput, calls=%fused_computation.98 | convolution fusion | flops 33816576 | bytes 5409024 | tf_op jit(solution)/shard_map/gf,fabr->gabr/dot_general | solution.py:43
  31.1 4.5 %collective-permute-start.5 = (f32[8,1,16,128]{3,0,2,1:T(8,128)S(1)}, f32[8,1,16,128]{3,0,2,1:T(8,128)S(1)}, u32[]{:S(2)}, u32[]{:S(2)}) collective-permute-start(f32[8,1,16,128]{3,0,2,1:T(8,128)S(1)} %get-tuple-element.264), channel_id=1, source_target_pairs={{0,32},{32,64},{64,96},{96,128},{128,160},{160,192},{192,224},{1,3... | collective-permute-start | bytes 196616 | tf_op jit(solution)/shard_map/ppermute | solution.py:14
  37.5 5.0 %collective-permute-start.6 = (f32[8,18,1,128]{3,0,2,1:T(8,128)S(1)}, f32[8,18,1,128]{3,0,2,1:T(8,128)S(1)}, u32[]{:S(2)}, u32[]{:S(2)}) collective-permute-start(f32[8,18,1,128]{3,0,2,1:T(8,128)S(1)} %get-tuple-element.258), channel_id=1, source_target_pairs={{1,0},{2,1},{3,2},{4,3},{5,4},{6,5},{7,6},{8,7},{9,8},{10,9},{11,1... | collective-permute-start | bytes 221192 | tf_op jit(solution)/shard_map/ppermute | solution.py:17
  42.5 1.9 collective-permute-start.7
  44.8 5.5 %collective-permute-done.7 = f32[8,18,1,128]{3,0,2,1:T(8,128)S(1)} collective-permute-done((f32[8,18,1,128]{3,0,2,1:T(8,128)S(1)}, f32[8,18,1,128]{3,0,2,1:T(8,128)S(1)}, u32[]{:S(2)}, u32[]{:S(2)}) %collective-permute-start.7) | collective-permute-done | bytes 73760 | tf_op jit(solution)/shard_map/ppermute | solution.py:14
  50.3 1.8 fusion.66
  53.2 37.7 %while.34 = (s32[]{:T(128)}, f32[4,8,512]{2,1,0:T(8,128)S(1)}, s32[4,512]{1,0:T(4,128)}, f32[4,3,512]{2,1,0:T(4,128)}, f32[8,2048]{1,0:T(8,128)S(1)}, /*index=5*/s32[]{:T(128)}, s32[]{:T(128)}, s32[]{}, s32[]{}) while((s32[]{:T(128)}, f32[4,8,512]{2,1,0:T(8,128)S(1)}, s32[4,512]{1,0:T(4,128)}, f32[4,3,512]{2,1,0:T(4,128)}, ...), condition=%wide.region_1.2_spmd.clone.clone, body=%wide.region_0.1_spmd.clone.clone.sunk | while | flops 124791808 | bytes 8558729 | solution.py:87
  54.9 4.2 %fusion.134 = f32[512,2048]{1,0:T(8,128)S(1)} fusion(f32[512]{0:T(512)S(1)} %get-tuple-element.379, s32[512]{0:T(512)S(1)} %get-tuple-element.380, f32[512]{0:T(512)S(1)} %get-tuple-element.381, s32[512]{0:T(512)S(1)} %get-tuple-element.382, f32[512]{0:T(512)S(1)} %get-tuple-element.383, ...), kind=kLoop, calls=%fused_computation.12.clone.clone.clone.clone.clone.1.clone.1 | loop fusion | flops 24117248 | bytes 4227072 | tf_op jit(solution)/shard_map/while/body/eval_jaxpr/dot_general | solution.py:79
  59.1 3.6 %fusion.135 = f32[4,8,512]{2,1,0:T(8,128)S(1)} fusion(f32[4,8,512]{2,1,0:T(8,128)S(1)} %get-tuple-element.413, s32[]{:T(128)} %get-tuple-element.412, f32[8,2048]{1,0:T(8,128)S(1)} %get-tuple-element.425, f32[512,2048]{1,0:T(8,128)S(1)} %fusion.134), kind=kOutput, calls=%fused_computation.45.clone.2 | convolution fusion | flops 100663296 | bytes 4276228 | tf_op jit(solution)/shard_map/while/body/eval_jaxpr/dot_general | solution.py:79
  64.3 4.2 %fusion.134 = f32[512,2048]{1,0:T(8,128)S(1)} fusion(f32[512]{0:T(512)S(1)} %get-tuple-element.379, s32[512]{0:T(512)S(1)} %get-tuple-element.380, f32[512]{0:T(512)S(1)} %get-tuple-element.381, s32[512]{0:T(512)S(1)} %get-tuple-element.382, f32[512]{0:T(512)S(1)} %get-tuple-element.383, ...), kind=kLoop, calls=%fused_computation.12.clone.clone.clone.clone.clone.1.clone.1 | loop fusion | flops 24117248 | bytes 4227072 | tf_op jit(solution)/shard_map/while/body/eval_jaxpr/dot_general | solution.py:79
  68.5 3.6 %fusion.135 = f32[4,8,512]{2,1,0:T(8,128)S(1)} fusion(f32[4,8,512]{2,1,0:T(8,128)S(1)} %get-tuple-element.413, s32[]{:T(128)} %get-tuple-element.412, f32[8,2048]{1,0:T(8,128)S(1)} %get-tuple-element.425, f32[512,2048]{1,0:T(8,128)S(1)} %fusion.134), kind=kOutput, calls=%fused_computation.45.clone.2 | convolution fusion | flops 100663296 | bytes 4276228 | tf_op jit(solution)/shard_map/while/body/eval_jaxpr/dot_general | solution.py:79
  73.7 4.2 %fusion.134 = f32[512,2048]{1,0:T(8,128)S(1)} fusion(f32[512]{0:T(512)S(1)} %get-tuple-element.379, s32[512]{0:T(512)S(1)} %get-tuple-element.380, f32[512]{0:T(512)S(1)} %get-tuple-element.381, s32[512]{0:T(512)S(1)} %get-tuple-element.382, f32[512]{0:T(512)S(1)} %get-tuple-element.383, ...), kind=kLoop, calls=%fused_computation.12.clone.clone.clone.clone.clone.1.clone.1 | loop fusion | flops 24117248 | bytes 4227072 | tf_op jit(solution)/shard_map/while/body/eval_jaxpr/dot_general | solution.py:79
  77.9 3.6 %fusion.135 = f32[4,8,512]{2,1,0:T(8,128)S(1)} fusion(f32[4,8,512]{2,1,0:T(8,128)S(1)} %get-tuple-element.413, s32[]{:T(128)} %get-tuple-element.412, f32[8,2048]{1,0:T(8,128)S(1)} %get-tuple-element.425, f32[512,2048]{1,0:T(8,128)S(1)} %fusion.134), kind=kOutput, calls=%fused_computation.45.clone.2 | convolution fusion | flops 100663296 | bytes 4276228 | tf_op jit(solution)/shard_map/while/body/eval_jaxpr/dot_general | solution.py:79
  83.1 4.2 %fusion.134 = f32[512,2048]{1,0:T(8,128)S(1)} fusion(f32[512]{0:T(512)S(1)} %get-tuple-element.379, s32[512]{0:T(512)S(1)} %get-tuple-element.380, f32[512]{0:T(512)S(1)} %get-tuple-element.381, s32[512]{0:T(512)S(1)} %get-tuple-element.382, f32[512]{0:T(512)S(1)} %get-tuple-element.383, ...), kind=kLoop, calls=%fused_computation.12.clone.clone.clone.clone.clone.1.clone.1 | loop fusion | flops 24117248 | bytes 4227072 | tf_op jit(solution)/shard_map/while/body/eval_jaxpr/dot_general | solution.py:79
  87.3 3.6 %fusion.135 = f32[4,8,512]{2,1,0:T(8,128)S(1)} fusion(f32[4,8,512]{2,1,0:T(8,128)S(1)} %get-tuple-element.413, s32[]{:T(128)} %get-tuple-element.412, f32[8,2048]{1,0:T(8,128)S(1)} %get-tuple-element.425, f32[512,2048]{1,0:T(8,128)S(1)} %fusion.134), kind=kOutput, calls=%fused_computation.45.clone.2 | convolution fusion | flops 100663296 | bytes 4276228 | tf_op jit(solution)/shard_map/while/body/eval_jaxpr/dot_general | solution.py:79
  90.9 13.9 %while.35 = (s32[]{:T(128)}, f32[9,4096]{1,0:T(8,128)S(1)}, f32[4,8,512]{2,1,0:T(8,128)S(1)}, f32[4,1,512]{2,1,0:T(1,128)}, s32[4,512]{1,0:T(4,128)S(1)}, /*index=5*/s32[]{:T(128)}, s32[]{:T(128)}) while((s32[]{:T(128)}, f32[9,4096]{1,0:T(8,128)S(1)}, f32[4,8,512]{2,1,0:T(8,128)S(1)}, f32[4,1,512]{2,1,0:T(1,128)}, ...), condition=%wide.region_6.7_spmd.clone, body=%wide.region_5.6_spmd.clone.sunk | while | flops 228667904 | bytes 356451 | solution.py:112
  91.6 2.8 %fusion.137 = f32[9,4096]{1,0:T(8,128)S(1)} fusion(s32[512]{0:T(512)S(1)} %bitcast.110, f32[9,4096]{1,0:T(8,128)S(1)} %get-tuple-element.438, pred[]{:T(512)S(6)} %compare.12, f32[1,512]{1,0:T(1,128)S(1)} %dynamic-slice_bitcast_fusion.4, f32[8,512]{1,0:T(8,128)S(1)} %dynamic-slice_bitcast_fusion.5), kind=kOutput, calls=%fused_computation.71.clone.1 | convolution fusion | flops 228667904 | bytes 315393 | tf_op jit(solution)/shard_map/while/body/eval_jaxpr/dot_general | solution.py:106
  95.1 2.8 %fusion.137 = f32[9,4096]{1,0:T(8,128)S(1)} fusion(s32[512]{0:T(512)S(1)} %bitcast.110, f32[9,4096]{1,0:T(8,128)S(1)} %get-tuple-element.438, pred[]{:T(512)S(6)} %compare.12, f32[1,512]{1,0:T(1,128)S(1)} %dynamic-slice_bitcast_fusion.4, f32[8,512]{1,0:T(8,128)S(1)} %dynamic-slice_bitcast_fusion.5), kind=kOutput, calls=%fused_computation.71.clone.1 | convolution fusion | flops 228667904 | bytes 315393 | tf_op jit(solution)/shard_map/while/body/eval_jaxpr/dot_general | solution.py:106
  98.5 2.8 %fusion.137 = f32[9,4096]{1,0:T(8,128)S(1)} fusion(s32[512]{0:T(512)S(1)} %bitcast.110, f32[9,4096]{1,0:T(8,128)S(1)} %get-tuple-element.438, pred[]{:T(512)S(6)} %compare.12, f32[1,512]{1,0:T(1,128)S(1)} %dynamic-slice_bitcast_fusion.4, f32[8,512]{1,0:T(8,128)S(1)} %dynamic-slice_bitcast_fusion.5), kind=kOutput, calls=%fused_computation.71.clone.1 | convolution fusion | flops 228667904 | bytes 315393 | tf_op jit(solution)/shard_map/while/body/eval_jaxpr/dot_general | solution.py:106
  102.0 2.8 %fusion.137 = f32[9,4096]{1,0:T(8,128)S(1)} fusion(s32[512]{0:T(512)S(1)} %bitcast.110, f32[9,4096]{1,0:T(8,128)S(1)} %get-tuple-element.438, pred[]{:T(512)S(6)} %compare.12, f32[1,512]{1,0:T(1,128)S(1)} %dynamic-slice_bitcast_fusion.4, f32[8,512]{1,0:T(8,128)S(1)} %dynamic-slice_bitcast_fusion.5), kind=kOutput, calls=%fused_computation.71.clone.1 | convolution fusion | flops 228667904 | bytes 315393 | tf_op jit(solution)/shard_map/while/body/eval_jaxpr/dot_general | solution.py:106
  105.4 11.9 %all-to-all-start.2 = ((s32[1,8,512]{2,0,1:T(1,128)}), s32[1,8,512]{2,0,1:T(1,128)S(1)}, u32[]{:S(2)}, u32[]{:S(2)}) async-start(s32[1,8,512]{2,0,1:T(1,128)} %bitcast.15), calls=%async_computation.2 | async-start | bytes 32768 | tf_op jit(solution)/shard_map/all_to_all | solution.py:137
  118.0 7.1 %all-to-all-done.2 = s32[1,8,512]{2,0,1:T(1,128)S(1)} async-done(((s32[1,8,512]{2,0,1:T(1,128)}), s32[1,8,512]{2,0,1:T(1,128)S(1)}, u32[]{:S(2)}, u32[]{:S(2)}) %all-to-all-start.2) | async-done | bytes 16416 | tf_op jit(solution)/shard_map/all_to_all | solution.py:137
  125.1 3.4 %all-to-all-start = ((f32[8,8,512]{2,0,1:T(8,128)}), f32[8,8,512]{2,0,1:T(8,128)S(1)}, u32[]{:S(2)}, u32[]{:S(2)}) async-start(f32[8,8,512]{2,0,1:T(8,128)} %bitcast.13), calls=%async_computation | async-start | bytes 262144 | tf_op jit(solution)/shard_map/all_to_all | solution.py:124
  131.1 6.4 %all-to-all-done = f32[8,8,512]{2,0,1:T(8,128)S(1)} async-done(((f32[8,8,512]{2,0,1:T(8,128)}), f32[8,8,512]{2,0,1:T(8,128)S(1)}, u32[]{:S(2)}, u32[]{:S(2)}) %all-to-all-start) | async-done | bytes 131104 | tf_op jit(solution)/shard_map/all_to_all | solution.py:124
  137.5 5.1 %all-to-all-start.3 = ((s32[32,1,128]{2,1,0:T(1,128)}), s32[32,1,128]{2,1,0:T(1,128)S(1)}, u32[]{:S(2)}, u32[]{:S(2)}) async-start(s32[32,1,128]{2,1,0:T(1,128)} %reshape.247), calls=%async_computation.3 | async-start | bytes 32768 | tf_op jit(solution)/shard_map/all_to_all | solution.py:136
  145.0 3.6 %all-to-all-done.3 = s32[32,1,128]{2,1,0:T(1,128)S(1)} async-done(((s32[32,1,128]{2,1,0:T(1,128)}), s32[32,1,128]{2,1,0:T(1,128)S(1)}, u32[]{:S(2)}, u32[]{:S(2)}) %all-to-all-start.3) | async-done | bytes 16416 | tf_op jit(solution)/shard_map/all_to_all | solution.py:136
  148.6 5.0 %all-to-all-start.1 = ((f32[32,1,1024]{2,1,0:T(1,128)}), f32[32,1,1024]{2,1,0:T(1,128)S(1)}, u32[]{:S(2)}, u32[]{:S(2)}) async-start(f32[32,1,1024]{2,1,0:T(1,128)} %reshape.245), calls=%async_computation.1 | async-start | bytes 262144 | tf_op jit(solution)/shard_map/all_to_all | solution.py:123
  154.8 5.5 %all-to-all-done.1 = f32[32,1,1024]{2,1,0:T(1,128)S(1)} async-done(((f32[32,1,1024]{2,1,0:T(1,128)}), f32[32,1,1024]{2,1,0:T(1,128)S(1)}, u32[]{:S(2)}, u32[]{:S(2)}) %all-to-all-start.1) | async-done | bytes 131104 | tf_op jit(solution)/shard_map/all_to_all | solution.py:123
  164.4 2.2 %copy.92 = f32[8,8,512]{2,1,0:T(8,128)S(1)} copy(f32[8,8,512]{1,0,2:T(8,128)} %bitcast_bitcast_fusion) | data formatting | bytes 262144
  166.6 22.3 %while.36 = (s32[]{:T(128)}, f32[8,4096]{1,0:T(8,128)S(1)}, f32[8,8,512]{2,1,0:T(8,128)S(1)}, s32[8,512]{1,0:T(8,128)S(1)}, s32[]{:T(128)}, /*index=5*/s32[]{:T(128)}) while((s32[]{:T(128)}, f32[8,4096]{1,0:T(8,128)S(1)}, f32[8,8,512]{2,1,0:T(8,128)S(1)}, s32[8,512]{1,0:T(8,128)S(1)}, s32[]{:T(128)}, /*index=5*/s32[]{:T(128)}) %tuple.111), condition=%wide.region_8.9_spmd.clone, body=%wide.region_7.8_spmd.clone.sunk | while | flops 203489280 | bytes 284759 | solution.py:167
  166.6 2.8 %fusion.139 = f32[8,4096]{1,0:T(8,128)S(1)} fusion(s32[512]{0:T(512)S(1)} %bitcast.111, f32[8,4096]{1,0:T(8,128)S(1)} %get-tuple-element.458, pred[]{:T(512)S(6)} %compare.13, f32[8,8,512]{2,1,0:T(8,128)S(1)} %get-tuple-element.465, s32[]{:T(128)} %get-tuple-element.457), kind=kOutput, calls=%fused_computation.82.clone.1 | convolution fusion | flops 203489280 | bytes 280581 | tf_op jit(solution)/shard_map/while/body/eval_jaxpr/dot_general | solution.py:161
  169.4 2.8 %fusion.139 = f32[8,4096]{1,0:T(8,128)S(1)} fusion(s32[512]{0:T(512)S(1)} %bitcast.111, f32[8,4096]{1,0:T(8,128)S(1)} %get-tuple-element.458, pred[]{:T(512)S(6)} %compare.13, f32[8,8,512]{2,1,0:T(8,128)S(1)} %get-tuple-element.465, s32[]{:T(128)} %get-tuple-element.457), kind=kOutput, calls=%fused_computation.82.clone.1 | convolution fusion | flops 203489280 | bytes 280581 | tf_op jit(solution)/shard_map/while/body/eval_jaxpr/dot_general | solution.py:161
  172.2 2.8 %fusion.139 = f32[8,4096]{1,0:T(8,128)S(1)} fusion(s32[512]{0:T(512)S(1)} %bitcast.111, f32[8,4096]{1,0:T(8,128)S(1)} %get-tuple-element.458, pred[]{:T(512)S(6)} %compare.13, f32[8,8,512]{2,1,0:T(8,128)S(1)} %get-tuple-element.465, s32[]{:T(128)} %get-tuple-element.457), kind=kOutput, calls=%fused_computation.82.clone.1 | convolution fusion | flops 203489280 | bytes 280581 | tf_op jit(solution)/shard_map/while/body/eval_jaxpr/dot_general | solution.py:161
  175.0 2.8 %fusion.139 = f32[8,4096]{1,0:T(8,128)S(1)} fusion(s32[512]{0:T(512)S(1)} %bitcast.111, f32[8,4096]{1,0:T(8,128)S(1)} %get-tuple-element.458, pred[]{:T(512)S(6)} %compare.13, f32[8,8,512]{2,1,0:T(8,128)S(1)} %get-tuple-element.465, s32[]{:T(128)} %get-tuple-element.457), kind=kOutput, calls=%fused_computation.82.clone.1 | convolution fusion | flops 203489280 | bytes 280581 | tf_op jit(solution)/shard_map/while/body/eval_jaxpr/dot_general | solution.py:161
  177.8 2.8 %fusion.139 = f32[8,4096]{1,0:T(8,128)S(1)} fusion(s32[512]{0:T(512)S(1)} %bitcast.111, f32[8,4096]{1,0:T(8,128)S(1)} %get-tuple-element.458, pred[]{:T(512)S(6)} %compare.13, f32[8,8,512]{2,1,0:T(8,128)S(1)} %get-tuple-element.465, s32[]{:T(128)} %get-tuple-element.457), kind=kOutput, calls=%fused_computation.82.clone.1 | convolution fusion | flops 203489280 | bytes 280581 | tf_op jit(solution)/shard_map/while/body/eval_jaxpr/dot_general | solution.py:161
  180.5 2.8 %fusion.139 = f32[8,4096]{1,0:T(8,128)S(1)} fusion(s32[512]{0:T(512)S(1)} %bitcast.111, f32[8,4096]{1,0:T(8,128)S(1)} %get-tuple-element.458, pred[]{:T(512)S(6)} %compare.13, f32[8,8,512]{2,1,0:T(8,128)S(1)} %get-tuple-element.465, s32[]{:T(128)} %get-tuple-element.457), kind=kOutput, calls=%fused_computation.82.clone.1 | convolution fusion | flops 203489280 | bytes 280581 | tf_op jit(solution)/shard_map/while/body/eval_jaxpr/dot_general | solution.py:161
  183.3 2.8 %fusion.139 = f32[8,4096]{1,0:T(8,128)S(1)} fusion(s32[512]{0:T(512)S(1)} %bitcast.111, f32[8,4096]{1,0:T(8,128)S(1)} %get-tuple-element.458, pred[]{:T(512)S(6)} %compare.13, f32[8,8,512]{2,1,0:T(8,128)S(1)} %get-tuple-element.465, s32[]{:T(128)} %get-tuple-element.457), kind=kOutput, calls=%fused_computation.82.clone.1 | convolution fusion | flops 203489280 | bytes 280581 | tf_op jit(solution)/shard_map/while/body/eval_jaxpr/dot_general | solution.py:161
  186.1 2.8 %fusion.139 = f32[8,4096]{1,0:T(8,128)S(1)} fusion(s32[512]{0:T(512)S(1)} %bitcast.111, f32[8,4096]{1,0:T(8,128)S(1)} %get-tuple-element.458, pred[]{:T(512)S(6)} %compare.13, f32[8,8,512]{2,1,0:T(8,128)S(1)} %get-tuple-element.465, s32[]{:T(128)} %get-tuple-element.457), kind=kOutput, calls=%fused_computation.82.clone.1 | convolution fusion | flops 203489280 | bytes 280581 | tf_op jit(solution)/shard_map/while/body/eval_jaxpr/dot_general | solution.py:161
  189.0 2.5 %collective-permute-start.8 = (f32[8,32,1]{2,1,0:T(8,128)S(1)}, f32[8,32,1]{2,1,0:T(8,128)S(1)}, u32[]{:S(2)}, u32[]{:S(2)}) collective-permute-start(f32[8,32,1]{2,1,0:T(8,128)S(1)} %get-tuple-element.279), channel_id=1, source_target_pairs={{0,32},{32,64},{64,96},{96,128},{128,160},{160,192},{192,224},{1,3... | collective-permute-start | bytes 3080 | tf_op jit(solution)/shard_map/ppermute | solution.py:14
  192.8 1.7 collective-permute-done.8
  194.6 4.1 %collective-permute-done.9 = f32[8,32,1]{2,1,0:T(8,128)S(1)} collective-permute-done((f32[8,32,1]{2,1,0:T(8,128)S(1)}, f32[8,32,1]{2,1,0:T(8,128)S(1)}, u32[]{:S(2)}, u32[]{:S(2)}) %collective-permute-start.9) | collective-permute-done | bytes 1056 | tf_op jit(solution)/shard_map/ppermute | solution.py:17
  198.8 2.6 %collective-permute-start.10 = (f32[8,1,130]{2,1,0:T(1,128)S(1)}, f32[8,1,130]{2,1,0:T(1,128)S(1)}, u32[]{:S(2)}, u32[]{:S(2)}) collective-permute-start(f32[8,1,130]{2,1,0:T(1,128)S(1)} %get-tuple-element.268), channel_id=1, source_target_pairs={{1,0},{2,1},{3,2},{4,3},{5,4},{6,5},{7,6},{8,7},{9,8},{10,9},{11,1... | collective-permute-start | bytes 12488 | tf_op jit(solution)/shard_map/ppermute | solution.py:17
  201.4 1.9 collective-permute-start.11
  204.5 4.0 %collective-permute-done.11 = f32[8,1,130]{2,1,0:T(1,128)S(1)} collective-permute-done((f32[8,1,130]{2,1,0:T(1,128)S(1)}, f32[8,1,130]{2,1,0:T(1,128)S(1)}, u32[]{:S(2)}, u32[]{:S(2)}) %collective-permute-start.11) | collective-permute-done | bytes 4192 | tf_op jit(solution)/shard_map/ppermute | solution.py:14
  (144 shorter events, 40.9 us)
Async XLA Ops:
  0.6 25.4 %copy-start = (f32[8,8]{1,0:T(8,128)S(1)}, f32[8,8]{1,0:T(8,128)}, u32[]{:S(2)}) copy-start(f32[8,8]{1,0:T(8,128)} %param.16) | copy-start | bytes 772
  0.6 10.1 %copy-start.20 = (s32[2048,1]{0,1:T(1,128)S(1)}, s32[2048,1]{0,1:T(1,128)}, u32[]{:S(2)}) copy-start(s32[2048,1]{0,1:T(1,128)} %param.18) | copy-start | bytes 24580
  3.9 9.7 %collective-permute-start = (f32[9,1,16,128]{3,0,2,1:T(8,128)}, f32[9,1,16,128]{3,0,2,1:T(8,128)S(1)}, u32[]{:S(2)}, u32[]{:S(2)}) collective-permute-start(f32[9,1,16,128]{3,0,2,1:T(8,128)} %get-tuple-element.260), channel_id=1, source_target_pairs={{0,32},{32,64},{64,96},{96,128},{128,160},{160,192},{192,224},{1,3... | collective-permute-start | bytes 221192 | tf_op jit(solution)/shard_map/ppermute | solution.py:14
  7.8 7.2 %collective-permute-start.1 = (f32[9,1,16,128]{3,0,2,1:T(8,128)}, f32[9,1,16,128]{3,0,2,1:T(8,128)S(1)}, u32[]{:S(2)}, u32[]{:S(2)}) collective-permute-start(f32[9,1,16,128]{3,0,2,1:T(8,128)} %get-tuple-element.261), channel_id=1, source_target_pairs={{32,0},{64,32},{96,64},{128,96},{160,128},{192,160},{224,192},{33,... | collective-permute-start | bytes 221192 | tf_op jit(solution)/shard_map/ppermute | solution.py:17
  11.5 3.5 %copy-start.1 = (f32[16,16,128]{2,1,0:T(8,128)S(1)}, f32[16,16,128]{2,1,0:T(8,128)}, u32[]{:S(2)}) copy-start(f32[16,16,128]{2,1,0:T(8,128)} %param.15) | copy-start | bytes 393220
  11.5 11.2 %copy-start.21 = (s32[2048]{0:T(1024)S(1)}, s32[2048]{0:T(1024)}, u32[]{:S(2)}) copy-start(s32[2048]{0:T(1024)} %param.19) | copy-start | bytes 24580
  11.5 11.8 %copy-start.22 = (s32[2048]{0:T(1024)S(1)}, s32[2048]{0:T(1024)}, u32[]{:S(2)}) copy-start(s32[2048]{0:T(1024)} %param.20) | copy-start | bytes 24580
  12.7 13.3 %copy-start.2 = (f32[8,16,16,127]{3,0,2,1:T(8,128)S(1)}, f32[8,16,16,127]{3,0,2,1:T(8,128)}, u32[]{:S(2)}) copy-start(f32[8,16,16,127]{3,0,2,1:T(8,128)} %get-tuple-element.266) | copy-start | bytes 3121156
  15.0 9.5 %collective-permute-start.2 = (f32[9,18,1,128]{3,0,2,1:T(8,128)S(1)}, f32[9,18,1,128]{3,0,2,1:T(8,128)S(1)}, u32[]{:S(2)}, u32[]{:S(2)}) collective-permute-start(f32[9,18,1,128]{3,0,2,1:T(8,128)S(1)} %get-tuple-element.257), channel_id=1, source_target_pairs={{0,1},{1,2},{2,3},{3,4},{4,5},{5,6},{6,7},{7,8},{8,9},{9,10},{10,1... | collective-permute-start | bytes 248840 | tf_op jit(solution)/shard_map/ppermute | solution.py:14
  17.0 8.4 %collective-permute-start.3 = (f32[9,18,1,128]{3,0,2,1:T(8,128)S(1)}, f32[9,18,1,128]{3,0,2,1:T(8,128)S(1)}, u32[]{:S(2)}, u32[]{:S(2)}) collective-permute-start(f32[9,18,1,128]{3,0,2,1:T(8,128)S(1)} %get-tuple-element.256), channel_id=1, source_target_pairs={{1,0},{2,1},{3,2},{4,3},{5,4},{6,5},{7,6},{8,7},{9,8},{10,9},{11,1... | collective-permute-start | bytes 248840 | tf_op jit(solution)/shard_map/ppermute | solution.py:17
  24.5 1.3 copy-start.3
  25.4 0.7 copy-start.4
  25.8 3.7 %copy-start.6 = (f32[16,16,128]{2,1,0:T(8,128)}, f32[16,16,128]{2,1,0:T(8,128)S(1)}, u32[]{:S(2)}) copy-start(f32[16,16,128]{2,1,0:T(8,128)S(1)} %get-tuple-element.270) | copy-start | bytes 393220
  25.8 3.7 %copy-start.8 = (f32[16,16,128]{2,1,0:T(8,128)}, f32[16,16,128]{2,1,0:T(8,128)S(1)}, u32[]{:S(2)}) copy-start(f32[16,16,128]{2,1,0:T(8,128)S(1)} %get-tuple-element.271) | copy-start | bytes 393220
  25.8 3.7 %copy-start.10 = (f32[16,16,128]{2,1,0:T(8,128)}, f32[16,16,128]{2,1,0:T(8,128)S(1)}, u32[]{:S(2)}) copy-start(f32[16,16,128]{2,1,0:T(8,128)S(1)} %get-tuple-element.272) | copy-start | bytes 393220
  25.8 3.7 %copy-start.12 = (f32[16,16,128]{2,1,0:T(8,128)}, f32[16,16,128]{2,1,0:T(8,128)S(1)}, u32[]{:S(2)}) copy-start(f32[16,16,128]{2,1,0:T(8,128)S(1)} %get-tuple-element.273) | copy-start | bytes 393220
  25.8 3.7 %copy-start.14 = (f32[16,16,128]{2,1,0:T(8,128)}, f32[16,16,128]{2,1,0:T(8,128)S(1)}, u32[]{:S(2)}) copy-start(f32[16,16,128]{2,1,0:T(8,128)S(1)} %get-tuple-element.274) | copy-start | bytes 393220
  25.8 3.7 %copy-start.16 = (f32[16,16,128]{2,1,0:T(8,128)}, f32[16,16,128]{2,1,0:T(8,128)S(1)}, u32[]{:S(2)}) copy-start(f32[16,16,128]{2,1,0:T(8,128)S(1)} %get-tuple-element.275) | copy-start | bytes 393220
  29.6 20.7 %copy-start.7 = (f32[16,16,128]{2,1,0:T(8,128)S(1)}, f32[16,16,128]{2,1,0:T(8,128)}, u32[]{:S(2)}) copy-start(f32[16,16,128]{2,1,0:T(8,128)} %copy-done.6) | copy-start | bytes 393220
  29.6 20.7 %copy-start.9 = (f32[16,16,128]{2,1,0:T(8,128)S(1)}, f32[16,16,128]{2,1,0:T(8,128)}, u32[]{:S(2)}) copy-start(f32[16,16,128]{2,1,0:T(8,128)} %copy-done.8) | copy-start | bytes 393220
  29.6 20.7 %copy-start.11 = (f32[16,16,128]{2,1,0:T(8,128)S(1)}, f32[16,16,128]{2,1,0:T(8,128)}, u32[]{:S(2)}) copy-start(f32[16,16,128]{2,1,0:T(8,128)} %copy-done.10) | copy-start | bytes 393220
  29.6 20.7 %copy-start.13 = (f32[16,16,128]{2,1,0:T(8,128)S(1)}, f32[16,16,128]{2,1,0:T(8,128)}, u32[]{:S(2)}) copy-start(f32[16,16,128]{2,1,0:T(8,128)} %copy-done.12) | copy-start | bytes 393220
  29.6 20.7 %copy-start.15 = (f32[16,16,128]{2,1,0:T(8,128)S(1)}, f32[16,16,128]{2,1,0:T(8,128)}, u32[]{:S(2)}) copy-start(f32[16,16,128]{2,1,0:T(8,128)} %copy-done.14) | copy-start | bytes 393220
  29.6 20.7 %copy-start.17 = (f32[16,16,128]{2,1,0:T(8,128)S(1)}, f32[16,16,128]{2,1,0:T(8,128)}, u32[]{:S(2)}) copy-start(f32[16,16,128]{2,1,0:T(8,128)} %copy-done.16) | copy-start | bytes 393220
  29.6 6.7 %collective-permute-start.4 = (f32[8,1,16,128]{3,0,2,1:T(8,128)S(1)}, f32[8,1,16,128]{3,0,2,1:T(8,128)S(1)}, u32[]{:S(2)}, u32[]{:S(2)}) collective-permute-start(f32[8,1,16,128]{3,0,2,1:T(8,128)S(1)} %get-tuple-element.265), channel_id=1, source_target_pairs={{32,0},{64,32},{96,64},{128,96},{160,128},{192,160},{224,192},{33,... | collective-permute-start | bytes 196616 | tf_op jit(solution)/shard_map/ppermute | solution.py:17
  31.1 6.4 %collective-permute-start.5 = (f32[8,1,16,128]{3,0,2,1:T(8,128)S(1)}, f32[8,1,16,128]{3,0,2,1:T(8,128)S(1)}, u32[]{:S(2)}, u32[]{:S(2)}) collective-permute-start(f32[8,1,16,128]{3,0,2,1:T(8,128)S(1)} %get-tuple-element.264), channel_id=1, source_target_pairs={{0,32},{32,64},{64,96},{96,128},{128,160},{160,192},{192,224},{1,3... | collective-permute-start | bytes 196616 | tf_op jit(solution)/shard_map/ppermute | solution.py:14
  37.5 7.3 %collective-permute-start.6 = (f32[8,18,1,128]{3,0,2,1:T(8,128)S(1)}, f32[8,18,1,128]{3,0,2,1:T(8,128)S(1)}, u32[]{:S(2)}, u32[]{:S(2)}) collective-permute-start(f32[8,18,1,128]{3,0,2,1:T(8,128)S(1)} %get-tuple-element.258), channel_id=1, source_target_pairs={{1,0},{2,1},{3,2},{4,3},{5,4},{6,5},{7,6},{8,7},{9,8},{10,9},{11,1... | collective-permute-start | bytes 221192 | tf_op jit(solution)/shard_map/ppermute | solution.py:17
  42.5 7.8 %collective-permute-start.7 = (f32[8,18,1,128]{3,0,2,1:T(8,128)S(1)}, f32[8,18,1,128]{3,0,2,1:T(8,128)S(1)}, u32[]{:S(2)}, u32[]{:S(2)}) collective-permute-start(f32[8,18,1,128]{3,0,2,1:T(8,128)S(1)} %get-tuple-element.259), channel_id=1, source_target_pairs={{0,1},{1,2},{2,3},{3,4},{4,5},{5,6},{6,7},{7,8},{8,9},{9,10},{10,1... | collective-permute-start | bytes 221192 | tf_op jit(solution)/shard_map/ppermute | solution.py:14
  52.1 1.1 copy-start.18
  53.2 37.7 %copy-start.19 = (f32[9,4096]{1,0:T(8,128)S(1)}, f32[9,4096]{1,0:T(8,128)}, u32[]{:S(2)}) copy-start(f32[9,4096]{1,0:T(8,128)} %custom-call) | copy-start | bytes 442372
  105.4 19.7 %all-to-all-start.2 = ((s32[1,8,512]{2,0,1:T(1,128)}), s32[1,8,512]{2,0,1:T(1,128)S(1)}, u32[]{:S(2)}, u32[]{:S(2)}) async-start(s32[1,8,512]{2,0,1:T(1,128)} %bitcast.15), calls=%async_computation.2 | async-start | bytes 32768 | tf_op jit(solution)/shard_map/all_to_all | solution.py:137
  125.1 12.4 %all-to-all-start = ((f32[8,8,512]{2,0,1:T(8,128)}), f32[8,8,512]{2,0,1:T(8,128)S(1)}, u32[]{:S(2)}, u32[]{:S(2)}) async-start(f32[8,8,512]{2,0,1:T(8,128)} %bitcast.13), calls=%async_computation | async-start | bytes 262144 | tf_op jit(solution)/shard_map/all_to_all | solution.py:124
  137.5 11.2 %all-to-all-start.3 = ((s32[32,1,128]{2,1,0:T(1,128)}), s32[32,1,128]{2,1,0:T(1,128)S(1)}, u32[]{:S(2)}, u32[]{:S(2)}) async-start(s32[32,1,128]{2,1,0:T(1,128)} %reshape.247), calls=%async_computation.3 | async-start | bytes 32768 | tf_op jit(solution)/shard_map/all_to_all | solution.py:136
  148.6 11.6 %all-to-all-start.1 = ((f32[32,1,1024]{2,1,0:T(1,128)}), f32[32,1,1024]{2,1,0:T(1,128)S(1)}, u32[]{:S(2)}, u32[]{:S(2)}) async-start(f32[32,1,1024]{2,1,0:T(1,128)} %reshape.245), calls=%async_computation.1 | async-start | bytes 262144 | tf_op jit(solution)/shard_map/all_to_all | solution.py:123
  166.6 22.3 %copy-start.5 = (f32[8,32,128]{2,1,0:T(8,128)S(1)}, f32[8,32,128]{2,1,0:T(8,128)}, u32[]{:S(2)}) copy-start(f32[8,32,128]{2,1,0:T(8,128)} %param.17) | copy-start | bytes 393220
  189.0 5.5 %collective-permute-start.8 = (f32[8,32,1]{2,1,0:T(8,128)S(1)}, f32[8,32,1]{2,1,0:T(8,128)S(1)}, u32[]{:S(2)}, u32[]{:S(2)}) collective-permute-start(f32[8,32,1]{2,1,0:T(8,128)S(1)} %get-tuple-element.279), channel_id=1, source_target_pairs={{0,32},{32,64},{64,96},{96,128},{128,160},{160,192},{192,224},{1,3... | collective-permute-start | bytes 3080 | tf_op jit(solution)/shard_map/ppermute | solution.py:14
  191.5 7.1 %collective-permute-start.9 = (f32[8,32,1]{2,1,0:T(8,128)S(1)}, f32[8,32,1]{2,1,0:T(8,128)S(1)}, u32[]{:S(2)}, u32[]{:S(2)}) collective-permute-start(f32[8,32,1]{2,1,0:T(8,128)S(1)} %get-tuple-element.278), channel_id=1, source_target_pairs={{32,0},{64,32},{96,64},{128,96},{160,128},{192,160},{224,192},{33,... | collective-permute-start | bytes 3080 | tf_op jit(solution)/shard_map/ppermute | solution.py:17
  198.8 5.7 %collective-permute-start.10 = (f32[8,1,130]{2,1,0:T(1,128)S(1)}, f32[8,1,130]{2,1,0:T(1,128)S(1)}, u32[]{:S(2)}, u32[]{:S(2)}) collective-permute-start(f32[8,1,130]{2,1,0:T(1,128)S(1)} %get-tuple-element.268), channel_id=1, source_target_pairs={{1,0},{2,1},{3,2},{4,3},{5,4},{6,5},{7,6},{8,7},{9,8},{10,9},{11,1... | collective-permute-start | bytes 12488 | tf_op jit(solution)/shard_map/ppermute | solution.py:17
  201.4 7.1 %collective-permute-start.11 = (f32[8,1,130]{2,1,0:T(1,128)S(1)}, f32[8,1,130]{2,1,0:T(1,128)S(1)}, u32[]{:S(2)}, u32[]{:S(2)}) collective-permute-start(f32[8,1,130]{2,1,0:T(1,128)S(1)} %get-tuple-element.269), channel_id=1, source_target_pairs={{0,1},{1,2},{2,3},{3,4},{4,5},{5,6},{6,7},{7,8},{8,9},{9,10},{10,1... | collective-permute-start | bytes 12488 | tf_op jit(solution)/shard_map/ppermute | solution.py:14
where the time goes:
time: 211 us; the launch traced here: 209 us
  starting transfers between devices  59.2 us (28%)
  matrix products  53 us (25%)
  waiting for transfers between devices  41.2 us (20%)
  local copies, waits for them, and re-layouts  28.5 us (14%)
  other arithmetic  25.8 us (12%)
    dot_general x8, matrix products, land(): jnp.dot(vals, placing, precision=lax.Precision.HIGHEST, preferred_element...  22.1 us
    ppermute x6, starting transfers between devices, extended(): lax.ppermute(lax.slice_in_dim(block, 0, width, axis=dim), axis, backward)  17.3 us
    dot_general x4, other arithmetic, interpolate(): lax.dot_general(shell, table, (((1,), (1,)), ((), ())), precision=lax.Pre...  16.7 us
    ppermute x6, starting transfers between devices, extended(): lax.ppermute(lax.slice_in_dim(block, block.shape[dim] - width, None, axis...  16.6 us
    dot_general x4, matrix products, interpolate(): lax.dot_general(shell, table, (((1,), (1,)), ((), ())), precision=lax.Pre...  14.6 us
    ppermute x6, waiting for transfers between devices, extended(): lax.ppermute(lax.slice_in_dim(block, block.shape[dim] - width, None, axis...  12.3 us
    all_to_all x1, starting transfers between devices, body(): lax.all_to_all(send_dest.reshape(1, n_lat, n_lon * slots_each), 'lat', sp...  11.9 us
    dot_general x4, matrix products, pack(): jnp.dot(rows, placing, precision=lax.Precision.HIGHEST, preferred_element...  11.1 us
  transfers between devices with their start and end apart: 16, of which 11 were waited for; matrix products, arithmetic and copies ran while one was open for 7% of the time, Pallas kernels for 0%

commit v1 on v0

v1 whole, which is shorter than its diff:
```python
import functools

import jax
import jax.numpy as jnp
from jax import lax
from jax.experimental import pallas as pl
from jax.experimental.pallas import tpu as pltpu
from jax.sharding import PartitionSpec as P

SH = 8
CAP = 16
BLOCK = 256
VMEM = pltpu.VMEM
F32 = jnp.float32
BF16 = jnp.bfloat16


def vspec():
    return pl.BlockSpec(memory_space=VMEM)


def sspec():
    return pl.BlockSpec(memory_space=pltpu.SMEM)


def iota(shape, dim):
    return lax.broadcasted_iota(jnp.int32, shape, dim)


def halves(x):
    high = x.astype(BF16)
    return high, (x - high.astype(F32)).astype(BF16)


def neighbours(axis, step):
    count = lax.axis_size(axis)
    return [(i, i + step) for i in range(count) if 0 <= i + step < count]


def theta_edges(corona, kappa, low, high):
    fields, _, tile_p, radial = low.shape[0] - 1, None, low.shape[2], low.shape[3]
    tile_t = corona.shape[1]
    low[:fields] = corona[:, 0:2]
    low[fields] = kappa[0:2]
    high[:fields] = corona[:, tile_t - 2 : tile_t]
    high[fields] = kappa[tile_t - 2 : tile_t]


def phi_edges(tile_t, tile_p, corona, kappa, from_low, from_high, low, high):
    fields = corona.shape[0]
    for f in range(fields + 1):
        for out, near, far in ((low, 0, 1), (high, tile_p - 1, tile_p - 2)):
            for at, col in ((0, near), (tile_t, far)):
                rows = pl.ds(col, tile_t, stride=tile_p)
                out[f, at : at + tile_t, :] = corona[f, rows, :] if f < fields else kappa[rows, :]
            out[f, 2 * tile_t : 2 * tile_t + 1, :] = from_low[f, 1, near : near + 1, :]
            out[f, 2 * tile_t + 1 : 2 * tile_t + 2, :] = from_high[f, 0, near : near + 1, :]


def ranks(face_t, owner, dest, rank_out, meta_out):
    n_dev = meta_out.shape[0]
    count = owner.shape[1]
    width = min(BLOCK, count)
    before = (iota((width, width), 0) < iota((width, width), 1)).astype(F32).astype(BF16)
    owners = iota((n_dev, width), 0)
    slots = iota((CAP, width), 0).astype(F32)
    carry = jnp.zeros((n_dev, 1), F32)
    meta = jnp.zeros((n_dev, 128), F32)
    for b in range(count // width):
        cols = slice(b * width, (b + 1) * width)
        hit = owners == owner[:, cols]
        hit_f = jnp.where(hit, 1.0, 0.0)
        hit_b = hit_f.astype(BF16)
        ahead = jnp.dot(hit_b, before, preferred_element_type=F32) + carry
        rank = jnp.sum(jnp.where(hit, ahead, 0.0), axis=0, keepdims=True)
        carry = ahead[:, width - 1 : width] + hit_f[:, width - 1 : width]
        rank_out[:, cols] = rank
        cell = dest[:, cols]
        cell_t = (cell % face_t).astype(F32)
        cell_p = (cell // face_t).astype(F32)
        mine = slots == rank
        rows = jnp.concatenate(
            [
                jnp.where(mine, cell_t, 0.0),
                jnp.where(mine, cell_p, 0.0),
                jnp.zeros((128 - 2 * CAP, width), F32),
            ],
            axis=0,
        ).astype(BF16)
        meta = meta + lax.dot_general(
            hit_b, rows, (((1,), (1,)), ((), ())), preferred_element_type=F32
        )
    meta_out[...] = meta


def flux(fields, mixing, cond, value, inner):
    kc, *kn = cond()
    radial = kc.shape[-1]
    lane = iota(kc.shape, 1)
    weights = [0.075 * (kc + k) for k in kn]
    k_up = jnp.where(lane == radial - 1, 0.0, pltpu.roll(kc, radial - 1, 1))
    k_down = jnp.where(lane == 0, 0.0, pltpu.roll(kc, 1, 1))
    up = 0.075 * (kc + k_up)
    down = 0.075 * (kc + k_down)
    total = 1.0 - ((weights[0] + weights[1]) + (weights[2] + weights[3]) + (up + down))
    up = jnp.where(lane == radial - 1, 0.0, up)
    down = jnp.where(lane == 0, 0.0, down)
    centres = [inner(f) for f in range(fields)]
    for g in range(fields):
        c = centres[g]
        acc = total * c
        for w, near in zip(weights, value(g)):
            acc = acc + w * near
        acc = acc + up * pltpu.roll(c, radial - 1, 1) + down * pltpu.roll(c, 1, 1)
        for f in range(fields):
            acc = acc + (0.3 * mixing[g, f]) * centres[f]
        yield g, acc


def main(
    n_dev, mixing, place, corona, kappa, t_low, t_high, p_low, p_high, base, frac, owner, rank,
    meta, stepped, message, wide, once, column,
):
    fields, tile_t, tile_p, radial = corona.shape
    wide_n = tile_p + 16
    for f in range(fields + 1):
        own = corona[f] if f < fields else kappa[...]
        wide[f, 2 : 2 + tile_t, 8 : 8 + tile_p, :] = own
        wide[f, 0:2, 8 : 8 + tile_p, :] = t_low[f]
        wide[f, 2 + tile_t : 4 + tile_t, 8 : 8 + tile_p, :] = t_high[f]
        for side, (halo, near, far) in enumerate(((p_low, 7, 6), (p_high, 8 + tile_p, 9 + tile_p))):
            for t in range(tile_t):
                wide[f, 2 + t, near : near + 1, :] = halo[f, t : t + 1, :]
            wide[f, 1, near : near + 1, :] = halo[f, 2 * tile_t : 2 * tile_t + 1, :]
            wide[f, 2 + tile_t, near : near + 1, :] = halo[f, 2 * tile_t + 1 : 2 * tile_t + 2, :]
            column[side, f, 8 : 8 + tile_t, :] = halo[f, 0:tile_t, :]
            column[side, f, 7:8, :] = halo[f, 2 * tile_t : 2 * tile_t + 1, :]
            column[side, f, 8 + tile_t : 9 + tile_t, :] = halo[f, 2 * tile_t + 1 : 2 * tile_t + 2, :]

    lat, lon, last_lat, last_lon = place[0], place[1], place[2], place[3]

    def around(ref, f, t, dt):
        return [
            ref[f, t + dt - 1, 8 : 8 + tile_p, :],
            ref[f, t + dt + 1, 8 : 8 + tile_p, :],
            ref[f, t + dt, 7 : 7 + tile_p, :],
            ref[f, t + dt, 9 : 9 + tile_p, :],
        ]

    def first_row(t, _):
        exists = jnp.logical_and(
            jnp.logical_or(t > 0, lat > 0), jnp.logical_or(t < tile_t + 1, lat < last_lat)
        )
        keep = jnp.where(exists, 1.0, 0.0)
        for g, acc in flux(
            fields,
            mixing,
            lambda: [wide[fields, t + 1, 8 : 8 + tile_p, :]] + around(wide, fields, t, 1),
            lambda f: around(wide, f, t, 1),
            lambda f: wide[f, t + 1, 8 : 8 + tile_p, :],
        ):
            once[g, t, 8 : 8 + tile_p, :] = acc * keep
        return 0

    lax.fori_loop(0, tile_t + 2, first_row, 0)

    for side, halo, own_col, at in ((0, p_low, 0, 7), (1, p_high, tile_p - 1, 8 + tile_p)):
        keep = jnp.where(lon > 0, 1.0, 0.0) if side == 0 else jnp.where(lon < last_lon, 1.0, 0.0)

        def beside(f, side=side, halo=halo, own_col=own_col):
            own = jnp.concatenate(
                [wide[f, 2 + t, 8 + own_col : 9 + own_col, :] for t in range(tile_t)], axis=0
            )
            return [
                column[side, f, 7 : 7 + tile_t, :],
                column[side, f, 9 : 9 + tile_t, :],
                halo[f, tile_t : 2 * tile_t, :],
                own,
            ]

        for g, acc in flux(
            fields,
            mixing,
            lambda: [column[side, fields, 8 : 8 + tile_t, :]] + beside(fields),
            beside,
            lambda f: column[side, f, 8 : 8 + tile_t, :],
        ):
            acc = acc * keep
            for t in range(tile_t):
                once[g, 1 + t, at : at + 1, :] = acc[t : t + 1, :]

    def second_row(t, _):
        for g, acc in flux(
            fields,
            mixing,
            lambda: [wide[fields, t + 2, 8 : 8 + tile_p, :]] + around(wide, fields, t, 2),
            lambda f: around(once, f, t, 1),
            lambda f: once[f, t + 1, 8 : 8 + tile_p, :],
        ):
            stepped[g, t] = acc
        return 0

    lax.fori_loop(0, tile_t, second_row, 0)

    columns = tile_t * tile_p
    lane = iota((columns, radial), 1)
    shell = jnp.zeros((columns, radial), F32)
    for f in range(fields):
        moved = pltpu.roll(stepped[f].reshape(columns, radial), (f * SH + SH) % radial, 1)
        shell = jnp.where(lane // SH == f, moved, shell)
    high = shell.astype(BF16).astype(F32)
    both = high + pltpu.roll(shell - high, fields * SH, 1)
    left = jnp.transpose(both).astype(BF16)

    count = base.shape[1]
    width = min(BLOCK, count)
    owners = iota((n_dev, width), 0)
    packed = jnp.zeros((n_dev, 2 * fields * CAP), F32)
    for b in range(count // width):
        cols = slice(b * width, (b + 1) * width)
        cell = base[:, cols]

        def pair(size, at, fraction):
            rows = iota((size, width), 0)
            return jnp.where(rows == at, 1.0 - fraction, jnp.where(rows == at + 1, fraction, 0.0))

        w_t = pair(tile_t, cell // (tile_p * SH), frac[0:1, cols])
        w_p = pair(tile_p, (cell // SH) % tile_p, frac[1:2, cols])
        w_r = pair(SH, cell % SH, frac[2:3, cols])
        table = (w_t[:, None, :] * w_p[None, :, :]).reshape(columns, width)
        table_high, table_low = halves(table)
        coarse = jnp.dot(left, table_high, preferred_element_type=F32)
        fine = jnp.dot(left[: fields * SH], table_low, preferred_element_type=F32)
        by_layer = coarse[: fields * SH] + (coarse[fields * SH :] + fine)
        value = jnp.sum(by_layer.reshape(fields, SH, width) * w_r[None], axis=1)
        order = rank[:, cols]
        placed = jnp.concatenate(
            [jnp.where(order == float(k), value, 0.0) for k in range(CAP)], axis=0
        )
        placed_high, placed_low = halves(placed)
        hit = jnp.where(owners == owner[:, cols], 1.0, 0.0).astype(BF16)
        packed = packed + lax.dot_general(
            hit,
            jnp.concatenate([placed_high, placed_low], axis=0),
            (((1,), (1,)), ((), ())),
            preferred_element_type=F32,
        )
    half = fields * CAP
    message[pl.ds(0, n_dev, stride=2), :] = packed[:, :half] + packed[:, half:]
    message[pl.ds(1, n_dev, stride=2), :] = meta[...]


def land(n_dev, got, prev, coupled, p_first, p_last, t_first, t_last):
    fields, face_p, face_t = prev.shape
    values = jnp.transpose(got[pl.ds(0, n_dev, stride=2), :])
    cells = jnp.transpose(got[pl.ds(1, n_dev, stride=2), :])
    along_t = iota((face_t, n_dev), 0).astype(F32)
    along_p = iota((face_p, n_dev), 0).astype(F32)
    rows = fields * face_p
    total = jnp.zeros((2 * rows, face_t), F32)
    for k in range(CAP):
        at_t = jnp.where(along_t == cells[k : k + 1, :], 1.0, 0.0).astype(BF16)
        at_p = along_p == cells[CAP + k : CAP + k + 1, :]
        value = values[k * fields : (k + 1) * fields, :]
        high = value.astype(BF16).astype(F32)
        parts = [
            jnp.where(at_p[None], part[:, None, :], 0.0).reshape(rows, n_dev).astype(BF16)
            for part in (high, value - high)
        ]
        total = total + lax.dot_general(
            jnp.concatenate(parts, axis=0),
            at_t,
            (((1,), (1,)), ((), ())),
            preferred_element_type=F32,
        )
    new = prev[...].reshape(rows, face_t) + (total[:rows] + total[rows:])
    coupled[...] = new.reshape(fields, face_p, face_t)
    turned = jnp.transpose(new)
    t_first[...] = turned[0:1, :]
    t_last[...] = turned[face_t - 1 : face_t, :]
    for f in range(fields):
        p_first[f : f + 1, :] = new[f * face_p : f * face_p + 1, :]
        p_last[f : f + 1, :] = new[(f + 1) * face_p - 1 : (f + 1) * face_p, :]


def smooth(coupled, p_low, p_high, t_low, t_high, out):
    fields, face_p, face_t = coupled.shape
    x = coupled[...]
    row = iota((face_p, face_t), 0)[None]
    lane = iota((face_p, face_t), 1)[None]

    def column(ref):
        return jnp.transpose(jnp.broadcast_to(ref[...], (face_t, fields * face_p))).reshape(x.shape)

    below = jnp.where(row == 0, p_low[...][:, None, :], pltpu.roll(x, 1, 1))
    above = jnp.where(row == face_p - 1, p_high[...][:, None, :], pltpu.roll(x, face_p - 1, 1))
    left = jnp.where(lane == 0, column(t_low), pltpu.roll(x, 1, 2))
    right = jnp.where(lane == face_t - 1, column(t_high), pltpu.roll(x, face_t - 1, 2))
    out[...] = x + 0.2 * (above + below + right + left - 4.0 * x)


def call(kernel, outs, specs, name, scratch=()):
    return pl.pallas_call(
        kernel,
        out_shape=[jax.ShapeDtypeStruct(s, F32) for s in outs],
        in_specs=specs,
        out_specs=[vspec()] * len(outs),
        scratch_shapes=list(scratch),
        name=name,
        compiler_params=pltpu.CompilerParams(vmem_limit_bytes=40 * 1024 * 1024),
    )


def body(corona, kappa, mixing, helio_prev, owner, dest_cell, corner_base, fractions):
    fields, tile_t, tile_p, radial = corona.shape
    n_lat, n_lon = lax.axis_size("lat"), lax.axis_size("lon")
    n_dev = n_lat * n_lon
    count = corner_base.shape[0]
    _, face_p, face_t = helio_prev.shape
    owner = owner.reshape(1, count)
    dest_cell = dest_cell.reshape(1, count)
    base = corner_base.reshape(1, count)
    place = jnp.stack(
        [lax.axis_index("lat"), lax.axis_index("lon"), jnp.int32(n_lat - 1), jnp.int32(n_lon - 1)]
    )

    edge = (fields + 1, 2, tile_p, radial)
    low, high = call(theta_edges, [edge] * 2, [vspec()] * 2, "theta_edges")(corona, kappa)
    t_low = lax.ppermute(high, "lat", neighbours("lat", 1))
    t_high = lax.ppermute(low, "lat", neighbours("lat", -1))

    rank, meta = call(
        functools.partial(ranks, face_t), [(1, count), (n_dev, 128)], [vspec()] * 2, "ranks"
    )(owner, dest_cell)

    edge = (fields + 1, 2 * tile_t + 8, radial)
    low, high = call(
        functools.partial(phi_edges, tile_t, tile_p), [edge] * 2, [vspec()] * 4, "phi_edges"
    )(
        corona.reshape(fields, tile_t * tile_p, radial),
        kappa.reshape(tile_t * tile_p, radial),
        t_low,
        t_high,
    )
    p_low = lax.ppermute(high, "lon", neighbours("lon", 1))
    p_high = lax.ppermute(low, "lon", neighbours("lon", -1))

    stepped, message = call(
        functools.partial(main, n_dev),
        [corona.shape, (2 * n_dev, 128)],
        [sspec()] * 2 + [vspec()] * 11,
        "steps",
        [
            VMEM((fields + 1, tile_t + 4, tile_p + 16, radial), F32),
            VMEM((fields, tile_t + 2, tile_p + 16, radial), F32),
            VMEM((2, fields + 1, tile_t + 16, radial), F32),
        ],
    )(
        mixing, place, corona, kappa, t_low, t_high, p_low, p_high, base, fractions, owner, rank,
        meta,
    )

    got = lax.all_to_all(message, ("lat", "lon"), split_axis=0, concat_axis=0, tiled=True)

    coupled, p_first, p_last, t_first, t_last = call(
        functools.partial(land, n_dev),
        [helio_prev.shape, (fields, face_t), (fields, face_t)] + [(1, fields * face_p)] * 2,
        [vspec()] * 2,
        "land",
    )(got, helio_prev)
    from_t_low = lax.ppermute(t_last, "lat", neighbours("lat", 1))
    from_t_high = lax.ppermute(t_first, "lat", neighbours("lat", -1))
    from_p_low = lax.ppermute(p_last, "lon", neighbours("lon", 1))
    from_p_high = lax.ppermute(p_first, "lon", neighbours("lon", -1))
    (face,) = call(smooth, [helio_prev.shape], [vspec()] * 5, "smooth")(
        coupled, from_p_low, from_p_high, from_t_low, from_t_high
    )
    return (stepped, face)


def solution(mesh):
    return jax.shard_map(
        body,
        mesh=mesh,
        in_specs=(
            P(None, "lat", "lon", None),
            P("lat", "lon", None),
            P(),
            P(None, "lon", "lat"),
            P(("lat", "lon"), None),
            P(("lat", "lon")),
            P(("lat", "lon")),
            P(None, ("lat", "lon")),
        ),
        out_specs=(P(None, "lat", "lon", None), P(None, "lon", "lat")),
        check_vma=False,
    )
```

time: 211 us -> 80.5 us (0.38)
  matrix products: 53 us -> 0 us
  starting transfers between devices: 59.2 us -> 24.8 us
  blocking collectives: 0 us -> 29.4 us
  waiting for transfers between devices: 41.2 us -> 11.9 us
  local copies, waits for them, and re-layouts: 28.5 us -> 2.17 us
  other arithmetic: 25.8 us -> 0.08 us
  Pallas kernels: 0 us -> 10.9 us
    dot_general x18 -> x0, matrix products: 53 us -> none  [the longest x8 22.1 us: land(): jnp.dot(vals, placing, precision=lax.Precision.HIGHEST, preferred_element...]
    all_to_all x0 -> x1, blocking collectives: none -> 29.4 us  [body(): lax.all_to_all(message, ('lat', 'lon'), split_axis=0, concat_axis=0, tile...]
    all_to_all x4 -> x0, starting transfers between devices: 25.3 us -> none  [the longest x1 11.9 us: body(): lax.all_to_all(send_dest.reshape(1, n_lat, n_lon * slots_each), 'lat', sp...]
    all_to_all x4 -> x0, waiting for transfers between devices: 22.6 us -> none  [the longest x1 7.11 us: body(): lax.all_to_all(send_dest.reshape(1, n_lat, n_lon * slots_each), 'lat', sp...]
    dot_general x4 -> x0, other arithmetic: 16.7 us -> none  [interpolate(): lax.dot_general(shell, table, (((1,), (1,)), ((), ())), precision=lax.Pre...]
    pallas_call x0 -> x6, Pallas kernels: none -> 10.9 us  [the longest x1 7.23 us: body(): call(functools.partial(main, n_dev), [corona.shape, (2 * n_dev, 128)], [s...]
    ppermute x12 -> x8, starting transfers between devices: 33.9 us -> 24.8 us  [the longest x1 5.75 us: body(): p_high = lax.ppermute(low, 'lon', neighbours('lon', -1))]
    unnamed x56 -> x20, local copies, waits for them, and re-layouts: 10.2 us -> 2.17 us
  transfers between devices with their start and end apart: 16 -> 8, of which waited for: 11 -> 4; matrix products, arithmetic and copies ran while one was open for 7% -> 0% of each run, Pallas kernels for 0% -> 2%
where the time goes in v1:
time: 80.5 us; the launch traced here: 80.1 us
  blocking collectives  29.4 us (37%)
  starting transfers between devices  24.8 us (31%)
  waiting for transfers between devices  11.9 us (15%)
  Pallas kernels  10.9 us (14%)
  local copies, waits for them, and re-layouts  2.17 us (3%)
  between operations  0.82 us (1%)
    all_to_all x1, blocking collectives, body(): lax.all_to_all(message, ('lat', 'lon'), split_axis=0, concat_axis=0, tile...  29.4 us
    pallas_call x1, Pallas kernels, body(): call(functools.partial(main, n_dev), [corona.shape, (2 * n_dev, 128)], [s...  7.23 us
    ppermute x1, starting transfers between devices, body(): p_high = lax.ppermute(low, 'lon', neighbours('lon', -1))  5.75 us
    ppermute x1, starting transfers between devices, body(): from_p_high = lax.ppermute(p_first, 'lon', neighbours('lon', -1))  5.75 us
    ppermute x1, waiting for transfers between devices, body(): t_high = lax.ppermute(low, 'lat', neighbours('lat', -1))  4.3 us
    ppermute x1, waiting for transfers between devices, body(): from_t_high = lax.ppermute(t_first, 'lat', neighbours('lat', -1))  4.15 us
    ppermute x1, starting transfers between devices, body(): t_low = lax.ppermute(high, 'lat', neighbours('lat', 1))  3.96 us
    ppermute x1, starting transfers between devices, body(): from_t_low = lax.ppermute(t_last, 'lat', neighbours('lat', 1))  2.94 us
  transfers between devices with their start and end apart: 8, of which 4 were waited for; matrix products, arithmetic and copies ran while one was open for 0% of the time, Pallas kernels for 2%

profile of v1, /device:TPU:8, one launch (start us, length us, event | category | flops | bytes accessed | tf_op | source)
XLA Modules:
  0.0 80.1 jit_solution(11225885115684896337)
XLA Ops:
  0.6 0.0 copy-start
  0.6 1.2 %copy-done = f32[8,16,16,128]{3,2,1,0:T(8,128)S(1)} copy-done((f32[8,16,16,128]{3,2,1,0:T(8,128)S(1)}, f32[8,16,16,128]{3,2,1,0:T(8,128)}, u32[]{:S(2)}) %copy-start) | copy-done | bytes 1048600
  1.9 0.0 copy-start.2
  1.9 0.9 %copy-done.2 = f32[16,16,128]{2,1,0:T(8,128)S(1)} copy-done((f32[16,16,128]{2,1,0:T(8,128)S(1)}, f32[16,16,128]{2,1,0:T(8,128)}, u32[]{:S(2)}) %copy-start.2) | copy-done | bytes 131096
  2.8 0.0 copy-start.1
  2.8 4.0 %collective-permute-start = (f32[9,2,16,128]{3,2,1,0:T(8,128)S(1)}, f32[9,2,16,128]{3,2,1,0:T(8,128)S(1)}, u32[]{:S(2)}, u32[]{:S(2)}) collective-permute-start(f32[9,2,16,128]{3,2,1,0:T(8,128)S(1)} %get-tuple-element.15), channel_id=1, source_target_pairs={{0,32},{32,64},{64,96},{96,128},{128,160},{160,192},{192,224},{1,3... | collective-permute-start | bytes 442376 | tf_op jit(solution)/shard_map/ppermute | solution.py:329
  6.8 1.3 %collective-permute-start.1 = (f32[9,2,16,128]{3,2,1,0:T(8,128)S(1)}, f32[9,2,16,128]{3,2,1,0:T(8,128)S(1)}, u32[]{:S(2)}, u32[]{:S(2)}) collective-permute-start(f32[9,2,16,128]{3,2,1,0:T(8,128)S(1)} %get-tuple-element.16), channel_id=1, source_target_pairs={{32,0},{64,32},{96,64},{128,96},{160,128},{192,160},{224,192},{33,... | collective-permute-start | bytes 442376 | tf_op jit(solution)/shard_map/ppermute | solution.py:330
  8.1 1.8 %collective-permute-done.from_low.t_low = f32[9,2,16,128]{3,2,1,0:T(8,128)S(1)} collective-permute-done((f32[9,2,16,128]{3,2,1,0:T(8,128)S(1)}, f32[9,2,16,128]{3,2,1,0:T(8,128)S(1)}, u32[]{:S(2)}, u32[]{:S(2)}) %collective-permute-start) | collective-permute-done | bytes 147488 | tf_op jit(solution)/shard_map/ppermute | solution.py:329
  9.8 4.3 %collective-permute-done.1.from_high.t_high = f32[9,2,16,128]{3,2,1,0:T(8,128)S(1)} collective-permute-done((f32[9,2,16,128]{3,2,1,0:T(8,128)S(1)}, f32[9,2,16,128]{3,2,1,0:T(8,128)S(1)}, u32[]{:S(2)}, u32[]{:S(2)}) %collective-permute-start.1) | collective-permute-done | bytes 147488 | tf_op jit(solution)/shard_map/ppermute | solution.py:330
  14.1 0.0 copy-start.6
  14.2 0.0 copy-start.8
  14.2 0.0 copy-start.3
  14.2 0.1 phi_edges.1
  14.3 0.0 copy-start.5
  14.3 1.9 %collective-permute-start.2 = (f32[9,40,128]{2,1,0:T(8,128)S(1)}, f32[9,40,128]{2,1,0:T(8,128)S(1)}, u32[]{:S(2)}, u32[]{:S(2)}) collective-permute-start(f32[9,40,128]{2,1,0:T(8,128)S(1)} %get-tuple-element.17), channel_id=1, source_target_pairs={{0,1},{1,2},{2,3},{3,4},{4,5},{5,6},{6,7},{7,8},{8,9},{9,10},{10,1... | collective-permute-start | bytes 552968 | tf_op jit(solution)/shard_map/ppermute | solution.py:345
  16.2 5.8 %collective-permute-start.3 = (f32[9,40,128]{2,1,0:T(8,128)S(1)}, f32[9,40,128]{2,1,0:T(8,128)S(1)}, u32[]{:S(2)}, u32[]{:S(2)}) collective-permute-start(f32[9,40,128]{2,1,0:T(8,128)S(1)} %get-tuple-element.18), channel_id=1, source_target_pairs={{1,0},{2,1},{3,2},{4,3},{5,4},{6,5},{7,6},{8,7},{9,8},{10,9},{11,1... | collective-permute-start | bytes 552968 | tf_op jit(solution)/shard_map/ppermute | solution.py:346
  22.0 0.0 copy-done.6
  22.0 0.0 copy-done.8
  22.0 0.0 copy-start.9
  22.0 1.2 %ranks.1 = (f32[1,2048]{1,0:T(1,128)S(1)}, f32[256,128]{1,0:T(8,128)S(1)}) custom-call(s32[1,2048]{1,0:T(1,128)S(1)} %bitcast.13, s32[1,2048]{1,0:T(1,128)S(1)} %bitcast.16), custom_call_target="tpu_custom_call" | custom-call | tf_op jit(solution)/shard_map/ranks/pallas_call | solution.py:332
  23.2 0.0 copy-start.7
  23.3 0.1 pad_add_fusion.place
  23.3 0.0 collective-permute-done.2.p_low
  23.3 1.7 %collective-permute-done.3.p_high = f32[9,40,128]{2,1,0:T(8,128)S(1)} collective-permute-done((f32[9,40,128]{2,1,0:T(8,128)S(1)}, f32[9,40,128]{2,1,0:T(8,128)S(1)}, u32[]{:S(2)}, u32[]{:S(2)}) %collective-permute-start.3) | collective-permute-done | bytes 184352 | tf_op jit(solution)/shard_map/ppermute | solution.py:346
  25.0 0.0 copy-done.1
  25.0 0.0 copy-done.3
  25.0 0.0 copy-done.5
  25.0 0.0 copy-done.9
  25.0 0.0 copy-done.7
  25.0 7.2 %steps.1 = (f32[8,16,16,128]{3,2,1,0:T(8,128)}, f32[512,128]{1,0:T(8,128)S(1)}) custom-call(f32[8,8]{1,0:T(8,128)S(1)} %copy-done.9, s32[4]{0:T(128)S(1)} %pad_add_fusion.place, f32[8,16,16,128]{3,2,1,0:T(8,128)S(1)} %copy-done.1, f32[16,16,128]{2,1,0:T(8,128)S(1)} %copy-done.3, f32[9,2,16,128]{3,2,1,0:T(8,128)S(1)} %collective-permute-done.from_low.t_low, ...), custom_call_target="tpu_custom_call" | custom-call | tf_op jit(solution)/shard_map/steps/pallas_call | solution.py:348
  32.3 0.0 copy-start.4
  32.3 29.4 %all_to_all.11 = f32[256,2,128]{2,1,0:T(2,128)S(1)} all-to-all(f32[256,2,128]{2,1,0:T(2,128)S(1)} %bitcast.12), channel_id=1, replica_groups=mesh['lat'=8,'lon'=32] {'lat','lon'}, dimensions={0} | all-to-all | bytes 524288 | tf_op jit(solution)/shard_map/all_to_all | solution.py:363
  61.7 0.0 copy-done.4
  61.7 1.4 %land.1 = (f32[8,32,128]{2,1,0:T(8,128)S(1)}, f32[8,128]{1,0:T(8,128)S(1)}, f32[8,128]{1,0:T(8,128)S(1)}, f32[1,256]{1,0:T(1,128)S(1)}, f32[1,256]{1,0:T(1,128)S(1)}) custom-call(f32[512,128]{1,0:T(8,128)S(1)} %bitcast.11, f32[8,32,128]{2,1,0:T(8,128)S(1)} %copy-done.4), custom_call_target="tpu_custom_call" | custom-call | tf_op jit(solution)/shard_map/land/pallas_call | solution.py:365
  63.1 1.9 %collective-permute-start.4 = (f32[8,128]{1,0:T(8,128)S(1)}, f32[8,128]{1,0:T(8,128)S(1)}, u32[]{:S(2)}, u32[]{:S(2)}) collective-permute-start(f32[8,128]{1,0:T(8,128)S(1)} %get-tuple-element.24), channel_id=1, source_target_pairs={{0,1},{1,2},{2,3},{3,4},{4,5},{5,6},{6,7},{7,8},{8,9},{9,10},{10,1... | collective-permute-start | bytes 12296 | tf_op jit(solution)/shard_map/ppermute | solution.py:373
  65.1 5.8 %collective-permute-start.5 = (f32[8,128]{1,0:T(8,128)S(1)}, f32[8,128]{1,0:T(8,128)S(1)}, u32[]{:S(2)}, u32[]{:S(2)}) collective-permute-start(f32[8,128]{1,0:T(8,128)S(1)} %get-tuple-element.25), channel_id=1, source_target_pairs={{1,0},{2,1},{3,2},{4,3},{5,4},{6,5},{7,6},{8,7},{9,8},{10,9},{11,1... | collective-permute-start | bytes 12296 | tf_op jit(solution)/shard_map/ppermute | solution.py:374
  70.8 2.9 %collective-permute-start.6 = (f32[1,256]{1,0:T(1,128)S(1)}, f32[1,256]{1,0:T(1,128)S(1)}, u32[]{:S(2)}, u32[]{:S(2)}) collective-permute-start(f32[1,256]{1,0:T(1,128)S(1)} %get-tuple-element.26), channel_id=1, source_target_pairs={{0,32},{32,64},{64,96},{96,128},{128,160},{160,192},{192,224},{1,3... | collective-permute-start | bytes 3080 | tf_op jit(solution)/shard_map/ppermute | solution.py:371
  73.8 1.3 %collective-permute-start.7 = (f32[1,256]{1,0:T(1,128)S(1)}, f32[1,256]{1,0:T(1,128)S(1)}, u32[]{:S(2)}, u32[]{:S(2)}) collective-permute-start(f32[1,256]{1,0:T(1,128)S(1)} %get-tuple-element.27), channel_id=1, source_target_pairs={{32,0},{64,32},{96,64},{128,96},{160,128},{192,160},{224,192},{33,... | collective-permute-start | bytes 3080 | tf_op jit(solution)/shard_map/ppermute | solution.py:372
  75.1 0.0 collective-permute-done.6.t_low
  75.1 4.2 %collective-permute-done.7.t_high = f32[1,256]{1,0:T(1,128)S(1)} collective-permute-done((f32[1,256]{1,0:T(1,128)S(1)}, f32[1,256]{1,0:T(1,128)S(1)}, u32[]{:S(2)}, u32[]{:S(2)}) %collective-permute-start.7) | collective-permute-done | bytes 1056 | tf_op jit(solution)/shard_map/ppermute | solution.py:372
  79.2 0.0 collective-permute-done.4.p_low
  79.2 0.0 collective-permute-done.5.p_high
  79.2 0.9 %smooth.1 = f32[8,32,128]{2,1,0:T(8,128)} custom-call(f32[8,32,128]{2,1,0:T(8,128)S(1)} %get-tuple-element.23.coupled, f32[8,128]{1,0:T(8,128)S(1)} %collective-permute-done.4.p_low, f32[8,128]{1,0:T(8,128)S(1)} %collective-permute-done.5.p_high, f32[1,256]{1,0:T(1,128)S(1)} %collective-permute-done.6.t_low, f32[1,256]{1,0:T(1,128)S(1)} %collective-permute-done.7.t_high), custom_call_target="tpu_custom_call" | custom-call | tf_op jit(solution)/shard_map/smooth/pallas_call | solution.py:375
  (1 shorter events, 0.0 us)
Async XLA Ops:
  0.6 1.2 %copy-start = (f32[8,16,16,128]{3,2,1,0:T(8,128)S(1)}, f32[8,16,16,128]{3,2,1,0:T(8,128)}, u32[]{:S(2)}) copy-start(f32[8,16,16,128]{3,2,1,0:T(8,128)} %corona.3) | copy-start | bytes 3145732
  1.9 0.9 %copy-start.2 = (f32[16,16,128]{2,1,0:T(8,128)S(1)}, f32[16,16,128]{2,1,0:T(8,128)}, u32[]{:S(2)}) copy-start(f32[16,16,128]{2,1,0:T(8,128)} %kappa.3) | copy-start | bytes 393220
  2.8 22.2 %copy-start.1 = (f32[8,16,16,128]{3,2,1,0:T(8,128)S(1)}, f32[8,16,16,128]{3,2,1,0:T(8,128)}, u32[]{:S(2)}) copy-start(f32[8,16,16,128]{3,2,1,0:T(8,128)} %corona.3) | copy-start | bytes 3145732
  2.8 7.0 %collective-permute-start = (f32[9,2,16,128]{3,2,1,0:T(8,128)S(1)}, f32[9,2,16,128]{3,2,1,0:T(8,128)S(1)}, u32[]{:S(2)}, u32[]{:S(2)}) collective-permute-start(f32[9,2,16,128]{3,2,1,0:T(8,128)S(1)} %get-tuple-element.15), channel_id=1, source_target_pairs={{0,32},{32,64},{64,96},{96,128},{128,160},{160,192},{192,224},{1,3... | collective-permute-start | bytes 442376 | tf_op jit(solution)/shard_map/ppermute | solution.py:329
  6.8 7.4 %collective-permute-start.1 = (f32[9,2,16,128]{3,2,1,0:T(8,128)S(1)}, f32[9,2,16,128]{3,2,1,0:T(8,128)S(1)}, u32[]{:S(2)}, u32[]{:S(2)}) collective-permute-start(f32[9,2,16,128]{3,2,1,0:T(8,128)S(1)} %get-tuple-element.16), channel_id=1, source_target_pairs={{32,0},{64,32},{96,64},{128,96},{160,128},{192,160},{224,192},{33,... | collective-permute-start | bytes 442376 | tf_op jit(solution)/shard_map/ppermute | solution.py:330
  14.1 7.8 %copy-start.6 = (s32[2048,1]{0,1:T(1,128)S(1)}, s32[2048,1]{0,1:T(1,128)}, u32[]{:S(2)}) copy-start(s32[2048,1]{0,1:T(1,128)} %param.12) | copy-start | bytes 24580
  14.2 7.8 %copy-start.8 = (s32[2048]{0:T(1024)S(1)}, s32[2048]{0:T(1024)}, u32[]{:S(2)}) copy-start(s32[2048]{0:T(1024)} %param.13) | copy-start | bytes 24580
  14.2 10.8 %copy-start.3 = (f32[16,16,128]{2,1,0:T(8,128)S(1)}, f32[16,16,128]{2,1,0:T(8,128)}, u32[]{:S(2)}) copy-start(f32[16,16,128]{2,1,0:T(8,128)} %kappa.3) | copy-start | bytes 393220
  14.3 10.7 %copy-start.5 = (f32[3,2048]{1,0:T(4,128)S(1)}, f32[3,2048]{1,0:T(4,128)}, u32[]{:S(2)}) copy-start(f32[3,2048]{1,0:T(4,128)} %frac.1) | copy-start | bytes 73732
  14.3 9.1 %collective-permute-start.2 = (f32[9,40,128]{2,1,0:T(8,128)S(1)}, f32[9,40,128]{2,1,0:T(8,128)S(1)}, u32[]{:S(2)}, u32[]{:S(2)}) collective-permute-start(f32[9,40,128]{2,1,0:T(8,128)S(1)} %get-tuple-element.17), channel_id=1, source_target_pairs={{0,1},{1,2},{2,3},{3,4},{4,5},{5,6},{6,7},{7,8},{8,9},{9,10},{10,1... | collective-permute-start | bytes 552968 | tf_op jit(solution)/shard_map/ppermute | solution.py:345
  16.2 8.8 %collective-permute-start.3 = (f32[9,40,128]{2,1,0:T(8,128)S(1)}, f32[9,40,128]{2,1,0:T(8,128)S(1)}, u32[]{:S(2)}, u32[]{:S(2)}) collective-permute-start(f32[9,40,128]{2,1,0:T(8,128)S(1)} %get-tuple-element.18), channel_id=1, source_target_pairs={{1,0},{2,1},{3,2},{4,3},{5,4},{6,5},{7,6},{8,7},{9,8},{10,9},{11,1... | collective-permute-start | bytes 552968 | tf_op jit(solution)/shard_map/ppermute | solution.py:346
  22.0 3.0 %copy-start.9 = (f32[8,8]{1,0:T(8,128)S(1)}, f32[8,8]{1,0:T(8,128)}, u32[]{:S(2)}) copy-start(f32[8,8]{1,0:T(8,128)} %mixing.1) | copy-start | bytes 772
  23.2 1.8 %copy-start.7 = (s32[2048]{0:T(1024)S(1)}, s32[2048]{0:T(1024)}, u32[]{:S(2)}) copy-start(s32[2048]{0:T(1024)} %param.14) | copy-start | bytes 24580
  32.3 29.5 %copy-start.4 = (f32[8,32,128]{2,1,0:T(8,128)S(1)}, f32[8,32,128]{2,1,0:T(8,128)}, u32[]{:S(2)}) copy-start(f32[8,32,128]{2,1,0:T(8,128)} %prev.1) | copy-start | bytes 393220
  63.1 16.1 %collective-permute-start.4 = (f32[8,128]{1,0:T(8,128)S(1)}, f32[8,128]{1,0:T(8,128)S(1)}, u32[]{:S(2)}, u32[]{:S(2)}) collective-permute-start(f32[8,128]{1,0:T(8,128)S(1)} %get-tuple-element.24), channel_id=1, source_target_pairs={{0,1},{1,2},{2,3},{3,4},{4,5},{5,6},{6,7},{7,8},{8,9},{9,10},{10,1... | collective-permute-start | bytes 12296 | tf_op jit(solution)/shard_map/ppermute | solution.py:373
  65.1 14.2 %collective-permute-start.5 = (f32[8,128]{1,0:T(8,128)S(1)}, f32[8,128]{1,0:T(8,128)S(1)}, u32[]{:S(2)}, u32[]{:S(2)}) collective-permute-start(f32[8,128]{1,0:T(8,128)S(1)} %get-tuple-element.25), channel_id=1, source_target_pairs={{1,0},{2,1},{3,2},{4,3},{5,4},{6,5},{7,6},{8,7},{9,8},{10,9},{11,1... | collective-permute-start | bytes 12296 | tf_op jit(solution)/shard_map/ppermute | solution.py:374
  70.8 4.3 %collective-permute-start.6 = (f32[1,256]{1,0:T(1,128)S(1)}, f32[1,256]{1,0:T(1,128)S(1)}, u32[]{:S(2)}, u32[]{:S(2)}) collective-permute-start(f32[1,256]{1,0:T(1,128)S(1)} %get-tuple-element.26), channel_id=1, source_target_pairs={{0,32},{32,64},{64,96},{96,128},{128,160},{160,192},{192,224},{1,3... | collective-permute-start | bytes 3080 | tf_op jit(solution)/shard_map/ppermute | solution.py:371
  73.8 5.5 %collective-permute-start.7 = (f32[1,256]{1,0:T(1,128)S(1)}, f32[1,256]{1,0:T(1,128)S(1)}, u32[]{:S(2)}, u32[]{:S(2)}) collective-permute-start(f32[1,256]{1,0:T(1,128)S(1)} %get-tuple-element.27), channel_id=1, source_target_pairs={{32,0},{64,32},{96,64},{128,96},{160,128},{192,160},{224,192},{33,... | collective-permute-start | bytes 3080 | tf_op jit(solution)/shard_map/ppermute | solution.py:372

commit v2 on v1

--- a/solution.py
+++ b/solution.py
@@ -32,29 +32,41 @@
     return high, (x - high.astype(F32)).astype(BF16)
 
 
-def neighbours(axis, step):
+def shifted(x, axis, step):
     count = lax.axis_size(axis)
-    return [(i, i + step) for i in range(count) if 0 <= i + step < count]
-
-
-def theta_edges(corona, kappa, low, high):
-    fields, _, tile_p, radial = low.shape[0] - 1, None, low.shape[2], low.shape[3]
-    tile_t = corona.shape[1]
-    low[:fields] = corona[:, 0:2]
-    low[fields] = kappa[0:2]
-    high[:fields] = corona[:, tile_t - 2 : tile_t]
-    high[fields] = kappa[tile_t - 2 : tile_t]
-
-
-def phi_edges(tile_t, tile_p, corona, kappa, from_low, from_high, low, high):
+    return lax.ppermute(x, axis, [(i, (i + step) % count) for i in range(count)])
+
+
+def theta_edges(corona, kappa, low, high, sems):
+    fields, tile_t = corona.shape[0], corona.shape[1]
+    copies = []
+    for side, (out, start) in enumerate(((low, 0), (high, tile_t - 2))):
+        rows = pl.ds(start, 2)
+        copies.append(
+            pltpu.make_async_copy(corona.at[:, rows], out.at[pl.ds(0, fields)], sems.at[2 * side])
+        )
+        copies.append(pltpu.make_async_copy(kappa.at[rows], out.at[fields], sems.at[2 * side + 1]))
+    for copy in copies:
+        copy.start()
+    for copy in copies:
+        copy.wait()
+
+
+def phi_edges(tile_t, tile_p, corona, kappa, low, high):
     fields = corona.shape[0]
     for f in range(fields + 1):
         for out, near, far in ((low, 0, 1), (high, tile_p - 1, tile_p - 2)):
             for at, col in ((0, near), (tile_t, far)):
                 rows = pl.ds(col, tile_t, stride=tile_p)
                 out[f, at : at + tile_t, :] = corona[f, rows, :] if f < fields else kappa[rows, :]
-            out[f, 2 * tile_t : 2 * tile_t + 1, :] = from_low[f, 1, near : near + 1, :]
-            out[f, 2 * tile_t + 1 : 2 * tile_t + 2, :] = from_high[f, 0, near : near + 1, :]
+
+
+def corner_cells(t_low, t_high, low, high):
+    count, _, tile_p, _ = t_low.shape
+    for f in range(count):
+        for out, col in ((low, 0), (high, tile_p - 1)):
+            out[2 * f : 2 * f + 1, :] = t_low[f, 1, col : col + 1, :]
+            out[2 * f + 1 : 2 * f + 2, :] = t_high[f, 0, col : col + 1, :]
 
 
 def ranks(face_t, owner, dest, rank_out, meta_out):
@@ -118,26 +130,28 @@
 
 
 def main(
-    n_dev, mixing, place, corona, kappa, t_low, t_high, p_low, p_high, base, frac, owner, rank,
-    meta, stepped, message, wide, once, column,
+    n_dev, mixing, place, corona, kappa, t_low, t_high, p_low, p_high, c_low, c_high, base, frac,
+    owner, rank, meta, stepped, message, wide, once, column,
 ):
     fields, tile_t, tile_p, radial = corona.shape
-    wide_n = tile_p + 16
+    lat, lon, last_lat, last_lon = place[0], place[1], place[2], place[3]
+    has_t = [jnp.where(lat > 0, 1.0, 0.0), jnp.where(lat < last_lat, 1.0, 0.0)]
+    has_p = [jnp.where(lon > 0, 1.0, 0.0), jnp.where(lon < last_lon, 1.0, 0.0)]
     for f in range(fields + 1):
         own = corona[f] if f < fields else kappa[...]
         wide[f, 2 : 2 + tile_t, 8 : 8 + tile_p, :] = own
-        wide[f, 0:2, 8 : 8 + tile_p, :] = t_low[f]
-        wide[f, 2 + tile_t : 4 + tile_t, 8 : 8 + tile_p, :] = t_high[f]
-        for side, (halo, near, far) in enumerate(((p_low, 7, 6), (p_high, 8 + tile_p, 9 + tile_p))):
-            for t in range(tile_t):
-                wide[f, 2 + t, near : near + 1, :] = halo[f, t : t + 1, :]
-            wide[f, 1, near : near + 1, :] = halo[f, 2 * tile_t : 2 * tile_t + 1, :]
-            wide[f, 2 + tile_t, near : near + 1, :] = halo[f, 2 * tile_t + 1 : 2 * tile_t + 2, :]
-            column[side, f, 8 : 8 + tile_t, :] = halo[f, 0:tile_t, :]
-            column[side, f, 7:8, :] = halo[f, 2 * tile_t : 2 * tile_t + 1, :]
-            column[side, f, 8 + tile_t : 9 + tile_t, :] = halo[f, 2 * tile_t + 1 : 2 * tile_t + 2, :]
-
-    lat, lon, last_lat, last_lon = place[0], place[1], place[2], place[3]
+        wide[f, 0:2, 8 : 8 + tile_p, :] = t_low[f] * has_t[0]
+        wide[f, 2 + tile_t : 4 + tile_t, 8 : 8 + tile_p, :] = t_high[f] * has_t[1]
+        for side, (halo, corner, near) in enumerate(
+            ((p_low, c_low, 7), (p_high, c_high, 8 + tile_p))
+        ):
+            column[side, f, 8 : 8 + tile_t, :] = halo[f, 0:tile_t, :] * has_p[side]
+            below = corner[2 * f : 2 * f + 1, :] * (has_p[side] * has_t[0])
+            above = corner[2 * f + 1 : 2 * f + 2, :] * (has_p[side] * has_t[1])
+            column[side, f, 7:8, :] = below
+            column[side, f, 8 + tile_t : 9 + tile_t, :] = above
+            for t in range(tile_t + 2):
+                wide[f, 1 + t, near : near + 1, :] = column[side, f, 7 + t : 8 + t, :]
 
     def around(ref, f, t, dt):
         return [
@@ -165,8 +179,6 @@
     lax.fori_loop(0, tile_t + 2, first_row, 0)
 
     for side, halo, own_col, at in ((0, p_low, 0, 7), (1, p_high, tile_p - 1, 8 + tile_p)):
-        keep = jnp.where(lon > 0, 1.0, 0.0) if side == 0 else jnp.where(lon < last_lon, 1.0, 0.0)
-
         def beside(f, side=side, halo=halo, own_col=own_col):
             own = jnp.concatenate(
                 [wide[f, 2 + t, 8 + own_col : 9 + own_col, :] for t in range(tile_t)], axis=0
@@ -174,7 +186,7 @@
             return [
                 column[side, f, 7 : 7 + tile_t, :],
                 column[side, f, 9 : 9 + tile_t, :],
-                halo[f, tile_t : 2 * tile_t, :],
+                halo[f, tile_t : 2 * tile_t, :] * has_p[side],
                 own,
             ]
 
@@ -185,7 +197,7 @@
             beside,
             lambda f: column[side, f, 8 : 8 + tile_t, :],
         ):
-            acc = acc * keep
+            acc = acc * has_p[side]
             for t in range(tile_t):
                 once[g, 1 + t, at : at + 1, :] = acc[t : t + 1, :]
 
@@ -283,23 +295,32 @@
         p_last[f : f + 1, :] = new[(f + 1) * face_p - 1 : (f + 1) * face_p, :]
 
 
-def smooth(coupled, p_low, p_high, t_low, t_high, out):
+def smooth(place, coupled, p_low, p_high, t_low, t_high, out):
     fields, face_p, face_t = coupled.shape
     x = coupled[...]
     row = iota((face_p, face_t), 0)[None]
     lane = iota((face_p, face_t), 1)[None]
 
-    def column(ref):
-        return jnp.transpose(jnp.broadcast_to(ref[...], (face_t, fields * face_p))).reshape(x.shape)
-
-    below = jnp.where(row == 0, p_low[...][:, None, :], pltpu.roll(x, 1, 1))
-    above = jnp.where(row == face_p - 1, p_high[...][:, None, :], pltpu.roll(x, face_p - 1, 1))
-    left = jnp.where(lane == 0, column(t_low), pltpu.roll(x, 1, 2))
-    right = jnp.where(lane == face_t - 1, column(t_high), pltpu.roll(x, face_t - 1, 2))
+    lat, lon, last_lat, last_lon = place[0], place[1], place[2], place[3]
+
+    def rim(ref, exists):
+        return ref[...] * jnp.where(exists, 1.0, 0.0)
+
+    def column(edge):
+        return jnp.transpose(jnp.broadcast_to(edge, (face_t, fields * face_p))).reshape(x.shape)
+
+    below = jnp.where(row == 0, rim(p_low, lon > 0)[:, None, :], pltpu.roll(x, 1, 1))
+    above = jnp.where(
+        row == face_p - 1, rim(p_high, lon < last_lon)[:, None, :], pltpu.roll(x, face_p - 1, 1)
+    )
+    left = jnp.where(lane == 0, column(rim(t_low, lat > 0)), pltpu.roll(x, 1, 2))
+    right = jnp.where(
+        lane == face_t - 1, column(rim(t_high, lat < last_lat)), pltpu.roll(x, face_t - 1, 2)
+    )
     out[...] = x + 0.2 * (above + below + right + left - 4.0 * x)
 
 
-def call(kernel, outs, specs, name, scratch=()):
+def call(kernel, outs, specs, name, scratch=(), room=40 * 1024 * 1024):
     return pl.pallas_call(
         kernel,
         out_shape=[jax.ShapeDtypeStruct(s, F32) for s in outs],
@@ -307,7 +328,7 @@
         out_specs=[vspec()] * len(outs),
         scratch_shapes=list(scratch),
         name=name,
-        compiler_params=pltpu.CompilerParams(vmem_limit_bytes=40 * 1024 * 1024),
+        compiler_params=pltpu.CompilerParams(vmem_limit_bytes=room),
     )
 
 
@@ -325,30 +346,37 @@
     )
 
     edge = (fields + 1, 2, tile_p, radial)
-    low, high = call(theta_edges, [edge] * 2, [vspec()] * 2, "theta_edges")(corona, kappa)
-    t_low = lax.ppermute(high, "lat", neighbours("lat", 1))
-    t_high = lax.ppermute(low, "lat", neighbours("lat", -1))
+    low, high = call(
+        theta_edges,
+        [edge] * 2,
+        [pl.BlockSpec(memory_space=pltpu.HBM)] * 2,
+        "theta_edges",
+        [pltpu.SemaphoreType.DMA((4,))],
+        64 * 1024 * 1024 - 600 * 1024,
+    )(corona, kappa)
+    t_low = shifted(high, "lat", 1)
+    t_high = shifted(low, "lat", -1)
+
+    edge = (fields + 1, 2 * tile_t, radial)
+    low, high = call(
+        functools.partial(phi_edges, tile_t, tile_p), [edge] * 2, [vspec()] * 2, "phi_edges"
+    )(corona.reshape(fields, tile_t * tile_p, radial), kappa.reshape(tile_t * tile_p, radial))
+    p_low = shifted(high, "lon", 1)
+    p_high = shifted(low, "lon", -1)
 
     rank, meta = call(
         functools.partial(ranks, face_t), [(1, count), (n_dev, 128)], [vspec()] * 2, "ranks"
     )(owner, dest_cell)
 
-    edge = (fields + 1, 2 * tile_t + 8, radial)
-    low, high = call(
-        functools.partial(phi_edges, tile_t, tile_p), [edge] * 2, [vspec()] * 4, "phi_edges"
-    )(
-        corona.reshape(fields, tile_t * tile_p, radial),
-        kappa.reshape(tile_t * tile_p, radial),
-        t_low,
-        t_high,
-    )
-    p_low = lax.ppermute(high, "lon", neighbours("lon", 1))
-    p_high = lax.ppermute(low, "lon", neighbours("lon", -1))
+    edge = (2 * (fields + 1), radial)
+    low, high = call(corner_cells, [edge] * 2, [vspec()] * 2, "corner_cells")(t_low, t_high)
+    c_low = shifted(high, "lon", 1)
+    c_high = shifted(low, "lon", -1)
 
     stepped, message = call(
         functools.partial(main, n_dev),
         [corona.shape, (2 * n_dev, 128)],
-        [sspec()] * 2 + [vspec()] * 11,
+        [sspec()] * 2 + [vspec()] * 13,
         "steps",
         [
             VMEM((fields + 1, tile_t + 4, tile_p + 16, radial), F32),
@@ -356,8 +384,8 @@
             VMEM((2, fields + 1, tile_t + 16, radial), F32),
         ],
     )(
-        mixing, place, corona, kappa, t_low, t_high, p_low, p_high, base, fractions, owner, rank,
-        meta,
+        mixing, place, corona, kappa, t_low, t_high, p_low, p_high, c_low, c_high, base, fractions,
+        owner, rank, meta,
     )
 
     got = lax.all_to_all(message, ("lat", "lon"), split_axis=0, concat_axis=0, tiled=True)
@@ -368,12 +396,12 @@
         [vspec()] * 2,
         "land",
     )(got, helio_prev)
-    from_t_low = lax.ppermute(t_last, "lat", neighbours("lat", 1))
-    from_t_high = lax.ppermute(t_first, "lat", neighbours("lat", -1))
-    from_p_low = lax.ppermute(p_last, "lon", neighbours("lon", 1))
-    from_p_high = lax.ppermute(p_first, "lon", neighbours("lon", -1))
-    (face,) = call(smooth, [helio_prev.shape], [vspec()] * 5, "smooth")(
-        coupled, from_p_low, from_p_high, from_t_low, from_t_high
+    from_t_low = shifted(t_last, "lat", 1)
+    from_t_high = shifted(t_first, "lat", -1)
+    from_p_low = shifted(p_last, "lon", 1)
+    from_p_high = shifted(p_first, "lon", -1)
+    (face,) = call(smooth, [helio_prev.shape], [sspec()] + [vspec()] * 5, "smooth")(
+        place, coupled, from_p_low, from_p_high, from_t_low, from_t_high
     )
     return (stepped, face)
 

time: 80.5 us -> 67.1 us (0.83)
  waiting for transfers between devices: 11.9 us -> 1.61 us
  starting transfers between devices: 24.8 us -> 21 us
  Pallas kernels: 10.9 us -> 13.1 us
  blocking collectives: 29.4 us -> 28.1 us
  local copies, waits for them, and re-layouts: 2.17 us -> 1.27 us
    ppermute x8 -> x10, waiting for transfers between devices: 11.9 us -> 1.61 us  [shifted(): lax.ppermute(x, axis, [(i, (i + step) % count) for i in range(count)])]
    ppermute x8 -> x10, starting transfers between devices: 24.8 us -> 21 us  [shifted(): lax.ppermute(x, axis, [(i, (i + step) % count) for i in range(count)])]
    pallas_call x2 -> x3, Pallas kernels: 0.9 us -> 3.2 us  [the longest x1 1.75 us: body(): call(theta_edges, [edge] * 2, [pl.BlockSpec(memory_space=pltpu.HBM)] * 2,...]
    all_to_all x1, blocking collectives: 29.4 us -> 28.1 us  [body(): lax.all_to_all(message, ('lat', 'lon'), split_axis=0, concat_axis=0, tile...]
    unnamed x20 -> x18, local copies, waits for them, and re-layouts: 2.17 us -> 1.27 us
  transfers between devices with their start and end apart: 8 -> 10, of which waited for: 4 -> 1; matrix products, arithmetic and copies ran while one was open for 0% -> 0% of each run, Pallas kernels for 2% -> 2%
where the time goes in v2:
time: 67.1 us; the launch traced here: 66 us
  blocking collectives  28.1 us (42%)
  starting transfers between devices  21 us (31%)
  Pallas kernels  13.1 us (20%)
  waiting for transfers between devices  1.61 us (2%)
  local copies, waits for them, and re-layouts  1.27 us (2%)
  between operations  0.78 us (1%)
    all_to_all x1, blocking collectives, body(): lax.all_to_all(message, ('lat', 'lon'), split_axis=0, concat_axis=0, tile...  28.1 us
    ppermute x10, starting transfers between devices, shifted(): lax.ppermute(x, axis, [(i, (i + step) % count) for i in range(count)])  21 us
    pallas_call x1, Pallas kernels, body(): call(functools.partial(main, n_dev), [corona.shape, (2 * n_dev, 128)], [s...  7.22 us
    pallas_call x1, Pallas kernels, body(): call(theta_edges, [edge] * 2, [pl.BlockSpec(memory_space=pltpu.HBM)] * 2,...  1.75 us
    ppermute x10, waiting for transfers between devices, shifted(): lax.ppermute(x, axis, [(i, (i + step) % count) for i in range(count)])  1.61 us
    pallas_call x1, Pallas kernels, body(): call(smooth, [helio_prev.shape], [sspec()] + [vspec()] * 5, 'smooth')  1.43 us
    pallas_call x1, Pallas kernels, body(): call(functools.partial(land, n_dev), [helio_prev.shape, (fields, face_t),...  1.39 us
  transfers between devices with their start and end apart: 10, of which 1 were waited for; matrix products, arithmetic and copies ran while one was open for 0% of the time, Pallas kernels for 2%

profile of v2, /device:TPU:8, one launch (start us, length us, event | category | flops | bytes accessed | tf_op | source)
XLA Modules:
  0.0 66.0 jit_solution(7633983621851833358)
XLA Ops:
  0.6 0.0 copy-start.2
  0.6 1.8 %theta_edges.1 = (f32[9,2,16,128]{3,2,1,0:T(8,128)}, f32[9,2,16,128]{3,2,1,0:T(8,128)}) custom-call(f32[8,16,16,128]{3,2,1,0:T(8,128)} %corona.3, f32[16,16,128]{2,1,0:T(8,128)} %kappa.3), custom_call_target="tpu_custom_call" | custom-call | tf_op jit(solution)/shard_map/theta_edges/pallas_call | solution.py:349
  2.4 2.0 %collective-permute-start = (f32[9,2,16,128]{3,2,1,0:T(8,128)}, f32[9,2,16,128]{3,2,1,0:T(8,128)S(1)}, u32[]{:S(2)}, u32[]{:S(2)}) collective-permute-start(f32[9,2,16,128]{3,2,1,0:T(8,128)} %get-tuple-element.17), channel_id=1, source_target_pairs={{0,32},{32,64},{64,96},{96,128},{128,160},{160,192},{192,224},{224... | collective-permute-start | bytes 442376 | tf_op jit(solution)/shard_map/ppermute | solution.py:37
  4.4 4.0 %collective-permute-start.1 = (f32[9,2,16,128]{3,2,1,0:T(8,128)}, f32[9,2,16,128]{3,2,1,0:T(8,128)S(1)}, u32[]{:S(2)}, u32[]{:S(2)}) collective-permute-start(f32[9,2,16,128]{3,2,1,0:T(8,128)} %get-tuple-element.18), channel_id=1, source_target_pairs={{0,224},{32,0},{64,32},{96,64},{128,96},{160,128},{192,160},{224,1... | collective-permute-start | bytes 442376 | tf_op jit(solution)/shard_map/ppermute | solution.py:37
  8.4 0.0 copy-done.2
  8.4 0.0 copy-start
  8.4 1.2 %copy-done = f32[8,16,16,128]{3,2,1,0:T(8,128)S(1)} copy-done((f32[8,16,16,128]{3,2,1,0:T(8,128)S(1)}, f32[8,16,16,128]{3,2,1,0:T(8,128)}, u32[]{:S(2)}) %copy-start) | copy-done | bytes 1048600
  9.6 0.0 copy-start.1
  9.7 0.1 phi_edges.1
  9.7 0.1 collective-permute-start.2
  9.8 3.8 %collective-permute-start.3 = (f32[9,32,128]{2,1,0:T(8,128)S(1)}, f32[9,32,128]{2,1,0:T(8,128)S(1)}, u32[]{:S(2)}, u32[]{:S(2)}) collective-permute-start(f32[9,32,128]{2,1,0:T(8,128)S(1)} %get-tuple-element.20), channel_id=1, source_target_pairs={{0,31},{1,0},{2,1},{3,2},{4,3},{5,4},{6,5},{7,6},{8,7},{9,8},{10,9... | collective-permute-start | bytes 442376 | tf_op jit(solution)/shard_map/ppermute | solution.py:37
  13.7 0.0 collective-permute-done.t_low
  13.7 0.0 collective-permute-done.1.t_high
  13.7 0.0 copy-start.5
  13.7 0.0 copy-start.7
  13.7 0.0 copy-start.6
  13.7 0.0 copy-start.8
  13.7 0.0 copy-start.4
  13.8 0.1 collective-permute-start.4
  13.9 3.8 %collective-permute-start.5 = (f32[18,128]{1,0:T(8,128)S(1)}, f32[18,128]{1,0:T(8,128)S(1)}, u32[]{:S(2)}, u32[]{:S(2)}) collective-permute-start(f32[18,128]{1,0:T(8,128)S(1)} %get-tuple-element.22), channel_id=1, source_target_pairs={{0,31},{1,0},{2,1},{3,2},{4,3},{5,4},{6,5},{7,6},{8,7},{9,8},{10,9... | collective-permute-start | bytes 27656 | tf_op jit(solution)/shard_map/ppermute | solution.py:37
  17.7 0.1 pad_add_fusion.place
  17.8 0.0 copy-done.5
  17.8 0.0 copy-done.7
  17.8 1.2 %ranks.1 = (f32[1,2048]{1,0:T(1,128)S(1)}, f32[256,128]{1,0:T(8,128)S(1)}) custom-call(s32[1,2048]{1,0:T(1,128)S(1)} %bitcast.13, s32[1,2048]{1,0:T(1,128)S(1)} %bitcast.16), custom_call_target="tpu_custom_call" | custom-call | tf_op jit(solution)/shard_map/ranks/pallas_call | solution.py:367
  19.0 0.0 collective-permute-done.2.p_low
  19.0 0.0 collective-permute-done.3.p_high
  19.0 0.0 collective-permute-done.4.c_low
  19.1 0.0 collective-permute-done.5.c_high
  19.1 0.0 copy-done.1
  19.1 0.0 copy-done.6
  19.1 0.0 copy-done.8
  19.1 0.0 copy-done.4
  19.1 7.2 %steps.1 = (f32[8,16,16,128]{3,2,1,0:T(8,128)}, f32[512,128]{1,0:T(8,128)S(1)}) custom-call(f32[8,8]{1,0:T(8,128)S(1)} %copy-done.8, s32[4]{0:T(128)S(1)} %pad_add_fusion.place, f32[8,16,16,128]{3,2,1,0:T(8,128)S(1)} %copy-done.1, f32[16,16,128]{2,1,0:T(8,128)S(1)} %copy-done.2, f32[9,2,16,128]{3,2,1,0:T(8,128)S(1)} %collective-permute-done.t_low, ...), custom_call_target="tpu_custom_call" | custom-call | tf_op jit(solution)/shard_map/steps/pallas_call | solution.py:376
  26.3 0.0 copy-start.3
  26.4 28.1 %all_to_all.11 = f32[256,2,128]{2,1,0:T(2,128)S(1)} all-to-all(f32[256,2,128]{2,1,0:T(2,128)S(1)} %bitcast.12), channel_id=1, replica_groups=mesh['lat'=8,'lon'=32] {'lat','lon'}, dimensions={0} | all-to-all | bytes 524288 | tf_op jit(solution)/shard_map/all_to_all | solution.py:391
  54.4 0.0 copy-done.3
  54.4 1.4 %land.1 = (f32[8,32,128]{2,1,0:T(8,128)S(1)}, f32[8,128]{1,0:T(8,128)S(1)}, f32[8,128]{1,0:T(8,128)S(1)}, f32[1,256]{1,0:T(1,128)S(1)}, f32[1,256]{1,0:T(1,128)S(1)}) custom-call(f32[512,128]{1,0:T(8,128)S(1)} %bitcast.11, f32[8,32,128]{2,1,0:T(8,128)S(1)} %copy-done.3), custom_call_target="tpu_custom_call" | custom-call | tf_op jit(solution)/shard_map/land/pallas_call | solution.py:393
  55.8 0.1 collective-permute-start.6
  55.9 3.8 %collective-permute-start.7 = (f32[8,128]{1,0:T(8,128)S(1)}, f32[8,128]{1,0:T(8,128)S(1)}, u32[]{:S(2)}, u32[]{:S(2)}) collective-permute-start(f32[8,128]{1,0:T(8,128)S(1)} %get-tuple-element.29), channel_id=1, source_target_pairs={{0,31},{1,0},{2,1},{3,2},{4,3},{5,4},{6,5},{7,6},{8,7},{9,8},{10,9... | collective-permute-start | bytes 12296 | tf_op jit(solution)/shard_map/ppermute | solution.py:37
  59.7 1.0 %collective-permute-start.8 = (f32[1,256]{1,0:T(1,128)S(1)}, f32[1,256]{1,0:T(1,128)S(1)}, u32[]{:S(2)}, u32[]{:S(2)}) collective-permute-start(f32[1,256]{1,0:T(1,128)S(1)} %get-tuple-element.30), channel_id=1, source_target_pairs={{0,32},{32,64},{64,96},{96,128},{128,160},{160,192},{192,224},{224... | collective-permute-start | bytes 3080 | tf_op jit(solution)/shard_map/ppermute | solution.py:37
  60.8 2.2 %collective-permute-start.9 = (f32[1,256]{1,0:T(1,128)S(1)}, f32[1,256]{1,0:T(1,128)S(1)}, u32[]{:S(2)}, u32[]{:S(2)}) collective-permute-start(f32[1,256]{1,0:T(1,128)S(1)} %get-tuple-element.31), channel_id=1, source_target_pairs={{0,224},{32,0},{64,32},{96,64},{128,96},{160,128},{192,160},{224,1... | collective-permute-start | bytes 3080 | tf_op jit(solution)/shard_map/ppermute | solution.py:37
  63.0 1.5 %collective-permute-done.8.t_low = f32[1,256]{1,0:T(1,128)S(1)} collective-permute-done((f32[1,256]{1,0:T(1,128)S(1)}, f32[1,256]{1,0:T(1,128)S(1)}, u32[]{:S(2)}, u32[]{:S(2)}) %collective-permute-start.8) | collective-permute-done | bytes 1056 | tf_op jit(solution)/shard_map/ppermute | solution.py:37
  64.5 0.0 collective-permute-done.9.t_high
  64.5 0.0 collective-permute-done.6.p_low
  64.5 0.0 collective-permute-done.7.p_high
  64.5 1.4 %smooth.1 = f32[8,32,128]{2,1,0:T(8,128)} custom-call(s32[4]{0:T(128)S(1)} %pad_add_fusion.place, f32[8,32,128]{2,1,0:T(8,128)S(1)} %get-tuple-element.27.coupled, f32[8,128]{1,0:T(8,128)S(1)} %collective-permute-done.6.p_low, f32[8,128]{1,0:T(8,128)S(1)} %collective-permute-done.7.p_high, f32[1,256]{1,0:T(1,128)S(1)} %collective-permute-done.8.t_low, ...), custom_call_target="tpu_custom_call" | custom-call | tf_op jit(solution)/shard_map/smooth/pallas_call | solution.py:403
  (1 shorter events, 0.0 us)
Async XLA Ops:
  0.6 7.8 %copy-start.2 = (f32[16,16,128]{2,1,0:T(8,128)S(1)}, f32[16,16,128]{2,1,0:T(8,128)}, u32[]{:S(2)}) copy-start(f32[16,16,128]{2,1,0:T(8,128)} %kappa.3) | copy-start | bytes 393220
  2.4 11.3 %collective-permute-start = (f32[9,2,16,128]{3,2,1,0:T(8,128)}, f32[9,2,16,128]{3,2,1,0:T(8,128)S(1)}, u32[]{:S(2)}, u32[]{:S(2)}) collective-permute-start(f32[9,2,16,128]{3,2,1,0:T(8,128)} %get-tuple-element.17), channel_id=1, source_target_pairs={{0,32},{32,64},{64,96},{96,128},{128,160},{160,192},{192,224},{224... | collective-permute-start | bytes 442376 | tf_op jit(solution)/shard_map/ppermute | solution.py:37
  4.4 9.3 %collective-permute-start.1 = (f32[9,2,16,128]{3,2,1,0:T(8,128)}, f32[9,2,16,128]{3,2,1,0:T(8,128)S(1)}, u32[]{:S(2)}, u32[]{:S(2)}) collective-permute-start(f32[9,2,16,128]{3,2,1,0:T(8,128)} %get-tuple-element.18), channel_id=1, source_target_pairs={{0,224},{32,0},{64,32},{96,64},{128,96},{160,128},{192,160},{224,1... | collective-permute-start | bytes 442376 | tf_op jit(solution)/shard_map/ppermute | solution.py:37
  8.4 1.2 %copy-start = (f32[8,16,16,128]{3,2,1,0:T(8,128)S(1)}, f32[8,16,16,128]{3,2,1,0:T(8,128)}, u32[]{:S(2)}) copy-start(f32[8,16,16,128]{3,2,1,0:T(8,128)} %corona.3) | copy-start | bytes 3145732
  9.6 9.5 %copy-start.1 = (f32[8,16,16,128]{3,2,1,0:T(8,128)S(1)}, f32[8,16,16,128]{3,2,1,0:T(8,128)}, u32[]{:S(2)}) copy-start(f32[8,16,16,128]{3,2,1,0:T(8,128)} %corona.3) | copy-start | bytes 3145732
  9.7 9.3 %collective-permute-start.2 = (f32[9,32,128]{2,1,0:T(8,128)S(1)}, f32[9,32,128]{2,1,0:T(8,128)S(1)}, u32[]{:S(2)}, u32[]{:S(2)}) collective-permute-start(f32[9,32,128]{2,1,0:T(8,128)S(1)} %get-tuple-element.19), channel_id=1, source_target_pairs={{0,1},{1,2},{2,3},{3,4},{4,5},{5,6},{6,7},{7,8},{8,9},{9,10},{10,1... | collective-permute-start | bytes 442376 | tf_op jit(solution)/shard_map/ppermute | solution.py:37
  9.8 9.2 %collective-permute-start.3 = (f32[9,32,128]{2,1,0:T(8,128)S(1)}, f32[9,32,128]{2,1,0:T(8,128)S(1)}, u32[]{:S(2)}, u32[]{:S(2)}) collective-permute-start(f32[9,32,128]{2,1,0:T(8,128)S(1)} %get-tuple-element.20), channel_id=1, source_target_pairs={{0,31},{1,0},{2,1},{3,2},{4,3},{5,4},{6,5},{7,6},{8,7},{9,8},{10,9... | collective-permute-start | bytes 442376 | tf_op jit(solution)/shard_map/ppermute | solution.py:37
  13.7 4.1 %copy-start.5 = (s32[2048,1]{0,1:T(1,128)S(1)}, s32[2048,1]{0,1:T(1,128)}, u32[]{:S(2)}) copy-start(s32[2048,1]{0,1:T(1,128)} %param.12) | copy-start | bytes 24580
  13.7 4.1 %copy-start.7 = (s32[2048]{0:T(1024)S(1)}, s32[2048]{0:T(1024)}, u32[]{:S(2)}) copy-start(s32[2048]{0:T(1024)} %param.13) | copy-start | bytes 24580
  13.7 5.4 %copy-start.6 = (s32[2048]{0:T(1024)S(1)}, s32[2048]{0:T(1024)}, u32[]{:S(2)}) copy-start(s32[2048]{0:T(1024)} %param.14) | copy-start | bytes 24580
  13.7 5.4 %copy-start.8 = (f32[8,8]{1,0:T(8,128)S(1)}, f32[8,8]{1,0:T(8,128)}, u32[]{:S(2)}) copy-start(f32[8,8]{1,0:T(8,128)} %mixing.1) | copy-start | bytes 772
  13.7 5.4 %copy-start.4 = (f32[3,2048]{1,0:T(4,128)S(1)}, f32[3,2048]{1,0:T(4,128)}, u32[]{:S(2)}) copy-start(f32[3,2048]{1,0:T(4,128)} %frac.1) | copy-start | bytes 73732
  13.8 5.3 %collective-permute-start.4 = (f32[18,128]{1,0:T(8,128)S(1)}, f32[18,128]{1,0:T(8,128)S(1)}, u32[]{:S(2)}, u32[]{:S(2)}) collective-permute-start(f32[18,128]{1,0:T(8,128)S(1)} %get-tuple-element.21), channel_id=1, source_target_pairs={{0,1},{1,2},{2,3},{3,4},{4,5},{5,6},{6,7},{7,8},{8,9},{9,10},{10,1... | collective-permute-start | bytes 27656 | tf_op jit(solution)/shard_map/ppermute | solution.py:37
  13.9 5.2 %collective-permute-start.5 = (f32[18,128]{1,0:T(8,128)S(1)}, f32[18,128]{1,0:T(8,128)S(1)}, u32[]{:S(2)}, u32[]{:S(2)}) collective-permute-start(f32[18,128]{1,0:T(8,128)S(1)} %get-tuple-element.22), channel_id=1, source_target_pairs={{0,31},{1,0},{2,1},{3,2},{4,3},{5,4},{6,5},{7,6},{8,7},{9,8},{10,9... | collective-permute-start | bytes 27656 | tf_op jit(solution)/shard_map/ppermute | solution.py:37
  26.3 28.1 %copy-start.3 = (f32[8,32,128]{2,1,0:T(8,128)S(1)}, f32[8,32,128]{2,1,0:T(8,128)}, u32[]{:S(2)}) copy-start(f32[8,32,128]{2,1,0:T(8,128)} %prev.1) | copy-start | bytes 393220
  55.8 8.7 %collective-permute-start.6 = (f32[8,128]{1,0:T(8,128)S(1)}, f32[8,128]{1,0:T(8,128)S(1)}, u32[]{:S(2)}, u32[]{:S(2)}) collective-permute-start(f32[8,128]{1,0:T(8,128)S(1)} %get-tuple-element.28), channel_id=1, source_target_pairs={{0,1},{1,2},{2,3},{3,4},{4,5},{5,6},{6,7},{7,8},{8,9},{9,10},{10,1... | collective-permute-start | bytes 12296 | tf_op jit(solution)/shard_map/ppermute | solution.py:37
  55.9 8.6 %collective-permute-start.7 = (f32[8,128]{1,0:T(8,128)S(1)}, f32[8,128]{1,0:T(8,128)S(1)}, u32[]{:S(2)}, u32[]{:S(2)}) collective-permute-start(f32[8,128]{1,0:T(8,128)S(1)} %get-tuple-element.29), channel_id=1, source_target_pairs={{0,31},{1,0},{2,1},{3,2},{4,3},{5,4},{6,5},{7,6},{8,7},{9,8},{10,9... | collective-permute-start | bytes 12296 | tf_op jit(solution)/shard_map/ppermute | solution.py:37
  59.7 4.8 %collective-permute-start.8 = (f32[1,256]{1,0:T(1,128)S(1)}, f32[1,256]{1,0:T(1,128)S(1)}, u32[]{:S(2)}, u32[]{:S(2)}) collective-permute-start(f32[1,256]{1,0:T(1,128)S(1)} %get-tuple-element.30), channel_id=1, source_target_pairs={{0,32},{32,64},{64,96},{96,128},{128,160},{160,192},{192,224},{224... | collective-permute-start | bytes 3080 | tf_op jit(solution)/shard_map/ppermute | solution.py:37
  60.8 3.7 %collective-permute-start.9 = (f32[1,256]{1,0:T(1,128)S(1)}, f32[1,256]{1,0:T(1,128)S(1)}, u32[]{:S(2)}, u32[]{:S(2)}) collective-permute-start(f32[1,256]{1,0:T(1,128)S(1)} %get-tuple-element.31), channel_id=1, source_target_pairs={{0,224},{32,0},{64,32},{96,64},{128,96},{160,128},{192,160},{224,1... | collective-permute-start | bytes 3080 | tf_op jit(solution)/shard_map/ppermute | solution.py:37

commit v3 on v2

--- a/solution.py
+++ b/solution.py
@@ -65,11 +65,22 @@
     count, _, tile_p, _ = t_low.shape
     for f in range(count):
         for out, col in ((low, 0), (high, tile_p - 1)):
-            out[2 * f : 2 * f + 1, :] = t_low[f, 1, col : col + 1, :]
-            out[2 * f + 1 : 2 * f + 2, :] = t_high[f, 0, col : col + 1, :]
-
-
-def ranks(face_t, owner, dest, rank_out, meta_out):
+            out[0, f : f + 1, :] = t_low[f, 1, col : col + 1, :]
+            out[1, f : f + 1, :] = t_high[f, 0, col : col + 1, :]
+
+
+def exists():
+    found = []
+    for axis in ("lat", "lon"):
+        at, count = lax.axis_index(axis), lax.axis_size(axis)
+        found.append([jnp.where(at > 0, 1.0, 0.0), jnp.where(at < count - 1, 1.0, 0.0)])
+    return found
+
+
+def plan(
+    face_t, tile_t, tile_p, owner, dest, base, frac, rank_out, meta_out, hit_out, high_out, low_out,
+    radial_out,
+):
     n_dev = meta_out.shape[0]
     count = owner.shape[1]
     width = min(BLOCK, count)
@@ -83,6 +94,7 @@
         hit = owners == owner[:, cols]
         hit_f = jnp.where(hit, 1.0, 0.0)
         hit_b = hit_f.astype(BF16)
+        hit_out[:, cols] = hit_b
         ahead = jnp.dot(hit_b, before, preferred_element_type=F32) + carry
         rank = jnp.sum(jnp.where(hit, ahead, 0.0), axis=0, keepdims=True)
         carry = ahead[:, width - 1 : width] + hit_f[:, width - 1 : width]
@@ -102,6 +114,17 @@
         meta = meta + lax.dot_general(
             hit_b, rows, (((1,), (1,)), ((), ())), preferred_element_type=F32
         )
+        corner = base[:, cols]
+
+        def pair(size, at, fraction):
+            rows = iota((size, width), 0)
+            return jnp.where(rows == at, 1.0 - fraction, jnp.where(rows == at + 1, fraction, 0.0))
+
+        w_t = pair(tile_t, corner // (tile_p * SH), frac[0:1, cols])
+        w_p = pair(tile_p, (corner // SH) % tile_p, frac[1:2, cols])
+        radial_out[:, cols] = pair(SH, corner % SH, frac[2:3, cols])
+        table = (w_t[:, None, :] * w_p[None, :, :]).reshape(tile_t * tile_p, width)
+        high_out[:, cols], low_out[:, cols] = halves(table)
     meta_out[...] = meta
 
 
@@ -129,27 +152,19 @@
         yield g, acc
 
 
-def main(
-    n_dev, mixing, place, corona, kappa, t_low, t_high, p_low, p_high, c_low, c_high, base, frac,
-    owner, rank, meta, stepped, message, wide, once, column,
-):
+def steps(mixing, corona, kappa, t_low, t_high, p_low, p_high, stepped, wide, once, column):
     fields, tile_t, tile_p, radial = corona.shape
-    lat, lon, last_lat, last_lon = place[0], place[1], place[2], place[3]
-    has_t = [jnp.where(lat > 0, 1.0, 0.0), jnp.where(lat < last_lat, 1.0, 0.0)]
-    has_p = [jnp.where(lon > 0, 1.0, 0.0), jnp.where(lon < last_lon, 1.0, 0.0)]
+    has_t, has_p = exists()
+    nothing = jnp.zeros((1, radial), F32)
     for f in range(fields + 1):
         own = corona[f] if f < fields else kappa[...]
         wide[f, 2 : 2 + tile_t, 8 : 8 + tile_p, :] = own
         wide[f, 0:2, 8 : 8 + tile_p, :] = t_low[f] * has_t[0]
         wide[f, 2 + tile_t : 4 + tile_t, 8 : 8 + tile_p, :] = t_high[f] * has_t[1]
-        for side, (halo, corner, near) in enumerate(
-            ((p_low, c_low, 7), (p_high, c_high, 8 + tile_p))
-        ):
+        for side, (halo, near) in enumerate(((p_low, 7), (p_high, 8 + tile_p))):
             column[side, f, 8 : 8 + tile_t, :] = halo[f, 0:tile_t, :] * has_p[side]
-            below = corner[2 * f : 2 * f + 1, :] * (has_p[side] * has_t[0])
-            above = corner[2 * f + 1 : 2 * f + 2, :] * (has_p[side] * has_t[1])
-            column[side, f, 7:8, :] = below
-            column[side, f, 8 + tile_t : 9 + tile_t, :] = above
+            column[side, f, 7:8, :] = nothing
+            column[side, f, 8 + tile_t : 9 + tile_t, :] = nothing
             for t in range(tile_t + 2):
                 wide[f, 1 + t, near : near + 1, :] = column[side, f, 7 + t : 8 + t, :]
 
@@ -162,10 +177,7 @@
         ]
 
     def first_row(t, _):
-        exists = jnp.logical_and(
-            jnp.logical_or(t > 0, lat > 0), jnp.logical_or(t < tile_t + 1, lat < last_lat)
-        )
-        keep = jnp.where(exists, 1.0, 0.0)
+        keep = jnp.where(t == 0, has_t[0], jnp.where(t == tile_t + 1, has_t[1], 1.0))
         for g, acc in flux(
             fields,
             mixing,
@@ -214,45 +226,62 @@
 
     lax.fori_loop(0, tile_t, second_row, 0)
 
+
+def route(
+    n_dev, kappa, p_low, p_high, own_low, own_high, c_low, c_high, stepped, rank, meta, hit,
+    table_high, table_low, w_r, patch, message, shell,
+):
+    fields, tile_t, tile_p, radial = stepped.shape
+    has_t, has_p = exists()
     columns = tile_t * tile_p
     lane = iota((columns, radial), 1)
-    shell = jnp.zeros((columns, radial), F32)
+    rows = jnp.zeros((columns, radial), F32)
     for f in range(fields):
         moved = pltpu.roll(stepped[f].reshape(columns, radial), (f * SH + SH) % radial, 1)
-        shell = jnp.where(lane // SH == f, moved, shell)
-    high = shell.astype(BF16).astype(F32)
-    both = high + pltpu.roll(shell - high, fields * SH, 1)
+        rows = jnp.where(lane // SH == f, moved, rows)
+    shell[...] = rows
+    for a in range(2):
+        for b, (halo, own, diagonal) in enumerate(
+            ((p_low, own_low, c_low), (p_high, own_high, c_high))
+        ):
+            t, p = a * (tile_t - 1), b * (tile_p - 1)
+            k_t, u_t = own[a, fields : fields + 1] * has_t[a], own[a, 0:fields] * has_t[a]
+            k_p = halo[fields, t : t + 1, :] * has_p[b]
+            u_p = jnp.concatenate([halo[f, t : t + 1, :] for f in range(fields)], axis=0) * has_p[b]
+            both = has_t[a] * has_p[b]
+            k_d, u_d = diagonal[a, fields : fields + 1] * both, diagonal[a, 0:fields] * both
+            k = kappa[t, p : p + 1, :]
+            by_t = 0.075 * ((k_t + k_d) * u_d - k_d * u_t)
+            by_p = 0.075 * ((k_p + k_d) * u_d - k_d * u_p)
+            extra = 0.075 * ((k + k_t) * by_t + (k + k_p) * by_p)
+            patch[2 * a + b] = extra
+            row = jnp.zeros((1, radial), F32)
+            for f in range(fields):
+                moved = pltpu.roll(extra[f : f + 1], (f * SH + SH) % radial, 1)
+                row = jnp.where(lane[0:1] // SH == f, moved, row)
+            at = t * tile_p + p
+            shell[at : at + 1, :] = shell[at : at + 1, :] + row
+    rows = shell[...]
+    high = rows.astype(BF16).astype(F32)
+    both = high + pltpu.roll(rows - high, fields * SH, 1)
     left = jnp.transpose(both).astype(BF16)
 
-    count = base.shape[1]
+    count = rank.shape[1]
     width = min(BLOCK, count)
-    owners = iota((n_dev, width), 0)
     packed = jnp.zeros((n_dev, 2 * fields * CAP), F32)
     for b in range(count // width):
         cols = slice(b * width, (b + 1) * width)
-        cell = base[:, cols]
-
-        def pair(size, at, fraction):
-            rows = iota((size, width), 0)
-            return jnp.where(rows == at, 1.0 - fraction, jnp.where(rows == at + 1, fraction, 0.0))
-
-        w_t = pair(tile_t, cell // (tile_p * SH), frac[0:1, cols])
-        w_p = pair(tile_p, (cell // SH) % tile_p, frac[1:2, cols])
-        w_r = pair(SH, cell % SH, frac[2:3, cols])
-        table = (w_t[:, None, :] * w_p[None, :, :]).reshape(columns, width)
-        table_high, table_low = halves(table)
-        coarse = jnp.dot(left, table_high, preferred_element_type=F32)
-        fine = jnp.dot(left[: fields * SH], table_low, preferred_element_type=F32)
+        coarse = jnp.dot(left, table_high[:, cols], preferred_element_type=F32)
+        fine = jnp.dot(left[: fields * SH], table_low[:, cols], preferred_element_type=F32)
         by_layer = coarse[: fields * SH] + (coarse[fields * SH :] + fine)
-        value = jnp.sum(by_layer.reshape(fields, SH, width) * w_r[None], axis=1)
+        value = jnp.sum(by_layer.reshape(fields, SH, width) * w_r[:, cols][None], axis=1)
         order = rank[:, cols]
         placed = jnp.concatenate(
             [jnp.where(order == float(k), value, 0.0) for k in range(CAP)], axis=0
         )
         placed_high, placed_low = halves(placed)
-        hit = jnp.where(owners == owner[:, cols], 1.0, 0.0).astype(BF16)
         packed = packed + lax.dot_general(
-            hit,
+            hit[:, cols],
             jnp.concatenate([placed_high, placed_low], axis=0),
             (((1,), (1,)), ((), ())),
             preferred_element_type=F32,
@@ -260,6 +289,18 @@
     half = fields * CAP
     message[pl.ds(0, n_dev, stride=2), :] = packed[:, :half] + packed[:, half:]
     message[pl.ds(1, n_dev, stride=2), :] = meta[...]
+
+
+def finish(stepped, patch, out):
+    fields, tile_t, tile_p, _ = stepped.shape
+    out[...] = stepped[...]
+    for a in range(2):
+        for b in range(2):
+            t, p = a * (tile_t - 1), b * (tile_p - 1)
+            for f in range(fields):
+                out[f, t, p : p + 1, :] = (
+                    stepped[f, t, p : p + 1, :] + patch[2 * a + b, f : f + 1, :]
+                )
 
 
 def land(n_dev, got, prev, coupled, p_first, p_last, t_first, t_last):
@@ -295,37 +336,38 @@
         p_last[f : f + 1, :] = new[(f + 1) * face_p - 1 : (f + 1) * face_p, :]
 
 
-def smooth(place, coupled, p_low, p_high, t_low, t_high, out):
+def smooth(coupled, p_low, p_high, t_low, t_high, out):
     fields, face_p, face_t = coupled.shape
     x = coupled[...]
     row = iota((face_p, face_t), 0)[None]
     lane = iota((face_p, face_t), 1)[None]
 
-    lat, lon, last_lat, last_lon = place[0], place[1], place[2], place[3]
-
-    def rim(ref, exists):
-        return ref[...] * jnp.where(exists, 1.0, 0.0)
+    has_t, has_p = exists()
+
+    def rim(ref, has):
+        return ref[...] * has
 
     def column(edge):
         return jnp.transpose(jnp.broadcast_to(edge, (face_t, fields * face_p))).reshape(x.shape)
 
-    below = jnp.where(row == 0, rim(p_low, lon > 0)[:, None, :], pltpu.roll(x, 1, 1))
+    below = jnp.where(row == 0, rim(p_low, has_p[0])[:, None, :], pltpu.roll(x, 1, 1))
     above = jnp.where(
-        row == face_p - 1, rim(p_high, lon < last_lon)[:, None, :], pltpu.roll(x, face_p - 1, 1)
-    )
-    left = jnp.where(lane == 0, column(rim(t_low, lat > 0)), pltpu.roll(x, 1, 2))
+        row == face_p - 1, rim(p_high, has_p[1])[:, None, :], pltpu.roll(x, face_p - 1, 1)
+    )
+    left = jnp.where(lane == 0, column(rim(t_low, has_t[0])), pltpu.roll(x, 1, 2))
     right = jnp.where(
-        lane == face_t - 1, column(rim(t_high, lat < last_lat)), pltpu.roll(x, face_t - 1, 2)
+        lane == face_t - 1, column(rim(t_high, has_t[1])), pltpu.roll(x, face_t - 1, 2)
     )
     out[...] = x + 0.2 * (above + below + right + left - 4.0 * x)
 
 
-def call(kernel, outs, specs, name, scratch=(), room=40 * 1024 * 1024):
+def call(kernel, outs, specs, name, scratch=(), out_spec=None, room=40 * 1024 * 1024):
+    outs = [s if isinstance(s, jax.ShapeDtypeStruct) else jax.ShapeDtypeStruct(s, F32) for s in outs]
     return pl.pallas_call(
         kernel,
-        out_shape=[jax.ShapeDtypeStruct(s, F32) for s in outs],
+        out_shape=outs,
         in_specs=specs,
-        out_specs=[vspec()] * len(outs),
+        out_specs=[out_spec or vspec()] * len(outs),
         scratch_shapes=list(scratch),
         name=name,
         compiler_params=pltpu.CompilerParams(vmem_limit_bytes=room),
@@ -341,10 +383,6 @@
     owner = owner.reshape(1, count)
     dest_cell = dest_cell.reshape(1, count)
     base = corner_base.reshape(1, count)
-    place = jnp.stack(
-        [lax.axis_index("lat"), lax.axis_index("lon"), jnp.int32(n_lat - 1), jnp.int32(n_lon - 1)]
-    )
-
     edge = (fields + 1, 2, tile_p, radial)
     low, high = call(
         theta_edges,
@@ -352,6 +390,7 @@
         [pl.BlockSpec(memory_space=pltpu.HBM)] * 2,
         "theta_edges",
         [pltpu.SemaphoreType.DMA((4,))],
+        pl.BlockSpec(memory_space=pltpu.HBM),
         64 * 1024 * 1024 - 600 * 1024,
     )(corona, kappa)
     t_low = shifted(high, "lat", 1)
@@ -364,29 +403,44 @@
     p_low = shifted(high, "lon", 1)
     p_high = shifted(low, "lon", -1)
 
-    rank, meta = call(
-        functools.partial(ranks, face_t), [(1, count), (n_dev, 128)], [vspec()] * 2, "ranks"
-    )(owner, dest_cell)
-
-    edge = (2 * (fields + 1), radial)
-    low, high = call(corner_cells, [edge] * 2, [vspec()] * 2, "corner_cells")(t_low, t_high)
-    c_low = shifted(high, "lon", 1)
-    c_high = shifted(low, "lon", -1)
-
-    stepped, message = call(
-        functools.partial(main, n_dev),
-        [corona.shape, (2 * n_dev, 128)],
-        [sspec()] * 2 + [vspec()] * 13,
+    table = jax.ShapeDtypeStruct((tile_t * tile_p, count), BF16)
+    rank, meta, hit, table_high, table_low, w_r = call(
+        functools.partial(plan, face_t, tile_t, tile_p),
+        [(1, count), (n_dev, 128), jax.ShapeDtypeStruct((n_dev, count), BF16), table, table]
+        + [(SH, count)],
+        [vspec()] * 4,
+        "plan",
+    )(owner, dest_cell, base, fractions)
+
+    own_low, own_high = call(
+        corner_cells, [(2, fields + 1, radial)] * 2, [vspec()] * 2, "corner_cells"
+    )(t_low, t_high)
+    c_low = shifted(own_high, "lon", 1)
+    c_high = shifted(own_low, "lon", -1)
+
+    (almost,) = call(
+        steps,
+        [corona.shape],
+        [sspec()] + [vspec()] * 6,
         "steps",
         [
             VMEM((fields + 1, tile_t + 4, tile_p + 16, radial), F32),
             VMEM((fields, tile_t + 2, tile_p + 16, radial), F32),
             VMEM((2, fields + 1, tile_t + 16, radial), F32),
         ],
+    )(mixing, corona, kappa, t_low, t_high, p_low, p_high)
+
+    patch, message = call(
+        functools.partial(route, n_dev),
+        [(4, fields, radial), (2 * n_dev, 128)],
+        [vspec()] * 14,
+        "route",
+        [VMEM((tile_t * tile_p, radial), F32)],
     )(
-        mixing, place, corona, kappa, t_low, t_high, p_low, p_high, c_low, c_high, base, fractions,
-        owner, rank, meta,
-    )
+        kappa, p_low, p_high, own_low, own_high, c_low, c_high, almost, rank, meta, hit, table_high,
+        table_low, w_r,
+    )
+    (stepped,) = call(finish, [corona.shape], [vspec()] * 2, "finish")(almost, patch)
 
     got = lax.all_to_all(message, ("lat", "lon"), split_axis=0, concat_axis=0, tiled=True)
 
@@ -400,8 +454,8 @@
     from_t_high = shifted(t_first, "lat", -1)
     from_p_low = shifted(p_last, "lon", 1)
     from_p_high = shifted(p_first, "lon", -1)
-    (face,) = call(smooth, [helio_prev.shape], [sspec()] + [vspec()] * 5, "smooth")(
-        place, coupled, from_p_low, from_p_high, from_t_low, from_t_high
+    (face,) = call(smooth, [helio_prev.shape], [vspec()] * 5, "smooth")(
+        coupled, from_p_low, from_p_high, from_t_low, from_t_high
     )
     return (stepped, face)
 

time: 67.1 us -> 71.7 us (1.069)
  Pallas kernels: 13.1 us -> 22.7 us
  starting transfers between devices: 21 us -> 17.9 us
  waiting for transfers between devices: 1.61 us -> 0.53 us
  blocking collectives: 28.1 us -> 27.3 us
    pallas_call x1, Pallas kernels: 1.75 us -> 10.1 us  [body(): call(theta_edges, [edge] * 2, [pl.BlockSpec(memory_space=pltpu.HBM)] * 2,...]
    ppermute x10, starting transfers between devices: 21 us -> 17.9 us  [shifted(): lax.ppermute(x, axis, [(i, (i + step) % count) for i in range(count)])]
    pallas_call x4 -> x6, Pallas kernels: 9.91 us -> 11.1 us  [the longest x1 5.45 us: body(): call(steps, [corona.shape], [sspec()] + [vspec()] * 6, 'steps', [VMEM((fi...]
    ppermute x10, waiting for transfers between devices: 1.61 us -> 0.53 us  [shifted(): lax.ppermute(x, axis, [(i, (i + step) % count) for i in range(count)])]
  transfers between devices with their start and end apart: 10 -> 10, of which waited for: 1 -> 1; matrix products, arithmetic and copies ran while one was open for 0% -> 0% of each run, Pallas kernels for 2% -> 12%
where the time goes in v3:
time: 71.7 us; the launch traced here: 70.6 us
  blocking collectives  27.3 us (38%)
  Pallas kernels  22.7 us (32%)
  starting transfers between devices  17.9 us (25%)
  local copies, waits for them, and re-layouts  1.36 us (2%)
  between operations  0.78 us (1%)
    all_to_all x1, blocking collectives, body(): lax.all_to_all(message, ('lat', 'lon'), split_axis=0, concat_axis=0, tile...  27.3 us
    ppermute x10, starting transfers between devices, shifted(): lax.ppermute(x, axis, [(i, (i + step) % count) for i in range(count)])  17.9 us
    pallas_call x1, Pallas kernels, body(): call(theta_edges, [edge] * 2, [pl.BlockSpec(memory_space=pltpu.HBM)] * 2,...  10.1 us
    pallas_call x1, Pallas kernels, body(): call(steps, [corona.shape], [sspec()] + [vspec()] * 6, 'steps', [VMEM((fi...  5.45 us
    pallas_call x1, Pallas kernels, body(): call(functools.partial(plan, face_t, tile_t, tile_p), [(1, count), (n_dev...  2.04 us
    pallas_call x1, Pallas kernels, body(): call(functools.partial(route, n_dev), [(4, fields, radial), (2 * n_dev, 1...  1.67 us
  transfers between devices with their start and end apart: 10, of which 1 were waited for; matrix products, arithmetic and copies ran while one was open for 0% of the time, Pallas kernels for 12%

profile of v3, /device:TPU:8, one launch (start us, length us, event | category | flops | bytes accessed | tf_op | source)
XLA Modules:
  0.0 70.6 jit_solution(109610232701359759)
XLA Ops:
  0.6 0.0 copy-start.2
  0.6 10.1 %theta_edges.1 = (f32[9,2,16,128]{3,2,1,0:T(8,128)}, f32[9,2,16,128]{3,2,1,0:T(8,128)}) custom-call(f32[8,16,16,128]{3,2,1,0:T(8,128)} %corona.3, f32[16,16,128]{2,1,0:T(8,128)} %kappa.5), custom_call_target="tpu_custom_call" | custom-call | tf_op jit(solution)/shard_map/theta_edges/pallas_call | solution.py:387
  10.7 2.0 %collective-permute-start = (f32[9,2,16,128]{3,2,1,0:T(8,128)}, f32[9,2,16,128]{3,2,1,0:T(8,128)S(1)}, u32[]{:S(2)}, u32[]{:S(2)}) collective-permute-start(f32[9,2,16,128]{3,2,1,0:T(8,128)} %get-tuple-element.21), channel_id=1, source_target_pairs={{0,32},{32,64},{64,96},{96,128},{128,160},{160,192},{192,224},{224... | collective-permute-start | bytes 442376 | tf_op jit(solution)/shard_map/ppermute | solution.py:37
  12.7 4.0 %collective-permute-start.1 = (f32[9,2,16,128]{3,2,1,0:T(8,128)}, f32[9,2,16,128]{3,2,1,0:T(8,128)S(1)}, u32[]{:S(2)}, u32[]{:S(2)}) collective-permute-start(f32[9,2,16,128]{3,2,1,0:T(8,128)} %get-tuple-element.22), channel_id=1, source_target_pairs={{0,224},{32,0},{64,32},{96,64},{128,96},{160,128},{192,160},{224,1... | collective-permute-start | bytes 442376 | tf_op jit(solution)/shard_map/ppermute | solution.py:37
  16.7 0.0 copy-done.2
  16.7 0.0 copy-start
  16.7 1.2 %copy-done = f32[8,16,16,128]{3,2,1,0:T(8,128)S(1)} copy-done((f32[8,16,16,128]{3,2,1,0:T(8,128)S(1)}, f32[8,16,16,128]{3,2,1,0:T(8,128)}, u32[]{:S(2)}) %copy-start) | copy-done | bytes 1048600
  18.0 0.0 copy-start.1
  18.0 0.1 phi_edges.1
  18.1 0.1 collective-permute-start.2
  18.2 0.0 copy-start.4
  18.2 3.8 %collective-permute-start.3 = (f32[9,32,128]{2,1,0:T(8,128)S(1)}, f32[9,32,128]{2,1,0:T(8,128)S(1)}, u32[]{:S(2)}, u32[]{:S(2)}) collective-permute-start(f32[9,32,128]{2,1,0:T(8,128)S(1)} %get-tuple-element.24), channel_id=1, source_target_pairs={{0,31},{1,0},{2,1},{3,2},{4,3},{5,4},{6,5},{7,6},{8,7},{9,8},{10,9... | collective-permute-start | bytes 442376 | tf_op jit(solution)/shard_map/ppermute | solution.py:37
  22.0 0.0 collective-permute-done.t_low
  22.0 0.0 collective-permute-done.1.t_high
  22.0 0.0 copy-start.6
  22.0 0.0 copy-start.7
  22.0 0.0 copy-start.5
  22.1 0.3 collective-permute-start.5
  22.4 0.3 collective-permute-start.4
  22.6 0.0 copy-done.4
  22.7 0.1 copy-done.6
  22.7 0.0 copy-done.7
  22.7 0.0 copy-done.5
  22.8 0.0 copy-start.8
  22.8 2.0 %plan.1 = (f32[1,2048]{1,0:T(1,128)S(1)}, f32[256,128]{1,0:T(8,128)S(1)}, bf16[256,2048]{1,0:T(8,128)(2,1)S(1)}, bf16[256,2048]{1,0:T(8,128)(2,1)S(1)}, bf16[256...) custom-call(s32[1,2048]{1,0:T(1,128)S(1)} %bitcast.11, s32[1,2048]{1,0:T(1,128)S(1)} %bitcast.12, s32[1,2048]{1,0:T(1,128)S(1)} %bitcast.13, ...), custom_call_target="tpu_custom_call" | custom-call | tf_op jit(solution)/shard_map/plan/pallas_call | solution.py:407
  24.8 0.0 collective-permute-done.2.p_low
  24.8 0.0 collective-permute-done.3.p_high
  24.8 0.0 copy-done.1
  24.8 0.0 copy-done.8
  24.8 5.4 %steps.1.stepped = f32[8,16,16,128]{3,2,1,0:T(8,128)S(1)} custom-call(f32[8,8]{1,0:T(8,128)S(1)} %copy-done.8, f32[8,16,16,128]{3,2,1,0:T(8,128)S(1)} %copy-done.1, f32[16,16,128]{2,1,0:T(8,128)S(1)} %copy-done.2, f32[9,2,16,128]{3,2,1,0:T(8,128)S(1)} %collective-permute-done.t_low, f32[9,2,16,128]{3,2,1,0:T(8,128)S(1)} %collective-permute-done.1.t_high, ...), custom_call_target="tpu_custom_call" | custom-call | tf_op jit(solution)/shard_map/steps/pallas_call | solution.py:421
  30.3 0.0 collective-permute-done.5.c_high
  30.3 0.0 collective-permute-done.4.c_low
  30.3 1.7 %route.1 = (f32[4,8,128]{2,1,0:T(8,128)S(1)}, f32[512,128]{1,0:T(8,128)S(1)}) custom-call(f32[16,16,128]{2,1,0:T(8,128)S(1)} %copy-done.2, f32[9,32,128]{2,1,0:T(8,128)S(1)} %collective-permute-done.2.p_low, f32[9,32,128]{2,1,0:T(8,128)S(1)} %collective-permute-done.3.p_high, f32[2,9,128]{2,1,0:T(8,128)S(1)} %get-tuple-element.25.own_low, ...), custom_call_target="tpu_custom_call" | custom-call | tf_op jit(solution)/shard_map/route/pallas_call | solution.py:433
  32.0 0.0 copy-start.3
  32.0 27.3 %all_to_all.11 = f32[256,2,128]{2,1,0:T(2,128)S(1)} all-to-all(f32[256,2,128]{2,1,0:T(2,128)S(1)} %bitcast.10), channel_id=1, replica_groups=mesh['lat'=8,'lon'=32] {'lat','lon'}, dimensions={0} | all-to-all | bytes 524288 | tf_op jit(solution)/shard_map/all_to_all | solution.py:445
  59.3 0.0 copy-done.3
  59.3 1.4 %land.1 = (f32[8,32,128]{2,1,0:T(8,128)S(1)}, f32[8,128]{1,0:T(8,128)S(1)}, f32[8,128]{1,0:T(8,128)S(1)}, f32[1,256]{1,0:T(1,128)S(1)}, f32[1,256]{1,0:T(1,128)S(1)}) custom-call(f32[512,128]{1,0:T(8,128)S(1)} %bitcast.9, f32[8,32,128]{2,1,0:T(8,128)S(1)} %copy-done.3), custom_call_target="tpu_custom_call" | custom-call | tf_op jit(solution)/shard_map/land/pallas_call | solution.py:447
  60.7 0.3 collective-permute-start.6
  61.0 3.8 %collective-permute-start.7 = (f32[8,128]{1,0:T(8,128)S(1)}, f32[8,128]{1,0:T(8,128)S(1)}, u32[]{:S(2)}, u32[]{:S(2)}) collective-permute-start(f32[8,128]{1,0:T(8,128)S(1)} %get-tuple-element.37), channel_id=1, source_target_pairs={{0,31},{1,0},{2,1},{3,2},{4,3},{5,4},{6,5},{7,6},{8,7},{9,8},{10,9... | collective-permute-start | bytes 12296 | tf_op jit(solution)/shard_map/ppermute | solution.py:37
  64.9 1.0 %collective-permute-start.8 = (f32[1,256]{1,0:T(1,128)S(1)}, f32[1,256]{1,0:T(1,128)S(1)}, u32[]{:S(2)}, u32[]{:S(2)}) collective-permute-start(f32[1,256]{1,0:T(1,128)S(1)} %get-tuple-element.38), channel_id=1, source_target_pairs={{0,32},{32,64},{64,96},{96,128},{128,160},{160,192},{192,224},{224... | collective-permute-start | bytes 3080 | tf_op jit(solution)/shard_map/ppermute | solution.py:37
  65.9 2.2 %collective-permute-start.9 = (f32[1,256]{1,0:T(1,128)S(1)}, f32[1,256]{1,0:T(1,128)S(1)}, u32[]{:S(2)}, u32[]{:S(2)}) collective-permute-start(f32[1,256]{1,0:T(1,128)S(1)} %get-tuple-element.39), channel_id=1, source_target_pairs={{0,224},{32,0},{64,32},{96,64},{128,96},{160,128},{192,160},{224,1... | collective-permute-start | bytes 3080 | tf_op jit(solution)/shard_map/ppermute | solution.py:37
  68.1 1.1 %finish.1 = f32[8,16,16,128]{3,2,1,0:T(8,128)} custom-call(f32[8,16,16,128]{3,2,1,0:T(8,128)S(1)} %steps.1.stepped, f32[4,8,128]{2,1,0:T(8,128)S(1)} %get-tuple-element.33.patch), custom_call_target="tpu_custom_call" | custom-call | tf_op jit(solution)/shard_map/finish/pallas_call | solution.py:443
  69.2 0.5 collective-permute-done.8.t_low
  69.6 0.0 collective-permute-done.9.t_high
  69.6 0.0 collective-permute-done.6.p_low
  69.6 0.0 collective-permute-done.7.p_high
  69.7 0.9 %smooth.1 = f32[8,32,128]{2,1,0:T(8,128)} custom-call(f32[8,32,128]{2,1,0:T(8,128)S(1)} %get-tuple-element.35.coupled, f32[8,128]{1,0:T(8,128)S(1)} %collective-permute-done.6.p_low, f32[8,128]{1,0:T(8,128)S(1)} %collective-permute-done.7.p_high, f32[1,256]{1,0:T(1,128)S(1)} %collective-permute-done.8.t_low, f32[1,256]{1,0:T(1,128)S(1)} %collective-permute-done.9.t_high), custom_call_target="tpu_custom_call" | custom-call | tf_op jit(solution)/shard_map/smooth/pallas_call | solution.py:457
  (1 shorter events, 0.0 us)
Async XLA Ops:
  0.6 16.1 %copy-start.2 = (f32[16,16,128]{2,1,0:T(8,128)S(1)}, f32[16,16,128]{2,1,0:T(8,128)}, u32[]{:S(2)}) copy-start(f32[16,16,128]{2,1,0:T(8,128)} %kappa.5) | copy-start | bytes 393220
  10.7 11.3 %collective-permute-start = (f32[9,2,16,128]{3,2,1,0:T(8,128)}, f32[9,2,16,128]{3,2,1,0:T(8,128)S(1)}, u32[]{:S(2)}, u32[]{:S(2)}) collective-permute-start(f32[9,2,16,128]{3,2,1,0:T(8,128)} %get-tuple-element.21), channel_id=1, source_target_pairs={{0,32},{32,64},{64,96},{96,128},{128,160},{160,192},{192,224},{224... | collective-permute-start | bytes 442376 | tf_op jit(solution)/shard_map/ppermute | solution.py:37
  12.7 9.3 %collective-permute-start.1 = (f32[9,2,16,128]{3,2,1,0:T(8,128)}, f32[9,2,16,128]{3,2,1,0:T(8,128)S(1)}, u32[]{:S(2)}, u32[]{:S(2)}) collective-permute-start(f32[9,2,16,128]{3,2,1,0:T(8,128)} %get-tuple-element.22), channel_id=1, source_target_pairs={{0,224},{32,0},{64,32},{96,64},{128,96},{160,128},{192,160},{224,1... | collective-permute-start | bytes 442376 | tf_op jit(solution)/shard_map/ppermute | solution.py:37
  16.7 1.2 %copy-start = (f32[8,16,16,128]{3,2,1,0:T(8,128)S(1)}, f32[8,16,16,128]{3,2,1,0:T(8,128)}, u32[]{:S(2)}) copy-start(f32[8,16,16,128]{3,2,1,0:T(8,128)} %corona.3) | copy-start | bytes 3145732
  18.0 6.9 %copy-start.1 = (f32[8,16,16,128]{3,2,1,0:T(8,128)S(1)}, f32[8,16,16,128]{3,2,1,0:T(8,128)}, u32[]{:S(2)}) copy-start(f32[8,16,16,128]{3,2,1,0:T(8,128)} %corona.3) | copy-start | bytes 3145732
  18.1 6.8 %collective-permute-start.2 = (f32[9,32,128]{2,1,0:T(8,128)S(1)}, f32[9,32,128]{2,1,0:T(8,128)S(1)}, u32[]{:S(2)}, u32[]{:S(2)}) collective-permute-start(f32[9,32,128]{2,1,0:T(8,128)S(1)} %get-tuple-element.23), channel_id=1, source_target_pairs={{0,1},{1,2},{2,3},{3,4},{4,5},{5,6},{6,7},{7,8},{8,9},{9,10},{10,1... | collective-permute-start | bytes 442376 | tf_op jit(solution)/shard_map/ppermute | solution.py:37
  18.2 4.5 %copy-start.4 = (f32[3,2048]{1,0:T(4,128)S(1)}, f32[3,2048]{1,0:T(4,128)}, u32[]{:S(2)}) copy-start(f32[3,2048]{1,0:T(4,128)} %frac.1) | copy-start | bytes 73732
  18.2 6.7 %collective-permute-start.3 = (f32[9,32,128]{2,1,0:T(8,128)S(1)}, f32[9,32,128]{2,1,0:T(8,128)S(1)}, u32[]{:S(2)}, u32[]{:S(2)}) collective-permute-start(f32[9,32,128]{2,1,0:T(8,128)S(1)} %get-tuple-element.24), channel_id=1, source_target_pairs={{0,31},{1,0},{2,1},{3,2},{4,3},{5,4},{6,5},{7,6},{8,7},{9,8},{10,9... | collective-permute-start | bytes 442376 | tf_op jit(solution)/shard_map/ppermute | solution.py:37
  22.0 0.7 copy-start.6
  22.0 0.7 %copy-start.7 = (s32[2048]{0:T(1024)S(1)}, s32[2048]{0:T(1024)}, u32[]{:S(2)}) copy-start(s32[2048]{0:T(1024)} %param.14) | copy-start | bytes 24580
  22.0 0.7 copy-start.5
  22.1 8.2 %collective-permute-start.5 = (f32[2,9,128]{2,1,0:T(8,128)S(1)}, f32[2,9,128]{2,1,0:T(8,128)S(1)}, u32[]{:S(2)}, u32[]{:S(2)}) collective-permute-start(f32[2,9,128]{2,1,0:T(8,128)S(1)} %get-tuple-element.25.own_low), channel_id=1, source_target_pairs={{0,31},{1,0},{2,1},{3,2},{4,3},{5,4},{6,5},{7,6},{8,7},{9,8},{10,9... | collective-permute-start | bytes 27656 | tf_op jit(solution)/shard_map/ppermute | solution.py:37
  22.4 7.9 %collective-permute-start.4 = (f32[2,9,128]{2,1,0:T(8,128)S(1)}, f32[2,9,128]{2,1,0:T(8,128)S(1)}, u32[]{:S(2)}, u32[]{:S(2)}) collective-permute-start(f32[2,9,128]{2,1,0:T(8,128)S(1)} %get-tuple-element.26.own_high), channel_id=1, source_target_pairs={{0,1},{1,2},{2,3},{3,4},{4,5},{5,6},{6,7},{7,8},{8,9},{9,10},{10,1... | collective-permute-start | bytes 27656 | tf_op jit(solution)/shard_map/ppermute | solution.py:37
  22.8 2.1 %copy-start.8 = (f32[8,8]{1,0:T(8,128)S(1)}, f32[8,8]{1,0:T(8,128)}, u32[]{:S(2)}) copy-start(f32[8,8]{1,0:T(8,128)} %mixing.1) | copy-start | bytes 772
  32.0 27.4 %copy-start.3 = (f32[8,32,128]{2,1,0:T(8,128)S(1)}, f32[8,32,128]{2,1,0:T(8,128)}, u32[]{:S(2)}) copy-start(f32[8,32,128]{2,1,0:T(8,128)} %prev.1) | copy-start | bytes 393220
  60.7 8.9 %collective-permute-start.6 = (f32[8,128]{1,0:T(8,128)S(1)}, f32[8,128]{1,0:T(8,128)S(1)}, u32[]{:S(2)}, u32[]{:S(2)}) collective-permute-start(f32[8,128]{1,0:T(8,128)S(1)} %get-tuple-element.36), channel_id=1, source_target_pairs={{0,1},{1,2},{2,3},{3,4},{4,5},{5,6},{6,7},{7,8},{8,9},{9,10},{10,1... | collective-permute-start | bytes 12296 | tf_op jit(solution)/shard_map/ppermute | solution.py:37
  61.0 8.6 %collective-permute-start.7 = (f32[8,128]{1,0:T(8,128)S(1)}, f32[8,128]{1,0:T(8,128)S(1)}, u32[]{:S(2)}, u32[]{:S(2)}) collective-permute-start(f32[8,128]{1,0:T(8,128)S(1)} %get-tuple-element.37), channel_id=1, source_target_pairs={{0,31},{1,0},{2,1},{3,2},{4,3},{5,4},{6,5},{7,6},{8,7},{9,8},{10,9... | collective-permute-start | bytes 12296 | tf_op jit(solution)/shard_map/ppermute | solution.py:37
  64.9 4.8 %collective-permute-start.8 = (f32[1,256]{1,0:T(1,128)S(1)}, f32[1,256]{1,0:T(1,128)S(1)}, u32[]{:S(2)}, u32[]{:S(2)}) collective-permute-start(f32[1,256]{1,0:T(1,128)S(1)} %get-tuple-element.38), channel_id=1, source_target_pairs={{0,32},{32,64},{64,96},{96,128},{128,160},{160,192},{192,224},{224... | collective-permute-start | bytes 3080 | tf_op jit(solution)/shard_map/ppermute | solution.py:37
  65.9 3.7 %collective-permute-start.9 = (f32[1,256]{1,0:T(1,128)S(1)}, f32[1,256]{1,0:T(1,128)S(1)}, u32[]{:S(2)}, u32[]{:S(2)}) collective-permute-start(f32[1,256]{1,0:T(1,128)S(1)} %get-tuple-element.39), channel_id=1, source_target_pairs={{0,224},{32,0},{64,32},{96,64},{128,96},{160,128},{192,160},{224,1... | collective-permute-start | bytes 3080 | tf_op jit(solution)/shard_map/ppermute | solution.py:37

commit v4 on v3

--- a/solution.py
+++ b/solution.py
@@ -128,116 +128,165 @@
     meta_out[...] = meta
 
 
-def flux(fields, mixing, cond, value, inner):
-    kc, *kn = cond()
+def spread(mixing, spread_out):
+    fields = mixing.shape[0]
+    for g in range(fields):
+        for f in range(fields):
+            spread_out[g * fields + f] = jnp.full(spread_out.shape[1:], 0.3 * mixing[g, f], F32)
+
+
+def flux(mix, conds, centres, near):
+    kc, *kn = conds
     radial = kc.shape[-1]
+    fields = len(centres)
     lane = iota(kc.shape, 1)
     weights = [0.075 * (kc + k) for k in kn]
-    k_up = jnp.where(lane == radial - 1, 0.0, pltpu.roll(kc, radial - 1, 1))
-    k_down = jnp.where(lane == 0, 0.0, pltpu.roll(kc, 1, 1))
-    up = 0.075 * (kc + k_up)
-    down = 0.075 * (kc + k_down)
+    up = 0.075 * (kc + jnp.where(lane == radial - 1, 0.0, pltpu.roll(kc, radial - 1, 1)))
+    down = 0.075 * (kc + jnp.where(lane == 0, 0.0, pltpu.roll(kc, 1, 1)))
     total = 1.0 - ((weights[0] + weights[1]) + (weights[2] + weights[3]) + (up + down))
     up = jnp.where(lane == radial - 1, 0.0, up)
     down = jnp.where(lane == 0, 0.0, down)
-    centres = [inner(f) for f in range(fields)]
     for g in range(fields):
         c = centres[g]
         acc = total * c
-        for w, near in zip(weights, value(g)):
-            acc = acc + w * near
+        for w, beside in zip(weights, near(g)):
+            acc = acc + w * beside
         acc = acc + up * pltpu.roll(c, radial - 1, 1) + down * pltpu.roll(c, 1, 1)
         for f in range(fields):
-            acc = acc + (0.3 * mixing[g, f]) * centres[f]
+            m = mix[g * fields + f]
+            acc = acc + jnp.concatenate([m] * (c.shape[0] // 8), axis=0) * centres[f]
         yield g, acc
 
 
-def steps(mixing, corona, kappa, t_low, t_high, p_low, p_high, stepped, wide, once, column):
+WIDE = 32
+
+
+def along_phi(ref, f, t, tile_p, dt=0, dp=0):
+    at = (t + dt) * WIDE + 8 + dp
+    if isinstance(t, jax.Array) and dp == 0:
+        at = pl.multiple_of(at, 8)
+    return ref[f, pl.ds(at, tile_p), :]
+
+
+def along_theta(ref, f, t, p, count):
+    return ref[f, pl.ds(t * WIDE + 8 + p, count, stride=WIDE), :]
+
+
+AROUND = ((-1, 0), (1, 0), (0, -1), (0, 1))
+
+
+def row_flux(mix, field, cond, t_field, t_cond, tile_p, fields):
+    last = cond.shape[0] - 1
+    return flux(
+        mix,
+        [along_phi(cond, last, t_cond, tile_p)]
+        + [along_phi(cond, last, t_cond, tile_p, *d) for d in AROUND],
+        [along_phi(field, f, t_field, tile_p) for f in range(fields)],
+        lambda g: [along_phi(field, g, t_field, tile_p, *d) for d in AROUND],
+    )
+
+
+def column_flux(mix, field, cond, t_field, t_cond, p, count, fields):
+    last = cond.shape[0] - 1
+    return flux(
+        mix,
+        [along_theta(cond, last, t_cond, p, count)]
+        + [along_theta(cond, last, t_cond + dt, p + dp, count) for dt, dp in AROUND],
+        [along_theta(field, f, t_field, p, count) for f in range(fields)],
+        lambda g: [along_theta(field, g, t_field + dt, p + dp, count) for dt, dp in AROUND],
+    )
+
+
+def inside(mixing, corona, kappa, once_out, twice_out, wide, once, mix):
+    fields, tile_t, tile_p, radial = corona.shape
+    spread(mixing, mix)
+    zeros = jnp.zeros((8, radial), F32)
+    plane = jnp.zeros((WIDE, radial), F32)
+    for f in range(fields + 1):
+        for t in range(tile_t + 2):
+            if t in (0, tile_t + 1):
+                wide[f, pl.ds(t * WIDE, WIDE), :] = plane
+                if f < fields:
+                    once[f, pl.ds(t * WIDE, WIDE), :] = plane
+                continue
+            for ref in (wide, once) if f < fields else (wide,):
+                ref[f, pl.ds(t * WIDE, 8), :] = zeros
+                ref[f, pl.ds(t * WIDE + 8 + tile_p, 8), :] = zeros
+            own = corona[f, t - 1] if f < fields else kappa[t - 1]
+            wide[f, pl.ds(t * WIDE + 8, tile_p), :] = own
+
+    def first(t, _):
+        for g, acc in row_flux(mix, wide, wide, t, t, tile_p, fields):
+            once[g, pl.ds(pl.multiple_of(t * WIDE + 8, 8), tile_p), :] = acc
+            once_out[g, t - 1] = acc
+        return 0
+
+    lax.fori_loop(1, tile_t + 1, first, 0)
+
+    def second(t, _):
+        for g, acc in row_flux(mix, once, wide, t, t, tile_p, fields):
+            twice_out[g, t - 1] = acc
+        return 0
+
+    lax.fori_loop(2, tile_t, second, 0)
+
+
+def around(
+    mixing, corona, kappa, t_low, t_high, p_low, p_high, once_in, twice_in, stepped, wide, once, mix,
+):
     fields, tile_t, tile_p, radial = corona.shape
     has_t, has_p = exists()
+    spread(mixing, mix)
     nothing = jnp.zeros((1, radial), F32)
     for f in range(fields + 1):
-        own = corona[f] if f < fields else kappa[...]
-        wide[f, 2 : 2 + tile_t, 8 : 8 + tile_p, :] = own
-        wide[f, 0:2, 8 : 8 + tile_p, :] = t_low[f] * has_t[0]
-        wide[f, 2 + tile_t : 4 + tile_t, 8 : 8 + tile_p, :] = t_high[f] * has_t[1]
-        for side, (halo, near) in enumerate(((p_low, 7), (p_high, 8 + tile_p))):
-            column[side, f, 8 : 8 + tile_t, :] = halo[f, 0:tile_t, :] * has_p[side]
-            column[side, f, 7:8, :] = nothing
-            column[side, f, 8 + tile_t : 9 + tile_t, :] = nothing
-            for t in range(tile_t + 2):
-                wide[f, 1 + t, near : near + 1, :] = column[side, f, 7 + t : 8 + t, :]
-
-    def around(ref, f, t, dt):
-        return [
-            ref[f, t + dt - 1, 8 : 8 + tile_p, :],
-            ref[f, t + dt + 1, 8 : 8 + tile_p, :],
-            ref[f, t + dt, 7 : 7 + tile_p, :],
-            ref[f, t + dt, 9 : 9 + tile_p, :],
-        ]
-
-    def first_row(t, _):
-        keep = jnp.where(t == 0, has_t[0], jnp.where(t == tile_t + 1, has_t[1], 1.0))
-        for g, acc in flux(
-            fields,
-            mixing,
-            lambda: [wide[fields, t + 1, 8 : 8 + tile_p, :]] + around(wide, fields, t, 1),
-            lambda f: around(wide, f, t, 1),
-            lambda f: wide[f, t + 1, 8 : 8 + tile_p, :],
-        ):
-            once[g, t, 8 : 8 + tile_p, :] = acc * keep
-        return 0
-
-    lax.fori_loop(0, tile_t + 2, first_row, 0)
-
-    for side, halo, own_col, at in ((0, p_low, 0, 7), (1, p_high, tile_p - 1, 8 + tile_p)):
-        def beside(f, side=side, halo=halo, own_col=own_col):
-            own = jnp.concatenate(
-                [wide[f, 2 + t, 8 + own_col : 9 + own_col, :] for t in range(tile_t)], axis=0
-            )
-            return [
-                column[side, f, 7 : 7 + tile_t, :],
-                column[side, f, 9 : 9 + tile_t, :],
-                halo[f, tile_t : 2 * tile_t, :] * has_p[side],
-                own,
-            ]
-
-        for g, acc in flux(
-            fields,
-            mixing,
-            lambda: [column[side, fields, 8 : 8 + tile_t, :]] + beside(fields),
-            beside,
-            lambda f: column[side, f, 8 : 8 + tile_t, :],
-        ):
-            acc = acc * has_p[side]
+        for t in range(tile_t):
+            own = corona[f, t] if f < fields else kappa[t]
+            wide[f, pl.ds((t + 2) * WIDE + 8, tile_p), :] = own
+        for k in range(2):
+            wide[f, pl.ds(k * WIDE + 8, tile_p), :] = t_low[f, k] * has_t[0]
+            wide[f, pl.ds((tile_t + 2 + k) * WIDE + 8, tile_p), :] = t_high[f, k] * has_t[1]
+        for side, (halo, near, far) in enumerate(((p_low, 7, 6), (p_high, 8 + tile_p, 9 + tile_p))):
+            for k, col in enumerate((near, far)):
+                cells = halo[f, k * tile_t : (k + 1) * tile_t, :] * has_p[side]
+                wide[f, pl.ds(2 * WIDE + col, tile_t, stride=WIDE), :] = cells
+            for t in (1, tile_t + 2):
+                wide[f, pl.ds(t * WIDE + near, 1), :] = nothing
+        if f < fields:
             for t in range(tile_t):
-                once[g, 1 + t, at : at + 1, :] = acc[t : t + 1, :]
-
-    def second_row(t, _):
-        for g, acc in flux(
-            fields,
-            mixing,
-            lambda: [wide[fields, t + 2, 8 : 8 + tile_p, :]] + around(wide, fields, t, 2),
-            lambda f: around(once, f, t, 1),
-            lambda f: once[f, t + 1, 8 : 8 + tile_p, :],
-        ):
-            stepped[g, t] = acc
-        return 0
-
-    lax.fori_loop(0, tile_t, second_row, 0)
+                once[f, pl.ds((t + 1) * WIDE + 8, tile_p), :] = once_in[f, t]
+
+    for t in (-1, 0, tile_t - 1, tile_t):
+        for g, acc in row_flux(mix, wide, wide, t + 2, t + 2, tile_p, fields):
+            if t in (-1, tile_t):
+                acc = acc * has_t[0 if t < 0 else 1]
+            once[g, pl.ds((t + 1) * WIDE + 8, tile_p), :] = acc
+    for p in (-1, 0, tile_p - 1, tile_p):
+        for g, acc in column_flux(mix, wide, wide, 2, 2, p, tile_t, fields):
+            if p in (-1, tile_p):
+                acc = acc * has_p[0 if p < 0 else 1]
+            once[g, pl.ds(WIDE + 8 + p, tile_t, stride=WIDE), :] = acc
+
+    for f in range(fields):
+        stepped[f] = twice_in[f]
+    for t in (0, 1, tile_t - 2, tile_t - 1):
+        for g, acc in row_flux(mix, once, wide, t + 1, t + 2, tile_p, fields):
+            stepped[g, t * tile_p : (t + 1) * tile_p, :] = acc
+    for p in (0, 1, tile_p - 2, tile_p - 1):
+        for g, acc in column_flux(mix, once, wide, 1, 2, p, tile_t, fields):
+            stepped[g, pl.ds(p, tile_t, stride=tile_p), :] = acc
 
 
 def route(
     n_dev, kappa, p_low, p_high, own_low, own_high, c_low, c_high, stepped, rank, meta, hit,
     table_high, table_low, w_r, patch, message, shell,
 ):
-    fields, tile_t, tile_p, radial = stepped.shape
+    fields, columns, radial = stepped.shape
+    tile_t, tile_p, _ = kappa.shape
     has_t, has_p = exists()
-    columns = tile_t * tile_p
     lane = iota((columns, radial), 1)
     rows = jnp.zeros((columns, radial), F32)
     for f in range(fields):
-        moved = pltpu.roll(stepped[f].reshape(columns, radial), (f * SH + SH) % radial, 1)
+        moved = pltpu.roll(stepped[f], (f * SH + SH) % radial, 1)
         rows = jnp.where(lane // SH == f, moved, rows)
     shell[...] = rows
     for a in range(2):
@@ -291,15 +340,14 @@
     message[pl.ds(1, n_dev, stride=2), :] = meta[...]
 
 
-def finish(stepped, patch, out):
-    fields, tile_t, tile_p, _ = stepped.shape
+def finish(tile_t, tile_p, stepped, patch, out):
     out[...] = stepped[...]
     for a in range(2):
         for b in range(2):
-            t, p = a * (tile_t - 1), b * (tile_p - 1)
-            for f in range(fields):
-                out[f, t, p : p + 1, :] = (
-                    stepped[f, t, p : p + 1, :] + patch[2 * a + b, f : f + 1, :]
+            at = a * (tile_t - 1) * tile_p + b * (tile_p - 1)
+            for f in range(stepped.shape[0]):
+                out[f, at : at + 1, :] = (
+                    stepped[f, at : at + 1, :] + patch[2 * a + b, f : f + 1, :]
                 )
 
 
@@ -361,13 +409,13 @@
     out[...] = x + 0.2 * (above + below + right + left - 4.0 * x)
 
 
-def call(kernel, outs, specs, name, scratch=(), out_spec=None, room=40 * 1024 * 1024):
+def call(kernel, outs, specs, name, scratch=(), room=40 * 1024 * 1024):
     outs = [s if isinstance(s, jax.ShapeDtypeStruct) else jax.ShapeDtypeStruct(s, F32) for s in outs]
     return pl.pallas_call(
         kernel,
         out_shape=outs,
         in_specs=specs,
-        out_specs=[out_spec or vspec()] * len(outs),
+        out_specs=[vspec()] * len(outs),
         scratch_shapes=list(scratch),
         name=name,
         compiler_params=pltpu.CompilerParams(vmem_limit_bytes=room),
@@ -390,8 +438,7 @@
         [pl.BlockSpec(memory_space=pltpu.HBM)] * 2,
         "theta_edges",
         [pltpu.SemaphoreType.DMA((4,))],
-        pl.BlockSpec(memory_space=pltpu.HBM),
-        64 * 1024 * 1024 - 600 * 1024,
+        room=58 * 1024 * 1024,
     )(corona, kappa)
     t_low = shifted(high, "lat", 1)
     t_high = shifted(low, "lat", -1)
@@ -412,23 +459,34 @@
         "plan",
     )(owner, dest_cell, base, fractions)
 
+    t_low, t_high, rank = lax.optimization_barrier((t_low, t_high, rank))
+    once, twice = call(
+        inside,
+        [corona.shape] * 2,
+        [sspec()] + [vspec()] * 2,
+        "inside",
+        [
+            VMEM((fields + 1, (tile_t + 2) * WIDE, radial), F32),
+            VMEM((fields, (tile_t + 2) * WIDE, radial), F32),
+            VMEM((fields * fields, 8, radial), F32),
+        ],
+    )(mixing, corona, kappa)
+
     own_low, own_high = call(
         corner_cells, [(2, fields + 1, radial)] * 2, [vspec()] * 2, "corner_cells"
     )(t_low, t_high)
     c_low = shifted(own_high, "lon", 1)
     c_high = shifted(own_low, "lon", -1)
 
-    (almost,) = call(
-        steps,
-        [corona.shape],
-        [sspec()] + [vspec()] * 6,
-        "steps",
-        [
-            VMEM((fields + 1, tile_t + 4, tile_p + 16, radial), F32),
-            VMEM((fields, tile_t + 2, tile_p + 16, radial), F32),
-            VMEM((2, fields + 1, tile_t + 16, radial), F32),
-        ],
-    )(mixing, corona, kappa, t_low, t_high, p_low, p_high)
+    flat = (fields, tile_t * tile_p, radial)
+    padded = [
+        VMEM((fields + 1, (tile_t + 4) * WIDE, radial), F32),
+        VMEM((fields, (tile_t + 2) * WIDE, radial), F32),
+        VMEM((fields * fields, 8, radial), F32),
+    ]
+    (almost,) = call(around, [flat], [sspec()] + [vspec()] * 8, "around", padded)(
+        mixing, corona, kappa, t_low, t_high, p_low, p_high, once, twice.reshape(flat)
+    )
 
     patch, message = call(
         functools.partial(route, n_dev),
@@ -440,7 +498,9 @@
         kappa, p_low, p_high, own_low, own_high, c_low, c_high, almost, rank, meta, hit, table_high,
         table_low, w_r,
     )
-    (stepped,) = call(finish, [corona.shape], [vspec()] * 2, "finish")(almost, patch)
+    (stepped,) = call(
+        functools.partial(finish, tile_t, tile_p), [flat], [vspec()] * 2, "finish"
+    )(almost, patch)
 
     got = lax.all_to_all(message, ("lat", "lon"), split_axis=0, concat_axis=0, tiled=True)
 
@@ -457,7 +517,7 @@
     (face,) = call(smooth, [helio_prev.shape], [vspec()] * 5, "smooth")(
         coupled, from_p_low, from_p_high, from_t_low, from_t_high
     )
-    return (stepped, face)
+    return (stepped.reshape(corona.shape), face)
 
 
 def solution(mesh):

time: 71.7 us -> 64.2 us (0.90)
  Pallas kernels: 22.7 us -> 17.4 us
  local copies, waits for them, and re-layouts: 1.36 us -> 0.11 us
    pallas_call x1, Pallas kernels: 10.1 us -> 1.81 us  [body(): call(theta_edges, [edge] * 2, [pl.BlockSpec(memory_space=pltpu.HBM)] * 2,...]
    pallas_call x2 -> x3, Pallas kernels: 6.5 us -> 9.43 us  [the longest x1 4.57 us: body(): call(inside, [corona.shape] * 2, [sspec()] + [vspec()] * 2, 'inside', [VM...]
    unnamed x18 -> x16, local copies, waits for them, and re-layouts: 1.36 us -> 0.11 us
  transfers between devices with their start and end apart: 10 -> 10, of which waited for: 1 -> 1; matrix products, arithmetic and copies ran while one was open for 0% -> 0% of each run, Pallas kernels for 12% -> 18%
where the time goes in v4:
time: 64.2 us; the launch traced here: 63.1 us
  blocking collectives  26.6 us (41%)
  starting transfers between devices  17.7 us (28%)
  Pallas kernels  17.4 us (27%)
  between operations  0.82 us (1%)
    all_to_all x1, blocking collectives, body(): lax.all_to_all(message, ('lat', 'lon'), split_axis=0, concat_axis=0, tile...  26.6 us
    ppermute x10, starting transfers between devices, shifted(): lax.ppermute(x, axis, [(i, (i + step) % count) for i in range(count)])  17.7 us
    pallas_call x1, Pallas kernels, body(): call(inside, [corona.shape] * 2, [sspec()] + [vspec()] * 2, 'inside', [VM...  4.57 us
    pallas_call x1, Pallas kernels, body(): call(around, [flat], [sspec()] + [vspec()] * 8, 'around', padded)  3.81 us
    pallas_call x1, Pallas kernels, body(): call(functools.partial(plan, face_t, tile_t, tile_p), [(1, count), (n_dev...  2.07 us
    pallas_call x1, Pallas kernels, body(): call(theta_edges, [edge] * 2, [pl.BlockSpec(memory_space=pltpu.HBM)] * 2,...  1.81 us
    pallas_call x1, Pallas kernels, body(): call(functools.partial(route, n_dev), [(4, fields, radial), (2 * n_dev, 1...  1.66 us
    pallas_call x1, Pallas kernels, body(): call(functools.partial(land, n_dev), [helio_prev.shape, (fields, face_t),...  1.39 us
  transfers between devices with their start and end apart: 10, of which 1 were waited for; matrix products, arithmetic and copies ran while one was open for 0% of the time, Pallas kernels for 18%

profile of v4, /device:TPU:8, one launch (start us, length us, event | category | flops | bytes accessed | tf_op | source)
XLA Modules:
  0.0 63.1 jit_solution(16382041839249056163)
XLA Ops:
  0.6 0.0 copy-start.1
  0.6 0.0 copy-start
  0.6 1.8 %theta_edges.1 = (f32[9,2,16,128]{3,2,1,0:T(8,128)}, f32[9,2,16,128]{3,2,1,0:T(8,128)}) custom-call(f32[8,16,16,128]{3,2,1,0:T(8,128)} %corona.5, f32[16,16,128]{2,1,0:T(8,128)} %kappa.7), custom_call_target="tpu_custom_call" | custom-call | tf_op jit(solution)/shard_map/theta_edges/pallas_call | solution.py:435
  2.5 2.0 %collective-permute-start = (f32[9,2,16,128]{3,2,1,0:T(8,128)}, f32[9,2,16,128]{3,2,1,0:T(8,128)S(1)}, u32[]{:S(2)}, u32[]{:S(2)}) collective-permute-start(f32[9,2,16,128]{3,2,1,0:T(8,128)} %get-tuple-element.26), channel_id=1, source_target_pairs={{0,32},{32,64},{64,96},{96,128},{128,160},{160,192},{192,224},{224... | collective-permute-start | bytes 442376 | tf_op jit(solution)/shard_map/ppermute | solution.py:37
  4.5 4.0 %collective-permute-start.1 = (f32[9,2,16,128]{3,2,1,0:T(8,128)}, f32[9,2,16,128]{3,2,1,0:T(8,128)S(1)}, u32[]{:S(2)}, u32[]{:S(2)}) collective-permute-start(f32[9,2,16,128]{3,2,1,0:T(8,128)} %get-tuple-element.27), channel_id=1, source_target_pairs={{0,224},{32,0},{64,32},{96,64},{128,96},{160,128},{192,160},{224,1... | collective-permute-start | bytes 442376 | tf_op jit(solution)/shard_map/ppermute | solution.py:37
  8.5 0.0 copy-done.1
  8.5 0.0 copy-done
  8.5 0.0 copy-start.3
  8.5 0.0 copy-start.6
  8.5 0.0 copy-start.7
  8.5 0.1 phi_edges.1
  8.6 0.0 copy-start.5
  8.6 0.1 collective-permute-start.2
  8.7 3.8 %collective-permute-start.3 = (f32[9,32,128]{2,1,0:T(8,128)S(1)}, f32[9,32,128]{2,1,0:T(8,128)S(1)}, u32[]{:S(2)}, u32[]{:S(2)}) collective-permute-start(f32[9,32,128]{2,1,0:T(8,128)S(1)} %get-tuple-element.32), channel_id=1, source_target_pairs={{0,31},{1,0},{2,1},{3,2},{4,3},{5,4},{6,5},{7,6},{8,7},{9,8},{10,9... | collective-permute-start | bytes 442376 | tf_op jit(solution)/shard_map/ppermute | solution.py:37
  12.6 0.0 copy-done.3
  12.6 0.0 copy-done.6
  12.6 0.0 copy-done.7
  12.6 0.0 copy-done.5
  12.6 2.1 %plan.1 = (f32[1,2048]{1,0:T(1,128)S(1)}, f32[256,128]{1,0:T(8,128)S(1)}, bf16[256,2048]{1,0:T(8,128)(2,1)S(1)}, bf16[256,2048]{1,0:T(8,128)(2,1)S(1)}, bf16[256...) custom-call(s32[1,2048]{1,0:T(1,128)S(1)} %bitcast.14, s32[1,2048]{1,0:T(1,128)S(1)} %bitcast.15, s32[1,2048]{1,0:T(1,128)S(1)} %bitcast.16, ...), custom_call_target="tpu_custom_call" | custom-call | tf_op jit(solution)/shard_map/plan/pallas_call | solution.py:454
  14.7 0.0 collective-permute-done.t_low
  14.7 0.0 collective-permute-done.1.t_high
  14.7 0.0 copy-start.4
  14.7 0.1 collective-permute-start.5
  14.8 0.5 collective-permute-start.4
  15.3 0.1 copy-done.4
  15.4 4.6 %inside.1 = (f32[8,16,16,128]{3,2,1,0:T(8,128)S(1)}, f32[8,16,16,128]{3,2,1,0:T(8,128)S(1)}) custom-call(f32[8,8]{1,0:T(8,128)S(1)} %copy-done.4, f32[8,16,16,128]{3,2,1,0:T(8,128)S(1)} %copy-done, f32[16,16,128]{2,1,0:T(8,128)S(1)} %copy-done.1), custom_call_target="tpu_custom_call" | custom-call | tf_op jit(solution)/shard_map/inside/pallas_call | solution.py:463
  19.9 0.0 collective-permute-done.2.p_low
  19.9 0.0 collective-permute-done.3.p_high
  20.0 3.8 %around.1.stepped = f32[8,256,128]{2,1,0:T(8,128)S(1)} custom-call(f32[8,8]{1,0:T(8,128)S(1)} %copy-done.4, f32[8,16,16,128]{3,2,1,0:T(8,128)S(1)} %copy-done, f32[16,16,128]{2,1,0:T(8,128)S(1)} %copy-done.1, f32[9,2,16,128]{3,2,1,0:T(8,128)S(1)} %collective-permute-done.t_low, f32[9,2,16,128]{3,2,1,0:T(8,128)S(1)} %collective-permute-done.1.t_high, ...), custom_call_target="tpu_custom_call" | custom-call | tf_op jit(solution)/shard_map/around/pallas_call | solution.py:487
  23.8 0.0 collective-permute-done.5.c_high
  23.8 0.0 collective-permute-done.4.c_low
  23.8 1.7 %route.1 = (f32[4,8,128]{2,1,0:T(8,128)S(1)}, f32[512,128]{1,0:T(8,128)S(1)}) custom-call(f32[16,16,128]{2,1,0:T(8,128)S(1)} %copy-done.1, f32[9,32,128]{2,1,0:T(8,128)S(1)} %collective-permute-done.2.p_low, f32[9,32,128]{2,1,0:T(8,128)S(1)} %collective-permute-done.3.p_high, f32[2,9,128]{2,1,0:T(8,128)S(1)} %get-tuple-element.35.own_low, ...), custom_call_target="tpu_custom_call" | custom-call | tf_op jit(solution)/shard_map/route/pallas_call | solution.py:491
  25.5 0.0 copy-start.2
  25.5 26.6 %all_to_all.11 = f32[256,2,128]{2,1,0:T(2,128)S(1)} all-to-all(f32[256,2,128]{2,1,0:T(2,128)S(1)} %bitcast.13), channel_id=1, replica_groups=mesh['lat'=8,'lon'=32] {'lat','lon'}, dimensions={0} | all-to-all | bytes 524288 | tf_op jit(solution)/shard_map/all_to_all | solution.py:505
  52.1 0.0 copy-done.2
  52.1 1.4 %land.1 = (f32[8,32,128]{2,1,0:T(8,128)S(1)}, f32[8,128]{1,0:T(8,128)S(1)}, f32[8,128]{1,0:T(8,128)S(1)}, f32[1,256]{1,0:T(1,128)S(1)}, f32[1,256]{1,0:T(1,128)S(1)}) custom-call(f32[512,128]{1,0:T(8,128)S(1)} %bitcast.11, f32[8,32,128]{2,1,0:T(8,128)S(1)} %copy-done.2), custom_call_target="tpu_custom_call" | custom-call | tf_op jit(solution)/shard_map/land/pallas_call | solution.py:507
  53.5 0.1 collective-permute-start.6
  53.6 3.8 %collective-permute-start.7 = (f32[8,128]{1,0:T(8,128)S(1)}, f32[8,128]{1,0:T(8,128)S(1)}, u32[]{:S(2)}, u32[]{:S(2)}) collective-permute-start(f32[8,128]{1,0:T(8,128)S(1)} %get-tuple-element.47), channel_id=1, source_target_pairs={{0,31},{1,0},{2,1},{3,2},{4,3},{5,4},{6,5},{7,6},{8,7},{9,8},{10,9... | collective-permute-start | bytes 12296 | tf_op jit(solution)/shard_map/ppermute | solution.py:37
  57.5 1.0 %collective-permute-start.8 = (f32[1,256]{1,0:T(1,128)S(1)}, f32[1,256]{1,0:T(1,128)S(1)}, u32[]{:S(2)}, u32[]{:S(2)}) collective-permute-start(f32[1,256]{1,0:T(1,128)S(1)} %get-tuple-element.48), channel_id=1, source_target_pairs={{0,32},{32,64},{64,96},{96,128},{128,160},{160,192},{192,224},{224... | collective-permute-start | bytes 3080 | tf_op jit(solution)/shard_map/ppermute | solution.py:37
  58.5 2.2 %collective-permute-start.9 = (f32[1,256]{1,0:T(1,128)S(1)}, f32[1,256]{1,0:T(1,128)S(1)}, u32[]{:S(2)}, u32[]{:S(2)}) collective-permute-start(f32[1,256]{1,0:T(1,128)S(1)} %get-tuple-element.49), channel_id=1, source_target_pairs={{0,224},{32,0},{64,32},{96,64},{128,96},{160,128},{192,160},{224,1... | collective-permute-start | bytes 3080 | tf_op jit(solution)/shard_map/ppermute | solution.py:37
  60.7 1.1 %finish.1 = f32[8,256,128]{2,1,0:T(8,128)} custom-call(f32[8,256,128]{2,1,0:T(8,128)S(1)} %around.1.stepped, f32[4,8,128]{2,1,0:T(8,128)S(1)} %get-tuple-element.43.patch), custom_call_target="tpu_custom_call" | custom-call | tf_op jit(solution)/shard_map/finish/pallas_call | solution.py:501
  61.7 0.5 collective-permute-done.8.t_low
  62.2 0.0 collective-permute-done.9.t_high
  62.2 0.0 collective-permute-done.6.p_low
  62.2 0.0 collective-permute-done.7.p_high
  62.2 0.9 %smooth.1 = f32[8,32,128]{2,1,0:T(8,128)} custom-call(f32[8,32,128]{2,1,0:T(8,128)S(1)} %get-tuple-element.45.coupled, f32[8,128]{1,0:T(8,128)S(1)} %collective-permute-done.6.p_low, f32[8,128]{1,0:T(8,128)S(1)} %collective-permute-done.7.p_high, f32[1,256]{1,0:T(1,128)S(1)} %collective-permute-done.8.t_low, f32[1,256]{1,0:T(1,128)S(1)} %collective-permute-done.9.t_high), custom_call_target="tpu_custom_call" | custom-call | tf_op jit(solution)/shard_map/smooth/pallas_call | solution.py:517
  (1 shorter events, 0.0 us)
Async XLA Ops:
  0.6 7.9 %copy-start.1 = (f32[16,16,128]{2,1,0:T(8,128)S(1)}, f32[16,16,128]{2,1,0:T(8,128)}, u32[]{:S(2)}) copy-start(f32[16,16,128]{2,1,0:T(8,128)} %kappa.7) | copy-start | bytes 393220
  0.6 7.9 %copy-start = (f32[8,16,16,128]{3,2,1,0:T(8,128)S(1)}, f32[8,16,16,128]{3,2,1,0:T(8,128)}, u32[]{:S(2)}) copy-start(f32[8,16,16,128]{3,2,1,0:T(8,128)} %corona.5) | copy-start | bytes 3145732
  2.5 12.2 %collective-permute-start = (f32[9,2,16,128]{3,2,1,0:T(8,128)}, f32[9,2,16,128]{3,2,1,0:T(8,128)S(1)}, u32[]{:S(2)}, u32[]{:S(2)}) collective-permute-start(f32[9,2,16,128]{3,2,1,0:T(8,128)} %get-tuple-element.26), channel_id=1, source_target_pairs={{0,32},{32,64},{64,96},{96,128},{128,160},{160,192},{192,224},{224... | collective-permute-start | bytes 442376 | tf_op jit(solution)/shard_map/ppermute | solution.py:37
  4.5 10.2 %collective-permute-start.1 = (f32[9,2,16,128]{3,2,1,0:T(8,128)}, f32[9,2,16,128]{3,2,1,0:T(8,128)S(1)}, u32[]{:S(2)}, u32[]{:S(2)}) collective-permute-start(f32[9,2,16,128]{3,2,1,0:T(8,128)} %get-tuple-element.27), channel_id=1, source_target_pairs={{0,224},{32,0},{64,32},{96,64},{128,96},{160,128},{192,160},{224,1... | collective-permute-start | bytes 442376 | tf_op jit(solution)/shard_map/ppermute | solution.py:37
  8.5 4.1 %copy-start.3 = (f32[3,2048]{1,0:T(4,128)S(1)}, f32[3,2048]{1,0:T(4,128)}, u32[]{:S(2)}) copy-start(f32[3,2048]{1,0:T(4,128)} %frac.1) | copy-start | bytes 73732
  8.5 4.1 %copy-start.6 = (s32[2048]{0:T(1024)S(1)}, s32[2048]{0:T(1024)}, u32[]{:S(2)}) copy-start(s32[2048]{0:T(1024)} %param.13) | copy-start | bytes 24580
  8.5 4.1 %copy-start.7 = (s32[2048]{0:T(1024)S(1)}, s32[2048]{0:T(1024)}, u32[]{:S(2)}) copy-start(s32[2048]{0:T(1024)} %param.14) | copy-start | bytes 24580
  8.6 4.0 %copy-start.5 = (s32[2048,1]{0,1:T(1,128)S(1)}, s32[2048,1]{0,1:T(1,128)}, u32[]{:S(2)}) copy-start(s32[2048,1]{0,1:T(1,128)} %param.12) | copy-start | bytes 24580
  8.6 11.3 %collective-permute-start.2 = (f32[9,32,128]{2,1,0:T(8,128)S(1)}, f32[9,32,128]{2,1,0:T(8,128)S(1)}, u32[]{:S(2)}, u32[]{:S(2)}) collective-permute-start(f32[9,32,128]{2,1,0:T(8,128)S(1)} %get-tuple-element.31), channel_id=1, source_target_pairs={{0,1},{1,2},{2,3},{3,4},{4,5},{5,6},{6,7},{7,8},{8,9},{9,10},{10,1... | collective-permute-start | bytes 442376 | tf_op jit(solution)/shard_map/ppermute | solution.py:37
  8.7 11.2 %collective-permute-start.3 = (f32[9,32,128]{2,1,0:T(8,128)S(1)}, f32[9,32,128]{2,1,0:T(8,128)S(1)}, u32[]{:S(2)}, u32[]{:S(2)}) collective-permute-start(f32[9,32,128]{2,1,0:T(8,128)S(1)} %get-tuple-element.32), channel_id=1, source_target_pairs={{0,31},{1,0},{2,1},{3,2},{4,3},{5,4},{6,5},{7,6},{8,7},{9,8},{10,9... | collective-permute-start | bytes 442376 | tf_op jit(solution)/shard_map/ppermute | solution.py:37
  14.7 0.7 %copy-start.4 = (f32[8,8]{1,0:T(8,128)S(1)}, f32[8,8]{1,0:T(8,128)}, u32[]{:S(2)}) copy-start(f32[8,8]{1,0:T(8,128)} %mixing.3) | copy-start | bytes 772
  14.7 9.1 %collective-permute-start.5 = (f32[2,9,128]{2,1,0:T(8,128)S(1)}, f32[2,9,128]{2,1,0:T(8,128)S(1)}, u32[]{:S(2)}, u32[]{:S(2)}) collective-permute-start(f32[2,9,128]{2,1,0:T(8,128)S(1)} %get-tuple-element.35.own_low), channel_id=1, source_target_pairs={{0,31},{1,0},{2,1},{3,2},{4,3},{5,4},{6,5},{7,6},{8,7},{9,8},{10,9... | collective-permute-start | bytes 27656 | tf_op jit(solution)/shard_map/ppermute | solution.py:37
  14.8 9.0 %collective-permute-start.4 = (f32[2,9,128]{2,1,0:T(8,128)S(1)}, f32[2,9,128]{2,1,0:T(8,128)S(1)}, u32[]{:S(2)}, u32[]{:S(2)}) collective-permute-start(f32[2,9,128]{2,1,0:T(8,128)S(1)} %get-tuple-element.36.own_high), channel_id=1, source_target_pairs={{0,1},{1,2},{2,3},{3,4},{4,5},{5,6},{6,7},{7,8},{8,9},{9,10},{10,1... | collective-permute-start | bytes 27656 | tf_op jit(solution)/shard_map/ppermute | solution.py:37
  25.5 26.7 %copy-start.2 = (f32[8,32,128]{2,1,0:T(8,128)S(1)}, f32[8,32,128]{2,1,0:T(8,128)}, u32[]{:S(2)}) copy-start(f32[8,32,128]{2,1,0:T(8,128)} %prev.1) | copy-start | bytes 393220
  53.5 8.7 %collective-permute-start.6 = (f32[8,128]{1,0:T(8,128)S(1)}, f32[8,128]{1,0:T(8,128)S(1)}, u32[]{:S(2)}, u32[]{:S(2)}) collective-permute-start(f32[8,128]{1,0:T(8,128)S(1)} %get-tuple-element.46), channel_id=1, source_target_pairs={{0,1},{1,2},{2,3},{3,4},{4,5},{5,6},{6,7},{7,8},{8,9},{9,10},{10,1... | collective-permute-start | bytes 12296 | tf_op jit(solution)/shard_map/ppermute | solution.py:37
  53.6 8.6 %collective-permute-start.7 = (f32[8,128]{1,0:T(8,128)S(1)}, f32[8,128]{1,0:T(8,128)S(1)}, u32[]{:S(2)}, u32[]{:S(2)}) collective-permute-start(f32[8,128]{1,0:T(8,128)S(1)} %get-tuple-element.47), channel_id=1, source_target_pairs={{0,31},{1,0},{2,1},{3,2},{4,3},{5,4},{6,5},{7,6},{8,7},{9,8},{10,9... | collective-permute-start | bytes 12296 | tf_op jit(solution)/shard_map/ppermute | solution.py:37
  57.5 4.8 %collective-permute-start.8 = (f32[1,256]{1,0:T(1,128)S(1)}, f32[1,256]{1,0:T(1,128)S(1)}, u32[]{:S(2)}, u32[]{:S(2)}) collective-permute-start(f32[1,256]{1,0:T(1,128)S(1)} %get-tuple-element.48), channel_id=1, source_target_pairs={{0,32},{32,64},{64,96},{96,128},{128,160},{160,192},{192,224},{224... | collective-permute-start | bytes 3080 | tf_op jit(solution)/shard_map/ppermute | solution.py:37
  58.5 3.7 %collective-permute-start.9 = (f32[1,256]{1,0:T(1,128)S(1)}, f32[1,256]{1,0:T(1,128)S(1)}, u32[]{:S(2)}, u32[]{:S(2)}) collective-permute-start(f32[1,256]{1,0:T(1,128)S(1)} %get-tuple-element.49), channel_id=1, source_target_pairs={{0,224},{32,0},{64,32},{96,64},{128,96},{160,128},{192,160},{224,1... | collective-permute-start | bytes 3080 | tf_op jit(solution)/shard_map/ppermute | solution.py:37

commit v5 on v3

--- a/solution.py
+++ b/solution.py
@@ -128,116 +128,142 @@
     meta_out[...] = meta
 
 
-def flux(fields, mixing, cond, value, inner):
-    kc, *kn = cond()
-    radial = kc.shape[-1]
-    lane = iota(kc.shape, 1)
-    weights = [0.075 * (kc + k) for k in kn]
-    k_up = jnp.where(lane == radial - 1, 0.0, pltpu.roll(kc, radial - 1, 1))
-    k_down = jnp.where(lane == 0, 0.0, pltpu.roll(kc, 1, 1))
-    up = 0.075 * (kc + k_up)
-    down = 0.075 * (kc + k_down)
-    total = 1.0 - ((weights[0] + weights[1]) + (weights[2] + weights[3]) + (up + down))
-    up = jnp.where(lane == radial - 1, 0.0, up)
-    down = jnp.where(lane == 0, 0.0, down)
-    centres = [inner(f) for f in range(fields)]
-    for g in range(fields):
-        c = centres[g]
-        acc = total * c
-        for w, near in zip(weights, value(g)):
-            acc = acc + w * near
-        acc = acc + up * pltpu.roll(c, radial - 1, 1) + down * pltpu.roll(c, 1, 1)
-        for f in range(fields):
-            acc = acc + (0.3 * mixing[g, f]) * centres[f]
-        yield g, acc
-
-
-def steps(mixing, corona, kappa, t_low, t_high, p_low, p_high, stepped, wide, once, column):
-    fields, tile_t, tile_p, radial = corona.shape
+def steps(
+    tile_t, tile_p, mixing, corona, kappa, t_low, t_high, p_low, p_high, stepped, wide, once, plane,
+    coef,
+):
+    fields = mixing.shape[0]
+    radial = corona.shape[1]
+    cells = tile_t * tile_p
+    pitch, inner = tile_p + 4, tile_p + 2
     has_t, has_p = exists()
-    nothing = jnp.zeros((1, radial), F32)
-    for f in range(fields + 1):
-        own = corona[f] if f < fields else kappa[...]
-        wide[f, 2 : 2 + tile_t, 8 : 8 + tile_p, :] = own
-        wide[f, 0:2, 8 : 8 + tile_p, :] = t_low[f] * has_t[0]
-        wide[f, 2 + tile_t : 4 + tile_t, 8 : 8 + tile_p, :] = t_high[f] * has_t[1]
-        for side, (halo, near) in enumerate(((p_low, 7), (p_high, 8 + tile_p))):
-            column[side, f, 8 : 8 + tile_t, :] = halo[f, 0:tile_t, :] * has_p[side]
-            column[side, f, 7:8, :] = nothing
-            column[side, f, 8 + tile_t : 9 + tile_t, :] = nothing
-            for t in range(tile_t + 2):
-                wide[f, 1 + t, near : near + 1, :] = column[side, f, 7 + t : 8 + t, :]
-
-    def around(ref, f, t, dt):
-        return [
-            ref[f, t + dt - 1, 8 : 8 + tile_p, :],
-            ref[f, t + dt + 1, 8 : 8 + tile_p, :],
-            ref[f, t + dt, 7 : 7 + tile_p, :],
-            ref[f, t + dt, 9 : 9 + tile_p, :],
-        ]
-
-    def first_row(t, _):
-        keep = jnp.where(t == 0, has_t[0], jnp.where(t == tile_t + 1, has_t[1], 1.0))
-        for g, acc in flux(
-            fields,
-            mixing,
-            lambda: [wide[fields, t + 1, 8 : 8 + tile_p, :]] + around(wide, fields, t, 1),
-            lambda f: around(wide, f, t, 1),
-            lambda f: wide[f, t + 1, 8 : 8 + tile_p, :],
-        ):
-            once[g, t, 8 : 8 + tile_p, :] = acc * keep
+
+    def at(t, p):
+        return (t + 2) * pitch + p + 2
+
+    def inside(t, p):
+        return (t + 1) * inner + p + 1
+
+    nothing = jnp.zeros((fields, radial), F32)
+    rows = 2 * tile_p
+    for k in range(2):
+        for ref, mask, t in ((t_low, has_t[0], k - 2), (t_high, has_t[1], tile_t + k)):
+            for p in range(tile_p):
+                wide[at(t, p)] = ref[pl.ds(k * tile_p + p, fields, stride=rows), :] * mask
+            plane[t + 2, 8 : 8 + tile_p, :] = (
+                ref[fields * rows + k * tile_p : fields * rows + (k + 1) * tile_p, :] * mask
+            )
+    rows = 2 * tile_t
+    for k in range(2):
+        for ref, mask, p in ((p_low, has_p[0], -1 - k), (p_high, has_p[1], tile_p + k)):
+            for t in range(tile_t):
+                wide[at(t, p)] = ref[pl.ds(k * tile_t + t, fields, stride=rows), :] * mask
+                row = fields * rows + k * tile_t + t
+                plane[t + 2, 8 + p : 9 + p, :] = ref[row : row + 1, :] * mask
+    for t in (-1, tile_t):
+        for p in (-1, tile_p):
+            wide[at(t, p)] = nothing
+            plane[t + 2, 8 + p : 9 + p, :] = nothing[0:1]
+
+    def own(t, _):
+        for p in range(tile_p):
+            wide[(t + 2) * pitch + p + 2] = corona[pl.ds(t * tile_p + p, fields, stride=cells), :]
+        plane[t + 2, 8 : 8 + tile_p, :] = kappa[t]
         return 0
 
-    lax.fori_loop(0, tile_t + 2, first_row, 0)
-
-    for side, halo, own_col, at in ((0, p_low, 0, 7), (1, p_high, tile_p - 1, 8 + tile_p)):
-        def beside(f, side=side, halo=halo, own_col=own_col):
-            own = jnp.concatenate(
-                [wide[f, 2 + t, 8 + own_col : 9 + own_col, :] for t in range(tile_t)], axis=0
+    lax.fori_loop(0, tile_t, own, 0)
+
+    span = coef.shape[2]
+    lane = iota((span, radial), 1)
+
+    def weigh(t, _):
+        def kap(dt, dp):
+            return plane[t + 1 + dt, 7 + dp : 7 + dp + span, :]
+
+        k = kap(0, 0)
+        around = [0.075 * (k + kap(*d)) for d in ((-1, 0), (1, 0), (0, -1), (0, 1))]
+        above = jnp.where(lane == radial - 1, 0.0, pltpu.roll(k, radial - 1, 1))
+        below = jnp.where(lane == 0, 0.0, pltpu.roll(k, 1, 1))
+        above, below = 0.075 * (k + above), 0.075 * (k + below)
+        for n, w in enumerate(around):
+            coef[t, n] = w
+        coef[t, 4] = jnp.where(lane == radial - 1, 0.0, above)
+        coef[t, 5] = jnp.where(lane == 0, 0.0, below)
+        coef[t, 6] = 1.0 - (
+            (around[0] + around[1]) + (around[2] + around[3]) + (above + below)
+        )
+        return 0
+
+    lax.fori_loop(0, tile_t + 2, weigh, 0)
+
+    row = iota((fields, radial), 0)
+    turned = []
+    for k in range(fields):
+        m = jnp.zeros((fields, radial), F32)
+        for g in range(fields):
+            m = jnp.where(row == g, 0.3 * mixing[g, (g - k) % fields], m)
+        turned.append(m)
+
+    def flux(ref, width, index, t, p):
+        def w(n):
+            return coef[t + 1, n, pl.ds(p + 1, fields, stride=0), :]
+
+        c = ref[index]
+        acc = (w(6) + turned[0]) * c
+        acc = acc + (w(0) * ref[index - width] + w(1) * ref[index + width])
+        acc = acc + (w(2) * ref[index - 1] + w(3) * ref[index + 1])
+        acc = acc + (w(4) * pltpu.roll(c, radial - 1, 1) + w(5) * pltpu.roll(c, 1, 1))
+        mixed = [turned[k] * pltpu.roll(c, k, 0) for k in range(1, fields)]
+        while len(mixed) > 1:
+            mixed = [a + b for a, b in zip(mixed[::2], mixed[1::2])] + mixed[len(mixed) & ~1 :]
+        return acc + mixed[0]
+
+    def first(t, _):
+        for p in range(-1, tile_p + 1):
+            once[(t + 1) * inner + p + 1] = flux(wide, pitch, (t + 2) * pitch + p + 2, t, p)
+        return 0
+
+    def rim(t, p):
+        once[inside(t, p)] = flux(wide, pitch, at(t, p), t, p)
+
+    lax.fori_loop(0, tile_t, first, 0)
+    for p in range(tile_p):
+        rim(-1, p)
+        rim(tile_t, p)
+
+    for mask, edge in (
+        (has_t[0], [(-1, p) for p in range(tile_p)]),
+        (has_t[1], [(tile_t, p) for p in range(tile_p)]),
+        (has_p[0], [(t, -1) for t in range(tile_t)]),
+        (has_p[1], [(t, tile_p) for t in range(tile_t)]),
+    ):
+
+        @pl.when(mask == 0.0)
+        def _(edge=edge):
+            for cell in edge:
+                once[inside(*cell)] = nothing
+
+    def second(t, _):
+        for p in range(tile_p):
+            stepped[pl.ds(t * tile_p + p, fields, stride=cells), :] = flux(
+                once, inner, (t + 1) * inner + p + 1, t, p
             )
-            return [
-                column[side, f, 7 : 7 + tile_t, :],
-                column[side, f, 9 : 9 + tile_t, :],
-                halo[f, tile_t : 2 * tile_t, :] * has_p[side],
-                own,
-            ]
-
-        for g, acc in flux(
-            fields,
-            mixing,
-            lambda: [column[side, fields, 8 : 8 + tile_t, :]] + beside(fields),
-            beside,
-            lambda f: column[side, f, 8 : 8 + tile_t, :],
-        ):
-            acc = acc * has_p[side]
-            for t in range(tile_t):
-                once[g, 1 + t, at : at + 1, :] = acc[t : t + 1, :]
-
-    def second_row(t, _):
-        for g, acc in flux(
-            fields,
-            mixing,
-            lambda: [wide[fields, t + 2, 8 : 8 + tile_p, :]] + around(wide, fields, t, 2),
-            lambda f: around(once, f, t, 1),
-            lambda f: once[f, t + 1, 8 : 8 + tile_p, :],
-        ):
-            stepped[g, t] = acc
         return 0
 
-    lax.fori_loop(0, tile_t, second_row, 0)
+    lax.fori_loop(0, tile_t, second, 0)
 
 
 def route(
     n_dev, kappa, p_low, p_high, own_low, own_high, c_low, c_high, stepped, rank, meta, hit,
     table_high, table_low, w_r, patch, message, shell,
 ):
-    fields, tile_t, tile_p, radial = stepped.shape
+    fields, columns, radial = stepped.shape
+    tile_t, tile_p, _ = kappa.shape
     has_t, has_p = exists()
-    columns = tile_t * tile_p
     lane = iota((columns, radial), 1)
     rows = jnp.zeros((columns, radial), F32)
     for f in range(fields):
-        moved = pltpu.roll(stepped[f].reshape(columns, radial), (f * SH + SH) % radial, 1)
+        moved = pltpu.roll(stepped[f], (f * SH + SH) % radial, 1)
         rows = jnp.where(lane // SH == f, moved, rows)
     shell[...] = rows
     for a in range(2):
@@ -291,15 +317,14 @@
     message[pl.ds(1, n_dev, stride=2), :] = meta[...]
 
 
-def finish(stepped, patch, out):
-    fields, tile_t, tile_p, _ = stepped.shape
+def finish(tile_t, tile_p, stepped, patch, out):
     out[...] = stepped[...]
     for a in range(2):
         for b in range(2):
-            t, p = a * (tile_t - 1), b * (tile_p - 1)
-            for f in range(fields):
-                out[f, t, p : p + 1, :] = (
-                    stepped[f, t, p : p + 1, :] + patch[2 * a + b, f : f + 1, :]
+            at = a * (tile_t - 1) * tile_p + b * (tile_p - 1)
+            for f in range(stepped.shape[0]):
+                out[f, at : at + 1, :] = (
+                    stepped[f, at : at + 1, :] + patch[2 * a + b, f : f + 1, :]
                 )
 
 
@@ -361,13 +386,13 @@
     out[...] = x + 0.2 * (above + below + right + left - 4.0 * x)
 
 
-def call(kernel, outs, specs, name, scratch=(), out_spec=None, room=40 * 1024 * 1024):
+def call(kernel, outs, specs, name, scratch=(), room=40 * 1024 * 1024):
     outs = [s if isinstance(s, jax.ShapeDtypeStruct) else jax.ShapeDtypeStruct(s, F32) for s in outs]
     return pl.pallas_call(
         kernel,
         out_shape=outs,
         in_specs=specs,
-        out_specs=[out_spec or vspec()] * len(outs),
+        out_specs=[vspec()] * len(outs),
         scratch_shapes=list(scratch),
         name=name,
         compiler_params=pltpu.CompilerParams(vmem_limit_bytes=room),
@@ -390,8 +415,7 @@
         [pl.BlockSpec(memory_space=pltpu.HBM)] * 2,
         "theta_edges",
         [pltpu.SemaphoreType.DMA((4,))],
-        pl.BlockSpec(memory_space=pltpu.HBM),
-        64 * 1024 * 1024 - 600 * 1024,
+        room=58 * 1024 * 1024,
     )(corona, kappa)
     t_low = shifted(high, "lat", 1)
     t_high = shifted(low, "lat", -1)
@@ -412,23 +436,35 @@
         "plan",
     )(owner, dest_cell, base, fractions)
 
+    t_low, t_high, rank = lax.optimization_barrier((t_low, t_high, rank))
     own_low, own_high = call(
         corner_cells, [(2, fields + 1, radial)] * 2, [vspec()] * 2, "corner_cells"
     )(t_low, t_high)
     c_low = shifted(own_high, "lon", 1)
     c_high = shifted(own_low, "lon", -1)
 
+    flat = (fields, tile_t * tile_p, radial)
     (almost,) = call(
-        steps,
-        [corona.shape],
+        functools.partial(steps, tile_t, tile_p),
+        [(fields * tile_t * tile_p, radial)],
         [sspec()] + [vspec()] * 6,
         "steps",
         [
-            VMEM((fields + 1, tile_t + 4, tile_p + 16, radial), F32),
-            VMEM((fields, tile_t + 2, tile_p + 16, radial), F32),
-            VMEM((2, fields + 1, tile_t + 16, radial), F32),
+            VMEM(((tile_t + 4) * (tile_p + 4), fields, radial), F32),
+            VMEM(((tile_t + 2) * (tile_p + 2), fields, radial), F32),
+            VMEM((tile_t + 4, tile_p + 16, radial), F32),
+            VMEM((tile_t + 2, 7, tile_p + 8, radial), F32),
         ],
-    )(mixing, corona, kappa, t_low, t_high, p_low, p_high)
+    )(
+        mixing,
+        corona.reshape(-1, radial),
+        kappa,
+        t_low.reshape(-1, radial),
+        t_high.reshape(-1, radial),
+        p_low.reshape(-1, radial),
+        p_high.reshape(-1, radial),
+    )
+    almost = almost.reshape(flat)
 
     patch, message = call(
         functools.partial(route, n_dev),
@@ -440,7 +476,9 @@
         kappa, p_low, p_high, own_low, own_high, c_low, c_high, almost, rank, meta, hit, table_high,
         table_low, w_r,
     )
-    (stepped,) = call(finish, [corona.shape], [vspec()] * 2, "finish")(almost, patch)
+    (stepped,) = call(
+        functools.partial(finish, tile_t, tile_p), [flat], [vspec()] * 2, "finish"
+    )(almost, patch)
 
     got = lax.all_to_all(message, ("lat", "lon"), split_axis=0, concat_axis=0, tiled=True)
 
@@ -457,7 +495,7 @@
     (face,) = call(smooth, [helio_prev.shape], [vspec()] * 5, "smooth")(
         coupled, from_p_low, from_p_high, from_t_low, from_t_high
     )
-    return (stepped, face)
+    return (stepped.reshape(corona.shape), face)
 
 
 def solution(mesh):

time: 71.7 us -> 64.2 us (0.90)
  Pallas kernels: 22.7 us -> 16.1 us
  blocking collectives: 27.3 us -> 23.8 us
  starting transfers between devices: 17.9 us -> 21.2 us
    pallas_call x1, Pallas kernels: 10.1 us -> 1.81 us  [body(): call(theta_edges, [edge] * 2, [pl.BlockSpec(memory_space=pltpu.HBM)] * 2,...]
    all_to_all x1, blocking collectives: 27.3 us -> 23.8 us  [body(): lax.all_to_all(message, ('lat', 'lon'), split_axis=0, concat_axis=0, tile...]
    ppermute x10, starting transfers between devices: 17.9 us -> 21.2 us  [shifted(): lax.ppermute(x, axis, [(i, (i + step) % count) for i in range(count)])]
    pallas_call x2, Pallas kernels: 6.5 us -> 8.16 us  [the longest x1 7.1 us: body(): call(functools.partial(steps, tile_t, tile_p), [(fields * tile_t * tile_p...]
  transfers between devices with their start and end apart: 10 -> 10, of which waited for: 1 -> 1; matrix products, arithmetic and copies ran while one was open for 0% -> 0% of each run, Pallas kernels for 12% -> 16%
where the time goes in v5:
time: 64.2 us; the launch traced here: 63.1 us
  blocking collectives  23.8 us (37%)
  starting transfers between devices  21.2 us (33%)
  Pallas kernels  16.1 us (25%)
  between operations  0.8 us (1%)
  local copies, waits for them, and re-layouts  0.72 us (1%)
    all_to_all x1, blocking collectives, body(): lax.all_to_all(message, ('lat', 'lon'), split_axis=0, concat_axis=0, tile...  23.8 us
    ppermute x10, starting transfers between devices, shifted(): lax.ppermute(x, axis, [(i, (i + step) % count) for i in range(count)])  21.2 us
    pallas_call x1, Pallas kernels, body(): call(functools.partial(steps, tile_t, tile_p), [(fields * tile_t * tile_p...  7.1 us
    pallas_call x1, Pallas kernels, body(): call(functools.partial(plan, face_t, tile_t, tile_p), [(1, count), (n_dev...  2.05 us
    pallas_call x1, Pallas kernels, body(): call(theta_edges, [edge] * 2, [pl.BlockSpec(memory_space=pltpu.HBM)] * 2,...  1.81 us
    pallas_call x1, Pallas kernels, body(): call(functools.partial(route, n_dev), [(4, fields, radial), (2 * n_dev, 1...  1.66 us
    pallas_call x1, Pallas kernels, body(): call(functools.partial(land, n_dev), [helio_prev.shape, (fields, face_t),...  1.4 us
  transfers between devices with their start and end apart: 10, of which 1 were waited for; matrix products, arithmetic and copies ran while one was open for 0% of the time, Pallas kernels for 16%

profile of v5, /device:TPU:8, one launch (start us, length us, event | category | flops | bytes accessed | tf_op | source)
XLA Modules:
  0.0 63.1 jit_solution(10123976341421095050)
XLA Ops:
  0.6 0.0 copy-start
  0.6 0.0 copy-start.1
  0.6 1.8 %theta_edges.1 = (f32[9,2,16,128]{3,2,1,0:T(8,128)}, f32[9,2,16,128]{3,2,1,0:T(8,128)}) custom-call(f32[8,16,16,128]{3,2,1,0:T(8,128)} %corona.1, f32[16,16,128]{2,1,0:T(8,128)} %kappa.5), custom_call_target="tpu_custom_call" | custom-call | tf_op jit(solution)/shard_map/theta_edges/pallas_call | solution.py:412
  2.5 2.0 %collective-permute-start = (f32[9,2,16,128]{3,2,1,0:T(8,128)}, f32[9,2,16,128]{3,2,1,0:T(8,128)S(1)}, u32[]{:S(2)}, u32[]{:S(2)}) collective-permute-start(f32[9,2,16,128]{3,2,1,0:T(8,128)} %get-tuple-element.24), channel_id=1, source_target_pairs={{0,32},{32,64},{64,96},{96,128},{128,160},{160,192},{192,224},{224... | collective-permute-start | bytes 442376 | tf_op jit(solution)/shard_map/ppermute | solution.py:37
  4.5 4.0 %collective-permute-start.1 = (f32[9,2,16,128]{3,2,1,0:T(8,128)}, f32[9,2,16,128]{3,2,1,0:T(8,128)S(1)}, u32[]{:S(2)}, u32[]{:S(2)}) collective-permute-start(f32[9,2,16,128]{3,2,1,0:T(8,128)} %get-tuple-element.25), channel_id=1, source_target_pairs={{0,224},{32,0},{64,32},{96,64},{128,96},{160,128},{192,160},{224,1... | collective-permute-start | bytes 442376 | tf_op jit(solution)/shard_map/ppermute | solution.py:37
  8.5 0.0 copy-done
  8.5 0.0 copy-done.1
  8.5 0.0 copy-start.3
  8.5 0.0 copy-start.5
  8.5 0.0 copy-start.6
  8.5 0.1 phi_edges.1
  8.6 0.0 copy-start.4
  8.6 0.1 collective-permute-start.2
  8.7 3.8 %collective-permute-start.3 = (f32[9,32,128]{2,1,0:T(8,128)S(1)}, f32[9,32,128]{2,1,0:T(8,128)S(1)}, u32[]{:S(2)}, u32[]{:S(2)}) collective-permute-start(f32[9,32,128]{2,1,0:T(8,128)S(1)} %get-tuple-element.30), channel_id=1, source_target_pairs={{0,31},{1,0},{2,1},{3,2},{4,3},{5,4},{6,5},{7,6},{8,7},{9,8},{10,9... | collective-permute-start | bytes 442376 | tf_op jit(solution)/shard_map/ppermute | solution.py:37
  12.6 0.0 copy-done.3
  12.6 0.0 copy-done.5
  12.6 0.0 copy-done.6
  12.6 0.0 copy-done.4
  12.6 2.0 %plan.1 = (f32[1,2048]{1,0:T(1,128)S(1)}, f32[256,128]{1,0:T(8,128)S(1)}, bf16[256,2048]{1,0:T(8,128)(2,1)S(1)}, bf16[256,2048]{1,0:T(8,128)(2,1)S(1)}, bf16[256...) custom-call(s32[1,2048]{1,0:T(1,128)S(1)} %bitcast.25, s32[1,2048]{1,0:T(1,128)S(1)} %bitcast.26, s32[1,2048]{1,0:T(1,128)S(1)} %bitcast.27, ...), custom_call_target="tpu_custom_call" | custom-call | tf_op jit(solution)/shard_map/plan/pallas_call | solution.py:431
  14.6 0.0 collective-permute-done.t_low
  14.6 0.0 collective-permute-done.1.t_high
  14.7 0.1 collective-permute-start.4
  14.8 3.8 %collective-permute-start.5 = (f32[2,9,128]{2,1,0:T(8,128)S(1)}, f32[2,9,128]{2,1,0:T(8,128)S(1)}, u32[]{:S(2)}, u32[]{:S(2)}) collective-permute-start(f32[2,9,128]{2,1,0:T(8,128)S(1)} %get-tuple-element.31.own_low), channel_id=1, source_target_pairs={{0,31},{1,0},{2,1},{3,2},{4,3},{5,4},{6,5},{7,6},{8,7},{9,8},{10,9... | collective-permute-start | bytes 27656 | tf_op jit(solution)/shard_map/ppermute | solution.py:37
  18.6 0.0 collective-permute-done.2.p_low
  18.6 0.0 collective-permute-done.3.p_high
  18.6 0.0 copy-start.7
  18.6 0.7 %copy-done.7 = f32[8,8]{1,0:T(8,128)S(1)} copy-done((f32[8,8]{1,0:T(8,128)S(1)}, f32[8,8]{1,0:T(8,128)}, u32[]{:S(2)}) %copy-start.7) | copy-done | bytes 280
  19.3 7.1 %steps.1 = f32[2048,128]{1,0:T(8,128)S(1)} custom-call(f32[8,8]{1,0:T(8,128)S(1)} %copy-done.7, f32[2048,128]{1,0:T(8,128)S(1)} %bitcast.17, f32[16,16,128]{2,1,0:T(8,128)S(1)} %copy-done.1, f32[288,128]{1,0:T(8,128)S(1)} %bitcast.22, f32[288,128]{1,0:T(8,128)S(1)} %bitcast.23, f32[288,128]{1,0:T(8,128)S(1)} %bitcast.20, f32[288,128]{1,0:T(8,128)S(1)} %bitcast.21), custom_call_target="tpu_custom_call" | custom-call | tf_op jit(solution)/shard_map/steps/pallas_call | solution.py:447
  26.4 0.0 collective-permute-done.4.c_low
  26.4 0.0 collective-permute-done.5.c_high
  26.4 1.7 %route.1 = (f32[4,8,128]{2,1,0:T(8,128)S(1)}, f32[512,128]{1,0:T(8,128)S(1)}) custom-call(f32[16,16,128]{2,1,0:T(8,128)S(1)} %copy-done.1, f32[9,32,128]{2,1,0:T(8,128)S(1)} %collective-permute-done.2.p_low, f32[9,32,128]{2,1,0:T(8,128)S(1)} %collective-permute-done.3.p_high, f32[2,9,128]{2,1,0:T(8,128)S(1)} %get-tuple-element.31.own_low, ...), custom_call_target="tpu_custom_call" | custom-call | tf_op jit(solution)/shard_map/route/pallas_call | solution.py:469
  28.1 0.0 copy-start.2
  28.1 23.8 %all_to_all.11 = f32[256,2,128]{2,1,0:T(2,128)S(1)} all-to-all(f32[256,2,128]{2,1,0:T(2,128)S(1)} %bitcast.24), channel_id=1, replica_groups=mesh['lat'=8,'lon'=32] {'lat','lon'}, dimensions={0} | all-to-all | bytes 524288 | tf_op jit(solution)/shard_map/all_to_all | solution.py:483
  51.9 0.0 copy-done.2
  51.9 1.4 %land.1 = (f32[8,32,128]{2,1,0:T(8,128)S(1)}, f32[8,128]{1,0:T(8,128)S(1)}, f32[8,128]{1,0:T(8,128)S(1)}, f32[1,256]{1,0:T(1,128)S(1)}, f32[1,256]{1,0:T(1,128)S(1)}) custom-call(f32[512,128]{1,0:T(8,128)S(1)} %bitcast.19, f32[8,32,128]{2,1,0:T(8,128)S(1)} %copy-done.2), custom_call_target="tpu_custom_call" | custom-call | tf_op jit(solution)/shard_map/land/pallas_call | solution.py:485
  53.3 0.3 collective-permute-start.6
  53.6 3.8 %collective-permute-start.7 = (f32[8,128]{1,0:T(8,128)S(1)}, f32[8,128]{1,0:T(8,128)S(1)}, u32[]{:S(2)}, u32[]{:S(2)}) collective-permute-start(f32[8,128]{1,0:T(8,128)S(1)} %get-tuple-element.43), channel_id=1, source_target_pairs={{0,31},{1,0},{2,1},{3,2},{4,3},{5,4},{6,5},{7,6},{8,7},{9,8},{10,9... | collective-permute-start | bytes 12296 | tf_op jit(solution)/shard_map/ppermute | solution.py:37
  57.4 1.0 %collective-permute-start.8 = (f32[1,256]{1,0:T(1,128)S(1)}, f32[1,256]{1,0:T(1,128)S(1)}, u32[]{:S(2)}, u32[]{:S(2)}) collective-permute-start(f32[1,256]{1,0:T(1,128)S(1)} %get-tuple-element.44), channel_id=1, source_target_pairs={{0,32},{32,64},{64,96},{96,128},{128,160},{160,192},{192,224},{224... | collective-permute-start | bytes 3080 | tf_op jit(solution)/shard_map/ppermute | solution.py:37
  58.5 2.2 %collective-permute-start.9 = (f32[1,256]{1,0:T(1,128)S(1)}, f32[1,256]{1,0:T(1,128)S(1)}, u32[]{:S(2)}, u32[]{:S(2)}) collective-permute-start(f32[1,256]{1,0:T(1,128)S(1)} %get-tuple-element.45), channel_id=1, source_target_pairs={{0,224},{32,0},{64,32},{96,64},{128,96},{160,128},{192,160},{224,1... | collective-permute-start | bytes 3080 | tf_op jit(solution)/shard_map/ppermute | solution.py:37
  60.7 1.1 %finish.1 = f32[8,256,128]{2,1,0:T(8,128)} custom-call(f32[8,256,128]{2,1,0:T(8,128)S(1)} %bitcast.15, f32[4,8,128]{2,1,0:T(8,128)S(1)} %get-tuple-element.39.patch), custom_call_target="tpu_custom_call" | custom-call | tf_op jit(solution)/shard_map/finish/pallas_call | solution.py:479
  61.7 0.5 collective-permute-done.8.t_low
  62.2 0.0 collective-permute-done.9.t_high
  62.2 0.0 collective-permute-done.6.p_low
  62.2 0.0 collective-permute-done.7.p_high
  62.2 0.9 %smooth.1 = f32[8,32,128]{2,1,0:T(8,128)} custom-call(f32[8,32,128]{2,1,0:T(8,128)S(1)} %get-tuple-element.41.coupled, f32[8,128]{1,0:T(8,128)S(1)} %collective-permute-done.6.p_low, f32[8,128]{1,0:T(8,128)S(1)} %collective-permute-done.7.p_high, f32[1,256]{1,0:T(1,128)S(1)} %collective-permute-done.8.t_low, f32[1,256]{1,0:T(1,128)S(1)} %collective-permute-done.9.t_high), custom_call_target="tpu_custom_call" | custom-call | tf_op jit(solution)/shard_map/smooth/pallas_call | solution.py:495
  (1 shorter events, 0.0 us)
Async XLA Ops:
  0.6 7.9 %copy-start = (f32[8,16,16,128]{3,2,1,0:T(8,128)S(1)}, f32[8,16,16,128]{3,2,1,0:T(8,128)}, u32[]{:S(2)}) copy-start(f32[8,16,16,128]{3,2,1,0:T(8,128)} %corona.1) | copy-start | bytes 3145732
  0.6 7.9 %copy-start.1 = (f32[16,16,128]{2,1,0:T(8,128)S(1)}, f32[16,16,128]{2,1,0:T(8,128)}, u32[]{:S(2)}) copy-start(f32[16,16,128]{2,1,0:T(8,128)} %kappa.5) | copy-start | bytes 393220
  2.5 12.2 %collective-permute-start = (f32[9,2,16,128]{3,2,1,0:T(8,128)}, f32[9,2,16,128]{3,2,1,0:T(8,128)S(1)}, u32[]{:S(2)}, u32[]{:S(2)}) collective-permute-start(f32[9,2,16,128]{3,2,1,0:T(8,128)} %get-tuple-element.24), channel_id=1, source_target_pairs={{0,32},{32,64},{64,96},{96,128},{128,160},{160,192},{192,224},{224... | collective-permute-start | bytes 442376 | tf_op jit(solution)/shard_map/ppermute | solution.py:37
  4.5 10.2 %collective-permute-start.1 = (f32[9,2,16,128]{3,2,1,0:T(8,128)}, f32[9,2,16,128]{3,2,1,0:T(8,128)S(1)}, u32[]{:S(2)}, u32[]{:S(2)}) collective-permute-start(f32[9,2,16,128]{3,2,1,0:T(8,128)} %get-tuple-element.25), channel_id=1, source_target_pairs={{0,224},{32,0},{64,32},{96,64},{128,96},{160,128},{192,160},{224,1... | collective-permute-start | bytes 442376 | tf_op jit(solution)/shard_map/ppermute | solution.py:37
  8.5 4.1 %copy-start.3 = (f32[3,2048]{1,0:T(4,128)S(1)}, f32[3,2048]{1,0:T(4,128)}, u32[]{:S(2)}) copy-start(f32[3,2048]{1,0:T(4,128)} %frac.1) | copy-start | bytes 73732
  8.5 4.1 %copy-start.5 = (s32[2048]{0:T(1024)S(1)}, s32[2048]{0:T(1024)}, u32[]{:S(2)}) copy-start(s32[2048]{0:T(1024)} %param.13) | copy-start | bytes 24580
  8.5 4.1 %copy-start.6 = (s32[2048]{0:T(1024)S(1)}, s32[2048]{0:T(1024)}, u32[]{:S(2)}) copy-start(s32[2048]{0:T(1024)} %param.14) | copy-start | bytes 24580
  8.6 4.0 %copy-start.4 = (s32[2048,1]{0,1:T(1,128)S(1)}, s32[2048,1]{0,1:T(1,128)}, u32[]{:S(2)}) copy-start(s32[2048,1]{0,1:T(1,128)} %param.12) | copy-start | bytes 24580
  8.6 10.0 %collective-permute-start.2 = (f32[9,32,128]{2,1,0:T(8,128)S(1)}, f32[9,32,128]{2,1,0:T(8,128)S(1)}, u32[]{:S(2)}, u32[]{:S(2)}) collective-permute-start(f32[9,32,128]{2,1,0:T(8,128)S(1)} %get-tuple-element.29), channel_id=1, source_target_pairs={{0,1},{1,2},{2,3},{3,4},{4,5},{5,6},{6,7},{7,8},{8,9},{9,10},{10,1... | collective-permute-start | bytes 442376 | tf_op jit(solution)/shard_map/ppermute | solution.py:37
  8.7 9.9 %collective-permute-start.3 = (f32[9,32,128]{2,1,0:T(8,128)S(1)}, f32[9,32,128]{2,1,0:T(8,128)S(1)}, u32[]{:S(2)}, u32[]{:S(2)}) collective-permute-start(f32[9,32,128]{2,1,0:T(8,128)S(1)} %get-tuple-element.30), channel_id=1, source_target_pairs={{0,31},{1,0},{2,1},{3,2},{4,3},{5,4},{6,5},{7,6},{8,7},{9,8},{10,9... | collective-permute-start | bytes 442376 | tf_op jit(solution)/shard_map/ppermute | solution.py:37
  14.7 11.7 %collective-permute-start.4 = (f32[2,9,128]{2,1,0:T(8,128)S(1)}, f32[2,9,128]{2,1,0:T(8,128)S(1)}, u32[]{:S(2)}, u32[]{:S(2)}) collective-permute-start(f32[2,9,128]{2,1,0:T(8,128)S(1)} %get-tuple-element.32.own_high), channel_id=1, source_target_pairs={{0,1},{1,2},{2,3},{3,4},{4,5},{5,6},{6,7},{7,8},{8,9},{9,10},{10,1... | collective-permute-start | bytes 27656 | tf_op jit(solution)/shard_map/ppermute | solution.py:37
  14.8 11.7 %collective-permute-start.5 = (f32[2,9,128]{2,1,0:T(8,128)S(1)}, f32[2,9,128]{2,1,0:T(8,128)S(1)}, u32[]{:S(2)}, u32[]{:S(2)}) collective-permute-start(f32[2,9,128]{2,1,0:T(8,128)S(1)} %get-tuple-element.31.own_low), channel_id=1, source_target_pairs={{0,31},{1,0},{2,1},{3,2},{4,3},{5,4},{6,5},{7,6},{8,7},{9,8},{10,9... | collective-permute-start | bytes 27656 | tf_op jit(solution)/shard_map/ppermute | solution.py:37
  18.6 0.7 %copy-start.7 = (f32[8,8]{1,0:T(8,128)S(1)}, f32[8,8]{1,0:T(8,128)}, u32[]{:S(2)}) copy-start(f32[8,8]{1,0:T(8,128)} %mixing.1) | copy-start | bytes 772
  28.1 23.8 %copy-start.2 = (f32[8,32,128]{2,1,0:T(8,128)S(1)}, f32[8,32,128]{2,1,0:T(8,128)}, u32[]{:S(2)}) copy-start(f32[8,32,128]{2,1,0:T(8,128)} %prev.1) | copy-start | bytes 393220
  53.3 8.9 %collective-permute-start.6 = (f32[8,128]{1,0:T(8,128)S(1)}, f32[8,128]{1,0:T(8,128)S(1)}, u32[]{:S(2)}, u32[]{:S(2)}) collective-permute-start(f32[8,128]{1,0:T(8,128)S(1)} %get-tuple-element.42), channel_id=1, source_target_pairs={{0,1},{1,2},{2,3},{3,4},{4,5},{5,6},{6,7},{7,8},{8,9},{9,10},{10,1... | collective-permute-start | bytes 12296 | tf_op jit(solution)/shard_map/ppermute | solution.py:37
  53.6 8.6 %collective-permute-start.7 = (f32[8,128]{1,0:T(8,128)S(1)}, f32[8,128]{1,0:T(8,128)S(1)}, u32[]{:S(2)}, u32[]{:S(2)}) collective-permute-start(f32[8,128]{1,0:T(8,128)S(1)} %get-tuple-element.43), channel_id=1, source_target_pairs={{0,31},{1,0},{2,1},{3,2},{4,3},{5,4},{6,5},{7,6},{8,7},{9,8},{10,9... | collective-permute-start | bytes 12296 | tf_op jit(solution)/shard_map/ppermute | solution.py:37
  57.4 4.8 %collective-permute-start.8 = (f32[1,256]{1,0:T(1,128)S(1)}, f32[1,256]{1,0:T(1,128)S(1)}, u32[]{:S(2)}, u32[]{:S(2)}) collective-permute-start(f32[1,256]{1,0:T(1,128)S(1)} %get-tuple-element.44), channel_id=1, source_target_pairs={{0,32},{32,64},{64,96},{96,128},{128,160},{160,192},{192,224},{224... | collective-permute-start | bytes 3080 | tf_op jit(solution)/shard_map/ppermute | solution.py:37
  58.5 3.7 %collective-permute-start.9 = (f32[1,256]{1,0:T(1,128)S(1)}, f32[1,256]{1,0:T(1,128)S(1)}, u32[]{:S(2)}, u32[]{:S(2)}) collective-permute-start(f32[1,256]{1,0:T(1,128)S(1)} %get-tuple-element.45), channel_id=1, source_target_pairs={{0,224},{32,0},{64,32},{96,64},{128,96},{160,128},{192,160},{224,1... | collective-permute-start | bytes 3080 | tf_op jit(solution)/shard_map/ppermute | solution.py:37

commit v6 on v4

--- a/solution.py
+++ b/solution.py
@@ -10,6 +10,7 @@
 SH = 8
 CAP = 16
 BLOCK = 256
+UNROLL = 16
 VMEM = pltpu.VMEM
 F32 = jnp.float32
 BF16 = jnp.bfloat16
@@ -197,43 +198,7 @@
     )
 
 
-def inside(mixing, corona, kappa, once_out, twice_out, wide, once, mix):
-    fields, tile_t, tile_p, radial = corona.shape
-    spread(mixing, mix)
-    zeros = jnp.zeros((8, radial), F32)
-    plane = jnp.zeros((WIDE, radial), F32)
-    for f in range(fields + 1):
-        for t in range(tile_t + 2):
-            if t in (0, tile_t + 1):
-                wide[f, pl.ds(t * WIDE, WIDE), :] = plane
-                if f < fields:
-                    once[f, pl.ds(t * WIDE, WIDE), :] = plane
-                continue
-            for ref in (wide, once) if f < fields else (wide,):
-                ref[f, pl.ds(t * WIDE, 8), :] = zeros
-                ref[f, pl.ds(t * WIDE + 8 + tile_p, 8), :] = zeros
-            own = corona[f, t - 1] if f < fields else kappa[t - 1]
-            wide[f, pl.ds(t * WIDE + 8, tile_p), :] = own
-
-    def first(t, _):
-        for g, acc in row_flux(mix, wide, wide, t, t, tile_p, fields):
-            once[g, pl.ds(pl.multiple_of(t * WIDE + 8, 8), tile_p), :] = acc
-            once_out[g, t - 1] = acc
-        return 0
-
-    lax.fori_loop(1, tile_t + 1, first, 0)
-
-    def second(t, _):
-        for g, acc in row_flux(mix, once, wide, t, t, tile_p, fields):
-            twice_out[g, t - 1] = acc
-        return 0
-
-    lax.fori_loop(2, tile_t, second, 0)
-
-
-def around(
-    mixing, corona, kappa, t_low, t_high, p_low, p_high, once_in, twice_in, stepped, wide, once, mix,
-):
+def steps(mixing, corona, kappa, t_low, t_high, p_low, p_high, stepped, wide, once, mix):
     fields, tile_t, tile_p, radial = corona.shape
     has_t, has_p = exists()
     spread(mixing, mix)
@@ -251,29 +216,39 @@
                 wide[f, pl.ds(2 * WIDE + col, tile_t, stride=WIDE), :] = cells
             for t in (1, tile_t + 2):
                 wide[f, pl.ds(t * WIDE + near, 1), :] = nothing
-        if f < fields:
-            for t in range(tile_t):
-                once[f, pl.ds((t + 1) * WIDE + 8, tile_p), :] = once_in[f, t]
-
-    for t in (-1, 0, tile_t - 1, tile_t):
+
+    def first(t):
         for g, acc in row_flux(mix, wide, wide, t + 2, t + 2, tile_p, fields):
-            if t in (-1, tile_t):
+            if isinstance(t, int) and t in (-1, tile_t):
                 acc = acc * has_t[0 if t < 0 else 1]
-            once[g, pl.ds((t + 1) * WIDE + 8, tile_p), :] = acc
-    for p in (-1, 0, tile_p - 1, tile_p):
+            at = (t + 1) * WIDE + 8
+            once[g, pl.ds(at if isinstance(t, int) else pl.multiple_of(at, 8), tile_p), :] = acc
+
+    def second(t):
+        for g, acc in row_flux(mix, once, wide, t + 1, t + 2, tile_p, fields):
+            stepped[g, t] = acc
+
+    first(-1)
+    first(tile_t)
+    for p in (-1, tile_p):
         for g, acc in column_flux(mix, wide, wide, 2, 2, p, tile_t, fields):
-            if p in (-1, tile_p):
-                acc = acc * has_p[0 if p < 0 else 1]
-            once[g, pl.ds(WIDE + 8 + p, tile_t, stride=WIDE), :] = acc
-
-    for f in range(fields):
-        stepped[f] = twice_in[f]
-    for t in (0, 1, tile_t - 2, tile_t - 1):
-        for g, acc in row_flux(mix, once, wide, t + 1, t + 2, tile_p, fields):
-            stepped[g, t * tile_p : (t + 1) * tile_p, :] = acc
-    for p in (0, 1, tile_p - 2, tile_p - 1):
-        for g, acc in column_flux(mix, once, wide, 1, 2, p, tile_t, fields):
-            stepped[g, pl.ds(p, tile_t, stride=tile_p), :] = acc
+            once[g, pl.ds(WIDE + 8 + p, tile_t, stride=WIDE), :] = acc * has_p[0 if p < 0 else 1]
+    for row in (first, second):
+        by_rows(row, tile_t)
+
+
+def by_rows(row, count):
+    if UNROLL >= count:
+        for t in range(count):
+            row(t)
+        return
+
+    def some(i, carry):
+        for k in range(UNROLL):
+            row(i * UNROLL + k)
+        return carry
+
+    lax.fori_loop(0, count // UNROLL, some, 0)
 
 
 def route(
@@ -460,18 +435,6 @@
     )(owner, dest_cell, base, fractions)
 
     t_low, t_high, rank = lax.optimization_barrier((t_low, t_high, rank))
-    once, twice = call(
-        inside,
-        [corona.shape] * 2,
-        [sspec()] + [vspec()] * 2,
-        "inside",
-        [
-            VMEM((fields + 1, (tile_t + 2) * WIDE, radial), F32),
-            VMEM((fields, (tile_t + 2) * WIDE, radial), F32),
-            VMEM((fields * fields, 8, radial), F32),
-        ],
-    )(mixing, corona, kappa)
-
     own_low, own_high = call(
         corner_cells, [(2, fields + 1, radial)] * 2, [vspec()] * 2, "corner_cells"
     )(t_low, t_high)
@@ -479,14 +442,18 @@
     c_high = shifted(own_low, "lon", -1)
 
     flat = (fields, tile_t * tile_p, radial)
-    padded = [
-        VMEM((fields + 1, (tile_t + 4) * WIDE, radial), F32),
-        VMEM((fields, (tile_t + 2) * WIDE, radial), F32),
-        VMEM((fields * fields, 8, radial), F32),
-    ]
-    (almost,) = call(around, [flat], [sspec()] + [vspec()] * 8, "around", padded)(
-        mixing, corona, kappa, t_low, t_high, p_low, p_high, once, twice.reshape(flat)
-    )
+    (almost,) = call(
+        steps,
+        [corona.shape],
+        [sspec()] + [vspec()] * 6,
+        "steps",
+        [
+            VMEM((fields + 1, (tile_t + 4) * WIDE, radial), F32),
+            VMEM((fields, (tile_t + 2) * WIDE, radial), F32),
+            VMEM((fields * fields, 8, radial), F32),
+        ],
+    )(mixing, corona, kappa, t_low, t_high, p_low, p_high)
+    almost = almost.reshape(flat)
 
     patch, message = call(
         functools.partial(route, n_dev),

time: 64.2 us -> 61.9 us (0.964)
  Pallas kernels: 17.4 us -> 13.1 us
  starting transfers between devices: 17.7 us -> 21 us
  blocking collectives: 26.6 us -> 25.4 us
    pallas_call x2 -> x1, Pallas kernels: 8.37 us -> 4.1 us  [body(): call(steps, [corona.shape], [sspec()] + [vspec()] * 6, 'steps', [VMEM((fi...]
    ppermute x10, starting transfers between devices: 17.7 us -> 21 us  [shifted(): lax.ppermute(x, axis, [(i, (i + step) % count) for i in range(count)])]
    all_to_all x1, blocking collectives: 26.6 us -> 25.4 us  [body(): lax.all_to_all(message, ('lat', 'lon'), split_axis=0, concat_axis=0, tile...]
  transfers between devices with their start and end apart: 10 -> 10, of which waited for: 1 -> 1; matrix products, arithmetic and copies ran while one was open for 0% -> 0% of each run, Pallas kernels for 18% -> 12%
where the time goes in v6:
time: 61.9 us; the launch traced here: 60.8 us
  blocking collectives  25.4 us (41%)
  starting transfers between devices  21 us (34%)
  Pallas kernels  13.1 us (21%)
  between operations  0.81 us (1%)
    all_to_all x1, blocking collectives, body(): lax.all_to_all(message, ('lat', 'lon'), split_axis=0, concat_axis=0, tile...  25.4 us
    ppermute x10, starting transfers between devices, shifted(): lax.ppermute(x, axis, [(i, (i + step) % count) for i in range(count)])  21 us
    pallas_call x1, Pallas kernels, body(): call(steps, [corona.shape], [sspec()] + [vspec()] * 6, 'steps', [VMEM((fi...  4.1 us
    pallas_call x1, Pallas kernels, body(): call(functools.partial(plan, face_t, tile_t, tile_p), [(1, count), (n_dev...  2.05 us
    pallas_call x1, Pallas kernels, body(): call(theta_edges, [edge] * 2, [pl.BlockSpec(memory_space=pltpu.HBM)] * 2,...  1.81 us
    pallas_call x1, Pallas kernels, body(): call(functools.partial(route, n_dev), [(4, fields, radial), (2 * n_dev, 1...  1.66 us
    pallas_call x1, Pallas kernels, body(): call(functools.partial(land, n_dev), [helio_prev.shape, (fields, face_t),...  1.39 us
  transfers between devices with their start and end apart: 10, of which 1 were waited for; matrix products, arithmetic and copies ran while one was open for 0% of the time, Pallas kernels for 12%

profile of v6, /device:TPU:8, one launch (start us, length us, event | category | flops | bytes accessed | tf_op | source)
XLA Modules:
  0.0 60.8 jit_solution(4822699102994363836)
XLA Ops:
  0.6 0.0 copy-start
  0.6 0.0 copy-start.1
  0.6 1.8 %theta_edges.1 = (f32[9,2,16,128]{3,2,1,0:T(8,128)}, f32[9,2,16,128]{3,2,1,0:T(8,128)}) custom-call(f32[8,16,16,128]{3,2,1,0:T(8,128)} %corona.3, f32[16,16,128]{2,1,0:T(8,128)} %kappa.5), custom_call_target="tpu_custom_call" | custom-call | tf_op jit(solution)/shard_map/theta_edges/pallas_call | solution.py:410
  2.5 2.0 %collective-permute-start = (f32[9,2,16,128]{3,2,1,0:T(8,128)}, f32[9,2,16,128]{3,2,1,0:T(8,128)S(1)}, u32[]{:S(2)}, u32[]{:S(2)}) collective-permute-start(f32[9,2,16,128]{3,2,1,0:T(8,128)} %get-tuple-element.24), channel_id=1, source_target_pairs={{0,32},{32,64},{64,96},{96,128},{128,160},{160,192},{192,224},{224... | collective-permute-start | bytes 442376 | tf_op jit(solution)/shard_map/ppermute | solution.py:38
  4.5 4.0 %collective-permute-start.1 = (f32[9,2,16,128]{3,2,1,0:T(8,128)}, f32[9,2,16,128]{3,2,1,0:T(8,128)S(1)}, u32[]{:S(2)}, u32[]{:S(2)}) collective-permute-start(f32[9,2,16,128]{3,2,1,0:T(8,128)} %get-tuple-element.25), channel_id=1, source_target_pairs={{0,224},{32,0},{64,32},{96,64},{128,96},{160,128},{192,160},{224,1... | collective-permute-start | bytes 442376 | tf_op jit(solution)/shard_map/ppermute | solution.py:38
  8.5 0.0 copy-done
  8.5 0.0 copy-done.1
  8.5 0.0 copy-start.3
  8.5 0.0 copy-start.5
  8.5 0.0 copy-start.6
  8.5 0.1 phi_edges.1
  8.6 0.0 copy-start.4
  8.6 0.1 collective-permute-start.2
  8.7 3.8 %collective-permute-start.3 = (f32[9,32,128]{2,1,0:T(8,128)S(1)}, f32[9,32,128]{2,1,0:T(8,128)S(1)}, u32[]{:S(2)}, u32[]{:S(2)}) collective-permute-start(f32[9,32,128]{2,1,0:T(8,128)S(1)} %get-tuple-element.30), channel_id=1, source_target_pairs={{0,31},{1,0},{2,1},{3,2},{4,3},{5,4},{6,5},{7,6},{8,7},{9,8},{10,9... | collective-permute-start | bytes 442376 | tf_op jit(solution)/shard_map/ppermute | solution.py:38
  12.6 0.0 copy-done.3
  12.6 0.0 copy-done.5
  12.6 0.0 copy-done.6
  12.6 0.0 copy-done.4
  12.6 2.0 %plan.1 = (f32[1,2048]{1,0:T(1,128)S(1)}, f32[256,128]{1,0:T(8,128)S(1)}, bf16[256,2048]{1,0:T(8,128)(2,1)S(1)}, bf16[256,2048]{1,0:T(8,128)(2,1)S(1)}, bf16[256...) custom-call(s32[1,2048]{1,0:T(1,128)S(1)} %bitcast.15, s32[1,2048]{1,0:T(1,128)S(1)} %bitcast.16, s32[1,2048]{1,0:T(1,128)S(1)} %bitcast.17, ...), custom_call_target="tpu_custom_call" | custom-call | tf_op jit(solution)/shard_map/plan/pallas_call | solution.py:429
  14.6 0.0 collective-permute-done.t_low
  14.6 0.0 collective-permute-done.1.t_high
  14.7 0.0 copy-start.7
  14.7 0.1 collective-permute-start.4
  14.8 3.8 %collective-permute-start.5 = (f32[2,9,128]{2,1,0:T(8,128)S(1)}, f32[2,9,128]{2,1,0:T(8,128)S(1)}, u32[]{:S(2)}, u32[]{:S(2)}) collective-permute-start(f32[2,9,128]{2,1,0:T(8,128)S(1)} %get-tuple-element.31.own_low), channel_id=1, source_target_pairs={{0,31},{1,0},{2,1},{3,2},{4,3},{5,4},{6,5},{7,6},{8,7},{9,8},{10,9... | collective-permute-start | bytes 27656 | tf_op jit(solution)/shard_map/ppermute | solution.py:38
  18.6 0.0 collective-permute-done.2.p_low
  18.6 0.0 collective-permute-done.3.p_high
  18.6 0.0 copy-done.7
  18.6 4.1 %steps.1 = f32[8,16,16,128]{3,2,1,0:T(8,128)S(1)} custom-call(f32[8,8]{1,0:T(8,128)S(1)} %copy-done.7, f32[8,16,16,128]{3,2,1,0:T(8,128)S(1)} %copy-done, f32[16,16,128]{2,1,0:T(8,128)S(1)} %copy-done.1, f32[9,2,16,128]{3,2,1,0:T(8,128)S(1)} %collective-permute-done.t_low, f32[9,2,16,128]{3,2,1,0:T(8,128)S(1)} %collective-permute-done.1.t_high, ...), custom_call_target="tpu_custom_call" | custom-call | tf_op jit(solution)/shard_map/steps/pallas_call | solution.py:445
  22.7 0.0 collective-permute-done.4.c_low
  22.8 0.0 collective-permute-done.5.c_high
  22.8 1.7 %route.1 = (f32[4,8,128]{2,1,0:T(8,128)S(1)}, f32[512,128]{1,0:T(8,128)S(1)}) custom-call(f32[16,16,128]{2,1,0:T(8,128)S(1)} %copy-done.1, f32[9,32,128]{2,1,0:T(8,128)S(1)} %collective-permute-done.2.p_low, f32[9,32,128]{2,1,0:T(8,128)S(1)} %collective-permute-done.3.p_high, f32[2,9,128]{2,1,0:T(8,128)S(1)} %get-tuple-element.31.own_low, ...), custom_call_target="tpu_custom_call" | custom-call | tf_op jit(solution)/shard_map/route/pallas_call | solution.py:458
  24.4 0.0 copy-start.2
  24.4 25.4 %all_to_all.11 = f32[256,2,128]{2,1,0:T(2,128)S(1)} all-to-all(f32[256,2,128]{2,1,0:T(2,128)S(1)} %bitcast.14), channel_id=1, replica_groups=mesh['lat'=8,'lon'=32] {'lat','lon'}, dimensions={0} | all-to-all | bytes 524288 | tf_op jit(solution)/shard_map/all_to_all | solution.py:472
  49.8 0.0 copy-done.2
  49.8 1.4 %land.1 = (f32[8,32,128]{2,1,0:T(8,128)S(1)}, f32[8,128]{1,0:T(8,128)S(1)}, f32[8,128]{1,0:T(8,128)S(1)}, f32[1,256]{1,0:T(1,128)S(1)}, f32[1,256]{1,0:T(1,128)S(1)}) custom-call(f32[512,128]{1,0:T(8,128)S(1)} %bitcast.13, f32[8,32,128]{2,1,0:T(8,128)S(1)} %copy-done.2), custom_call_target="tpu_custom_call" | custom-call | tf_op jit(solution)/shard_map/land/pallas_call | solution.py:474
  51.2 0.1 collective-permute-start.6
  51.3 3.8 %collective-permute-start.7 = (f32[8,128]{1,0:T(8,128)S(1)}, f32[8,128]{1,0:T(8,128)S(1)}, u32[]{:S(2)}, u32[]{:S(2)}) collective-permute-start(f32[8,128]{1,0:T(8,128)S(1)} %get-tuple-element.43), channel_id=1, source_target_pairs={{0,31},{1,0},{2,1},{3,2},{4,3},{5,4},{6,5},{7,6},{8,7},{9,8},{10,9... | collective-permute-start | bytes 12296 | tf_op jit(solution)/shard_map/ppermute | solution.py:38
  55.1 1.0 %collective-permute-start.8 = (f32[1,256]{1,0:T(1,128)S(1)}, f32[1,256]{1,0:T(1,128)S(1)}, u32[]{:S(2)}, u32[]{:S(2)}) collective-permute-start(f32[1,256]{1,0:T(1,128)S(1)} %get-tuple-element.44), channel_id=1, source_target_pairs={{0,32},{32,64},{64,96},{96,128},{128,160},{160,192},{192,224},{224... | collective-permute-start | bytes 3080 | tf_op jit(solution)/shard_map/ppermute | solution.py:38
  56.2 2.2 %collective-permute-start.9 = (f32[1,256]{1,0:T(1,128)S(1)}, f32[1,256]{1,0:T(1,128)S(1)}, u32[]{:S(2)}, u32[]{:S(2)}) collective-permute-start(f32[1,256]{1,0:T(1,128)S(1)} %get-tuple-element.45), channel_id=1, source_target_pairs={{0,224},{32,0},{64,32},{96,64},{128,96},{160,128},{192,160},{224,1... | collective-permute-start | bytes 3080 | tf_op jit(solution)/shard_map/ppermute | solution.py:38
  58.4 1.1 %finish.1 = f32[8,256,128]{2,1,0:T(8,128)} custom-call(f32[8,256,128]{2,1,0:T(8,128)S(1)} %bitcast.10, f32[4,8,128]{2,1,0:T(8,128)S(1)} %get-tuple-element.39.patch), custom_call_target="tpu_custom_call" | custom-call | tf_op jit(solution)/shard_map/finish/pallas_call | solution.py:468
  59.4 0.5 collective-permute-done.8.t_low
  59.9 0.0 collective-permute-done.9.t_high
  59.9 0.0 collective-permute-done.6.p_low
  59.9 0.0 collective-permute-done.7.p_high
  59.9 0.9 %smooth.1 = f32[8,32,128]{2,1,0:T(8,128)} custom-call(f32[8,32,128]{2,1,0:T(8,128)S(1)} %get-tuple-element.41.coupled, f32[8,128]{1,0:T(8,128)S(1)} %collective-permute-done.6.p_low, f32[8,128]{1,0:T(8,128)S(1)} %collective-permute-done.7.p_high, f32[1,256]{1,0:T(1,128)S(1)} %collective-permute-done.8.t_low, f32[1,256]{1,0:T(1,128)S(1)} %collective-permute-done.9.t_high), custom_call_target="tpu_custom_call" | custom-call | tf_op jit(solution)/shard_map/smooth/pallas_call | solution.py:484
  (1 shorter events, 0.0 us)
Async XLA Ops:
  0.6 7.9 %copy-start = (f32[8,16,16,128]{3,2,1,0:T(8,128)S(1)}, f32[8,16,16,128]{3,2,1,0:T(8,128)}, u32[]{:S(2)}) copy-start(f32[8,16,16,128]{3,2,1,0:T(8,128)} %corona.3) | copy-start | bytes 3145732
  0.6 7.9 %copy-start.1 = (f32[16,16,128]{2,1,0:T(8,128)S(1)}, f32[16,16,128]{2,1,0:T(8,128)}, u32[]{:S(2)}) copy-start(f32[16,16,128]{2,1,0:T(8,128)} %kappa.5) | copy-start | bytes 393220
  2.5 12.2 %collective-permute-start = (f32[9,2,16,128]{3,2,1,0:T(8,128)}, f32[9,2,16,128]{3,2,1,0:T(8,128)S(1)}, u32[]{:S(2)}, u32[]{:S(2)}) collective-permute-start(f32[9,2,16,128]{3,2,1,0:T(8,128)} %get-tuple-element.24), channel_id=1, source_target_pairs={{0,32},{32,64},{64,96},{96,128},{128,160},{160,192},{192,224},{224... | collective-permute-start | bytes 442376 | tf_op jit(solution)/shard_map/ppermute | solution.py:38
  4.5 10.2 %collective-permute-start.1 = (f32[9,2,16,128]{3,2,1,0:T(8,128)}, f32[9,2,16,128]{3,2,1,0:T(8,128)S(1)}, u32[]{:S(2)}, u32[]{:S(2)}) collective-permute-start(f32[9,2,16,128]{3,2,1,0:T(8,128)} %get-tuple-element.25), channel_id=1, source_target_pairs={{0,224},{32,0},{64,32},{96,64},{128,96},{160,128},{192,160},{224,1... | collective-permute-start | bytes 442376 | tf_op jit(solution)/shard_map/ppermute | solution.py:38
  8.5 4.1 %copy-start.3 = (f32[3,2048]{1,0:T(4,128)S(1)}, f32[3,2048]{1,0:T(4,128)}, u32[]{:S(2)}) copy-start(f32[3,2048]{1,0:T(4,128)} %frac.1) | copy-start | bytes 73732
  8.5 4.1 %copy-start.5 = (s32[2048]{0:T(1024)S(1)}, s32[2048]{0:T(1024)}, u32[]{:S(2)}) copy-start(s32[2048]{0:T(1024)} %param.13) | copy-start | bytes 24580
  8.5 4.1 %copy-start.6 = (s32[2048]{0:T(1024)S(1)}, s32[2048]{0:T(1024)}, u32[]{:S(2)}) copy-start(s32[2048]{0:T(1024)} %param.14) | copy-start | bytes 24580
  8.6 4.0 %copy-start.4 = (s32[2048,1]{0,1:T(1,128)S(1)}, s32[2048,1]{0,1:T(1,128)}, u32[]{:S(2)}) copy-start(s32[2048,1]{0,1:T(1,128)} %param.12) | copy-start | bytes 24580
  8.6 10.0 %collective-permute-start.2 = (f32[9,32,128]{2,1,0:T(8,128)S(1)}, f32[9,32,128]{2,1,0:T(8,128)S(1)}, u32[]{:S(2)}, u32[]{:S(2)}) collective-permute-start(f32[9,32,128]{2,1,0:T(8,128)S(1)} %get-tuple-element.29), channel_id=1, source_target_pairs={{0,1},{1,2},{2,3},{3,4},{4,5},{5,6},{6,7},{7,8},{8,9},{9,10},{10,1... | collective-permute-start | bytes 442376 | tf_op jit(solution)/shard_map/ppermute | solution.py:38
  8.7 9.9 %collective-permute-start.3 = (f32[9,32,128]{2,1,0:T(8,128)S(1)}, f32[9,32,128]{2,1,0:T(8,128)S(1)}, u32[]{:S(2)}, u32[]{:S(2)}) collective-permute-start(f32[9,32,128]{2,1,0:T(8,128)S(1)} %get-tuple-element.30), channel_id=1, source_target_pairs={{0,31},{1,0},{2,1},{3,2},{4,3},{5,4},{6,5},{7,6},{8,7},{9,8},{10,9... | collective-permute-start | bytes 442376 | tf_op jit(solution)/shard_map/ppermute | solution.py:38
  14.7 4.0 %copy-start.7 = (f32[8,8]{1,0:T(8,128)S(1)}, f32[8,8]{1,0:T(8,128)}, u32[]{:S(2)}) copy-start(f32[8,8]{1,0:T(8,128)} %mixing.1) | copy-start | bytes 772
  14.7 8.1 %collective-permute-start.4 = (f32[2,9,128]{2,1,0:T(8,128)S(1)}, f32[2,9,128]{2,1,0:T(8,128)S(1)}, u32[]{:S(2)}, u32[]{:S(2)}) collective-permute-start(f32[2,9,128]{2,1,0:T(8,128)S(1)} %get-tuple-element.32.own_high), channel_id=1, source_target_pairs={{0,1},{1,2},{2,3},{3,4},{4,5},{5,6},{6,7},{7,8},{8,9},{9,10},{10,1... | collective-permute-start | bytes 27656 | tf_op jit(solution)/shard_map/ppermute | solution.py:38
  14.8 8.0 %collective-permute-start.5 = (f32[2,9,128]{2,1,0:T(8,128)S(1)}, f32[2,9,128]{2,1,0:T(8,128)S(1)}, u32[]{:S(2)}, u32[]{:S(2)}) collective-permute-start(f32[2,9,128]{2,1,0:T(8,128)S(1)} %get-tuple-element.31.own_low), channel_id=1, source_target_pairs={{0,31},{1,0},{2,1},{3,2},{4,3},{5,4},{6,5},{7,6},{8,7},{9,8},{10,9... | collective-permute-start | bytes 27656 | tf_op jit(solution)/shard_map/ppermute | solution.py:38
  24.4 25.4 %copy-start.2 = (f32[8,32,128]{2,1,0:T(8,128)S(1)}, f32[8,32,128]{2,1,0:T(8,128)}, u32[]{:S(2)}) copy-start(f32[8,32,128]{2,1,0:T(8,128)} %prev.1) | copy-start | bytes 393220
  51.2 8.7 %collective-permute-start.6 = (f32[8,128]{1,0:T(8,128)S(1)}, f32[8,128]{1,0:T(8,128)S(1)}, u32[]{:S(2)}, u32[]{:S(2)}) collective-permute-start(f32[8,128]{1,0:T(8,128)S(1)} %get-tuple-element.42), channel_id=1, source_target_pairs={{0,1},{1,2},{2,3},{3,4},{4,5},{5,6},{6,7},{7,8},{8,9},{9,10},{10,1... | collective-permute-start | bytes 12296 | tf_op jit(solution)/shard_map/ppermute | solution.py:38
  51.3 8.6 %collective-permute-start.7 = (f32[8,128]{1,0:T(8,128)S(1)}, f32[8,128]{1,0:T(8,128)S(1)}, u32[]{:S(2)}, u32[]{:S(2)}) collective-permute-start(f32[8,128]{1,0:T(8,128)S(1)} %get-tuple-element.43), channel_id=1, source_target_pairs={{0,31},{1,0},{2,1},{3,2},{4,3},{5,4},{6,5},{7,6},{8,7},{9,8},{10,9... | collective-permute-start | bytes 12296 | tf_op jit(solution)/shard_map/ppermute | solution.py:38
  55.1 4.8 %collective-permute-start.8 = (f32[1,256]{1,0:T(1,128)S(1)}, f32[1,256]{1,0:T(1,128)S(1)}, u32[]{:S(2)}, u32[]{:S(2)}) collective-permute-start(f32[1,256]{1,0:T(1,128)S(1)} %get-tuple-element.44), channel_id=1, source_target_pairs={{0,32},{32,64},{64,96},{96,128},{128,160},{160,192},{192,224},{224... | collective-permute-start | bytes 3080 | tf_op jit(solution)/shard_map/ppermute | solution.py:38
  56.2 3.7 %collective-permute-start.9 = (f32[1,256]{1,0:T(1,128)S(1)}, f32[1,256]{1,0:T(1,128)S(1)}, u32[]{:S(2)}, u32[]{:S(2)}) collective-permute-start(f32[1,256]{1,0:T(1,128)S(1)} %get-tuple-element.45), channel_id=1, source_target_pairs={{0,224},{32,0},{64,32},{96,64},{128,96},{160,128},{192,160},{224,1... | collective-permute-start | bytes 3080 | tf_op jit(solution)/shard_map/ppermute | solution.py:38

commit v7 on v6

--- a/solution.py
+++ b/solution.py
@@ -33,49 +33,74 @@
     return high, (x - high.astype(F32)).astype(BF16)
 
 
-def shifted(x, axis, step):
+def swapped(first, second, axis):
     count = lax.axis_size(axis)
-    return lax.ppermute(x, axis, [(i, (i + step) % count) for i in range(count)])
-
-
-def theta_edges(corona, kappa, low, high, sems):
+    other = [(i + (1 if i % 2 else -1)) % count for i in range(count)]
+    return (
+        lax.ppermute(first, axis, [(i, i ^ 1) for i in range(count)]),
+        lax.ppermute(second, axis, list(enumerate(other))),
+    )
+
+
+def parity(axis):
+    return lax.rem(lax.axis_index(axis), 2)
+
+
+def sides(axis):
+    at, count = lax.axis_index(axis), lax.axis_size(axis)
+    odd = parity(axis).astype(F32)
+    low = jnp.where(at > 0, 1.0, 0.0)
+    high = jnp.where(at < count - 1, 1.0, 0.0)
+    return (odd * low, (1.0 - odd) * low), ((1.0 - odd) * high, odd * high)
+
+
+def blend(weights, first, second):
+    return first * weights[0] + second * weights[1]
+
+
+def theta_edges(corona, kappa, first, second, sems):
     fields, tile_t = corona.shape[0], corona.shape[1]
+    odd = parity("lat")
     copies = []
-    for side, (out, start) in enumerate(((low, 0), (high, tile_t - 2))):
+    for n, (out, start) in enumerate(
+        ((first, (1 - odd) * (tile_t - 2)), (second, odd * (tile_t - 2)))
+    ):
         rows = pl.ds(start, 2)
         copies.append(
-            pltpu.make_async_copy(corona.at[:, rows], out.at[pl.ds(0, fields)], sems.at[2 * side])
+            pltpu.make_async_copy(corona.at[:, rows], out.at[pl.ds(0, fields)], sems.at[2 * n])
         )
-        copies.append(pltpu.make_async_copy(kappa.at[rows], out.at[fields], sems.at[2 * side + 1]))
+        copies.append(pltpu.make_async_copy(kappa.at[rows], out.at[fields], sems.at[2 * n + 1]))
     for copy in copies:
         copy.start()
     for copy in copies:
         copy.wait()
 
 
-def phi_edges(tile_t, tile_p, corona, kappa, low, high):
+def phi_edges(tile_t, tile_p, corona, kappa, first, second):
     fields = corona.shape[0]
-    for f in range(fields + 1):
-        for out, near, far in ((low, 0, 1), (high, tile_p - 1, tile_p - 2)):
+    odd = parity("lon")
+    for out, upper in ((first, 1 - odd), (second, odd)):
+        near = upper * (tile_p - 1)
+        far = upper * (tile_p - 3) + 1
+        for f in range(fields + 1):
             for at, col in ((0, near), (tile_t, far)):
                 rows = pl.ds(col, tile_t, stride=tile_p)
                 out[f, at : at + tile_t, :] = corona[f, rows, :] if f < fields else kappa[rows, :]
 
 
-def corner_cells(t_low, t_high, low, high):
-    count, _, tile_p, _ = t_low.shape
-    for f in range(count):
-        for out, col in ((low, 0), (high, tile_p - 1)):
-            out[0, f : f + 1, :] = t_low[f, 1, col : col + 1, :]
-            out[1, f : f + 1, :] = t_high[f, 0, col : col + 1, :]
-
-
-def exists():
-    found = []
-    for axis in ("lat", "lon"):
-        at, count = lax.axis_index(axis), lax.axis_size(axis)
-        found.append([jnp.where(at > 0, 1.0, 0.0), jnp.where(at < count - 1, 1.0, 0.0)])
-    return found
+def corner_cells(t_first, t_second, low, high, first, second):
+    count, _, tile_p, _ = t_first.shape
+    weights = sides("lat")
+    for a, row in ((0, 1), (1, 0)):
+        for f in range(count):
+            for out, col in ((low, 0), (high, tile_p - 1)):
+                cell = slice(col, col + 1)
+                out[a, f : f + 1, :] = blend(
+                    weights[a], t_first[f, row, cell, :], t_second[f, row, cell, :]
+                )
+    odd = parity("lon").astype(F32)
+    first[...] = blend((odd, 1.0 - odd), low[...], high[...])
+    second[...] = blend((1.0 - odd, odd), low[...], high[...])
 
 
 def plan(
@@ -198,9 +223,13 @@
     )
 
 
-def steps(mixing, corona, kappa, t_low, t_high, p_low, p_high, stepped, wide, once, mix):
+def steps(
+    mixing, corona, kappa, t_first, t_second, p_first, p_second, stepped, wide, once, mix,
+):
     fields, tile_t, tile_p, radial = corona.shape
-    has_t, has_p = exists()
+    by_t, by_p = sides("lat"), sides("lon")
+    has_t = [low + high for low, high in by_t]
+    has_p = [low + high for low, high in by_p]
     spread(mixing, mix)
     nothing = jnp.zeros((1, radial), F32)
     for f in range(fields + 1):
@@ -208,11 +237,14 @@
             own = corona[f, t] if f < fields else kappa[t]
             wide[f, pl.ds((t + 2) * WIDE + 8, tile_p), :] = own
         for k in range(2):
-            wide[f, pl.ds(k * WIDE + 8, tile_p), :] = t_low[f, k] * has_t[0]
-            wide[f, pl.ds((tile_t + 2 + k) * WIDE + 8, tile_p), :] = t_high[f, k] * has_t[1]
-        for side, (halo, near, far) in enumerate(((p_low, 7, 6), (p_high, 8 + tile_p, 9 + tile_p))):
+            for side, t in enumerate((k, tile_t + 2 + k)):
+                wide[f, pl.ds(t * WIDE + 8, tile_p), :] = blend(
+                    by_t[side], t_first[f, k], t_second[f, k]
+                )
+        for side, (near, far) in enumerate(((7, 6), (8 + tile_p, 9 + tile_p))):
             for k, col in enumerate((near, far)):
-                cells = halo[f, k * tile_t : (k + 1) * tile_t, :] * has_p[side]
+                rows = slice(k * tile_t, (k + 1) * tile_t)
+                cells = blend(by_p[side], p_first[f, rows, :], p_second[f, rows, :])
                 wide[f, pl.ds(2 * WIDE + col, tile_t, stride=WIDE), :] = cells
             for t in (1, tile_t + 2):
                 wide[f, pl.ds(t * WIDE + near, 1), :] = nothing
@@ -252,12 +284,12 @@
 
 
 def route(
-    n_dev, kappa, p_low, p_high, own_low, own_high, c_low, c_high, stepped, rank, meta, hit,
+    n_dev, kappa, p_first, p_second, own_low, own_high, c_first, c_second, stepped, rank, meta, hit,
     table_high, table_low, w_r, patch, message, shell,
 ):
     fields, columns, radial = stepped.shape
     tile_t, tile_p, _ = kappa.shape
-    has_t, has_p = exists()
+    sides_p = sides("lon")
     lane = iota((columns, radial), 1)
     rows = jnp.zeros((columns, radial), F32)
     for f in range(fields):
@@ -265,15 +297,17 @@
         rows = jnp.where(lane // SH == f, moved, rows)
     shell[...] = rows
     for a in range(2):
-        for b, (halo, own, diagonal) in enumerate(
-            ((p_low, own_low, c_low), (p_high, own_high, c_high))
-        ):
+        for b, own in enumerate((own_low, own_high)):
             t, p = a * (tile_t - 1), b * (tile_p - 1)
-            k_t, u_t = own[a, fields : fields + 1] * has_t[a], own[a, 0:fields] * has_t[a]
-            k_p = halo[fields, t : t + 1, :] * has_p[b]
-            u_p = jnp.concatenate([halo[f, t : t + 1, :] for f in range(fields)], axis=0) * has_p[b]
-            both = has_t[a] * has_p[b]
-            k_d, u_d = diagonal[a, fields : fields + 1] * both, diagonal[a, 0:fields] * both
+
+            def beside(f, t=t, weights=sides_p[b]):
+                return blend(weights, p_first[f, t : t + 1, :], p_second[f, t : t + 1, :])
+
+            k_t, u_t = own[a, fields : fields + 1], own[a, 0:fields]
+            k_p = beside(fields)
+            u_p = jnp.concatenate([beside(f) for f in range(fields)], axis=0)
+            diagonal = blend(sides_p[b], c_first[a], c_second[a])
+            k_d, u_d = diagonal[fields : fields + 1], diagonal[0:fields]
             k = kappa[t, p : p + 1, :]
             by_t = 0.075 * ((k_t + k_d) * u_d - k_d * u_t)
             by_p = 0.075 * ((k_p + k_d) * u_d - k_d * u_p)
@@ -326,7 +360,7 @@
                 )
 
 
-def land(n_dev, got, prev, coupled, p_first, p_last, t_first, t_last):
+def land(n_dev, got, prev, coupled, p_first, p_second, t_first, t_second):
     fields, face_p, face_t = prev.shape
     values = jnp.transpose(got[pl.ds(0, n_dev, stride=2), :])
     cells = jnp.transpose(got[pl.ds(1, n_dev, stride=2), :])
@@ -350,37 +384,38 @@
             preferred_element_type=F32,
         )
     new = prev[...].reshape(rows, face_t) + (total[:rows] + total[rows:])
+
+    def edge(face, p):
+        at = [f * face_p + p for f in range(fields)]
+        return jnp.concatenate([face[k : k + 1, :] for k in at], axis=0)
+
     coupled[...] = new.reshape(fields, face_p, face_t)
     turned = jnp.transpose(new)
-    t_first[...] = turned[0:1, :]
-    t_last[...] = turned[face_t - 1 : face_t, :]
-    for f in range(fields):
-        p_first[f : f + 1, :] = new[f * face_p : f * face_p + 1, :]
-        p_last[f : f + 1, :] = new[(f + 1) * face_p - 1 : (f + 1) * face_p, :]
-
-
-def smooth(coupled, p_low, p_high, t_low, t_high, out):
+    for axis, low, high, first, second in (
+        ("lat", turned[0:1, :], turned[face_t - 1 : face_t, :], t_first, t_second),
+        ("lon", edge(new, 0), edge(new, face_p - 1), p_first, p_second),
+    ):
+        odd = parity(axis).astype(F32)
+        first[...] = blend((odd, 1.0 - odd), low, high)
+        second[...] = blend((1.0 - odd, odd), low, high)
+
+
+def smooth(coupled, p_first, p_second, t_first, t_second, out):
     fields, face_p, face_t = coupled.shape
     x = coupled[...]
     row = iota((face_p, face_t), 0)[None]
     lane = iota((face_p, face_t), 1)[None]
 
-    has_t, has_p = exists()
-
-    def rim(ref, has):
-        return ref[...] * has
+    t_low, t_high = [blend(w, t_first[...], t_second[...]) for w in sides("lat")]
+    p_low, p_high = [blend(w, p_first[...], p_second[...]) for w in sides("lon")]
 
     def column(edge):
         return jnp.transpose(jnp.broadcast_to(edge, (face_t, fields * face_p))).reshape(x.shape)
 
-    below = jnp.where(row == 0, rim(p_low, has_p[0])[:, None, :], pltpu.roll(x, 1, 1))
-    above = jnp.where(
-        row == face_p - 1, rim(p_high, has_p[1])[:, None, :], pltpu.roll(x, face_p - 1, 1)
-    )
-    left = jnp.where(lane == 0, column(rim(t_low, has_t[0])), pltpu.roll(x, 1, 2))
-    right = jnp.where(
-        lane == face_t - 1, column(rim(t_high, has_t[1])), pltpu.roll(x, face_t - 1, 2)
-    )
+    below = jnp.where(row == 0, p_low[:, None, :], pltpu.roll(x, 1, 1))
+    above = jnp.where(row == face_p - 1, p_high[:, None, :], pltpu.roll(x, face_p - 1, 1))
+    left = jnp.where(lane == 0, column(t_low), pltpu.roll(x, 1, 2))
+    right = jnp.where(lane == face_t - 1, column(t_high), pltpu.roll(x, face_t - 1, 2))
     out[...] = x + 0.2 * (above + below + right + left - 4.0 * x)
 
 
@@ -407,7 +442,7 @@
     dest_cell = dest_cell.reshape(1, count)
     base = corner_base.reshape(1, count)
     edge = (fields + 1, 2, tile_p, radial)
-    low, high = call(
+    first, second = call(
         theta_edges,
         [edge] * 2,
         [pl.BlockSpec(memory_space=pltpu.HBM)] * 2,
@@ -415,15 +450,13 @@
         [pltpu.SemaphoreType.DMA((4,))],
         room=58 * 1024 * 1024,
     )(corona, kappa)
-    t_low = shifted(high, "lat", 1)
-    t_high = shifted(low, "lat", -1)
+    t_first, t_second = swapped(first, second, "lat")
 
     edge = (fields + 1, 2 * tile_t, radial)
-    low, high = call(
+    first, second = call(
         functools.partial(phi_edges, tile_t, tile_p), [edge] * 2, [vspec()] * 2, "phi_edges"
     )(corona.reshape(fields, tile_t * tile_p, radial), kappa.reshape(tile_t * tile_p, radial))
-    p_low = shifted(high, "lon", 1)
-    p_high = shifted(low, "lon", -1)
+    p_first, p_second = swapped(first, second, "lon")
 
     table = jax.ShapeDtypeStruct((tile_t * tile_p, count), BF16)
     rank, meta, hit, table_high, table_low, w_r = call(
@@ -434,12 +467,11 @@
         "plan",
     )(owner, dest_cell, base, fractions)
 
-    t_low, t_high, rank = lax.optimization_barrier((t_low, t_high, rank))
-    own_low, own_high = call(
-        corner_cells, [(2, fields + 1, radial)] * 2, [vspec()] * 2, "corner_cells"
-    )(t_low, t_high)
-    c_low = shifted(own_high, "lon", 1)
-    c_high = shifted(own_low, "lon", -1)
+    t_first, t_second, rank = lax.optimization_barrier((t_first, t_second, rank))
+    own_low, own_high, first, second = call(
+        corner_cells, [(2, fields + 1, radial)] * 4, [vspec()] * 2, "corner_cells"
+    )(t_first, t_second)
+    c_first, c_second = swapped(first, second, "lon")
 
     flat = (fields, tile_t * tile_p, radial)
     (almost,) = call(
@@ -452,7 +484,7 @@
             VMEM((fields, (tile_t + 2) * WIDE, radial), F32),
             VMEM((fields * fields, 8, radial), F32),
         ],
-    )(mixing, corona, kappa, t_low, t_high, p_low, p_high)
+    )(mixing, corona, kappa, t_first, t_second, p_first, p_second)
     almost = almost.reshape(flat)
 
     patch, message = call(
@@ -462,8 +494,8 @@
         "route",
         [VMEM((tile_t * tile_p, radial), F32)],
     )(
-        kappa, p_low, p_high, own_low, own_high, c_low, c_high, almost, rank, meta, hit, table_high,
-        table_low, w_r,
+        kappa, p_first, p_second, own_low, own_high, c_first, c_second, almost, rank, meta, hit,
+        table_high, table_low, w_r,
     )
     (stepped,) = call(
         functools.partial(finish, tile_t, tile_p), [flat], [vspec()] * 2, "finish"
@@ -471,18 +503,16 @@
 
     got = lax.all_to_all(message, ("lat", "lon"), split_axis=0, concat_axis=0, tiled=True)
 
-    coupled, p_first, p_last, t_first, t_last = call(
+    coupled, p_first, p_second, t_first, t_second = call(
         functools.partial(land, n_dev),
         [helio_prev.shape, (fields, face_t), (fields, face_t)] + [(1, fields * face_p)] * 2,
         [vspec()] * 2,
         "land",
     )(got, helio_prev)
-    from_t_low = shifted(t_last, "lat", 1)
-    from_t_high = shifted(t_first, "lat", -1)
-    from_p_low = shifted(p_last, "lon", 1)
-    from_p_high = shifted(p_first, "lon", -1)
+    p_first, p_second = swapped(p_first, p_second, "lon")
+    t_first, t_second = swapped(t_first, t_second, "lat")
     (face,) = call(smooth, [helio_prev.shape], [vspec()] * 5, "smooth")(
-        coupled, from_p_low, from_p_high, from_t_low, from_t_high
+        coupled, p_first, p_second, t_first, t_second
     )
     return (stepped.reshape(corona.shape), face)
 

time: 61.9 us -> 58.4 us (0.943); the launches traced: 60.8 us -> 58.2 us
  starting transfers between devices: 21 us -> 15.2 us
  waiting for transfers between devices: 0.51 us -> 4.08 us
    ppermute x10, starting transfers between devices: 21 us -> 15.2 us  [the longest x5 11.9 us: swapped(): lax.ppermute(second, axis, list(enumerate(other)))]
    ppermute x10, waiting for transfers between devices: 0.51 us -> 4.08 us  [the longest x5 2.62 us: swapped(): lax.ppermute(second, axis, list(enumerate(other)))]
  transfers between devices with their start and end apart: 10 -> 10, of which waited for: 1 -> 3; matrix products, arithmetic and copies ran while one was open for 0% -> 0% of each run, Pallas kernels for 12% -> 13%
where the time goes in v7:
time: 58.4 us; the launch traced here: 58.2 us
  blocking collectives  24.9 us (43%)
  starting transfers between devices  15.2 us (26%)
  Pallas kernels  13.2 us (23%)
  waiting for transfers between devices  4.08 us (7%)
  between operations  0.8 us (1%)
    all_to_all x1, blocking collectives, body(): lax.all_to_all(message, ('lat', 'lon'), split_axis=0, concat_axis=0, tile...  24.9 us
    ppermute x5, starting transfers between devices, swapped(): lax.ppermute(second, axis, list(enumerate(other)))  11.9 us
    pallas_call x1, Pallas kernels, body(): call(steps, [corona.shape], [sspec()] + [vspec()] * 6, 'steps', [VMEM((fi...  4.14 us
    ppermute x5, starting transfers between devices, swapped(): lax.ppermute(first, axis, [(i, i ^ 1) for i in range(count)])  3.34 us
    ppermute x5, waiting for transfers between devices, swapped(): lax.ppermute(second, axis, list(enumerate(other)))  2.62 us
    pallas_call x1, Pallas kernels, body(): call(functools.partial(plan, face_t, tile_t, tile_p), [(1, count), (n_dev...  2.05 us
    pallas_call x1, Pallas kernels, body(): call(theta_edges, [edge] * 2, [pl.BlockSpec(memory_space=pltpu.HBM)] * 2,...  1.83 us
    pallas_call x1, Pallas kernels, body(): call(functools.partial(route, n_dev), [(4, fields, radial), (2 * n_dev, 1...  1.67 us
  transfers between devices with their start and end apart: 10, of which 3 were waited for; matrix products, arithmetic and copies ran while one was open for 0% of the time, Pallas kernels for 13%

profile of v7, /device:TPU:8, one launch (start us, length us, event | category | flops | bytes accessed | tf_op | source)
XLA Modules:
  0.0 58.2 jit_solution(8191440566024545936)
XLA Ops:
  0.6 0.0 copy-start.1
  0.6 0.0 copy-start
  0.6 1.8 %theta_edges.1 = (f32[9,2,16,128]{3,2,1,0:T(8,128)}, f32[9,2,16,128]{3,2,1,0:T(8,128)}) custom-call(f32[8,16,16,128]{3,2,1,0:T(8,128)} %corona.3, f32[16,16,128]{2,1,0:T(8,128)} %kappa.5), custom_call_target="tpu_custom_call" | custom-call | tf_op jit(solution)/shard_map/theta_edges/pallas_call | solution.py:445
  2.5 2.0 %collective-permute-start = (f32[9,2,16,128]{3,2,1,0:T(8,128)}, f32[9,2,16,128]{3,2,1,0:T(8,128)S(1)}, u32[]{:S(2)}, u32[]{:S(2)}) collective-permute-start(f32[9,2,16,128]{3,2,1,0:T(8,128)} %get-tuple-element.26), channel_id=1, source_target_pairs={{0,32},{32,0},{64,96},{96,64},{128,160},{160,128},{192,224},{224,1... | collective-permute-start | bytes 442376 | tf_op jit(solution)/shard_map/ppermute | solution.py:40
  4.5 4.9 %collective-permute-start.1 = (f32[9,2,16,128]{3,2,1,0:T(8,128)}, f32[9,2,16,128]{3,2,1,0:T(8,128)S(1)}, u32[]{:S(2)}, u32[]{:S(2)}) collective-permute-start(f32[9,2,16,128]{3,2,1,0:T(8,128)} %get-tuple-element.27), channel_id=1, source_target_pairs={{0,224},{32,64},{64,32},{96,128},{128,96},{160,192},{192,160},{224... | collective-permute-start | bytes 442376 | tf_op jit(solution)/shard_map/ppermute | solution.py:41
  9.4 0.0 copy-done.1
  9.4 0.0 copy-done
  9.4 0.0 copy-start.3
  9.4 0.0 copy-start.5
  9.4 0.0 copy-start.6
  9.5 0.1 phi_edges.1
  9.6 0.0 copy-start.4
  9.6 0.1 collective-permute-start.2
  9.7 2.7 %collective-permute-start.3 = (f32[9,32,128]{2,1,0:T(8,128)S(1)}, f32[9,32,128]{2,1,0:T(8,128)S(1)}, u32[]{:S(2)}, u32[]{:S(2)}) collective-permute-start(f32[9,32,128]{2,1,0:T(8,128)S(1)} %get-tuple-element.32), channel_id=1, source_target_pairs={{0,31},{1,2},{2,1},{3,4},{4,3},{5,6},{6,5},{7,8},{8,7},{9,10},{10,... | collective-permute-start | bytes 442376 | tf_op jit(solution)/shard_map/ppermute | solution.py:41
  12.4 0.0 copy-done.3
  12.4 0.0 copy-done.5
  12.4 0.0 copy-done.6
  12.4 0.0 copy-done.4
  12.4 2.1 %plan.1 = (f32[1,2048]{1,0:T(1,128)S(1)}, f32[256,128]{1,0:T(8,128)S(1)}, bf16[256,2048]{1,0:T(8,128)(2,1)S(1)}, bf16[256,2048]{1,0:T(8,128)(2,1)S(1)}, bf16[256...) custom-call(s32[1,2048]{1,0:T(1,128)S(1)} %bitcast.15, s32[1,2048]{1,0:T(1,128)S(1)} %bitcast.16, s32[1,2048]{1,0:T(1,128)S(1)} %bitcast.17, ...), custom_call_target="tpu_custom_call" | custom-call | tf_op jit(solution)/shard_map/plan/pallas_call | solution.py:462
  14.5 0.0 collective-permute-done.t_first
  14.5 0.0 collective-permute-done.1.t_second
  14.5 0.0 copy-start.7
  14.6 0.1 collective-permute-start.4
  14.7 1.4 %collective-permute-start.5 = (f32[2,9,128]{2,1,0:T(8,128)S(1)}, f32[2,9,128]{2,1,0:T(8,128)S(1)}, u32[]{:S(2)}, u32[]{:S(2)}) collective-permute-start(f32[2,9,128]{2,1,0:T(8,128)S(1)} %get-tuple-element.36), channel_id=1, source_target_pairs={{0,31},{1,2},{2,1},{3,4},{4,3},{5,6},{6,5},{7,8},{8,7},{9,10},{10,... | collective-permute-start | bytes 27656 | tf_op jit(solution)/shard_map/ppermute | solution.py:41
  16.1 0.0 collective-permute-done.2.p_first
  16.1 0.3 collective-permute-done.3.p_second
  16.5 0.0 copy-done.7
  16.5 4.1 %steps.1 = f32[8,16,16,128]{3,2,1,0:T(8,128)S(1)} custom-call(f32[8,8]{1,0:T(8,128)S(1)} %copy-done.7, f32[8,16,16,128]{3,2,1,0:T(8,128)S(1)} %copy-done, f32[16,16,128]{2,1,0:T(8,128)S(1)} %copy-done.1, f32[9,2,16,128]{3,2,1,0:T(8,128)S(1)} %collective-permute-done.t_first, f32[9,2,16,128]{3,2,1,0:T(8,128)S(1)} %collective-permute-done.1.t_second, ...), custom_call_target="tpu_custom_call" | custom-call | tf_op jit(solution)/shard_map/steps/pallas_call | solution.py:477
  20.6 0.0 collective-permute-done.4.c_first
  20.6 0.0 collective-permute-done.5.c_second
  20.6 1.7 %route.1 = (f32[4,8,128]{2,1,0:T(8,128)S(1)}, f32[512,128]{1,0:T(8,128)S(1)}) custom-call(f32[16,16,128]{2,1,0:T(8,128)S(1)} %copy-done.1, f32[9,32,128]{2,1,0:T(8,128)S(1)} %collective-permute-done.2.p_first, f32[9,32,128]{2,1,0:T(8,128)S(1)} %collective-permute-done.3.p_second, f32[2,9,128]{2,1,0:T(8,128)S(1)} %get-tuple-element.33.own_low, ...), custom_call_target="tpu_custom_call" | custom-call | tf_op jit(solution)/shard_map/route/pallas_call | solution.py:490
  22.3 0.0 copy-start.2
  22.3 24.9 %all_to_all.11 = f32[256,2,128]{2,1,0:T(2,128)S(1)} all-to-all(f32[256,2,128]{2,1,0:T(2,128)S(1)} %bitcast.14), channel_id=1, replica_groups=mesh['lat'=8,'lon'=32] {'lat','lon'}, dimensions={0} | all-to-all | bytes 524288 | tf_op jit(solution)/shard_map/all_to_all | solution.py:504
  47.2 0.0 copy-done.2
  47.3 1.4 %land.1 = (f32[8,32,128]{2,1,0:T(8,128)S(1)}, f32[8,128]{1,0:T(8,128)S(1)}, f32[8,128]{1,0:T(8,128)S(1)}, f32[1,256]{1,0:T(1,128)S(1)}, f32[1,256]{1,0:T(1,128)S(1)}) custom-call(f32[512,128]{1,0:T(8,128)S(1)} %bitcast.13, f32[8,32,128]{2,1,0:T(8,128)S(1)} %copy-done.2), custom_call_target="tpu_custom_call" | custom-call | tf_op jit(solution)/shard_map/land/pallas_call | solution.py:506
  48.6 0.1 collective-permute-start.6
  48.7 2.8 %collective-permute-start.7 = (f32[8,128]{1,0:T(8,128)S(1)}, f32[8,128]{1,0:T(8,128)S(1)}, u32[]{:S(2)}, u32[]{:S(2)}) collective-permute-start(f32[8,128]{1,0:T(8,128)S(1)} %get-tuple-element.47), channel_id=1, source_target_pairs={{0,31},{1,2},{2,1},{3,4},{4,3},{5,6},{6,5},{7,8},{8,7},{9,10},{10,... | collective-permute-start | bytes 12296 | tf_op jit(solution)/shard_map/ppermute | solution.py:41
  51.5 1.1 %collective-permute-start.8 = (f32[1,256]{1,0:T(1,128)S(1)}, f32[1,256]{1,0:T(1,128)S(1)}, u32[]{:S(2)}, u32[]{:S(2)}) collective-permute-start(f32[1,256]{1,0:T(1,128)S(1)} %get-tuple-element.48), channel_id=1, source_target_pairs={{0,32},{32,0},{64,96},{96,64},{128,160},{160,128},{192,224},{224,1... | collective-permute-start | bytes 3080 | tf_op jit(solution)/shard_map/ppermute | solution.py:40
  52.6 0.0 collective-permute-start.9
  52.6 1.1 %finish.1 = f32[8,256,128]{2,1,0:T(8,128)} custom-call(f32[8,256,128]{2,1,0:T(8,128)S(1)} %bitcast.10, f32[4,8,128]{2,1,0:T(8,128)S(1)} %get-tuple-element.43.patch), custom_call_target="tpu_custom_call" | custom-call | tf_op jit(solution)/shard_map/finish/pallas_call | solution.py:500
  53.6 1.5 %collective-permute-done.8.t_first = f32[1,256]{1,0:T(1,128)S(1)} collective-permute-done((f32[1,256]{1,0:T(1,128)S(1)}, f32[1,256]{1,0:T(1,128)S(1)}, u32[]{:S(2)}, u32[]{:S(2)}) %collective-permute-start.8) | collective-permute-done | bytes 1056 | tf_op jit(solution)/shard_map/ppermute | solution.py:40
  55.1 2.3 %collective-permute-done.9.t_second = f32[1,256]{1,0:T(1,128)S(1)} collective-permute-done((f32[1,256]{1,0:T(1,128)S(1)}, f32[1,256]{1,0:T(1,128)S(1)}, u32[]{:S(2)}, u32[]{:S(2)}) %collective-permute-start.9) | collective-permute-done | bytes 1056 | tf_op jit(solution)/shard_map/ppermute | solution.py:41
  57.3 0.0 collective-permute-done.6.p_first
  57.3 0.0 collective-permute-done.7.p_second
  57.3 0.9 %smooth.1 = f32[8,32,128]{2,1,0:T(8,128)} custom-call(f32[8,32,128]{2,1,0:T(8,128)S(1)} %get-tuple-element.45.coupled, f32[8,128]{1,0:T(8,128)S(1)} %collective-permute-done.6.p_first, f32[8,128]{1,0:T(8,128)S(1)} %collective-permute-done.7.p_second, f32[1,256]{1,0:T(1,128)S(1)} %collective-permute-done.8.t_first, f32[1,256]{1,0:T(1,128)S(1)} %collective-permute-done.9.t_second), custom_call_target="tpu_custom_call" | custom-call | tf_op jit(solution)/shard_map/smooth/pallas_call | solution.py:514
  (1 shorter events, 0.0 us)
Async XLA Ops:
  0.6 8.8 %copy-start.1 = (f32[16,16,128]{2,1,0:T(8,128)S(1)}, f32[16,16,128]{2,1,0:T(8,128)}, u32[]{:S(2)}) copy-start(f32[16,16,128]{2,1,0:T(8,128)} %kappa.5) | copy-start | bytes 393220
  0.6 8.8 %copy-start = (f32[8,16,16,128]{3,2,1,0:T(8,128)S(1)}, f32[8,16,16,128]{3,2,1,0:T(8,128)}, u32[]{:S(2)}) copy-start(f32[8,16,16,128]{3,2,1,0:T(8,128)} %corona.3) | copy-start | bytes 3145732
  2.5 12.0 %collective-permute-start = (f32[9,2,16,128]{3,2,1,0:T(8,128)}, f32[9,2,16,128]{3,2,1,0:T(8,128)S(1)}, u32[]{:S(2)}, u32[]{:S(2)}) collective-permute-start(f32[9,2,16,128]{3,2,1,0:T(8,128)} %get-tuple-element.26), channel_id=1, source_target_pairs={{0,32},{32,0},{64,96},{96,64},{128,160},{160,128},{192,224},{224,1... | collective-permute-start | bytes 442376 | tf_op jit(solution)/shard_map/ppermute | solution.py:40
  4.5 10.0 %collective-permute-start.1 = (f32[9,2,16,128]{3,2,1,0:T(8,128)}, f32[9,2,16,128]{3,2,1,0:T(8,128)S(1)}, u32[]{:S(2)}, u32[]{:S(2)}) collective-permute-start(f32[9,2,16,128]{3,2,1,0:T(8,128)} %get-tuple-element.27), channel_id=1, source_target_pairs={{0,224},{32,64},{64,32},{96,128},{128,96},{160,192},{192,160},{224... | collective-permute-start | bytes 442376 | tf_op jit(solution)/shard_map/ppermute | solution.py:41
  9.4 3.0 %copy-start.3 = (f32[3,2048]{1,0:T(4,128)S(1)}, f32[3,2048]{1,0:T(4,128)}, u32[]{:S(2)}) copy-start(f32[3,2048]{1,0:T(4,128)} %frac.1) | copy-start | bytes 73732
  9.4 3.0 %copy-start.5 = (s32[2048]{0:T(1024)S(1)}, s32[2048]{0:T(1024)}, u32[]{:S(2)}) copy-start(s32[2048]{0:T(1024)} %param.13) | copy-start | bytes 24580
  9.4 3.0 %copy-start.6 = (s32[2048]{0:T(1024)S(1)}, s32[2048]{0:T(1024)}, u32[]{:S(2)}) copy-start(s32[2048]{0:T(1024)} %param.14) | copy-start | bytes 24580
  9.6 2.9 %copy-start.4 = (s32[2048,1]{0,1:T(1,128)S(1)}, s32[2048,1]{0,1:T(1,128)}, u32[]{:S(2)}) copy-start(s32[2048,1]{0,1:T(1,128)} %param.12) | copy-start | bytes 24580
  9.6 6.5 %collective-permute-start.2 = (f32[9,32,128]{2,1,0:T(8,128)S(1)}, f32[9,32,128]{2,1,0:T(8,128)S(1)}, u32[]{:S(2)}, u32[]{:S(2)}) collective-permute-start(f32[9,32,128]{2,1,0:T(8,128)S(1)} %get-tuple-element.31), channel_id=1, source_target_pairs={{0,1},{1,0},{2,3},{3,2},{4,5},{5,4},{6,7},{7,6},{8,9},{9,8},{10,11... | collective-permute-start | bytes 442376 | tf_op jit(solution)/shard_map/ppermute | solution.py:40
  9.7 6.8 %collective-permute-start.3 = (f32[9,32,128]{2,1,0:T(8,128)S(1)}, f32[9,32,128]{2,1,0:T(8,128)S(1)}, u32[]{:S(2)}, u32[]{:S(2)}) collective-permute-start(f32[9,32,128]{2,1,0:T(8,128)S(1)} %get-tuple-element.32), channel_id=1, source_target_pairs={{0,31},{1,2},{2,1},{3,4},{4,3},{5,6},{6,5},{7,8},{8,7},{9,10},{10,... | collective-permute-start | bytes 442376 | tf_op jit(solution)/shard_map/ppermute | solution.py:41
  14.5 1.9 %copy-start.7 = (f32[8,8]{1,0:T(8,128)S(1)}, f32[8,8]{1,0:T(8,128)}, u32[]{:S(2)}) copy-start(f32[8,8]{1,0:T(8,128)} %mixing.1) | copy-start | bytes 772
  14.6 6.0 %collective-permute-start.4 = (f32[2,9,128]{2,1,0:T(8,128)S(1)}, f32[2,9,128]{2,1,0:T(8,128)S(1)}, u32[]{:S(2)}, u32[]{:S(2)}) collective-permute-start(f32[2,9,128]{2,1,0:T(8,128)S(1)} %get-tuple-element.35), channel_id=1, source_target_pairs={{0,1},{1,0},{2,3},{3,2},{4,5},{5,4},{6,7},{7,6},{8,9},{9,8},{10,11... | collective-permute-start | bytes 27656 | tf_op jit(solution)/shard_map/ppermute | solution.py:40
  14.7 5.9 %collective-permute-start.5 = (f32[2,9,128]{2,1,0:T(8,128)S(1)}, f32[2,9,128]{2,1,0:T(8,128)S(1)}, u32[]{:S(2)}, u32[]{:S(2)}) collective-permute-start(f32[2,9,128]{2,1,0:T(8,128)S(1)} %get-tuple-element.36), channel_id=1, source_target_pairs={{0,31},{1,2},{2,1},{3,4},{4,3},{5,6},{6,5},{7,8},{8,7},{9,10},{10,... | collective-permute-start | bytes 27656 | tf_op jit(solution)/shard_map/ppermute | solution.py:41
  22.3 25.0 %copy-start.2 = (f32[8,32,128]{2,1,0:T(8,128)S(1)}, f32[8,32,128]{2,1,0:T(8,128)}, u32[]{:S(2)}) copy-start(f32[8,32,128]{2,1,0:T(8,128)} %prev.1) | copy-start | bytes 393220
  48.6 8.7 %collective-permute-start.6 = (f32[8,128]{1,0:T(8,128)S(1)}, f32[8,128]{1,0:T(8,128)S(1)}, u32[]{:S(2)}, u32[]{:S(2)}) collective-permute-start(f32[8,128]{1,0:T(8,128)S(1)} %get-tuple-element.46), channel_id=1, source_target_pairs={{0,1},{1,0},{2,3},{3,2},{4,5},{5,4},{6,7},{7,6},{8,9},{9,8},{10,11... | collective-permute-start | bytes 12296 | tf_op jit(solution)/shard_map/ppermute | solution.py:40
  48.7 8.6 %collective-permute-start.7 = (f32[8,128]{1,0:T(8,128)S(1)}, f32[8,128]{1,0:T(8,128)S(1)}, u32[]{:S(2)}, u32[]{:S(2)}) collective-permute-start(f32[8,128]{1,0:T(8,128)S(1)} %get-tuple-element.47), channel_id=1, source_target_pairs={{0,31},{1,2},{2,1},{3,4},{4,3},{5,6},{6,5},{7,8},{8,7},{9,10},{10,... | collective-permute-start | bytes 12296 | tf_op jit(solution)/shard_map/ppermute | solution.py:41
  51.5 3.6 %collective-permute-start.8 = (f32[1,256]{1,0:T(1,128)S(1)}, f32[1,256]{1,0:T(1,128)S(1)}, u32[]{:S(2)}, u32[]{:S(2)}) collective-permute-start(f32[1,256]{1,0:T(1,128)S(1)} %get-tuple-element.48), channel_id=1, source_target_pairs={{0,32},{32,0},{64,96},{96,64},{128,160},{160,128},{192,224},{224,1... | collective-permute-start | bytes 3080 | tf_op jit(solution)/shard_map/ppermute | solution.py:40
  52.6 4.8 %collective-permute-start.9 = (f32[1,256]{1,0:T(1,128)S(1)}, f32[1,256]{1,0:T(1,128)S(1)}, u32[]{:S(2)}, u32[]{:S(2)}) collective-permute-start(f32[1,256]{1,0:T(1,128)S(1)} %get-tuple-element.49), channel_id=1, source_target_pairs={{0,224},{32,64},{64,32},{96,128},{128,96},{160,192},{192,160},{224... | collective-permute-start | bytes 3080 | tf_op jit(solution)/shard_map/ppermute | solution.py:41

commit v8 on v7

--- a/solution.py
+++ b/solution.py
@@ -76,37 +76,25 @@
         copy.wait()
 
 
-def phi_edges(tile_t, tile_p, corona, kappa, first, second):
+def phi_edges(tile_t, tile_p, corona, kappa, t_first, t_second, first, second):
     fields = corona.shape[0]
     odd = parity("lon")
+    weights = sides("lat")
     for out, upper in ((first, 1 - odd), (second, odd)):
         near = upper * (tile_p - 1)
         far = upper * (tile_p - 3) + 1
+        cell = pl.ds(near, 1)
         for f in range(fields + 1):
             for at, col in ((0, near), (tile_t, far)):
                 rows = pl.ds(col, tile_t, stride=tile_p)
                 out[f, at : at + tile_t, :] = corona[f, rows, :] if f < fields else kappa[rows, :]
-
-
-def corner_cells(t_first, t_second, low, high, first, second):
-    count, _, tile_p, _ = t_first.shape
-    weights = sides("lat")
-    for a, row in ((0, 1), (1, 0)):
-        for f in range(count):
-            for out, col in ((low, 0), (high, tile_p - 1)):
-                cell = slice(col, col + 1)
-                out[a, f : f + 1, :] = blend(
+            for a, row in ((0, 1), (1, 0)):
+                out[f, 2 * tile_t + a : 2 * tile_t + a + 1, :] = blend(
                     weights[a], t_first[f, row, cell, :], t_second[f, row, cell, :]
                 )
-    odd = parity("lon").astype(F32)
-    first[...] = blend((odd, 1.0 - odd), low[...], high[...])
-    second[...] = blend((1.0 - odd, odd), low[...], high[...])
-
-
-def plan(
-    face_t, tile_t, tile_p, owner, dest, base, frac, rank_out, meta_out, hit_out, high_out, low_out,
-    radial_out,
-):
+
+
+def ranks(face_t, owner, dest, rank_out, meta_out, hit_out):
     n_dev = meta_out.shape[0]
     count = owner.shape[1]
     width = min(BLOCK, count)
@@ -140,6 +128,14 @@
         meta = meta + lax.dot_general(
             hit_b, rows, (((1,), (1,)), ((), ())), preferred_element_type=F32
         )
+    meta_out[...] = meta
+
+
+def tables(tile_t, tile_p, base, frac, high_out, low_out, radial_out):
+    count = base.shape[1]
+    width = min(BLOCK, count)
+    for b in range(count // width):
+        cols = slice(b * width, (b + 1) * width)
         corner = base[:, cols]
 
         def pair(size, at, fraction):
@@ -151,7 +147,6 @@
         radial_out[:, cols] = pair(SH, corner % SH, frac[2:3, cols])
         table = (w_t[:, None, :] * w_p[None, :, :]).reshape(tile_t * tile_p, width)
         high_out[:, cols], low_out[:, cols] = halves(table)
-    meta_out[...] = meta
 
 
 def spread(mixing, spread_out):
@@ -223,15 +218,15 @@
     )
 
 
-def steps(
-    mixing, corona, kappa, t_first, t_second, p_first, p_second, stepped, wide, once, mix,
+def main(
+    n_dev, mixing, corona, kappa, t_first, t_second, p_first, p_second, rank, meta, hit, table_high,
+    table_low, w_r, out, message, stepped, wide, once, mix, sem,
 ):
     fields, tile_t, tile_p, radial = corona.shape
     by_t, by_p = sides("lat"), sides("lon")
     has_t = [low + high for low, high in by_t]
     has_p = [low + high for low, high in by_p]
     spread(mixing, mix)
-    nothing = jnp.zeros((1, radial), F32)
     for f in range(fields + 1):
         for t in range(tile_t):
             own = corona[f, t] if f < fields else kappa[t]
@@ -246,8 +241,11 @@
                 rows = slice(k * tile_t, (k + 1) * tile_t)
                 cells = blend(by_p[side], p_first[f, rows, :], p_second[f, rows, :])
                 wide[f, pl.ds(2 * WIDE + col, tile_t, stride=WIDE), :] = cells
-            for t in (1, tile_t + 2):
-                wide[f, pl.ds(t * WIDE + near, 1), :] = nothing
+            for a, t in enumerate((1, tile_t + 2)):
+                row = slice(2 * tile_t + a, 2 * tile_t + a + 1)
+                wide[f, pl.ds(t * WIDE + near, 1), :] = blend(
+                    by_p[side], p_first[f, row, :], p_second[f, row, :]
+                )
 
     def first(t):
         for g, acc in row_flux(mix, wide, wide, t + 2, t + 2, tile_p, fields):
@@ -268,58 +266,14 @@
     for row in (first, second):
         by_rows(row, tile_t)
 
-
-def by_rows(row, count):
-    if UNROLL >= count:
-        for t in range(count):
-            row(t)
-        return
-
-    def some(i, carry):
-        for k in range(UNROLL):
-            row(i * UNROLL + k)
-        return carry
-
-    lax.fori_loop(0, count // UNROLL, some, 0)
-
-
-def route(
-    n_dev, kappa, p_first, p_second, own_low, own_high, c_first, c_second, stepped, rank, meta, hit,
-    table_high, table_low, w_r, patch, message, shell,
-):
-    fields, columns, radial = stepped.shape
-    tile_t, tile_p, _ = kappa.shape
-    sides_p = sides("lon")
+    copy = pltpu.make_async_copy(stepped, out, sem)
+    copy.start()
+    columns = tile_t * tile_p
     lane = iota((columns, radial), 1)
     rows = jnp.zeros((columns, radial), F32)
     for f in range(fields):
-        moved = pltpu.roll(stepped[f], (f * SH + SH) % radial, 1)
+        moved = pltpu.roll(stepped[f].reshape(columns, radial), (f * SH + SH) % radial, 1)
         rows = jnp.where(lane // SH == f, moved, rows)
-    shell[...] = rows
-    for a in range(2):
-        for b, own in enumerate((own_low, own_high)):
-            t, p = a * (tile_t - 1), b * (tile_p - 1)
-
-            def beside(f, t=t, weights=sides_p[b]):
-                return blend(weights, p_first[f, t : t + 1, :], p_second[f, t : t + 1, :])
-
-            k_t, u_t = own[a, fields : fields + 1], own[a, 0:fields]
-            k_p = beside(fields)
-            u_p = jnp.concatenate([beside(f) for f in range(fields)], axis=0)
-            diagonal = blend(sides_p[b], c_first[a], c_second[a])
-            k_d, u_d = diagonal[fields : fields + 1], diagonal[0:fields]
-            k = kappa[t, p : p + 1, :]
-            by_t = 0.075 * ((k_t + k_d) * u_d - k_d * u_t)
-            by_p = 0.075 * ((k_p + k_d) * u_d - k_d * u_p)
-            extra = 0.075 * ((k + k_t) * by_t + (k + k_p) * by_p)
-            patch[2 * a + b] = extra
-            row = jnp.zeros((1, radial), F32)
-            for f in range(fields):
-                moved = pltpu.roll(extra[f : f + 1], (f * SH + SH) % radial, 1)
-                row = jnp.where(lane[0:1] // SH == f, moved, row)
-            at = t * tile_p + p
-            shell[at : at + 1, :] = shell[at : at + 1, :] + row
-    rows = shell[...]
     high = rows.astype(BF16).astype(F32)
     both = high + pltpu.roll(rows - high, fields * SH, 1)
     left = jnp.transpose(both).astype(BF16)
@@ -347,17 +301,21 @@
     half = fields * CAP
     message[pl.ds(0, n_dev, stride=2), :] = packed[:, :half] + packed[:, half:]
     message[pl.ds(1, n_dev, stride=2), :] = meta[...]
-
-
-def finish(tile_t, tile_p, stepped, patch, out):
-    out[...] = stepped[...]
-    for a in range(2):
-        for b in range(2):
-            at = a * (tile_t - 1) * tile_p + b * (tile_p - 1)
-            for f in range(stepped.shape[0]):
-                out[f, at : at + 1, :] = (
-                    stepped[f, at : at + 1, :] + patch[2 * a + b, f : f + 1, :]
-                )
+    copy.wait()
+
+
+def by_rows(row, count):
+    if UNROLL >= count:
+        for t in range(count):
+            row(t)
+        return
+
+    def some(i, carry):
+        for k in range(UNROLL):
+            row(i * UNROLL + k)
+        return carry
+
+    lax.fori_loop(0, count // UNROLL, some, 0)
 
 
 def land(n_dev, got, prev, coupled, p_first, p_second, t_first, t_second):
@@ -419,13 +377,13 @@
     out[...] = x + 0.2 * (above + below + right + left - 4.0 * x)
 
 
-def call(kernel, outs, specs, name, scratch=(), room=40 * 1024 * 1024):
+def call(kernel, outs, specs, name, scratch=(), out_specs=None, room=40 * 1024 * 1024):
     outs = [s if isinstance(s, jax.ShapeDtypeStruct) else jax.ShapeDtypeStruct(s, F32) for s in outs]
     return pl.pallas_call(
         kernel,
         out_shape=outs,
         in_specs=specs,
-        out_specs=[vspec()] * len(outs),
+        out_specs=out_specs or [vspec()] * len(outs),
         scratch_shapes=list(scratch),
         name=name,
         compiler_params=pltpu.CompilerParams(vmem_limit_bytes=room),
@@ -452,54 +410,50 @@
     )(corona, kappa)
     t_first, t_second = swapped(first, second, "lat")
 
-    edge = (fields + 1, 2 * tile_t, radial)
+    rank, meta, hit = call(
+        functools.partial(ranks, face_t),
+        [(1, count), (n_dev, 128), jax.ShapeDtypeStruct((n_dev, count), BF16)],
+        [vspec()] * 2,
+        "ranks",
+    )(owner, dest_cell)
+    t_first, t_second, rank = lax.optimization_barrier((t_first, t_second, rank))
+
+    edge = (fields + 1, 2 * tile_t + 8, radial)
     first, second = call(
-        functools.partial(phi_edges, tile_t, tile_p), [edge] * 2, [vspec()] * 2, "phi_edges"
-    )(corona.reshape(fields, tile_t * tile_p, radial), kappa.reshape(tile_t * tile_p, radial))
+        functools.partial(phi_edges, tile_t, tile_p), [edge] * 2, [vspec()] * 4, "phi_edges"
+    )(
+        corona.reshape(fields, tile_t * tile_p, radial),
+        kappa.reshape(tile_t * tile_p, radial),
+        t_first,
+        t_second,
+    )
     p_first, p_second = swapped(first, second, "lon")
 
     table = jax.ShapeDtypeStruct((tile_t * tile_p, count), BF16)
-    rank, meta, hit, table_high, table_low, w_r = call(
-        functools.partial(plan, face_t, tile_t, tile_p),
-        [(1, count), (n_dev, 128), jax.ShapeDtypeStruct((n_dev, count), BF16), table, table]
-        + [(SH, count)],
-        [vspec()] * 4,
-        "plan",
-    )(owner, dest_cell, base, fractions)
-
-    t_first, t_second, rank = lax.optimization_barrier((t_first, t_second, rank))
-    own_low, own_high, first, second = call(
-        corner_cells, [(2, fields + 1, radial)] * 4, [vspec()] * 2, "corner_cells"
-    )(t_first, t_second)
-    c_first, c_second = swapped(first, second, "lon")
-
-    flat = (fields, tile_t * tile_p, radial)
-    (almost,) = call(
-        steps,
-        [corona.shape],
-        [sspec()] + [vspec()] * 6,
-        "steps",
+    table_high, table_low, w_r = call(
+        functools.partial(tables, tile_t, tile_p),
+        [table, table, (SH, count)],
+        [vspec()] * 2,
+        "tables",
+    )(base, fractions)
+
+    stepped, message = call(
+        functools.partial(main, n_dev),
+        [corona.shape, (2 * n_dev, 128)],
+        [sspec()] + [vspec()] * 12,
+        "main",
         [
+            VMEM(corona.shape, F32),
             VMEM((fields + 1, (tile_t + 4) * WIDE, radial), F32),
             VMEM((fields, (tile_t + 2) * WIDE, radial), F32),
             VMEM((fields * fields, 8, radial), F32),
+            pltpu.SemaphoreType.DMA,
         ],
-    )(mixing, corona, kappa, t_first, t_second, p_first, p_second)
-    almost = almost.reshape(flat)
-
-    patch, message = call(
-        functools.partial(route, n_dev),
-        [(4, fields, radial), (2 * n_dev, 128)],
-        [vspec()] * 14,
-        "route",
-        [VMEM((tile_t * tile_p, radial), F32)],
+        [pl.BlockSpec(memory_space=pltpu.HBM), vspec()],
     )(
-        kappa, p_first, p_second, own_low, own_high, c_first, c_second, almost, rank, meta, hit,
-        table_high, table_low, w_r,
-    )
-    (stepped,) = call(
-        functools.partial(finish, tile_t, tile_p), [flat], [vspec()] * 2, "finish"
-    )(almost, patch)
+        mixing, corona, kappa, t_first, t_second, p_first, p_second, rank, meta, hit, table_high,
+        table_low, w_r,
+    )
 
     got = lax.all_to_all(message, ("lat", "lon"), split_axis=0, concat_axis=0, tiled=True)
 
@@ -514,7 +468,7 @@
     (face,) = call(smooth, [helio_prev.shape], [vspec()] * 5, "smooth")(
         coupled, p_first, p_second, t_first, t_second
     )
-    return (stepped.reshape(corona.shape), face)
+    return (stepped, face)
 
 
 def solution(mesh):

time: 58.4 us -> 66.3 us (1.14)
  waiting for transfers between devices: 4.08 us -> 9.7 us
  local copies, waits for them, and re-layouts: 0.04 us -> 2.1 us
  blocking collectives: 24.9 us -> 26.8 us
  starting transfers between devices: 15.2 us -> 13.7 us
    ppermute x5 -> x4, waiting for transfers between devices: 2.62 us -> 7.18 us  [swapped(): lax.ppermute(second, axis, list(enumerate(other)))]
    unnamed x16, local copies, waits for them, and re-layouts: 0.04 us -> 2.1 us
    all_to_all x1, blocking collectives: 24.9 us -> 26.8 us  [body(): lax.all_to_all(message, ('lat', 'lon'), split_axis=0, concat_axis=0, tile...]
    ppermute x5 -> x4, starting transfers between devices: 11.9 us -> 10.5 us  [swapped(): lax.ppermute(second, axis, list(enumerate(other)))]
    ppermute x5 -> x4, waiting for transfers between devices: 1.47 us -> 2.52 us  [swapped(): lax.ppermute(first, axis, [(i, i ^ 1) for i in range(count)])]
    pallas_call x5 -> x3, Pallas kernels: 8.95 us -> 8.65 us  [the longest x1 6.81 us: body(): call(functools.partial(main, n_dev), [corona.shape, (2 * n_dev, 128)], [s...]
    ppermute x5 -> x4, starting transfers between devices: 3.34 us -> 3.24 us  [swapped(): lax.ppermute(first, axis, [(i, i ^ 1) for i in range(count)])]
  transfers between devices with their start and end apart: 10 -> 8, of which waited for: 3 -> 4; matrix products, arithmetic and copies ran while one was open for 0% -> 0% of each run, Pallas kernels for 13% -> 3%
where the time goes in v8:
time: 66.3 us; the launch traced here: 66 us
  blocking collectives  26.8 us (40%)
  starting transfers between devices  13.7 us (21%)
  Pallas kernels  12.9 us (19%)
  waiting for transfers between devices  9.7 us (15%)
  local copies, waits for them, and re-layouts  2.1 us (3%)
  between operations  0.75 us (1%)
    all_to_all x1, blocking collectives, body(): lax.all_to_all(message, ('lat', 'lon'), split_axis=0, concat_axis=0, tile...  26.8 us
    ppermute x4, starting transfers between devices, swapped(): lax.ppermute(second, axis, list(enumerate(other)))  10.5 us
    ppermute x4, waiting for transfers between devices, swapped(): lax.ppermute(second, axis, list(enumerate(other)))  7.18 us
    pallas_call x1, Pallas kernels, body(): call(functools.partial(main, n_dev), [corona.shape, (2 * n_dev, 128)], [s...  6.81 us
    ppermute x4, starting transfers between devices, swapped(): lax.ppermute(first, axis, [(i, i ^ 1) for i in range(count)])  3.24 us
    ppermute x4, waiting for transfers between devices, swapped(): lax.ppermute(first, axis, [(i, i ^ 1) for i in range(count)])  2.52 us
    unnamed x16, local copies, waits for them, and re-layouts  2.1 us
    pallas_call x1, Pallas kernels, body(): call(theta_edges, [edge] * 2, [pl.BlockSpec(memory_space=pltpu.HBM)] * 2,...  1.83 us
  transfers between devices with their start and end apart: 8, of which 4 were waited for; matrix products, arithmetic and copies ran while one was open for 0% of the time, Pallas kernels for 3%

profile of v8, /device:TPU:8, one launch (start us, length us, event | category | flops | bytes accessed | tf_op | source)
XLA Modules:
  0.0 66.0 jit_solution(6375678683994621563)
XLA Ops:
  0.6 0.0 copy-start.1
  0.6 0.0 copy-start
  0.6 1.8 %theta_edges.1 = (f32[9,2,16,128]{3,2,1,0:T(8,128)}, f32[9,2,16,128]{3,2,1,0:T(8,128)}) custom-call(f32[8,16,16,128]{3,2,1,0:T(8,128)} %corona.3, f32[16,16,128]{2,1,0:T(8,128)} %kappa.3), custom_call_target="tpu_custom_call" | custom-call | tf_op jit(solution)/shard_map/theta_edges/pallas_call | solution.py:403
  2.5 2.0 %collective-permute-start = (f32[9,2,16,128]{3,2,1,0:T(8,128)}, f32[9,2,16,128]{3,2,1,0:T(8,128)S(1)}, u32[]{:S(2)}, u32[]{:S(2)}) collective-permute-start(f32[9,2,16,128]{3,2,1,0:T(8,128)} %get-tuple-element.22), channel_id=1, source_target_pairs={{0,32},{32,0},{64,96},{96,64},{128,160},{160,128},{192,224},{224,1... | collective-permute-start | bytes 442376 | tf_op jit(solution)/shard_map/ppermute | solution.py:40
  4.5 4.9 %collective-permute-start.1 = (f32[9,2,16,128]{3,2,1,0:T(8,128)}, f32[9,2,16,128]{3,2,1,0:T(8,128)S(1)}, u32[]{:S(2)}, u32[]{:S(2)}) collective-permute-start(f32[9,2,16,128]{3,2,1,0:T(8,128)} %get-tuple-element.23), channel_id=1, source_target_pairs={{0,224},{32,64},{64,32},{96,128},{128,96},{160,192},{192,160},{224... | collective-permute-start | bytes 442376 | tf_op jit(solution)/shard_map/ppermute | solution.py:41
  9.4 0.0 copy-start.5
  9.4 0.7 %copy-done.5 = s32[2048,1]{0,1:T(1,128)S(1)} copy-done((s32[2048,1]{0,1:T(1,128)S(1)}, s32[2048,1]{0,1:T(1,128)}, u32[]{:S(2)}) %copy-start.5) | copy-done | bytes 8216
  10.1 0.0 copy-start.6
  10.1 0.7 %copy-done.6 = s32[2048]{0:T(1024)S(1)} copy-done((s32[2048]{0:T(1024)S(1)}, s32[2048]{0:T(1024)}, u32[]{:S(2)}) %copy-start.6) | copy-done | bytes 8216
  10.8 1.3 %ranks.1 = (f32[1,2048]{1,0:T(1,128)S(1)}, f32[256,128]{1,0:T(8,128)S(1)}, bf16[256,2048]{1,0:T(8,128)(2,1)S(1)}) custom-call(s32[1,2048]{1,0:T(1,128)S(1)} %bitcast.12, s32[1,2048]{1,0:T(1,128)S(1)} %bitcast.13), custom_call_target="tpu_custom_call" | custom-call | tf_op jit(solution)/shard_map/ranks/pallas_call | solution.py:413
  12.2 0.0 collective-permute-done.t_first
  12.2 1.0 %collective-permute-done.1.t_second = f32[9,2,16,128]{3,2,1,0:T(8,128)S(1)} collective-permute-done((f32[9,2,16,128]{3,2,1,0:T(8,128)}, f32[9,2,16,128]{3,2,1,0:T(8,128)S(1)}, u32[]{:S(2)}, u32[]{:S(2)}) %collective-permute-start.1) | collective-permute-done | bytes 147488 | tf_op jit(solution)/shard_map/ppermute | solution.py:41
  13.2 0.0 copy-done.1
  13.2 0.0 copy-done
  13.2 0.0 copy-start.3
  13.2 0.0 copy-start.4
  13.2 0.1 phi_edges.1
  13.4 0.1 collective-permute-start.2
  13.5 2.7 %collective-permute-start.3 = (f32[9,40,128]{2,1,0:T(8,128)S(1)}, f32[9,40,128]{2,1,0:T(8,128)S(1)}, u32[]{:S(2)}, u32[]{:S(2)}) collective-permute-start(f32[9,40,128]{2,1,0:T(8,128)S(1)} %get-tuple-element.28), channel_id=1, source_target_pairs={{0,31},{1,2},{2,1},{3,4},{4,3},{5,6},{6,5},{7,8},{8,7},{9,10},{10,... | collective-permute-start | bytes 552968 | tf_op jit(solution)/shard_map/ppermute | solution.py:41
  16.2 0.0 copy-done.3
  16.2 0.0 copy-done.4
  16.2 0.5 tables.1
  16.8 0.0 collective-permute-done.2.p_first
  16.8 3.9 %collective-permute-done.3.p_second = f32[9,40,128]{2,1,0:T(8,128)S(1)} collective-permute-done((f32[9,40,128]{2,1,0:T(8,128)S(1)}, f32[9,40,128]{2,1,0:T(8,128)S(1)}, u32[]{:S(2)}, u32[]{:S(2)}) %collective-permute-start.3) | collective-permute-done | bytes 184352 | tf_op jit(solution)/shard_map/ppermute | solution.py:41
  20.6 0.0 copy-start.7
  20.6 0.7 %copy-done.7 = f32[8,8]{1,0:T(8,128)S(1)} copy-done((f32[8,8]{1,0:T(8,128)S(1)}, f32[8,8]{1,0:T(8,128)}, u32[]{:S(2)}) %copy-start.7) | copy-done | bytes 280
  21.3 6.8 %main.1 = (f32[8,16,16,128]{3,2,1,0:T(8,128)}, f32[512,128]{1,0:T(8,128)S(1)}) custom-call(f32[8,8]{1,0:T(8,128)S(1)} %copy-done.7, f32[8,16,16,128]{3,2,1,0:T(8,128)S(1)} %copy-done, f32[16,16,128]{2,1,0:T(8,128)S(1)} %copy-done.1, f32[9,2,16,128]{3,2,1,0:T(8,128)S(1)} %collective-permute-done.t_first, ...), custom_call_target="tpu_custom_call" | custom-call | tf_op jit(solution)/shard_map/main/pallas_call | solution.py:440
  28.1 0.0 copy-start.2
  28.1 26.8 %all_to_all.11 = f32[256,2,128]{2,1,0:T(2,128)S(1)} all-to-all(f32[256,2,128]{2,1,0:T(2,128)S(1)} %bitcast.10), channel_id=1, replica_groups=mesh['lat'=8,'lon'=32] {'lat','lon'}, dimensions={0} | all-to-all | bytes 524288 | tf_op jit(solution)/shard_map/all_to_all | solution.py:458
  55.0 0.0 copy-done.2
  55.0 1.4 %land.1 = (f32[8,32,128]{2,1,0:T(8,128)S(1)}, f32[8,128]{1,0:T(8,128)S(1)}, f32[8,128]{1,0:T(8,128)S(1)}, f32[1,256]{1,0:T(1,128)S(1)}, f32[1,256]{1,0:T(1,128)S(1)}) custom-call(f32[512,128]{1,0:T(8,128)S(1)} %bitcast.9, f32[8,32,128]{2,1,0:T(8,128)S(1)} %copy-done.2), custom_call_target="tpu_custom_call" | custom-call | tf_op jit(solution)/shard_map/land/pallas_call | solution.py:460
  56.4 0.1 collective-permute-start.4
  56.5 2.8 %collective-permute-start.5 = (f32[8,128]{1,0:T(8,128)S(1)}, f32[8,128]{1,0:T(8,128)S(1)}, u32[]{:S(2)}, u32[]{:S(2)}) collective-permute-start(f32[8,128]{1,0:T(8,128)S(1)} %get-tuple-element.39), channel_id=1, source_target_pairs={{0,31},{1,2},{2,1},{3,4},{4,3},{5,6},{6,5},{7,8},{8,7},{9,10},{10,... | collective-permute-start | bytes 12296 | tf_op jit(solution)/shard_map/ppermute | solution.py:41
  59.3 1.1 %collective-permute-start.6 = (f32[1,256]{1,0:T(1,128)S(1)}, f32[1,256]{1,0:T(1,128)S(1)}, u32[]{:S(2)}, u32[]{:S(2)}) collective-permute-start(f32[1,256]{1,0:T(1,128)S(1)} %get-tuple-element.40), channel_id=1, source_target_pairs={{0,32},{32,0},{64,96},{96,64},{128,160},{160,128},{192,224},{224,1... | collective-permute-start | bytes 3080 | tf_op jit(solution)/shard_map/ppermute | solution.py:40
  60.3 0.0 collective-permute-start.7
  60.3 2.5 %collective-permute-done.6.t_first = f32[1,256]{1,0:T(1,128)S(1)} collective-permute-done((f32[1,256]{1,0:T(1,128)S(1)}, f32[1,256]{1,0:T(1,128)S(1)}, u32[]{:S(2)}, u32[]{:S(2)}) %collective-permute-start.6) | collective-permute-done | bytes 1056 | tf_op jit(solution)/shard_map/ppermute | solution.py:40
  62.8 2.3 %collective-permute-done.7.t_second = f32[1,256]{1,0:T(1,128)S(1)} collective-permute-done((f32[1,256]{1,0:T(1,128)S(1)}, f32[1,256]{1,0:T(1,128)S(1)}, u32[]{:S(2)}, u32[]{:S(2)}) %collective-permute-start.7) | collective-permute-done | bytes 1056 | tf_op jit(solution)/shard_map/ppermute | solution.py:41
  65.1 0.0 collective-permute-done.4.p_first
  65.1 0.0 collective-permute-done.5.p_second
  65.1 0.9 %smooth.1 = f32[8,32,128]{2,1,0:T(8,128)} custom-call(f32[8,32,128]{2,1,0:T(8,128)S(1)} %get-tuple-element.37.coupled, f32[8,128]{1,0:T(8,128)S(1)} %collective-permute-done.4.p_first, f32[8,128]{1,0:T(8,128)S(1)} %collective-permute-done.5.p_second, f32[1,256]{1,0:T(1,128)S(1)} %collective-permute-done.6.t_first, f32[1,256]{1,0:T(1,128)S(1)} %collective-permute-done.7.t_second), custom_call_target="tpu_custom_call" | custom-call | tf_op jit(solution)/shard_map/smooth/pallas_call | solution.py:468
Async XLA Ops:
  0.6 12.6 %copy-start.1 = (f32[16,16,128]{2,1,0:T(8,128)S(1)}, f32[16,16,128]{2,1,0:T(8,128)}, u32[]{:S(2)}) copy-start(f32[16,16,128]{2,1,0:T(8,128)} %kappa.3) | copy-start | bytes 393220
  0.6 12.6 %copy-start = (f32[8,16,16,128]{3,2,1,0:T(8,128)S(1)}, f32[8,16,16,128]{3,2,1,0:T(8,128)}, u32[]{:S(2)}) copy-start(f32[8,16,16,128]{3,2,1,0:T(8,128)} %corona.3) | copy-start | bytes 3145732
  2.5 9.7 %collective-permute-start = (f32[9,2,16,128]{3,2,1,0:T(8,128)}, f32[9,2,16,128]{3,2,1,0:T(8,128)S(1)}, u32[]{:S(2)}, u32[]{:S(2)}) collective-permute-start(f32[9,2,16,128]{3,2,1,0:T(8,128)} %get-tuple-element.22), channel_id=1, source_target_pairs={{0,32},{32,0},{64,96},{96,64},{128,160},{160,128},{192,224},{224,1... | collective-permute-start | bytes 442376 | tf_op jit(solution)/shard_map/ppermute | solution.py:40
  4.5 8.7 %collective-permute-start.1 = (f32[9,2,16,128]{3,2,1,0:T(8,128)}, f32[9,2,16,128]{3,2,1,0:T(8,128)S(1)}, u32[]{:S(2)}, u32[]{:S(2)}) collective-permute-start(f32[9,2,16,128]{3,2,1,0:T(8,128)} %get-tuple-element.23), channel_id=1, source_target_pairs={{0,224},{32,64},{64,32},{96,128},{128,96},{160,192},{192,160},{224... | collective-permute-start | bytes 442376 | tf_op jit(solution)/shard_map/ppermute | solution.py:41
  9.4 0.7 %copy-start.5 = (s32[2048,1]{0,1:T(1,128)S(1)}, s32[2048,1]{0,1:T(1,128)}, u32[]{:S(2)}) copy-start(s32[2048,1]{0,1:T(1,128)} %param.12) | copy-start | bytes 24580
  10.1 0.7 %copy-start.6 = (s32[2048]{0:T(1024)S(1)}, s32[2048]{0:T(1024)}, u32[]{:S(2)}) copy-start(s32[2048]{0:T(1024)} %param.13) | copy-start | bytes 24580
  13.2 3.0 %copy-start.3 = (f32[3,2048]{1,0:T(4,128)S(1)}, f32[3,2048]{1,0:T(4,128)}, u32[]{:S(2)}) copy-start(f32[3,2048]{1,0:T(4,128)} %frac.1) | copy-start | bytes 73732
  13.2 3.0 %copy-start.4 = (s32[2048]{0:T(1024)S(1)}, s32[2048]{0:T(1024)}, u32[]{:S(2)}) copy-start(s32[2048]{0:T(1024)} %param.14) | copy-start | bytes 24580
  13.4 3.4 %collective-permute-start.2 = (f32[9,40,128]{2,1,0:T(8,128)S(1)}, f32[9,40,128]{2,1,0:T(8,128)S(1)}, u32[]{:S(2)}, u32[]{:S(2)}) collective-permute-start(f32[9,40,128]{2,1,0:T(8,128)S(1)} %get-tuple-element.27), channel_id=1, source_target_pairs={{0,1},{1,0},{2,3},{3,2},{4,5},{5,4},{6,7},{7,6},{8,9},{9,8},{10,11... | collective-permute-start | bytes 552968 | tf_op jit(solution)/shard_map/ppermute | solution.py:40
  13.5 7.2 %collective-permute-start.3 = (f32[9,40,128]{2,1,0:T(8,128)S(1)}, f32[9,40,128]{2,1,0:T(8,128)S(1)}, u32[]{:S(2)}, u32[]{:S(2)}) collective-permute-start(f32[9,40,128]{2,1,0:T(8,128)S(1)} %get-tuple-element.28), channel_id=1, source_target_pairs={{0,31},{1,2},{2,1},{3,4},{4,3},{5,6},{6,5},{7,8},{8,7},{9,10},{10,... | collective-permute-start | bytes 552968 | tf_op jit(solution)/shard_map/ppermute | solution.py:41
  20.6 0.7 %copy-start.7 = (f32[8,8]{1,0:T(8,128)S(1)}, f32[8,8]{1,0:T(8,128)}, u32[]{:S(2)}) copy-start(f32[8,8]{1,0:T(8,128)} %mixing.1) | copy-start | bytes 772
  28.1 26.9 %copy-start.2 = (f32[8,32,128]{2,1,0:T(8,128)S(1)}, f32[8,32,128]{2,1,0:T(8,128)}, u32[]{:S(2)}) copy-start(f32[8,32,128]{2,1,0:T(8,128)} %prev.1) | copy-start | bytes 393220
  56.4 8.7 %collective-permute-start.4 = (f32[8,128]{1,0:T(8,128)S(1)}, f32[8,128]{1,0:T(8,128)S(1)}, u32[]{:S(2)}, u32[]{:S(2)}) collective-permute-start(f32[8,128]{1,0:T(8,128)S(1)} %get-tuple-element.38), channel_id=1, source_target_pairs={{0,1},{1,0},{2,3},{3,2},{4,5},{5,4},{6,7},{7,6},{8,9},{9,8},{10,11... | collective-permute-start | bytes 12296 | tf_op jit(solution)/shard_map/ppermute | solution.py:40
  56.5 8.6 %collective-permute-start.5 = (f32[8,128]{1,0:T(8,128)S(1)}, f32[8,128]{1,0:T(8,128)S(1)}, u32[]{:S(2)}, u32[]{:S(2)}) collective-permute-start(f32[8,128]{1,0:T(8,128)S(1)} %get-tuple-element.39), channel_id=1, source_target_pairs={{0,31},{1,2},{2,1},{3,4},{4,3},{5,6},{6,5},{7,8},{8,7},{9,10},{10,... | collective-permute-start | bytes 12296 | tf_op jit(solution)/shard_map/ppermute | solution.py:41
  59.3 3.6 %collective-permute-start.6 = (f32[1,256]{1,0:T(1,128)S(1)}, f32[1,256]{1,0:T(1,128)S(1)}, u32[]{:S(2)}, u32[]{:S(2)}) collective-permute-start(f32[1,256]{1,0:T(1,128)S(1)} %get-tuple-element.40), channel_id=1, source_target_pairs={{0,32},{32,0},{64,96},{96,64},{128,160},{160,128},{192,224},{224,1... | collective-permute-start | bytes 3080 | tf_op jit(solution)/shard_map/ppermute | solution.py:40
  60.3 4.8 %collective-permute-start.7 = (f32[1,256]{1,0:T(1,128)S(1)}, f32[1,256]{1,0:T(1,128)S(1)}, u32[]{:S(2)}, u32[]{:S(2)}) collective-permute-start(f32[1,256]{1,0:T(1,128)S(1)} %get-tuple-element.41), channel_id=1, source_target_pairs={{0,224},{32,64},{64,32},{96,128},{128,96},{160,192},{192,160},{224... | collective-permute-start | bytes 3080 | tf_op jit(solution)/shard_map/ppermute | solution.py:41

commit v9 on v7

--- a/solution.py
+++ b/solution.py
@@ -285,11 +285,14 @@
 
 def route(
     n_dev, kappa, p_first, p_second, own_low, own_high, c_first, c_second, stepped, rank, meta, hit,
-    table_high, table_low, w_r, patch, message, shell,
+    table_high, table_low, w_r, out, message, shell, tiles, sems,
 ):
     fields, columns, radial = stepped.shape
     tile_t, tile_p, _ = kappa.shape
     sides_p = sides("lon")
+    whole = pltpu.make_async_copy(stepped, out, sems.at[4])
+    whole.start()
+    corrections = []
     lane = iota((columns, radial), 1)
     rows = jnp.zeros((columns, radial), F32)
     for f in range(fields):
@@ -312,7 +315,16 @@
             by_t = 0.075 * ((k_t + k_d) * u_d - k_d * u_t)
             by_p = 0.075 * ((k_p + k_d) * u_d - k_d * u_p)
             extra = 0.075 * ((k + k_t) * by_t + (k + k_p) * by_p)
-            patch[2 * a + b] = extra
+            n, start = 2 * a + b, t * tile_p + b * (tile_p - 8)
+            within = p % 8
+            for f in range(fields):
+                tiles[n, f] = stepped[f, start : start + 8, :]
+                tiles[n, f, within : within + 1, :] = (
+                    stepped[f, start + within : start + within + 1, :] + extra[f : f + 1]
+                )
+            corrections.append(
+                pltpu.make_async_copy(tiles.at[n], out.at[:, pl.ds(start, 8)], sems.at[n])
+            )
             row = jnp.zeros((1, radial), F32)
             for f in range(fields):
                 moved = pltpu.roll(extra[f : f + 1], (f * SH + SH) % radial, 1)
@@ -328,6 +340,10 @@
     width = min(BLOCK, count)
     packed = jnp.zeros((n_dev, 2 * fields * CAP), F32)
     for b in range(count // width):
+        if b == count // width // 2:
+            whole.wait()
+            for copy in corrections:
+                copy.start()
         cols = slice(b * width, (b + 1) * width)
         coarse = jnp.dot(left, table_high[:, cols], preferred_element_type=F32)
         fine = jnp.dot(left[: fields * SH], table_low[:, cols], preferred_element_type=F32)
@@ -347,17 +363,8 @@
     half = fields * CAP
     message[pl.ds(0, n_dev, stride=2), :] = packed[:, :half] + packed[:, half:]
     message[pl.ds(1, n_dev, stride=2), :] = meta[...]
-
-
-def finish(tile_t, tile_p, stepped, patch, out):
-    out[...] = stepped[...]
-    for a in range(2):
-        for b in range(2):
-            at = a * (tile_t - 1) * tile_p + b * (tile_p - 1)
-            for f in range(stepped.shape[0]):
-                out[f, at : at + 1, :] = (
-                    stepped[f, at : at + 1, :] + patch[2 * a + b, f : f + 1, :]
-                )
+    for copy in corrections:
+        copy.wait()
 
 
 def land(n_dev, got, prev, coupled, p_first, p_second, t_first, t_second):
@@ -419,13 +426,13 @@
     out[...] = x + 0.2 * (above + below + right + left - 4.0 * x)
 
 
-def call(kernel, outs, specs, name, scratch=(), room=40 * 1024 * 1024):
+def call(kernel, outs, specs, name, scratch=(), out_specs=None, room=40 * 1024 * 1024):
     outs = [s if isinstance(s, jax.ShapeDtypeStruct) else jax.ShapeDtypeStruct(s, F32) for s in outs]
     return pl.pallas_call(
         kernel,
         out_shape=outs,
         in_specs=specs,
-        out_specs=[vspec()] * len(outs),
+        out_specs=out_specs or [vspec()] * len(outs),
         scratch_shapes=list(scratch),
         name=name,
         compiler_params=pltpu.CompilerParams(vmem_limit_bytes=room),
@@ -487,20 +494,21 @@
     )(mixing, corona, kappa, t_first, t_second, p_first, p_second)
     almost = almost.reshape(flat)
 
-    patch, message = call(
+    stepped, message = call(
         functools.partial(route, n_dev),
-        [(4, fields, radial), (2 * n_dev, 128)],
+        [flat, (2 * n_dev, 128)],
         [vspec()] * 14,
         "route",
-        [VMEM((tile_t * tile_p, radial), F32)],
+        [
+            VMEM((tile_t * tile_p, radial), F32),
+            VMEM((4, fields, 8, radial), F32),
+            pltpu.SemaphoreType.DMA((5,)),
+        ],
+        [pl.BlockSpec(memory_space=pltpu.HBM), vspec()],
     )(
         kappa, p_first, p_second, own_low, own_high, c_first, c_second, almost, rank, meta, hit,
         table_high, table_low, w_r,
     )
-    (stepped,) = call(
-        functools.partial(finish, tile_t, tile_p), [flat], [vspec()] * 2, "finish"
-    )(almost, patch)
-
     got = lax.all_to_all(message, ("lat", "lon"), split_axis=0, concat_axis=0, tiled=True)
 
     coupled, p_first, p_second, t_first, t_second = call(

time: 58.4 us -> 59.2 us (1.014)
  waiting for transfers between devices: 4.08 us -> 5.14 us
    ppermute x5, waiting for transfers between devices: 1.47 us -> 2.52 us  [swapped(): lax.ppermute(first, axis, [(i, i ^ 1) for i in range(count)])]
    pallas_call x2 -> x1, Pallas kernels: 2.72 us -> 2.46 us  [body(): call(functools.partial(route, n_dev), [flat, (2 * n_dev, 128)], [vspec()]...]
  transfers between devices with their start and end apart: 10 -> 10, of which waited for: 3 -> 3; matrix products, arithmetic and copies ran while one was open for 0% -> 0% of each run, Pallas kernels for 13% -> 11%
where the time goes in v9:
time: 59.2 us; the launch traced here: 59 us
  blocking collectives  24.9 us (42%)
  starting transfers between devices  15.2 us (26%)
  Pallas kernels  12.9 us (22%)
  waiting for transfers between devices  5.14 us (9%)
  between operations  0.8 us (1%)
    all_to_all x1, blocking collectives, body(): lax.all_to_all(message, ('lat', 'lon'), split_axis=0, concat_axis=0, tile...  24.9 us
    ppermute x5, starting transfers between devices, swapped(): lax.ppermute(second, axis, list(enumerate(other)))  11.9 us
    pallas_call x1, Pallas kernels, body(): call(steps, [corona.shape], [sspec()] + [vspec()] * 6, 'steps', [VMEM((fi...  4.13 us
    ppermute x5, starting transfers between devices, swapped(): lax.ppermute(first, axis, [(i, i ^ 1) for i in range(count)])  3.34 us
    ppermute x5, waiting for transfers between devices, swapped(): lax.ppermute(second, axis, list(enumerate(other)))  2.62 us
    ppermute x5, waiting for transfers between devices, swapped(): lax.ppermute(first, axis, [(i, i ^ 1) for i in range(count)])  2.52 us
    pallas_call x1, Pallas kernels, body(): call(functools.partial(route, n_dev), [flat, (2 * n_dev, 128)], [vspec()]...  2.46 us
    pallas_call x1, Pallas kernels, body(): call(functools.partial(plan, face_t, tile_t, tile_p), [(1, count), (n_dev...  2.05 us
  transfers between devices with their start and end apart: 10, of which 3 were waited for; matrix products, arithmetic and copies ran while one was open for 0% of the time, Pallas kernels for 11%

profile of v9, /device:TPU:8, one launch (start us, length us, event | category | flops | bytes accessed | tf_op | source)
XLA Modules:
  0.0 59.0 jit_solution(14089651432485516993)
XLA Ops:
  0.6 0.0 copy-start.1
  0.6 0.0 copy-start
  0.6 1.8 %theta_edges.1 = (f32[9,2,16,128]{3,2,1,0:T(8,128)}, f32[9,2,16,128]{3,2,1,0:T(8,128)}) custom-call(f32[8,16,16,128]{3,2,1,0:T(8,128)} %corona.3, f32[16,16,128]{2,1,0:T(8,128)} %kappa.5), custom_call_target="tpu_custom_call" | custom-call | tf_op jit(solution)/shard_map/theta_edges/pallas_call | solution.py:452
  2.5 2.0 %collective-permute-start.2 = (f32[9,2,16,128]{3,2,1,0:T(8,128)}, f32[9,2,16,128]{3,2,1,0:T(8,128)S(1)}, u32[]{:S(2)}, u32[]{:S(2)}) collective-permute-start(f32[9,2,16,128]{3,2,1,0:T(8,128)} %get-tuple-element.28), channel_id=1, source_target_pairs={{0,32},{32,0},{64,96},{96,64},{128,160},{160,128},{192,224},{224,1... | collective-permute-start | bytes 442376 | tf_op jit(solution)/shard_map/ppermute | solution.py:40
  4.5 4.9 %collective-permute-start.3 = (f32[9,2,16,128]{3,2,1,0:T(8,128)}, f32[9,2,16,128]{3,2,1,0:T(8,128)S(1)}, u32[]{:S(2)}, u32[]{:S(2)}) collective-permute-start(f32[9,2,16,128]{3,2,1,0:T(8,128)} %get-tuple-element.29), channel_id=1, source_target_pairs={{0,224},{32,64},{64,32},{96,128},{128,96},{160,192},{192,160},{224... | collective-permute-start | bytes 442376 | tf_op jit(solution)/shard_map/ppermute | solution.py:41
  9.4 0.0 copy-done.1
  9.4 0.0 copy-done
  9.4 0.0 copy-start.3
  9.4 0.0 copy-start.5
  9.4 0.0 copy-start.6
  9.5 0.1 phi_edges.1
  9.6 0.0 copy-start.4
  9.6 0.1 collective-permute-start
  9.7 2.7 %collective-permute-start.1 = (f32[9,32,128]{2,1,0:T(8,128)S(1)}, f32[9,32,128]{2,1,0:T(8,128)S(1)}, u32[]{:S(2)}, u32[]{:S(2)}) collective-permute-start(f32[9,32,128]{2,1,0:T(8,128)S(1)} %get-tuple-element.27), channel_id=1, source_target_pairs={{0,31},{1,2},{2,1},{3,4},{4,3},{5,6},{6,5},{7,8},{8,7},{9,10},{10,... | collective-permute-start | bytes 442376 | tf_op jit(solution)/shard_map/ppermute | solution.py:41
  12.4 0.0 copy-done.3
  12.4 0.0 copy-done.5
  12.4 0.0 copy-done.6
  12.4 0.0 copy-done.4
  12.4 2.0 %plan.1 = (f32[1,2048]{1,0:T(1,128)S(1)}, f32[256,128]{1,0:T(8,128)S(1)}, bf16[256,2048]{1,0:T(8,128)(2,1)S(1)}, bf16[256,2048]{1,0:T(8,128)(2,1)S(1)}, bf16[256...) custom-call(s32[1,2048]{1,0:T(1,128)S(1)} %bitcast.14, s32[1,2048]{1,0:T(1,128)S(1)} %bitcast.15, s32[1,2048]{1,0:T(1,128)S(1)} %bitcast.16, ...), custom_call_target="tpu_custom_call" | custom-call | tf_op jit(solution)/shard_map/plan/pallas_call | solution.py:469
  14.5 0.0 collective-permute-done.2.t_first
  14.5 0.0 collective-permute-done.3.t_second
  14.5 0.0 copy-start.7
  14.6 0.1 collective-permute-start.4
  14.7 1.4 %collective-permute-start.5 = (f32[2,9,128]{2,1,0:T(8,128)S(1)}, f32[2,9,128]{2,1,0:T(8,128)S(1)}, u32[]{:S(2)}, u32[]{:S(2)}) collective-permute-start(f32[2,9,128]{2,1,0:T(8,128)S(1)} %get-tuple-element.36), channel_id=1, source_target_pairs={{0,31},{1,2},{2,1},{3,4},{4,3},{5,6},{6,5},{7,8},{8,7},{9,10},{10,... | collective-permute-start | bytes 27656 | tf_op jit(solution)/shard_map/ppermute | solution.py:41
  16.1 0.0 collective-permute-done.p_first
  16.1 0.3 collective-permute-done.1.p_second
  16.5 0.0 copy-done.7
  16.5 4.1 %steps.1 = f32[8,16,16,128]{3,2,1,0:T(8,128)S(1)} custom-call(f32[8,8]{1,0:T(8,128)S(1)} %copy-done.7, f32[8,16,16,128]{3,2,1,0:T(8,128)S(1)} %copy-done, f32[16,16,128]{2,1,0:T(8,128)S(1)} %copy-done.1, f32[9,2,16,128]{3,2,1,0:T(8,128)S(1)} %collective-permute-done.2.t_first, f32[9,2,16,128]{3,2,1,0:T(8,128)S(1)} %collective-permute-done.3.t_second, ...), custom_call_target="tpu_custom_call" | custom-call | tf_op jit(solution)/shard_map/steps/pallas_call | solution.py:484
  20.6 0.0 collective-permute-done.4.c_first
  20.6 0.0 collective-permute-done.5.c_second
  20.6 2.5 %route.1 = (f32[8,256,128]{2,1,0:T(8,128)}, f32[512,128]{1,0:T(8,128)S(1)}) custom-call(f32[16,16,128]{2,1,0:T(8,128)S(1)} %copy-done.1, f32[9,32,128]{2,1,0:T(8,128)S(1)} %collective-permute-done.p_first, f32[9,32,128]{2,1,0:T(8,128)S(1)} %collective-permute-done.1.p_second, f32[2,9,128]{2,1,0:T(8,128)S(1)} %get-tuple-element.33.own_low, ...), custom_call_target="tpu_custom_call" | custom-call | tf_op jit(solution)/shard_map/route/pallas_call | solution.py:497
  23.1 0.0 copy-start.2
  23.1 24.9 %all_to_all.11 = f32[256,2,128]{2,1,0:T(2,128)S(1)} all-to-all(f32[256,2,128]{2,1,0:T(2,128)S(1)} %bitcast.13), channel_id=1, replica_groups=mesh['lat'=8,'lon'=32] {'lat','lon'}, dimensions={0} | all-to-all | bytes 524288 | tf_op jit(solution)/shard_map/all_to_all | solution.py:512
  48.0 0.0 copy-done.2
  48.0 1.4 %land.1 = (f32[8,32,128]{2,1,0:T(8,128)S(1)}, f32[8,128]{1,0:T(8,128)S(1)}, f32[8,128]{1,0:T(8,128)S(1)}, f32[1,256]{1,0:T(1,128)S(1)}, f32[1,256]{1,0:T(1,128)S(1)}) custom-call(f32[512,128]{1,0:T(8,128)S(1)} %bitcast.12, f32[8,32,128]{2,1,0:T(8,128)S(1)} %copy-done.2), custom_call_target="tpu_custom_call" | custom-call | tf_op jit(solution)/shard_map/land/pallas_call | solution.py:514
  49.4 0.1 collective-permute-start.6
  49.5 2.8 %collective-permute-start.7 = (f32[8,128]{1,0:T(8,128)S(1)}, f32[8,128]{1,0:T(8,128)S(1)}, u32[]{:S(2)}, u32[]{:S(2)}) collective-permute-start(f32[8,128]{1,0:T(8,128)S(1)} %get-tuple-element.47), channel_id=1, source_target_pairs={{0,31},{1,2},{2,1},{3,4},{4,3},{5,6},{6,5},{7,8},{8,7},{9,10},{10,... | collective-permute-start | bytes 12296 | tf_op jit(solution)/shard_map/ppermute | solution.py:41
  52.3 1.1 %collective-permute-start.8 = (f32[1,256]{1,0:T(1,128)S(1)}, f32[1,256]{1,0:T(1,128)S(1)}, u32[]{:S(2)}, u32[]{:S(2)}) collective-permute-start(f32[1,256]{1,0:T(1,128)S(1)} %get-tuple-element.48), channel_id=1, source_target_pairs={{0,32},{32,0},{64,96},{96,64},{128,160},{160,128},{192,224},{224,1... | collective-permute-start | bytes 3080 | tf_op jit(solution)/shard_map/ppermute | solution.py:40
  53.4 0.0 collective-permute-start.9
  53.4 2.5 %collective-permute-done.8.t_first = f32[1,256]{1,0:T(1,128)S(1)} collective-permute-done((f32[1,256]{1,0:T(1,128)S(1)}, f32[1,256]{1,0:T(1,128)S(1)}, u32[]{:S(2)}, u32[]{:S(2)}) %collective-permute-start.8) | collective-permute-done | bytes 1056 | tf_op jit(solution)/shard_map/ppermute | solution.py:40
  55.9 2.3 %collective-permute-done.9.t_second = f32[1,256]{1,0:T(1,128)S(1)} collective-permute-done((f32[1,256]{1,0:T(1,128)S(1)}, f32[1,256]{1,0:T(1,128)S(1)}, u32[]{:S(2)}, u32[]{:S(2)}) %collective-permute-start.9) | collective-permute-done | bytes 1056 | tf_op jit(solution)/shard_map/ppermute | solution.py:41
  58.1 0.0 collective-permute-done.6.p_first
  58.1 0.0 collective-permute-done.7.p_second
  58.1 0.9 %smooth.1 = f32[8,32,128]{2,1,0:T(8,128)} custom-call(f32[8,32,128]{2,1,0:T(8,128)S(1)} %get-tuple-element.45.coupled, f32[8,128]{1,0:T(8,128)S(1)} %collective-permute-done.6.p_first, f32[8,128]{1,0:T(8,128)S(1)} %collective-permute-done.7.p_second, f32[1,256]{1,0:T(1,128)S(1)} %collective-permute-done.8.t_first, f32[1,256]{1,0:T(1,128)S(1)} %collective-permute-done.9.t_second), custom_call_target="tpu_custom_call" | custom-call | tf_op jit(solution)/shard_map/smooth/pallas_call | solution.py:522
  (1 shorter events, 0.0 us)
Async XLA Ops:
  0.6 8.8 %copy-start.1 = (f32[16,16,128]{2,1,0:T(8,128)S(1)}, f32[16,16,128]{2,1,0:T(8,128)}, u32[]{:S(2)}) copy-start(f32[16,16,128]{2,1,0:T(8,128)} %kappa.5) | copy-start | bytes 393220
  0.6 8.8 %copy-start = (f32[8,16,16,128]{3,2,1,0:T(8,128)S(1)}, f32[8,16,16,128]{3,2,1,0:T(8,128)}, u32[]{:S(2)}) copy-start(f32[8,16,16,128]{3,2,1,0:T(8,128)} %corona.3) | copy-start | bytes 3145732
  2.5 12.0 %collective-permute-start.2 = (f32[9,2,16,128]{3,2,1,0:T(8,128)}, f32[9,2,16,128]{3,2,1,0:T(8,128)S(1)}, u32[]{:S(2)}, u32[]{:S(2)}) collective-permute-start(f32[9,2,16,128]{3,2,1,0:T(8,128)} %get-tuple-element.28), channel_id=1, source_target_pairs={{0,32},{32,0},{64,96},{96,64},{128,160},{160,128},{192,224},{224,1... | collective-permute-start | bytes 442376 | tf_op jit(solution)/shard_map/ppermute | solution.py:40
  4.5 10.0 %collective-permute-start.3 = (f32[9,2,16,128]{3,2,1,0:T(8,128)}, f32[9,2,16,128]{3,2,1,0:T(8,128)S(1)}, u32[]{:S(2)}, u32[]{:S(2)}) collective-permute-start(f32[9,2,16,128]{3,2,1,0:T(8,128)} %get-tuple-element.29), channel_id=1, source_target_pairs={{0,224},{32,64},{64,32},{96,128},{128,96},{160,192},{192,160},{224... | collective-permute-start | bytes 442376 | tf_op jit(solution)/shard_map/ppermute | solution.py:41
  9.4 3.0 %copy-start.3 = (f32[3,2048]{1,0:T(4,128)S(1)}, f32[3,2048]{1,0:T(4,128)}, u32[]{:S(2)}) copy-start(f32[3,2048]{1,0:T(4,128)} %frac.1) | copy-start | bytes 73732
  9.4 3.0 %copy-start.5 = (s32[2048]{0:T(1024)S(1)}, s32[2048]{0:T(1024)}, u32[]{:S(2)}) copy-start(s32[2048]{0:T(1024)} %param.13) | copy-start | bytes 24580
  9.4 3.0 %copy-start.6 = (s32[2048]{0:T(1024)S(1)}, s32[2048]{0:T(1024)}, u32[]{:S(2)}) copy-start(s32[2048]{0:T(1024)} %param.14) | copy-start | bytes 24580
  9.6 2.9 %copy-start.4 = (s32[2048,1]{0,1:T(1,128)S(1)}, s32[2048,1]{0,1:T(1,128)}, u32[]{:S(2)}) copy-start(s32[2048,1]{0,1:T(1,128)} %param.12) | copy-start | bytes 24580
  9.6 6.5 %collective-permute-start = (f32[9,32,128]{2,1,0:T(8,128)S(1)}, f32[9,32,128]{2,1,0:T(8,128)S(1)}, u32[]{:S(2)}, u32[]{:S(2)}) collective-permute-start(f32[9,32,128]{2,1,0:T(8,128)S(1)} %get-tuple-element.26), channel_id=1, source_target_pairs={{0,1},{1,0},{2,3},{3,2},{4,5},{5,4},{6,7},{7,6},{8,9},{9,8},{10,11... | collective-permute-start | bytes 442376 | tf_op jit(solution)/shard_map/ppermute | solution.py:40
  9.7 6.8 %collective-permute-start.1 = (f32[9,32,128]{2,1,0:T(8,128)S(1)}, f32[9,32,128]{2,1,0:T(8,128)S(1)}, u32[]{:S(2)}, u32[]{:S(2)}) collective-permute-start(f32[9,32,128]{2,1,0:T(8,128)S(1)} %get-tuple-element.27), channel_id=1, source_target_pairs={{0,31},{1,2},{2,1},{3,4},{4,3},{5,6},{6,5},{7,8},{8,7},{9,10},{10,... | collective-permute-start | bytes 442376 | tf_op jit(solution)/shard_map/ppermute | solution.py:41
  14.5 1.9 %copy-start.7 = (f32[8,8]{1,0:T(8,128)S(1)}, f32[8,8]{1,0:T(8,128)}, u32[]{:S(2)}) copy-start(f32[8,8]{1,0:T(8,128)} %mixing.1) | copy-start | bytes 772
  14.6 6.0 %collective-permute-start.4 = (f32[2,9,128]{2,1,0:T(8,128)S(1)}, f32[2,9,128]{2,1,0:T(8,128)S(1)}, u32[]{:S(2)}, u32[]{:S(2)}) collective-permute-start(f32[2,9,128]{2,1,0:T(8,128)S(1)} %get-tuple-element.35), channel_id=1, source_target_pairs={{0,1},{1,0},{2,3},{3,2},{4,5},{5,4},{6,7},{7,6},{8,9},{9,8},{10,11... | collective-permute-start | bytes 27656 | tf_op jit(solution)/shard_map/ppermute | solution.py:40
  14.7 5.9 %collective-permute-start.5 = (f32[2,9,128]{2,1,0:T(8,128)S(1)}, f32[2,9,128]{2,1,0:T(8,128)S(1)}, u32[]{:S(2)}, u32[]{:S(2)}) collective-permute-start(f32[2,9,128]{2,1,0:T(8,128)S(1)} %get-tuple-element.36), channel_id=1, source_target_pairs={{0,31},{1,2},{2,1},{3,4},{4,3},{5,6},{6,5},{7,8},{8,7},{9,10},{10,... | collective-permute-start | bytes 27656 | tf_op jit(solution)/shard_map/ppermute | solution.py:41
  23.1 25.0 %copy-start.2 = (f32[8,32,128]{2,1,0:T(8,128)S(1)}, f32[8,32,128]{2,1,0:T(8,128)}, u32[]{:S(2)}) copy-start(f32[8,32,128]{2,1,0:T(8,128)} %prev.1) | copy-start | bytes 393220
  49.4 8.7 %collective-permute-start.6 = (f32[8,128]{1,0:T(8,128)S(1)}, f32[8,128]{1,0:T(8,128)S(1)}, u32[]{:S(2)}, u32[]{:S(2)}) collective-permute-start(f32[8,128]{1,0:T(8,128)S(1)} %get-tuple-element.46), channel_id=1, source_target_pairs={{0,1},{1,0},{2,3},{3,2},{4,5},{5,4},{6,7},{7,6},{8,9},{9,8},{10,11... | collective-permute-start | bytes 12296 | tf_op jit(solution)/shard_map/ppermute | solution.py:40
  49.5 8.6 %collective-permute-start.7 = (f32[8,128]{1,0:T(8,128)S(1)}, f32[8,128]{1,0:T(8,128)S(1)}, u32[]{:S(2)}, u32[]{:S(2)}) collective-permute-start(f32[8,128]{1,0:T(8,128)S(1)} %get-tuple-element.47), channel_id=1, source_target_pairs={{0,31},{1,2},{2,1},{3,4},{4,3},{5,6},{6,5},{7,8},{8,7},{9,10},{10,... | collective-permute-start | bytes 12296 | tf_op jit(solution)/shard_map/ppermute | solution.py:41
  52.3 3.6 %collective-permute-start.8 = (f32[1,256]{1,0:T(1,128)S(1)}, f32[1,256]{1,0:T(1,128)S(1)}, u32[]{:S(2)}, u32[]{:S(2)}) collective-permute-start(f32[1,256]{1,0:T(1,128)S(1)} %get-tuple-element.48), channel_id=1, source_target_pairs={{0,32},{32,0},{64,96},{96,64},{128,160},{160,128},{192,224},{224,1... | collective-permute-start | bytes 3080 | tf_op jit(solution)/shard_map/ppermute | solution.py:40
  53.4 4.8 %collective-permute-start.9 = (f32[1,256]{1,0:T(1,128)S(1)}, f32[1,256]{1,0:T(1,128)S(1)}, u32[]{:S(2)}, u32[]{:S(2)}) collective-permute-start(f32[1,256]{1,0:T(1,128)S(1)} %get-tuple-element.49), channel_id=1, source_target_pairs={{0,224},{32,64},{64,32},{96,128},{128,96},{160,192},{192,160},{224... | collective-permute-start | bytes 3080 | tf_op jit(solution)/shard_map/ppermute | solution.py:41

commit v10 on v7

--- a/solution.py
+++ b/solution.py
@@ -36,10 +36,8 @@
 def swapped(first, second, axis):
     count = lax.axis_size(axis)
     other = [(i + (1 if i % 2 else -1)) % count for i in range(count)]
-    return (
-        lax.ppermute(first, axis, [(i, i ^ 1) for i in range(count)]),
-        lax.ppermute(second, axis, list(enumerate(other))),
-    )
+    second = lax.ppermute(second, axis, list(enumerate(other)))
+    return lax.ppermute(first, axis, [(i, i ^ 1) for i in range(count)]), second
 
 
 def parity(axis):
@@ -224,7 +222,7 @@
 
 
 def steps(
-    mixing, corona, kappa, t_first, t_second, p_first, p_second, stepped, wide, once, mix,
+    mixing, corona, kappa, t_first, t_second, p_second, p_first, stepped, wide, once, mix,
 ):
     fields, tile_t, tile_p, radial = corona.shape
     by_t, by_p = sides("lat"), sides("lon")
@@ -284,7 +282,7 @@
 
 
 def route(
-    n_dev, kappa, p_first, p_second, own_low, own_high, c_first, c_second, stepped, rank, meta, hit,
+    n_dev, kappa, p_first, p_second, own_low, own_high, c_second, c_first, stepped, rank, meta, hit,
     table_high, table_low, w_r, patch, message, shell,
 ):
     fields, columns, radial = stepped.shape
@@ -360,7 +358,7 @@
                 )
 
 
-def land(n_dev, got, prev, coupled, p_first, p_second, t_first, t_second):
+def land(n_dev, got, prev, coupled, t_first, t_second, p_second, p_first):
     fields, face_p, face_t = prev.shape
     values = jnp.transpose(got[pl.ds(0, n_dev, stride=2), :])
     cells = jnp.transpose(got[pl.ds(1, n_dev, stride=2), :])
@@ -396,17 +394,17 @@
         ("lon", edge(new, 0), edge(new, face_p - 1), p_first, p_second),
     ):
         odd = parity(axis).astype(F32)
-        first[...] = blend((odd, 1.0 - odd), low, high)
-        second[...] = blend((1.0 - odd, odd), low, high)
-
-
-def smooth(coupled, p_first, p_second, t_first, t_second, out):
+        first[...] = jnp.broadcast_to(blend((odd, 1.0 - odd), low, high), first.shape)
+        second[...] = jnp.broadcast_to(blend((1.0 - odd, odd), low, high), second.shape)
+
+
+def smooth(coupled, t_first, t_second, p_second, p_first, out):
     fields, face_p, face_t = coupled.shape
     x = coupled[...]
     row = iota((face_p, face_t), 0)[None]
     lane = iota((face_p, face_t), 1)[None]
 
-    t_low, t_high = [blend(w, t_first[...], t_second[...]) for w in sides("lat")]
+    t_low, t_high = [blend(w, t_first[0:1], t_second[0:1]) for w in sides("lat")]
     p_low, p_high = [blend(w, p_first[...], p_second[...]) for w in sides("lon")]
 
     def column(edge):
@@ -484,7 +482,7 @@
             VMEM((fields, (tile_t + 2) * WIDE, radial), F32),
             VMEM((fields * fields, 8, radial), F32),
         ],
-    )(mixing, corona, kappa, t_first, t_second, p_first, p_second)
+    )(mixing, corona, kappa, t_first, t_second, p_second, p_first)
     almost = almost.reshape(flat)
 
     patch, message = call(
@@ -494,7 +492,7 @@
         "route",
         [VMEM((tile_t * tile_p, radial), F32)],
     )(
-        kappa, p_first, p_second, own_low, own_high, c_first, c_second, almost, rank, meta, hit,
+        kappa, p_first, p_second, own_low, own_high, c_second, c_first, almost, rank, meta, hit,
         table_high, table_low, w_r,
     )
     (stepped,) = call(
@@ -503,16 +501,16 @@
 
     got = lax.all_to_all(message, ("lat", "lon"), split_axis=0, concat_axis=0, tiled=True)
 
-    coupled, p_first, p_second, t_first, t_second = call(
+    coupled, t_first, t_second, p_second, p_first = call(
         functools.partial(land, n_dev),
-        [helio_prev.shape, (fields, face_t), (fields, face_t)] + [(1, fields * face_p)] * 2,
+        [helio_prev.shape] + [(16, fields * face_p)] * 2 + [(fields, face_t)] * 2,
         [vspec()] * 2,
         "land",
     )(got, helio_prev)
+    t_first, t_second = swapped(t_first, t_second, "lat")
     p_first, p_second = swapped(p_first, p_second, "lon")
-    t_first, t_second = swapped(t_first, t_second, "lat")
     (face,) = call(smooth, [helio_prev.shape], [vspec()] * 5, "smooth")(
-        coupled, p_first, p_second, t_first, t_second
+        coupled, t_first, t_second, p_second, p_first
     )
     return (stepped.reshape(corona.shape), face)
 

time: 58.4 us -> 57.1 us (0.978)
  the two profiles are of different devices: /device:TPU:8 before, /device:TPU:32 now
where the time goes in v10:
time: 57.1 us; the launch traced here: 56.9 us
  blocking collectives  25.6 us (45%)
  Pallas kernels  13.2 us (23%)
  starting transfers between devices  11.6 us (20%)
  waiting for transfers between devices  5.65 us (10%)
  between operations  0.78 us (1%)
    all_to_all x1, blocking collectives, body(): lax.all_to_all(message, ('lat', 'lon'), split_axis=0, concat_axis=0, tile...  25.6 us
    ppermute x5, starting transfers between devices, swapped(): second = lax.ppermute(second, axis, list(enumerate(other)))  8.54 us
    ppermute x5, waiting for transfers between devices, swapped(): second = lax.ppermute(second, axis, list(enumerate(other)))  5.64 us
    pallas_call x1, Pallas kernels, body(): call(steps, [corona.shape], [sspec()] + [vspec()] * 6, 'steps', [VMEM((fi...  4.14 us
    ppermute x5, starting transfers between devices, swapped(): lax.ppermute(first, axis, [(i, i ^ 1) for i in range(count)])  3.09 us
    pallas_call x1, Pallas kernels, body(): call(functools.partial(plan, face_t, tile_t, tile_p), [(1, count), (n_dev...  2.04 us
    pallas_call x1, Pallas kernels, body(): call(theta_edges, [edge] * 2, [pl.BlockSpec(memory_space=pltpu.HBM)] * 2,...  1.83 us
    pallas_call x1, Pallas kernels, body(): call(functools.partial(route, n_dev), [(4, fields, radial), (2 * n_dev, 1...  1.67 us
  transfers between devices with their start and end apart: 10, of which 3 were waited for; matrix products, arithmetic and copies ran while one was open for 0% of the time, Pallas kernels for 13%

profile of v10, /device:TPU:32, one launch (start us, length us, event | category | flops | bytes accessed | tf_op | source)
XLA Modules:
  0.0 56.9 jit_solution(17245664092799267219)
XLA Ops:
  0.6 0.0 copy-start.1
  0.6 0.0 copy-start
  0.6 1.8 %theta_edges.1 = (f32[9,2,16,128]{3,2,1,0:T(8,128)}, f32[9,2,16,128]{3,2,1,0:T(8,128)}) custom-call(f32[8,16,16,128]{3,2,1,0:T(8,128)} %corona.3, f32[16,16,128]{2,1,0:T(8,128)} %kappa.5), custom_call_target="tpu_custom_call" | custom-call | tf_op jit(solution)/shard_map/theta_edges/pallas_call | solution.py:443
  2.5 1.9 %collective-permute-start = (f32[9,2,16,128]{3,2,1,0:T(8,128)}, f32[9,2,16,128]{3,2,1,0:T(8,128)S(1)}, u32[]{:S(2)}, u32[]{:S(2)}) collective-permute-start(f32[9,2,16,128]{3,2,1,0:T(8,128)} %get-tuple-element.26), channel_id=1, source_target_pairs={{0,32},{32,0},{64,96},{96,64},{128,160},{160,128},{192,224},{224,1... | collective-permute-start | bytes 442376 | tf_op jit(solution)/shard_map/ppermute | solution.py:40
  4.4 2.0 %collective-permute-start.1 = (f32[9,2,16,128]{3,2,1,0:T(8,128)}, f32[9,2,16,128]{3,2,1,0:T(8,128)S(1)}, u32[]{:S(2)}, u32[]{:S(2)}) collective-permute-start(f32[9,2,16,128]{3,2,1,0:T(8,128)} %get-tuple-element.27), channel_id=1, source_target_pairs={{0,224},{32,64},{64,32},{96,128},{128,96},{160,192},{192,160},{224... | collective-permute-start | bytes 442376 | tf_op jit(solution)/shard_map/ppermute | solution.py:39
  6.4 0.0 copy-done.1
  6.4 0.0 copy-done
  6.4 0.0 copy-start.3
  6.4 0.0 copy-start.5
  6.4 0.0 copy-start.6
  6.4 0.1 phi_edges.1
  6.5 0.0 copy-start.4
  6.6 4.2 %collective-permute-start.2 = (f32[9,32,128]{2,1,0:T(8,128)S(1)}, f32[9,32,128]{2,1,0:T(8,128)S(1)}, u32[]{:S(2)}, u32[]{:S(2)}) collective-permute-start(f32[9,32,128]{2,1,0:T(8,128)S(1)} %get-tuple-element.31), channel_id=1, source_target_pairs={{0,31},{1,2},{2,1},{3,4},{4,3},{5,6},{6,5},{7,8},{8,7},{9,10},{10,... | collective-permute-start | bytes 442376 | tf_op jit(solution)/shard_map/ppermute | solution.py:39
  10.7 0.0 collective-permute-start.3
  10.7 0.0 copy-done.3
  10.7 0.0 copy-done.5
  10.7 0.0 copy-done.6
  10.8 0.0 copy-done.4
  10.8 2.0 %plan.1 = (f32[1,2048]{1,0:T(1,128)S(1)}, f32[256,128]{1,0:T(8,128)S(1)}, bf16[256,2048]{1,0:T(8,128)(2,1)S(1)}, bf16[256,2048]{1,0:T(8,128)(2,1)S(1)}, bf16[256...) custom-call(s32[1,2048]{1,0:T(1,128)S(1)} %bitcast.15, s32[1,2048]{1,0:T(1,128)S(1)} %bitcast.16, s32[1,2048]{1,0:T(1,128)S(1)} %bitcast.17, ...), custom_call_target="tpu_custom_call" | custom-call | tf_op jit(solution)/shard_map/plan/pallas_call | solution.py:460
  12.8 0.0 collective-permute-done.t_first
  12.8 0.0 collective-permute-done.1.t_second
  12.8 0.0 copy-start.7
  12.9 1.4 %collective-permute-start.4 = (f32[2,9,128]{2,1,0:T(8,128)S(1)}, f32[2,9,128]{2,1,0:T(8,128)S(1)}, u32[]{:S(2)}, u32[]{:S(2)}) collective-permute-start(f32[2,9,128]{2,1,0:T(8,128)S(1)} %get-tuple-element.35), channel_id=1, source_target_pairs={{0,31},{1,2},{2,1},{3,4},{4,3},{5,6},{6,5},{7,8},{8,7},{9,10},{10,... | collective-permute-start | bytes 27656 | tf_op jit(solution)/shard_map/ppermute | solution.py:39
  14.3 0.0 collective-permute-start.5
  14.3 0.2 collective-permute-done.2.p_second
  14.5 0.0 collective-permute-done.3.p_first
  14.5 0.0 copy-done.7
  14.5 4.1 %steps.1 = f32[8,16,16,128]{3,2,1,0:T(8,128)S(1)} custom-call(f32[8,8]{1,0:T(8,128)S(1)} %copy-done.7, f32[8,16,16,128]{3,2,1,0:T(8,128)S(1)} %copy-done, f32[16,16,128]{2,1,0:T(8,128)S(1)} %copy-done.1, f32[9,2,16,128]{3,2,1,0:T(8,128)S(1)} %collective-permute-done.t_first, f32[9,2,16,128]{3,2,1,0:T(8,128)S(1)} %collective-permute-done.1.t_second, ...), custom_call_target="tpu_custom_call" | custom-call | tf_op jit(solution)/shard_map/steps/pallas_call | solution.py:475
  18.7 0.8 %collective-permute-done.4.c_second = f32[2,9,128]{2,1,0:T(8,128)S(1)} collective-permute-done((f32[2,9,128]{2,1,0:T(8,128)S(1)}, f32[2,9,128]{2,1,0:T(8,128)S(1)}, u32[]{:S(2)}, u32[]{:S(2)}) %collective-permute-start.4) | collective-permute-done | bytes 9248 | tf_op jit(solution)/shard_map/ppermute | solution.py:39
  19.5 0.0 collective-permute-done.5.c_first
  19.5 1.7 %route.1 = (f32[4,8,128]{2,1,0:T(8,128)S(1)}, f32[512,128]{1,0:T(8,128)S(1)}) custom-call(f32[16,16,128]{2,1,0:T(8,128)S(1)} %copy-done.1, f32[9,32,128]{2,1,0:T(8,128)S(1)} %collective-permute-done.3.p_first, f32[9,32,128]{2,1,0:T(8,128)S(1)} %collective-permute-done.2.p_second, f32[2,9,128]{2,1,0:T(8,128)S(1)} %get-tuple-element.33.own_low, ...), custom_call_target="tpu_custom_call" | custom-call | tf_op jit(solution)/shard_map/route/pallas_call | solution.py:488
  21.1 0.0 copy-start.2
  21.2 25.6 %all_to_all.11 = f32[256,2,128]{2,1,0:T(2,128)S(1)} all-to-all(f32[256,2,128]{2,1,0:T(2,128)S(1)} %bitcast.14), channel_id=1, replica_groups=mesh['lat'=8,'lon'=32] {'lat','lon'}, dimensions={0} | all-to-all | bytes 524288 | tf_op jit(solution)/shard_map/all_to_all | solution.py:502
  46.7 0.0 copy-done.2
  46.7 1.4 %land.1 = (f32[8,32,128]{2,1,0:T(8,128)S(1)}, f32[16,256]{1,0:T(8,128)S(1)}, f32[16,256]{1,0:T(8,128)S(1)}, f32[8,128]{1,0:T(8,128)S(1)}, f32[8,128]{1,0:T(8,128)S(1)}) custom-call(f32[512,128]{1,0:T(8,128)S(1)} %bitcast.13, f32[8,32,128]{2,1,0:T(8,128)S(1)} %copy-done.2), custom_call_target="tpu_custom_call" | custom-call | tf_op jit(solution)/shard_map/land/pallas_call | solution.py:504
  48.1 1.1 %collective-permute-start.6 = (f32[16,256]{1,0:T(8,128)S(1)}, f32[16,256]{1,0:T(8,128)S(1)}, u32[]{:S(2)}, u32[]{:S(2)}) collective-permute-start(f32[16,256]{1,0:T(8,128)S(1)} %get-tuple-element.46), channel_id=1, source_target_pairs={{0,32},{32,0},{64,96},{96,64},{128,160},{160,128},{192,224},{224,1... | collective-permute-start | bytes 49160 | tf_op jit(solution)/shard_map/ppermute | solution.py:40
  49.3 0.3 collective-permute-start.7
  49.6 0.6 %collective-permute-start.8 = (f32[8,128]{1,0:T(8,128)S(1)}, f32[8,128]{1,0:T(8,128)S(1)}, u32[]{:S(2)}, u32[]{:S(2)}) collective-permute-start(f32[8,128]{1,0:T(8,128)S(1)} %get-tuple-element.48), channel_id=1, source_target_pairs={{0,31},{1,2},{2,1},{3,4},{4,3},{5,6},{6,5},{7,8},{8,7},{9,10},{10,... | collective-permute-start | bytes 12296 | tf_op jit(solution)/shard_map/ppermute | solution.py:39
  50.2 0.0 collective-permute-start.9
  50.3 1.1 %finish.1 = f32[8,256,128]{2,1,0:T(8,128)} custom-call(f32[8,256,128]{2,1,0:T(8,128)S(1)} %bitcast.10, f32[4,8,128]{2,1,0:T(8,128)S(1)} %get-tuple-element.43.patch), custom_call_target="tpu_custom_call" | custom-call | tf_op jit(solution)/shard_map/finish/pallas_call | solution.py:498
  51.3 4.6 %collective-permute-done.8.p_second = f32[8,128]{1,0:T(8,128)S(1)} collective-permute-done((f32[8,128]{1,0:T(8,128)S(1)}, f32[8,128]{1,0:T(8,128)S(1)}, u32[]{:S(2)}, u32[]{:S(2)}) %collective-permute-start.8) | collective-permute-done | bytes 4128 | tf_op jit(solution)/shard_map/ppermute | solution.py:39
  55.9 0.0 collective-permute-done.9.p_first
  55.9 0.0 collective-permute-done.6.t_first
  55.9 0.0 collective-permute-done.7.t_second
  56.0 0.9 %smooth.1 = f32[8,32,128]{2,1,0:T(8,128)} custom-call(f32[8,32,128]{2,1,0:T(8,128)S(1)} %get-tuple-element.45.coupled, f32[16,256]{1,0:T(8,128)S(1)} %collective-permute-done.6.t_first, f32[16,256]{1,0:T(8,128)S(1)} %collective-permute-done.7.t_second, f32[8,128]{1,0:T(8,128)S(1)} %collective-permute-done.8.p_second, f32[8,128]{1,0:T(8,128)S(1)} %collective-permute-done.9.p_first), custom_call_target="tpu_custom_call" | custom-call | tf_op jit(solution)/shard_map/smooth/pallas_call | solution.py:512
  (1 shorter events, 0.0 us)
Async XLA Ops:
  0.6 5.8 %copy-start.1 = (f32[16,16,128]{2,1,0:T(8,128)S(1)}, f32[16,16,128]{2,1,0:T(8,128)}, u32[]{:S(2)}) copy-start(f32[16,16,128]{2,1,0:T(8,128)} %kappa.5) | copy-start | bytes 393220
  0.6 5.8 %copy-start = (f32[8,16,16,128]{3,2,1,0:T(8,128)S(1)}, f32[8,16,16,128]{3,2,1,0:T(8,128)}, u32[]{:S(2)}) copy-start(f32[8,16,16,128]{3,2,1,0:T(8,128)} %corona.3) | copy-start | bytes 3145732
  2.5 10.3 %collective-permute-start = (f32[9,2,16,128]{3,2,1,0:T(8,128)}, f32[9,2,16,128]{3,2,1,0:T(8,128)S(1)}, u32[]{:S(2)}, u32[]{:S(2)}) collective-permute-start(f32[9,2,16,128]{3,2,1,0:T(8,128)} %get-tuple-element.26), channel_id=1, source_target_pairs={{0,32},{32,0},{64,96},{96,64},{128,160},{160,128},{192,224},{224,1... | collective-permute-start | bytes 442376 | tf_op jit(solution)/shard_map/ppermute | solution.py:40
  4.4 8.4 %collective-permute-start.1 = (f32[9,2,16,128]{3,2,1,0:T(8,128)}, f32[9,2,16,128]{3,2,1,0:T(8,128)S(1)}, u32[]{:S(2)}, u32[]{:S(2)}) collective-permute-start(f32[9,2,16,128]{3,2,1,0:T(8,128)} %get-tuple-element.27), channel_id=1, source_target_pairs={{0,224},{32,64},{64,32},{96,128},{128,96},{160,192},{192,160},{224... | collective-permute-start | bytes 442376 | tf_op jit(solution)/shard_map/ppermute | solution.py:39
  6.4 4.3 %copy-start.3 = (f32[3,2048]{1,0:T(4,128)S(1)}, f32[3,2048]{1,0:T(4,128)}, u32[]{:S(2)}) copy-start(f32[3,2048]{1,0:T(4,128)} %frac.1) | copy-start | bytes 73732
  6.4 4.3 %copy-start.5 = (s32[2048]{0:T(1024)S(1)}, s32[2048]{0:T(1024)}, u32[]{:S(2)}) copy-start(s32[2048]{0:T(1024)} %param.13) | copy-start | bytes 24580
  6.4 4.3 %copy-start.6 = (s32[2048]{0:T(1024)S(1)}, s32[2048]{0:T(1024)}, u32[]{:S(2)}) copy-start(s32[2048]{0:T(1024)} %param.14) | copy-start | bytes 24580
  6.5 4.2 %copy-start.4 = (s32[2048,1]{0,1:T(1,128)S(1)}, s32[2048,1]{0,1:T(1,128)}, u32[]{:S(2)}) copy-start(s32[2048,1]{0,1:T(1,128)} %param.12) | copy-start | bytes 24580
  6.6 8.0 %collective-permute-start.2 = (f32[9,32,128]{2,1,0:T(8,128)S(1)}, f32[9,32,128]{2,1,0:T(8,128)S(1)}, u32[]{:S(2)}, u32[]{:S(2)}) collective-permute-start(f32[9,32,128]{2,1,0:T(8,128)S(1)} %get-tuple-element.31), channel_id=1, source_target_pairs={{0,31},{1,2},{2,1},{3,4},{4,3},{5,6},{6,5},{7,8},{8,7},{9,10},{10,... | collective-permute-start | bytes 442376 | tf_op jit(solution)/shard_map/ppermute | solution.py:39
  10.7 3.8 %collective-permute-start.3 = (f32[9,32,128]{2,1,0:T(8,128)S(1)}, f32[9,32,128]{2,1,0:T(8,128)S(1)}, u32[]{:S(2)}, u32[]{:S(2)}) collective-permute-start(f32[9,32,128]{2,1,0:T(8,128)S(1)} %get-tuple-element.32), channel_id=1, source_target_pairs={{0,1},{1,0},{2,3},{3,2},{4,5},{5,4},{6,7},{7,6},{8,9},{9,8},{10,11... | collective-permute-start | bytes 442376 | tf_op jit(solution)/shard_map/ppermute | solution.py:40
  12.8 1.7 %copy-start.7 = (f32[8,8]{1,0:T(8,128)S(1)}, f32[8,8]{1,0:T(8,128)}, u32[]{:S(2)}) copy-start(f32[8,8]{1,0:T(8,128)} %mixing.1) | copy-start | bytes 772
  12.9 6.6 %collective-permute-start.4 = (f32[2,9,128]{2,1,0:T(8,128)S(1)}, f32[2,9,128]{2,1,0:T(8,128)S(1)}, u32[]{:S(2)}, u32[]{:S(2)}) collective-permute-start(f32[2,9,128]{2,1,0:T(8,128)S(1)} %get-tuple-element.35), channel_id=1, source_target_pairs={{0,31},{1,2},{2,1},{3,4},{4,3},{5,6},{6,5},{7,8},{8,7},{9,10},{10,... | collective-permute-start | bytes 27656 | tf_op jit(solution)/shard_map/ppermute | solution.py:39
  14.3 5.2 %collective-permute-start.5 = (f32[2,9,128]{2,1,0:T(8,128)S(1)}, f32[2,9,128]{2,1,0:T(8,128)S(1)}, u32[]{:S(2)}, u32[]{:S(2)}) collective-permute-start(f32[2,9,128]{2,1,0:T(8,128)S(1)} %get-tuple-element.36), channel_id=1, source_target_pairs={{0,1},{1,0},{2,3},{3,2},{4,5},{5,4},{6,7},{7,6},{8,9},{9,8},{10,11... | collective-permute-start | bytes 27656 | tf_op jit(solution)/shard_map/ppermute | solution.py:40
  21.1 25.6 %copy-start.2 = (f32[8,32,128]{2,1,0:T(8,128)S(1)}, f32[8,32,128]{2,1,0:T(8,128)}, u32[]{:S(2)}) copy-start(f32[8,32,128]{2,1,0:T(8,128)} %prev.1) | copy-start | bytes 393220
  48.1 7.8 %collective-permute-start.6 = (f32[16,256]{1,0:T(8,128)S(1)}, f32[16,256]{1,0:T(8,128)S(1)}, u32[]{:S(2)}, u32[]{:S(2)}) collective-permute-start(f32[16,256]{1,0:T(8,128)S(1)} %get-tuple-element.46), channel_id=1, source_target_pairs={{0,32},{32,0},{64,96},{96,64},{128,160},{160,128},{192,224},{224,1... | collective-permute-start | bytes 49160 | tf_op jit(solution)/shard_map/ppermute | solution.py:40
  49.3 6.7 %collective-permute-start.7 = (f32[16,256]{1,0:T(8,128)S(1)}, f32[16,256]{1,0:T(8,128)S(1)}, u32[]{:S(2)}, u32[]{:S(2)}) collective-permute-start(f32[16,256]{1,0:T(8,128)S(1)} %get-tuple-element.47), channel_id=1, source_target_pairs={{0,224},{32,64},{64,32},{96,128},{128,96},{160,192},{192,160},{224... | collective-permute-start | bytes 49160 | tf_op jit(solution)/shard_map/ppermute | solution.py:39
  49.6 6.4 %collective-permute-start.8 = (f32[8,128]{1,0:T(8,128)S(1)}, f32[8,128]{1,0:T(8,128)S(1)}, u32[]{:S(2)}, u32[]{:S(2)}) collective-permute-start(f32[8,128]{1,0:T(8,128)S(1)} %get-tuple-element.48), channel_id=1, source_target_pairs={{0,31},{1,2},{2,1},{3,4},{4,3},{5,6},{6,5},{7,8},{8,7},{9,10},{10,... | collective-permute-start | bytes 12296 | tf_op jit(solution)/shard_map/ppermute | solution.py:39
  50.2 5.7 %collective-permute-start.9 = (f32[8,128]{1,0:T(8,128)S(1)}, f32[8,128]{1,0:T(8,128)S(1)}, u32[]{:S(2)}, u32[]{:S(2)}) collective-permute-start(f32[8,128]{1,0:T(8,128)S(1)} %get-tuple-element.49), channel_id=1, source_target_pairs={{0,1},{1,0},{2,3},{3,2},{4,5},{5,4},{6,7},{7,6},{8,9},{9,8},{10,11... | collective-permute-start | bytes 12296 | tf_op jit(solution)/shard_map/ppermute | solution.py:40

commit v11 on v10

--- a/solution.py
+++ b/solution.py
@@ -394,8 +394,8 @@
         ("lon", edge(new, 0), edge(new, face_p - 1), p_first, p_second),
     ):
         odd = parity(axis).astype(F32)
-        first[...] = jnp.broadcast_to(blend((odd, 1.0 - odd), low, high), first.shape)
-        second[...] = jnp.broadcast_to(blend((1.0 - odd, odd), low, high), second.shape)
+        first[...] = blend((odd, 1.0 - odd), low, high)
+        second[...] = blend((1.0 - odd, odd), low, high)
 
 
 def smooth(coupled, t_first, t_second, p_second, p_first, out):
@@ -404,7 +404,7 @@
     row = iota((face_p, face_t), 0)[None]
     lane = iota((face_p, face_t), 1)[None]
 
-    t_low, t_high = [blend(w, t_first[0:1], t_second[0:1]) for w in sides("lat")]
+    t_low, t_high = [blend(w, t_first[...], t_second[...]) for w in sides("lat")]
     p_low, p_high = [blend(w, p_first[...], p_second[...]) for w in sides("lon")]
 
     def column(edge):
@@ -503,7 +503,7 @@
 
     coupled, t_first, t_second, p_second, p_first = call(
         functools.partial(land, n_dev),
-        [helio_prev.shape] + [(16, fields * face_p)] * 2 + [(fields, face_t)] * 2,
+        [helio_prev.shape] + [(1, fields * face_p)] * 2 + [(fields, face_t)] * 2,
         [vspec()] * 2,
         "land",
     )(got, helio_prev)

time: 57.1 us -> 57.4 us (level)
  the two profiles are of different devices: /device:TPU:32 before, /device:TPU:8 now
where the time goes in v11:
time: 57.4 us; the launch traced here: 56.3 us
  blocking collectives  24.4 us (43%)
  starting transfers between devices  14 us (24%)
  Pallas kernels  13.2 us (23%)
  waiting for transfers between devices  3.97 us (7%)
  between operations  0.78 us (1%)
    all_to_all x1, blocking collectives, body(): lax.all_to_all(message, ('lat', 'lon'), split_axis=0, concat_axis=0, tile...  24.4 us
    ppermute x5, starting transfers between devices, swapped(): second = lax.ppermute(second, axis, list(enumerate(other)))  11.1 us
    pallas_call x1, Pallas kernels, body(): call(steps, [corona.shape], [sspec()] + [vspec()] * 6, 'steps', [VMEM((fi...  4.14 us
    ppermute x5, starting transfers between devices, swapped(): lax.ppermute(first, axis, [(i, i ^ 1) for i in range(count)])  2.88 us
    ppermute x5, waiting for transfers between devices, swapped(): second = lax.ppermute(second, axis, list(enumerate(other)))  2.57 us
    pallas_call x1, Pallas kernels, body(): call(functools.partial(plan, face_t, tile_t, tile_p), [(1, count), (n_dev...  2.05 us
    pallas_call x1, Pallas kernels, body(): call(theta_edges, [edge] * 2, [pl.BlockSpec(memory_space=pltpu.HBM)] * 2,...  1.83 us
    pallas_call x1, Pallas kernels, body(): call(functools.partial(route, n_dev), [(4, fields, radial), (2 * n_dev, 1...  1.67 us
  transfers between devices with their start and end apart: 10, of which 3 were waited for; matrix products, arithmetic and copies ran while one was open for 0% of the time, Pallas kernels for 13%

profile of v11, /device:TPU:8, one launch (start us, length us, event | category | flops | bytes accessed | tf_op | source)
XLA Modules:
  0.0 56.3 jit_solution(9639477768573821628)
XLA Ops:
  0.6 0.0 copy-start.1
  0.6 0.0 copy-start
  0.6 1.8 %theta_edges.1 = (f32[9,2,16,128]{3,2,1,0:T(8,128)}, f32[9,2,16,128]{3,2,1,0:T(8,128)}) custom-call(f32[8,16,16,128]{3,2,1,0:T(8,128)} %corona.3, f32[16,16,128]{2,1,0:T(8,128)} %kappa.5), custom_call_target="tpu_custom_call" | custom-call | tf_op jit(solution)/shard_map/theta_edges/pallas_call | solution.py:443
  2.5 2.0 %collective-permute-start = (f32[9,2,16,128]{3,2,1,0:T(8,128)}, f32[9,2,16,128]{3,2,1,0:T(8,128)S(1)}, u32[]{:S(2)}, u32[]{:S(2)}) collective-permute-start(f32[9,2,16,128]{3,2,1,0:T(8,128)} %get-tuple-element.26), channel_id=1, source_target_pairs={{0,32},{32,0},{64,96},{96,64},{128,160},{160,128},{192,224},{224,1... | collective-permute-start | bytes 442376 | tf_op jit(solution)/shard_map/ppermute | solution.py:40
  4.5 4.9 %collective-permute-start.1 = (f32[9,2,16,128]{3,2,1,0:T(8,128)}, f32[9,2,16,128]{3,2,1,0:T(8,128)S(1)}, u32[]{:S(2)}, u32[]{:S(2)}) collective-permute-start(f32[9,2,16,128]{3,2,1,0:T(8,128)} %get-tuple-element.27), channel_id=1, source_target_pairs={{0,224},{32,64},{64,32},{96,128},{128,96},{160,192},{192,160},{224... | collective-permute-start | bytes 442376 | tf_op jit(solution)/shard_map/ppermute | solution.py:39
  9.4 0.0 copy-done.1
  9.4 0.0 copy-done
  9.4 0.0 copy-start.3
  9.4 0.0 copy-start.5
  9.4 0.0 copy-start.6
  9.5 0.1 phi_edges.1
  9.6 0.0 copy-start.4
  9.6 1.6 %collective-permute-start.2 = (f32[9,32,128]{2,1,0:T(8,128)S(1)}, f32[9,32,128]{2,1,0:T(8,128)S(1)}, u32[]{:S(2)}, u32[]{:S(2)}) collective-permute-start(f32[9,32,128]{2,1,0:T(8,128)S(1)} %get-tuple-element.31), channel_id=1, source_target_pairs={{0,31},{1,2},{2,1},{3,4},{4,3},{5,6},{6,5},{7,8},{8,7},{9,10},{10,... | collective-permute-start | bytes 442376 | tf_op jit(solution)/shard_map/ppermute | solution.py:39
  11.2 0.1 collective-permute-start.3
  11.3 0.0 copy-done.3
  11.3 0.0 copy-done.5
  11.3 0.0 copy-done.6
  11.3 0.0 copy-done.4
  11.3 2.0 %plan.1 = (f32[1,2048]{1,0:T(1,128)S(1)}, f32[256,128]{1,0:T(8,128)S(1)}, bf16[256,2048]{1,0:T(8,128)(2,1)S(1)}, bf16[256,2048]{1,0:T(8,128)(2,1)S(1)}, bf16[256...) custom-call(s32[1,2048]{1,0:T(1,128)S(1)} %bitcast.15, s32[1,2048]{1,0:T(1,128)S(1)} %bitcast.16, s32[1,2048]{1,0:T(1,128)S(1)} %bitcast.17, ...), custom_call_target="tpu_custom_call" | custom-call | tf_op jit(solution)/shard_map/plan/pallas_call | solution.py:460
  13.3 0.0 collective-permute-done.t_first
  13.4 0.0 collective-permute-done.1.t_second
  13.4 0.0 copy-start.7
  13.4 2.3 %collective-permute-start.4 = (f32[2,9,128]{2,1,0:T(8,128)S(1)}, f32[2,9,128]{2,1,0:T(8,128)S(1)}, u32[]{:S(2)}, u32[]{:S(2)}) collective-permute-start(f32[2,9,128]{2,1,0:T(8,128)S(1)} %get-tuple-element.35), channel_id=1, source_target_pairs={{0,31},{1,2},{2,1},{3,4},{4,3},{5,6},{6,5},{7,8},{8,7},{9,10},{10,... | collective-permute-start | bytes 27656 | tf_op jit(solution)/shard_map/ppermute | solution.py:39
  15.8 0.0 collective-permute-start.5
  15.8 0.6 %collective-permute-done.2.p_second = f32[9,32,128]{2,1,0:T(8,128)S(1)} collective-permute-done((f32[9,32,128]{2,1,0:T(8,128)S(1)}, f32[9,32,128]{2,1,0:T(8,128)S(1)}, u32[]{:S(2)}, u32[]{:S(2)}) %collective-permute-start.2) | collective-permute-done | bytes 147488 | tf_op jit(solution)/shard_map/ppermute | solution.py:39
  16.4 0.0 collective-permute-done.3.p_first
  16.4 0.0 copy-done.7
  16.4 4.1 %steps.1 = f32[8,16,16,128]{3,2,1,0:T(8,128)S(1)} custom-call(f32[8,8]{1,0:T(8,128)S(1)} %copy-done.7, f32[8,16,16,128]{3,2,1,0:T(8,128)S(1)} %copy-done, f32[16,16,128]{2,1,0:T(8,128)S(1)} %copy-done.1, f32[9,2,16,128]{3,2,1,0:T(8,128)S(1)} %collective-permute-done.t_first, f32[9,2,16,128]{3,2,1,0:T(8,128)S(1)} %collective-permute-done.1.t_second, ...), custom_call_target="tpu_custom_call" | custom-call | tf_op jit(solution)/shard_map/steps/pallas_call | solution.py:475
  20.5 0.0 collective-permute-done.4.c_second
  20.5 0.0 collective-permute-done.5.c_first
  20.5 1.7 %route.1 = (f32[4,8,128]{2,1,0:T(8,128)S(1)}, f32[512,128]{1,0:T(8,128)S(1)}) custom-call(f32[16,16,128]{2,1,0:T(8,128)S(1)} %copy-done.1, f32[9,32,128]{2,1,0:T(8,128)S(1)} %collective-permute-done.3.p_first, f32[9,32,128]{2,1,0:T(8,128)S(1)} %collective-permute-done.2.p_second, f32[2,9,128]{2,1,0:T(8,128)S(1)} %get-tuple-element.33.own_low, ...), custom_call_target="tpu_custom_call" | custom-call | tf_op jit(solution)/shard_map/route/pallas_call | solution.py:488
  22.2 0.0 copy-start.2
  22.2 24.4 %all_to_all.11 = f32[256,2,128]{2,1,0:T(2,128)S(1)} all-to-all(f32[256,2,128]{2,1,0:T(2,128)S(1)} %bitcast.14), channel_id=1, replica_groups=mesh['lat'=8,'lon'=32] {'lat','lon'}, dimensions={0} | all-to-all | bytes 524288 | tf_op jit(solution)/shard_map/all_to_all | solution.py:502
  46.6 0.0 copy-done.2
  46.6 1.4 %land.1 = (f32[8,32,128]{2,1,0:T(8,128)S(1)}, f32[1,256]{1,0:T(1,128)S(1)}, f32[1,256]{1,0:T(1,128)S(1)}, f32[8,128]{1,0:T(8,128)S(1)}, f32[8,128]{1,0:T(8,128)S(1)}) custom-call(f32[512,128]{1,0:T(8,128)S(1)} %bitcast.13, f32[8,32,128]{2,1,0:T(8,128)S(1)} %copy-done.2), custom_call_target="tpu_custom_call" | custom-call | tf_op jit(solution)/shard_map/land/pallas_call | solution.py:504
  48.0 1.8 %collective-permute-start.8 = (f32[8,128]{1,0:T(8,128)S(1)}, f32[8,128]{1,0:T(8,128)S(1)}, u32[]{:S(2)}, u32[]{:S(2)}) collective-permute-start(f32[8,128]{1,0:T(8,128)S(1)} %get-tuple-element.48), channel_id=1, source_target_pairs={{0,31},{1,2},{2,1},{3,4},{4,3},{5,6},{6,5},{7,8},{8,7},{9,10},{10,... | collective-permute-start | bytes 12296 | tf_op jit(solution)/shard_map/ppermute | solution.py:39
  49.8 0.0 collective-permute-start.9
  49.8 0.8 %collective-permute-start.6 = (f32[1,256]{1,0:T(1,128)S(1)}, f32[1,256]{1,0:T(1,128)S(1)}, u32[]{:S(2)}, u32[]{:S(2)}) collective-permute-start(f32[1,256]{1,0:T(1,128)S(1)} %get-tuple-element.46), channel_id=1, source_target_pairs={{0,32},{32,0},{64,96},{96,64},{128,160},{160,128},{192,224},{224,1... | collective-permute-start | bytes 3080 | tf_op jit(solution)/shard_map/ppermute | solution.py:40
  50.6 0.3 collective-permute-start.7
  50.9 1.1 %finish.1 = f32[8,256,128]{2,1,0:T(8,128)} custom-call(f32[8,256,128]{2,1,0:T(8,128)S(1)} %bitcast.10, f32[4,8,128]{2,1,0:T(8,128)S(1)} %get-tuple-element.43.patch), custom_call_target="tpu_custom_call" | custom-call | tf_op jit(solution)/shard_map/finish/pallas_call | solution.py:498
  52.0 1.4 %collective-permute-done.6.t_first = f32[1,256]{1,0:T(1,128)S(1)} collective-permute-done((f32[1,256]{1,0:T(1,128)S(1)}, f32[1,256]{1,0:T(1,128)S(1)}, u32[]{:S(2)}, u32[]{:S(2)}) %collective-permute-start.6) | collective-permute-done | bytes 1056 | tf_op jit(solution)/shard_map/ppermute | solution.py:40
  53.4 2.0 %collective-permute-done.7.t_second = f32[1,256]{1,0:T(1,128)S(1)} collective-permute-done((f32[1,256]{1,0:T(1,128)S(1)}, f32[1,256]{1,0:T(1,128)S(1)}, u32[]{:S(2)}, u32[]{:S(2)}) %collective-permute-start.7) | collective-permute-done | bytes 1056 | tf_op jit(solution)/shard_map/ppermute | solution.py:39
  55.4 0.0 collective-permute-done.8.p_second
  55.4 0.0 collective-permute-done.9.p_first
  55.4 0.9 %smooth.1 = f32[8,32,128]{2,1,0:T(8,128)} custom-call(f32[8,32,128]{2,1,0:T(8,128)S(1)} %get-tuple-element.45.coupled, f32[1,256]{1,0:T(1,128)S(1)} %collective-permute-done.6.t_first, f32[1,256]{1,0:T(1,128)S(1)} %collective-permute-done.7.t_second, f32[8,128]{1,0:T(8,128)S(1)} %collective-permute-done.8.p_second, f32[8,128]{1,0:T(8,128)S(1)} %collective-permute-done.9.p_first), custom_call_target="tpu_custom_call" | custom-call | tf_op jit(solution)/shard_map/smooth/pallas_call | solution.py:512
  (1 shorter events, 0.0 us)
Async XLA Ops:
  0.6 8.8 %copy-start.1 = (f32[16,16,128]{2,1,0:T(8,128)S(1)}, f32[16,16,128]{2,1,0:T(8,128)}, u32[]{:S(2)}) copy-start(f32[16,16,128]{2,1,0:T(8,128)} %kappa.5) | copy-start | bytes 393220
  0.6 8.8 %copy-start = (f32[8,16,16,128]{3,2,1,0:T(8,128)S(1)}, f32[8,16,16,128]{3,2,1,0:T(8,128)}, u32[]{:S(2)}) copy-start(f32[8,16,16,128]{3,2,1,0:T(8,128)} %corona.3) | copy-start | bytes 3145732
  2.5 10.9 %collective-permute-start = (f32[9,2,16,128]{3,2,1,0:T(8,128)}, f32[9,2,16,128]{3,2,1,0:T(8,128)S(1)}, u32[]{:S(2)}, u32[]{:S(2)}) collective-permute-start(f32[9,2,16,128]{3,2,1,0:T(8,128)} %get-tuple-element.26), channel_id=1, source_target_pairs={{0,32},{32,0},{64,96},{96,64},{128,160},{160,128},{192,224},{224,1... | collective-permute-start | bytes 442376 | tf_op jit(solution)/shard_map/ppermute | solution.py:40
  4.5 8.9 %collective-permute-start.1 = (f32[9,2,16,128]{3,2,1,0:T(8,128)}, f32[9,2,16,128]{3,2,1,0:T(8,128)S(1)}, u32[]{:S(2)}, u32[]{:S(2)}) collective-permute-start(f32[9,2,16,128]{3,2,1,0:T(8,128)} %get-tuple-element.27), channel_id=1, source_target_pairs={{0,224},{32,64},{64,32},{96,128},{128,96},{160,192},{192,160},{224... | collective-permute-start | bytes 442376 | tf_op jit(solution)/shard_map/ppermute | solution.py:39
  9.4 1.8 %copy-start.3 = (f32[3,2048]{1,0:T(4,128)S(1)}, f32[3,2048]{1,0:T(4,128)}, u32[]{:S(2)}) copy-start(f32[3,2048]{1,0:T(4,128)} %frac.1) | copy-start | bytes 73732
  9.4 1.8 %copy-start.5 = (s32[2048]{0:T(1024)S(1)}, s32[2048]{0:T(1024)}, u32[]{:S(2)}) copy-start(s32[2048]{0:T(1024)} %param.13) | copy-start | bytes 24580
  9.4 1.8 %copy-start.6 = (s32[2048]{0:T(1024)S(1)}, s32[2048]{0:T(1024)}, u32[]{:S(2)}) copy-start(s32[2048]{0:T(1024)} %param.14) | copy-start | bytes 24580
  9.6 1.7 %copy-start.4 = (s32[2048,1]{0,1:T(1,128)S(1)}, s32[2048,1]{0,1:T(1,128)}, u32[]{:S(2)}) copy-start(s32[2048,1]{0,1:T(1,128)} %param.12) | copy-start | bytes 24580
  9.6 6.8 %collective-permute-start.2 = (f32[9,32,128]{2,1,0:T(8,128)S(1)}, f32[9,32,128]{2,1,0:T(8,128)S(1)}, u32[]{:S(2)}, u32[]{:S(2)}) collective-permute-start(f32[9,32,128]{2,1,0:T(8,128)S(1)} %get-tuple-element.31), channel_id=1, source_target_pairs={{0,31},{1,2},{2,1},{3,4},{4,3},{5,6},{6,5},{7,8},{8,7},{9,10},{10,... | collective-permute-start | bytes 442376 | tf_op jit(solution)/shard_map/ppermute | solution.py:39
  11.2 5.2 %collective-permute-start.3 = (f32[9,32,128]{2,1,0:T(8,128)S(1)}, f32[9,32,128]{2,1,0:T(8,128)S(1)}, u32[]{:S(2)}, u32[]{:S(2)}) collective-permute-start(f32[9,32,128]{2,1,0:T(8,128)S(1)} %get-tuple-element.32), channel_id=1, source_target_pairs={{0,1},{1,0},{2,3},{3,2},{4,5},{5,4},{6,7},{7,6},{8,9},{9,8},{10,11... | collective-permute-start | bytes 442376 | tf_op jit(solution)/shard_map/ppermute | solution.py:40
  13.4 3.0 %copy-start.7 = (f32[8,8]{1,0:T(8,128)S(1)}, f32[8,8]{1,0:T(8,128)}, u32[]{:S(2)}) copy-start(f32[8,8]{1,0:T(8,128)} %mixing.1) | copy-start | bytes 772
  13.4 7.1 %collective-permute-start.4 = (f32[2,9,128]{2,1,0:T(8,128)S(1)}, f32[2,9,128]{2,1,0:T(8,128)S(1)}, u32[]{:S(2)}, u32[]{:S(2)}) collective-permute-start(f32[2,9,128]{2,1,0:T(8,128)S(1)} %get-tuple-element.35), channel_id=1, source_target_pairs={{0,31},{1,2},{2,1},{3,4},{4,3},{5,6},{6,5},{7,8},{8,7},{9,10},{10,... | collective-permute-start | bytes 27656 | tf_op jit(solution)/shard_map/ppermute | solution.py:39
  15.8 4.7 %collective-permute-start.5 = (f32[2,9,128]{2,1,0:T(8,128)S(1)}, f32[2,9,128]{2,1,0:T(8,128)S(1)}, u32[]{:S(2)}, u32[]{:S(2)}) collective-permute-start(f32[2,9,128]{2,1,0:T(8,128)S(1)} %get-tuple-element.36), channel_id=1, source_target_pairs={{0,1},{1,0},{2,3},{3,2},{4,5},{5,4},{6,7},{7,6},{8,9},{9,8},{10,11... | collective-permute-start | bytes 27656 | tf_op jit(solution)/shard_map/ppermute | solution.py:40
  22.2 24.4 %copy-start.2 = (f32[8,32,128]{2,1,0:T(8,128)S(1)}, f32[8,32,128]{2,1,0:T(8,128)}, u32[]{:S(2)}) copy-start(f32[8,32,128]{2,1,0:T(8,128)} %prev.1) | copy-start | bytes 393220
  48.0 7.4 %collective-permute-start.8 = (f32[8,128]{1,0:T(8,128)S(1)}, f32[8,128]{1,0:T(8,128)S(1)}, u32[]{:S(2)}, u32[]{:S(2)}) collective-permute-start(f32[8,128]{1,0:T(8,128)S(1)} %get-tuple-element.48), channel_id=1, source_target_pairs={{0,31},{1,2},{2,1},{3,4},{4,3},{5,6},{6,5},{7,8},{8,7},{9,10},{10,... | collective-permute-start | bytes 12296 | tf_op jit(solution)/shard_map/ppermute | solution.py:39
  49.8 5.6 %collective-permute-start.9 = (f32[8,128]{1,0:T(8,128)S(1)}, f32[8,128]{1,0:T(8,128)S(1)}, u32[]{:S(2)}, u32[]{:S(2)}) collective-permute-start(f32[8,128]{1,0:T(8,128)S(1)} %get-tuple-element.49), channel_id=1, source_target_pairs={{0,1},{1,0},{2,3},{3,2},{4,5},{5,4},{6,7},{7,6},{8,9},{9,8},{10,11... | collective-permute-start | bytes 12296 | tf_op jit(solution)/shard_map/ppermute | solution.py:40
  49.8 3.6 %collective-permute-start.6 = (f32[1,256]{1,0:T(1,128)S(1)}, f32[1,256]{1,0:T(1,128)S(1)}, u32[]{:S(2)}, u32[]{:S(2)}) collective-permute-start(f32[1,256]{1,0:T(1,128)S(1)} %get-tuple-element.46), channel_id=1, source_target_pairs={{0,32},{32,0},{64,96},{96,64},{128,160},{160,128},{192,224},{224,1... | collective-permute-start | bytes 3080 | tf_op jit(solution)/shard_map/ppermute | solution.py:40
  50.6 4.8 %collective-permute-start.7 = (f32[1,256]{1,0:T(1,128)S(1)}, f32[1,256]{1,0:T(1,128)S(1)}, u32[]{:S(2)}, u32[]{:S(2)}) collective-permute-start(f32[1,256]{1,0:T(1,128)S(1)} %get-tuple-element.47), channel_id=1, source_target_pairs={{0,224},{32,64},{64,32},{96,128},{128,96},{160,192},{192,160},{224... | collective-permute-start | bytes 3080 | tf_op jit(solution)/shard_map/ppermute | solution.py:39
